TPU v7x, 32 devices: a whole 2x2x4 slice. The times are simulated.
32 devices in a mesh: dp: 4 (over z), ctx: 8 (over y, x, core).
Axes of the slice: x: 2, y: 2, z: 4, core: 2. Of those that a mesh axis runs over, the one named last changes fastest.
Arguments:
- layer_in: bfloat16 [4, 4096, 2048], P('dp', 'ctx'), may hold values from -6 to 6
- positions: int32 [4, 4096], P('dp', 'ctx'), may hold values from 0 to 4095, as said below
- attn_gain: bfloat16 [2048], P(('dp', 'ctx')), may hold values from 0.5 to 1.5
- query_proj: bfloat16 [2048, 2048], P(('dp', 'ctx')), may hold values from -0.125 to 0.125
- key_proj: bfloat16 [2048, 256], P(('dp', 'ctx')), may hold values from -0.125 to 0.125
- value_proj: bfloat16 [2048, 256], P(('dp', 'ctx')), may hold values from -0.125 to 0.125
- merge_proj: bfloat16 [2048, 2048], P(('dp', 'ctx')), may hold values from -1 to 1
- ffn_gain: bfloat16 [2048], P(('dp', 'ctx')), may hold values from 0.5 to 1.5
- gate_proj: bfloat16 [2048, 5632], P(('dp', 'ctx')), may hold values from -0.125 to 0.125
- up_proj: bfloat16 [2048, 5632], P(('dp', 'ctx')), may hold values from -0.125 to 0.125
- down_proj: bfloat16 [5632, 2048], P(('dp', 'ctx')), may hold values from -0.078125 to 0.078125
- out_grad: bfloat16 [4, 4096, 2048], P('dp', 'ctx'), may hold values from -6 to 6
Outputs:
- layer_out: bfloat16 [4, 4096, 2048], P('dp', 'ctx')
- input_grad: bfloat16 [4, 4096, 2048], P('dp', 'ctx')
- attngain_grad: float32 [2048], P(('dp', 'ctx'))
- query_grad: float32 [2048, 2048], P(('dp', 'ctx'))
- key_grad: float32 [2048, 256], P(('dp', 'ctx'))
- value_grad: float32 [2048, 256], P(('dp', 'ctx'))
- merge_grad: float32 [2048, 2048], P(('dp', 'ctx'))
- ffngain_grad: float32 [2048], P(('dp', 'ctx'))
- gate_grad: float32 [2048, 5632], P(('dp', 'ctx'))
- up_grad: float32 [2048, 5632], P(('dp', 'ctx'))
- down_grad: float32 [5632, 2048], P(('dp', 'ctx'))
Inputs may be any that keep to these rules, and one draw needn't show every extreme that they name: Each sequence's row holds every position 0 to 4095 once, in runs of 256 consecutive increasing positions that start at multiples of 256; the order of the runs is drawn per sequence.
All inputs are finite; a program needn't handle non-finite values.
Results may differ from a plain program's by a relative error of at most 0.02.
Values may be sent and summed in bfloat16 or wider, within the bound.
A program may use at most 384 MiB of HBM per device.

v0:
```python
import math

import jax
import jax.numpy as jnp
from jax import lax
from jax.sharding import PartitionSpec as P

HD = 64


EPS = 1e-05
NEG = -1e30


def angles(positions, head_dim):
    half = head_dim // 2
    freq = 10000.0 ** (-(jnp.arange(half, dtype=jnp.float32) * 2.0 / head_dim))
    turned = positions.astype(jnp.float32)[..., None] * freq
    return (jnp.cos(turned)[:, :, None, :], jnp.sin(turned)[:, :, None, :])


def rotate(values, cosine, sine):
    half = values.shape[-1] // 2
    first = values[..., :half]
    second = values[..., half:]
    return jnp.concatenate([first * cosine - second * sine, second * cosine + first * sine], -1)


def unrotate(grads, cosine, sine):
    half = grads.shape[-1] // 2
    first = grads[..., :half]
    second = grads[..., half:]
    return jnp.concatenate([first * cosine + second * sine, second * cosine - first * sine], -1)


def normalize(rows):
    factor = lax.rsqrt(jnp.mean(rows * rows, -1, keepdims=True) + EPS)
    return (rows * factor, factor)


def norm_back(upstream, normed, factor, gain):
    scaled = upstream * gain
    inner = jnp.mean(scaled * normed, -1, keepdims=True)
    return (factor * (scaled - normed * inner), jnp.sum(upstream * normed, 0))


def body(
    layer_in,
    positions,
    attn_gain,
    query_proj,
    key_proj,
    value_proj,
    merge_proj,
    ffn_gain,
    gate_proj,
    up_proj,
    down_proj,
    out_grad,
):
    seqs, length_dev, model_width = layer_in.shape
    row_count = seqs * length_dev
    head_dim = HD
    kv_width = key_proj.shape[1]
    kv_heads = kv_width // head_dim
    head_width = query_proj.shape[1]
    groups = head_width // kv_width
    scale = head_dim ** (-0.5)
    cosine, sine = angles(positions, head_dim)
    gain_one, query_all, key_all, value_all, merge_all = (
        lax.all_gather(attn_gain, ("dp", "ctx"), axis=0, tiled=True),
        lax.all_gather(query_proj, ("dp", "ctx"), axis=0, tiled=True),
        lax.all_gather(key_proj, ("dp", "ctx"), axis=0, tiled=True),
        lax.all_gather(value_proj, ("dp", "ctx"), axis=0, tiled=True),
        lax.all_gather(merge_proj, ("dp", "ctx"), axis=0, tiled=True),
    )
    rows_in = layer_in.astype(jnp.float32).reshape(row_count, model_width)
    normed_one, factor_one = normalize(rows_in)
    first_in = (normed_one * gain_one.astype(jnp.float32)).astype(jnp.bfloat16)
    query_raw = jnp.dot(first_in, query_all, preferred_element_type=jnp.float32)
    key_raw = jnp.dot(first_in, key_all, preferred_element_type=jnp.float32)
    value_raw = jnp.dot(first_in, value_all, preferred_element_type=jnp.float32)
    queries = rotate(query_raw.reshape(seqs, length_dev, kv_heads * groups, head_dim), cosine, sine)
    queries = queries.astype(jnp.bfloat16).reshape(seqs, length_dev, kv_heads, groups, head_dim)
    keys = rotate(key_raw.reshape(seqs, length_dev, kv_heads, head_dim), cosine, sine)
    keys = keys.astype(jnp.bfloat16).reshape(seqs, length_dev, kv_width)
    values = value_raw.astype(jnp.bfloat16).reshape(seqs, length_dev, kv_width)
    start_state = (
        jnp.full((seqs, kv_heads, groups, length_dev), NEG, jnp.float32),
        jnp.zeros((seqs, kv_heads, groups, length_dev), jnp.float32),
        jnp.zeros((seqs, kv_heads, groups, length_dev, head_dim), jnp.float32),
    )
    carry = start_state
    key_piece = lax.all_gather(keys, "ctx", axis=1, tiled=True)
    value_piece = lax.all_gather(values, "ctx", axis=1, tiled=True)
    pos_piece = lax.all_gather(positions, "ctx", axis=1, tiled=True)
    count = key_piece.shape[1]
    fold_width = math.gcd(count, 512)
    steps = count // fold_width
    key_blocks = key_piece.reshape(seqs, steps, fold_width, kv_heads, head_dim).swapaxes(0, 1)
    value_blocks = value_piece.reshape(seqs, steps, fold_width, kv_heads, head_dim).swapaxes(0, 1)
    pos_blocks = pos_piece.reshape(seqs, steps, fold_width).swapaxes(0, 1)

    def one_step(state, blocks):
        running_top, weight_sum, accum = state
        key_part, value_part, pos_part = blocks
        scores = (
            jnp.einsum("sqhgd,skhd->shgqk", queries, key_part, preferred_element_type=jnp.float32)
            * scale
        )
        allowed = positions[:, None, None, :, None] >= pos_part[:, None, None, None, :]
        scores = jnp.where(allowed, scores, NEG)
        new_top = jnp.maximum(running_top, jnp.max(scores, -1))
        probs = jnp.where(allowed, jnp.exp(scores - new_top[..., None]), 0.0)
        decay = jnp.exp(running_top - new_top)
        weight_sum = weight_sum * decay + jnp.sum(probs, -1)
        accum = accum * decay[..., None] + jnp.einsum(
            "shgqk,skhd->shgqd",
            probs.astype(jnp.bfloat16),
            value_part,
            preferred_element_type=jnp.float32,
        )
        return ((new_top, weight_sum, accum), None)

    carry, unused = lax.scan(one_step, carry, (key_blocks, value_blocks, pos_blocks))
    running_top, weight_sum, accum = carry
    log_sum = running_top + jnp.log(weight_sum)
    attended = accum / weight_sum[..., None]
    mixed = attended.transpose(0, 3, 1, 2, 4).reshape(row_count, head_width).astype(jnp.bfloat16)
    middle = rows_in + jnp.dot(mixed, merge_all, preferred_element_type=jnp.float32)
    normed_two, factor_two = normalize(middle)
    gain_two, gate_all, up_all, down_all = (
        lax.all_gather(ffn_gain, ("dp", "ctx"), axis=0, tiled=True),
        lax.all_gather(gate_proj, ("dp", "ctx"), axis=0, tiled=True),
        lax.all_gather(up_proj, ("dp", "ctx"), axis=0, tiled=True),
        lax.all_gather(down_proj, ("dp", "ctx"), axis=0, tiled=True),
    )
    second_in = (normed_two * gain_two.astype(jnp.float32)).astype(jnp.bfloat16)
    gate = jnp.dot(second_in, gate_all, preferred_element_type=jnp.float32)
    lift = jnp.dot(second_in, up_all, preferred_element_type=jnp.float32)
    sigma = jax.nn.sigmoid(gate)
    activated = gate * sigma
    hidden = (activated * lift).astype(jnp.bfloat16)
    result = middle + jnp.dot(hidden, down_all, preferred_element_type=jnp.float32)
    layer_out = result.astype(jnp.bfloat16).reshape(layer_in.shape)
    gain_two, gate_all, up_all, down_all = (
        lax.all_gather(ffn_gain, ("dp", "ctx"), axis=0, tiled=True),
        lax.all_gather(gate_proj, ("dp", "ctx"), axis=0, tiled=True),
        lax.all_gather(up_proj, ("dp", "ctx"), axis=0, tiled=True),
        lax.all_gather(down_proj, ("dp", "ctx"), axis=0, tiled=True),
    )
    grad_rows = out_grad.reshape(row_count, model_width)
    down_term = jnp.einsum("rf,rd->fd", hidden, grad_rows, preferred_element_type=jnp.float32)
    grad_hidden = jnp.einsum("rd,fd->rf", grad_rows, down_all, preferred_element_type=jnp.float32)
    grad_gate = (grad_hidden * lift * sigma * (1.0 + gate * (1.0 - sigma))).astype(jnp.bfloat16)
    grad_lift = (grad_hidden * activated).astype(jnp.bfloat16)
    gate_term = jnp.einsum("rd,rf->df", second_in, grad_gate, preferred_element_type=jnp.float32)
    up_term = jnp.einsum("rd,rf->df", second_in, grad_lift, preferred_element_type=jnp.float32)
    grad_second = jnp.einsum("rf,df->rd", grad_gate, gate_all, preferred_element_type=jnp.float32)
    grad_second = grad_second + jnp.einsum(
        "rf,df->rd", grad_lift, up_all, preferred_element_type=jnp.float32
    )
    grad_norm_two, gain_two_term = norm_back(
        grad_second, normed_two, factor_two, gain_two.astype(jnp.float32)
    )
    grad_middle = grad_rows.astype(jnp.float32) + grad_norm_two
    grad_branch = grad_middle.astype(jnp.bfloat16)
    gain_one, query_all, key_all, value_all, merge_all = (
        lax.all_gather(attn_gain, ("dp", "ctx"), axis=0, tiled=True),
        lax.all_gather(query_proj, ("dp", "ctx"), axis=0, tiled=True),
        lax.all_gather(key_proj, ("dp", "ctx"), axis=0, tiled=True),
        lax.all_gather(value_proj, ("dp", "ctx"), axis=0, tiled=True),
        lax.all_gather(merge_proj, ("dp", "ctx"), axis=0, tiled=True),
    )
    merge_term = jnp.einsum("ra,rd->ad", mixed, grad_branch, preferred_element_type=jnp.float32)
    grad_mixed = jnp.einsum(
        "rd,ad->ra", grad_branch, merge_all, preferred_element_type=jnp.float32
    ).astype(jnp.bfloat16)
    grad_heads = grad_mixed.reshape(seqs, length_dev, kv_heads, groups, head_dim).transpose(
        0, 2, 3, 1, 4
    )
    delta = jnp.sum(grad_heads.astype(jnp.float32) * attended, -1)
    all_keys, all_values, all_pos = (
        lax.all_gather(keys, "ctx", axis=1, tiled=True),
        lax.all_gather(values, "ctx", axis=1, tiled=True),
        lax.all_gather(positions, "ctx", axis=1, tiled=True),
    )
    total_len = all_keys.shape[1]
    width = math.gcd(total_len, 512)
    steps = total_len // width
    key_blocks = all_keys.reshape(seqs, steps, width, kv_heads, head_dim).swapaxes(0, 1)
    value_blocks = all_values.reshape(seqs, steps, width, kv_heads, head_dim).swapaxes(0, 1)
    pos_blocks = all_pos.reshape(seqs, steps, width).swapaxes(0, 1)

    def back_step(query_sum, blocks):
        key_part, value_part, pos_part = blocks
        scores = (
            jnp.einsum("sqhgd,skhd->shgqk", queries, key_part, preferred_element_type=jnp.float32)
            * scale
        )
        allowed = positions[:, None, None, :, None] >= pos_part[:, None, None, None, :]
        probs = jnp.where(allowed, jnp.exp(scores - log_sum[..., None]), 0.0)
        grad_probs = jnp.einsum(
            "shgqd,skhd->shgqk", grad_heads, value_part, preferred_element_type=jnp.float32
        )
        grad_scores = (probs * (grad_probs - delta[..., None])).astype(jnp.bfloat16)
        query_sum = query_sum + jnp.einsum(
            "shgqk,skhd->sqhgd", grad_scores, key_part, preferred_element_type=jnp.float32
        )
        key_part_grad = (
            jnp.einsum(
                "shgqk,sqhgd->skhd", grad_scores, queries, preferred_element_type=jnp.float32
            )
            * scale
        )
        value_part_grad = jnp.einsum(
            "shgqk,shgqd->skhd",
            probs.astype(jnp.bfloat16),
            grad_heads,
            preferred_element_type=jnp.float32,
        )
        joined = jnp.concatenate(
            [
                key_part_grad.reshape(seqs, width, kv_width),
                value_part_grad.reshape(seqs, width, kv_width),
            ],
            -1,
        )
        return (query_sum, joined)

    query_start = jnp.zeros((seqs, length_dev, kv_heads, groups, head_dim), jnp.float32)
    query_sum, kv_parts = lax.scan(back_step, query_start, (key_blocks, value_blocks, pos_blocks))
    kv_terms = kv_parts.swapaxes(0, 1).reshape(seqs, total_len, 2 * kv_width)
    kv_sums = lax.psum_scatter(
        kv_terms.astype(jnp.bfloat16), "ctx", scatter_dimension=1, tiled=True
    ).astype(jnp.float32)
    grad_query = unrotate(
        (query_sum * scale).reshape(seqs, length_dev, kv_heads * groups, head_dim), cosine, sine
    )
    grad_query = grad_query.reshape(row_count, head_width).astype(jnp.bfloat16)
    grad_key = unrotate(
        kv_sums[..., :kv_width].reshape(seqs, length_dev, kv_heads, head_dim), cosine, sine
    )
    grad_key = grad_key.reshape(row_count, kv_width).astype(jnp.bfloat16)
    grad_value = kv_sums[..., kv_width:].reshape(row_count, kv_width).astype(jnp.bfloat16)
    query_term = jnp.einsum("rd,ra->da", first_in, grad_query, preferred_element_type=jnp.float32)
    key_term = jnp.einsum("rd,ra->da", first_in, grad_key, preferred_element_type=jnp.float32)
    value_term = jnp.einsum("rd,ra->da", first_in, grad_value, preferred_element_type=jnp.float32)
    grad_first = jnp.einsum("ra,da->rd", grad_query, query_all, preferred_element_type=jnp.float32)
    grad_first = grad_first + jnp.einsum(
        "ra,da->rd", grad_key, key_all, preferred_element_type=jnp.float32
    )
    grad_first = grad_first + jnp.einsum(
        "ra,da->rd", grad_value, value_all, preferred_element_type=jnp.float32
    )
    grad_norm_one, gain_one_term = norm_back(
        grad_first, normed_one, factor_one, gain_one.astype(jnp.float32)
    )
    input_grad = (grad_middle + grad_norm_one).astype(jnp.bfloat16).reshape(layer_in.shape)
    shares = (
        lax.psum_scatter(gain_one_term, ("dp", "ctx"), scatter_dimension=0, tiled=True),
        lax.psum_scatter(query_term, ("dp", "ctx"), scatter_dimension=0, tiled=True),
        lax.psum_scatter(key_term, ("dp", "ctx"), scatter_dimension=0, tiled=True),
        lax.psum_scatter(value_term, ("dp", "ctx"), scatter_dimension=0, tiled=True),
        lax.psum_scatter(merge_term, ("dp", "ctx"), scatter_dimension=0, tiled=True),
        lax.psum_scatter(gain_two_term, ("dp", "ctx"), scatter_dimension=0, tiled=True),
        lax.psum_scatter(gate_term, ("dp", "ctx"), scatter_dimension=0, tiled=True),
        lax.psum_scatter(up_term, ("dp", "ctx"), scatter_dimension=0, tiled=True),
        lax.psum_scatter(down_term, ("dp", "ctx"), scatter_dimension=0, tiled=True),
    )
    return (
        layer_out,
        input_grad,
        shares[0],
        shares[1],
        shares[2],
        shares[3],
        shares[4],
        shares[5],
        shares[6],
        shares[7],
        shares[8],
    )


def solution(mesh):
    placed = (
        P("dp", "ctx", None),
        P("dp", "ctx"),
        P(("dp", "ctx")),
        P(("dp", "ctx"), None),
        P(("dp", "ctx"), None),
        P(("dp", "ctx"), None),
        P(("dp", "ctx"), None),
        P(("dp", "ctx")),
        P(("dp", "ctx"), None),
        P(("dp", "ctx"), None),
        P(("dp", "ctx"), None),
        P("dp", "ctx", None),
    )
    return jax.shard_map(
        body,
        mesh=mesh,
        in_specs=placed,
        out_specs=(
            P("dp", "ctx", None),
            P("dp", "ctx", None),
            P(("dp", "ctx")),
            P(("dp", "ctx"), None),
            P(("dp", "ctx"), None),
            P(("dp", "ctx"), None),
            P(("dp", "ctx"), None),
            P(("dp", "ctx")),
            P(("dp", "ctx"), None),
            P(("dp", "ctx"), None),
            P(("dp", "ctx"), None),
        ),
        check_vma=False,
    )
```

profile of v0, /device:TPU:0, one launch (start us, length us, event | category | flops | bytes accessed | tf_op | source)
XLA Modules:
  0.0 3617.0 jit_solution(545838347991811225)
XLA Ops:
  10.4 42.1 %all-reduce.5 = (bf16[2048]{0:T(1024)(128)(2,1)S(1)}, bf16[2048]{0:T(1024)(128)(2,1)S(1)}) all-reduce(bf16[2048]{0:T(1024)(128)(2,1)S(1)} %dynamic-update-slice, bf16[2048]{0:T(1024)(128)(2,1)S(1)} %dynamic-update-slice.1), channel_id=1, replica_groups=mesh['dp'=4,'ctx'=8] {'dp','ctx'}, use_global_device_ids=true, to_apply=%add | all-reduce | flops 4096 | bytes 16384
  72.5 50.3 %all-gather.17.cloned.1.call-done = bf16[2048,256]{1,0:T(8,128)(2,1)} async-done(((bf16[64,256]{1,0:T(8,128)(2,1)}), bf16[2048,256]{1,0:T(8,128)(2,1)}) %all-gather.17.cloned.1.call-update) | async-done | bytes 1048592 | tf_op jit(solution)/shard_map/all_gather | solution.py:74
  157.0 25.8 all-gather.27.cloned.1.call-done
  196.8 66.2 %all-gather.15.cloned.1.call-done = bf16[2048,2048]{1,0:T(8,128)(2,1)} async-done(((bf16[64,2048]{1,0:T(8,128)(2,1)}), bf16[2048,2048]{1,0:T(8,128)(2,1)}) %all-gather.15.cloned.1.call-update) | async-done | bytes 8388624 | tf_op jit(solution)/shard_map/all_gather | solution.py:72
  283.3 393.4 %while.28 = (s32[]{:T(128)}, f32[1,4,8,512]{3,2,1,0:T(8,128)S(1)}, f32[1,4,8,512]{3,2,1,0:T(8,128)S(1)}, f32[1,4,8,512,64]{3,4,2,1,0:T(8,128)}, s32[1,512]{1,0:T...) while((s32[]{:T(128)}, f32[1,4,8,512]{3,2,1,0:T(8,128)S(1)}, ...), condition=%wide.region_4.5_spmd.clone, body=%wide.region_1.4_spmd.clone.sunk | while | flops 2260041728 | bytes 113778816 | solution.py:125
  408.7 20.9 bitcast_add_fusion.7
  556.9 21.4 bitcast_add_fusion.7
  694.1 19.9 fusion.108
  733.3 45.8 %all-gather.25.cloned.1.call-done = bf16[5632,2048]{1,0:T(8,128)(2,1)} async-done(((bf16[176,2048]{1,0:T(8,128)(2,1)}), bf16[5632,2048]{1,0:T(8,128)(2,1)}) %all-gather.25.cloned.1.call-update) | async-done | bytes 23068688 | tf_op jit(solution)/shard_map/all_gather | solution.py:136
  779.1 28.2 multiply_convert_fusion
  864.5 569.3 %while.29 = (s32[]{:T(128)}, f32[1,512,4,8,64]{1,4,3,2,0:T(8,128)}, bf16[8,1,512,512]{3,2,0,1:T(8,128)(2,1)}, bf16[8,1,512,4,64]{2,4,3,1,0:T(8,128)(2,1)}, s32[1...) while((s32[]{:T(128)}, f32[1,512,4,8,64]{1,4,3,2,0:T(8,128)}, ...), condition=%wide.region_9.10_spmd.clone, body=%wide.region_8.9_spmd.clone.sunk | while | flops 5456265216 | bytes 181608656 | solution.py:232
  880.2 19.7 fusion.182
  1306.6 19.7 fusion.182
  1434.1 49.4 %reduce-scatter.9.cloned.1.call-done = bf16[1,512,512]{2,1,0:T(8,128)(2,1)} async-done(((bf16[1,4096,512]{2,1,0:T(8,128)(2,1)}), bf16[1,512,512]{2,1,0:T(8,128)(2,1)}) %reduce-scatter.9.cloned.1.call-update) | async-done | bytes 524304 | tf_op jit(solution)/shard_map/reduce_scatter | solution.py:234
  1517.0 21.0 fusion.113
  1538.0 21.0 fusion.114
  1560.6 21.0 fusion.75
  1615.3 39.8 %all-reduce.4 = (f32[2048]{0:T(1024)S(1)}, f32[2048]{0:T(1024)S(1)}) all-reduce(f32[2048]{0:T(1024)S(1)} %get-tuple-element.251, f32[2048]{0:T(1024)S(1)} %copy-done.40), channel_id=4, replica_groups=mesh['dp'=4,'ctx'=8] {'dp','ctx'}, use_global_device_ids=true, to_apply=%region_13.14.clone | all-reduce | flops 4096 | bytes 32768
  1662.2 97.4 %reduce-scatter.15.cloned.1.call-done = f32[64,256]{1,0:T(8,128)} async-done(((f32[2048,256]{1,0:T(8,128)}), f32[64,256]{1,0:T(8,128)}) %reduce-scatter.15.cloned.1.call-update) | async-done | bytes 65552 | tf_op jit(solution)/shard_map/reduce_scatter | solution.py:264
  1759.6 181.6 %reduce-scatter.11.cloned.1.call-done = f32[64,2048]{1,0:T(8,128)} async-done(((f32[2048,2048]{1,0:T(8,128)}), f32[64,2048]{1,0:T(8,128)}) %reduce-scatter.11.cloned.1.call-update) | async-done | bytes 524304 | tf_op jit(solution)/shard_map/reduce_scatter | solution.py:262
  1941.3 187.4 %reduce-scatter.17.cloned.1.call-done = f32[64,2048]{1,0:T(8,128)} async-done(((f32[2048,2048]{1,0:T(8,128)}), f32[64,2048]{1,0:T(8,128)}) %reduce-scatter.17.cloned.1.call-update) | async-done | bytes 524304 | tf_op jit(solution)/shard_map/reduce_scatter | solution.py:265
  2128.7 489.6 %reduce-scatter.19.cloned.1.call-done = f32[64,5632]{1,0:T(8,128)} async-done(((f32[2048,5632]{1,0:T(8,128)}), f32[64,5632]{1,0:T(8,128)}) %reduce-scatter.19.cloned.1.call-update) | async-done | bytes 1441808 | tf_op jit(solution)/shard_map/reduce_scatter | solution.py:267
  2618.3 495.9 %reduce-scatter.21.cloned.1.call-done = f32[64,5632]{1,0:T(8,128)} async-done(((f32[2048,5632]{1,0:T(8,128)}), f32[64,5632]{1,0:T(8,128)}) %reduce-scatter.21.cloned.1.call-update) | async-done | bytes 1441808 | tf_op jit(solution)/shard_map/reduce_scatter | solution.py:268
  3114.2 496.0 %reduce-scatter.23.cloned.1.call-done = f32[176,2048]{1,0:T(8,128)} async-done(((f32[5632,2048]{1,0:T(8,128)}), f32[176,2048]{1,0:T(8,128)}) %reduce-scatter.23.cloned.1.call-update) | async-done | bytes 1441808 | tf_op jit(solution)/shard_map/reduce_scatter | solution.py:269
  (338 shorter events, 1140.4 us)
Async XLA Ops:
  7.2 62.4 %copy-start.2 = (bf16[1,512,2048]{2,1,0:T(8,128)(2,1)S(1)}, bf16[1,512,2048]{2,1,0:T(8,128)(2,1)}, u32[]{:S(2)}) copy-start(bf16[1,512,2048]{2,1,0:T(8,128)(2,1)} %param.16) | copy-start | bytes 6291460
  7.2 60.1 %all-gather.11.cloned.1.call-start = ((), (), s32[]{:S(2)}) async-start(), calls=%async_computation.8 | async-start | bytes 1081344 | tf_op jit(solution)/shard_map/all_gather | solution.py:73
  7.9 114.9 %all-gather.17.cloned.1.call-start = ((), (), s32[]{:S(2)}) async-start(), calls=%async_computation.11 | async-start | bytes 1081344 | tf_op jit(solution)/shard_map/all_gather | solution.py:74
  8.7 143.8 %all-gather.13.cloned.1.call-start = ((), (), s32[]{:S(2)}) async-start(), calls=%async_computation.9 | async-start | bytes 2359296 | tf_op jit(solution)/shard_map/all_gather | solution.py:94
  52.6 222.7 %copy-start.32 = (f32[2048]{0:T(1024)}, f32[2048]{0:T(1024)S(1)}, u32[]{:S(2)}) copy-start(f32[2048]{0:T(1024)S(1)} %convert_element_type.161) | copy-start | bytes 24580
  55.4 219.9 %copy-start.37 = (f32[512]{0:T(512)}, f32[512]{0:T(512)S(1)}, u32[]{:S(2)}) copy-start(f32[512]{0:T(512)S(1)} %add_rsqrt_fusion.1) | copy-start | bytes 6148
  55.7 226.7 %copy-start.20 = (f32[512,32]{0,1:T(8,128)}, f32[512,32]{0,1:T(8,128)S(1)}, u32[]{:S(2)}) copy-start(f32[512,32]{0,1:T(8,128)S(1)} %get-tuple-element.312) | copy-start | bytes 196612
  55.7 226.7 %copy-start.22 = (f32[512,32]{0,1:T(8,128)}, f32[512,32]{0,1:T(8,128)S(1)}, u32[]{:S(2)}) copy-start(f32[512,32]{0,1:T(8,128)S(1)} %get-tuple-element.313) | copy-start | bytes 196612
  72.4 56.6 %copy-start.29 = (s32[1,512]{1,0:T(1,128)S(1)}, s32[1,512]{1,0:T(1,128)}, u32[]{:S(2)}) copy-start(s32[1,512]{1,0:T(1,128)} %param.17) | copy-start | bytes 6148
  72.5 110.3 %all-gather.27.cloned.1.call-start = ((), (), s32[]{:S(2)}) async-start(), calls=%async_computation.24 | async-start | bytes 2359296 | tf_op jit(solution)/shard_map/all_gather | solution.py:95
  125.5 137.4 %all-gather.15.cloned.1.call-start = ((), (), s32[]{:S(2)}) async-start(), calls=%async_computation.10 | async-start | bytes 8650752 | tf_op jit(solution)/shard_map/all_gather | solution.py:72
  126.1 555.7 %all-gather.19.cloned.1.call-start = ((), (), s32[]{:S(2)}) async-start(), calls=%async_computation.12 | async-start | bytes 8650752 | tf_op jit(solution)/shard_map/all_gather | solution.py:75
  126.7 567.4 %all-gather.21.cloned.1.call-start = ((), (), s32[]{:S(2)}) async-start(), calls=%async_computation.13 | async-start | bytes 23789568 | tf_op jit(solution)/shard_map/all_gather | solution.py:134
  127.4 586.5 %all-gather.23.cloned.1.call-start = ((), (), s32[]{:S(2)}) async-start(), calls=%async_computation.14 | async-start | bytes 23789568 | tf_op jit(solution)/shard_map/all_gather | solution.py:135
  128.2 650.9 %all-gather.25.cloned.1.call-start = ((), (), s32[]{:S(2)}) async-start(), calls=%async_computation.15 | async-start | bytes 23789568 | tf_op jit(solution)/shard_map/all_gather | solution.py:136
  128.9 1354.5 %reduce-scatter.9.cloned.1.call-start = ((), (), s32[]{:S(2)}) async-start(), calls=%async_computation.16 | async-start | bytes 4718592 | tf_op jit(solution)/shard_map/reduce_scatter | solution.py:234
  1433.8 51.0 %copy-start.38 = (f32[512]{0:T(512)S(1)}, f32[512]{0:T(512)}, u32[]{:S(2)}) copy-start(f32[512]{0:T(512)} %copy-done.37) | copy-start | bytes 6148
  1433.8 228.4 %reduce-scatter.13.cloned.1.call-start = ((), (), s32[]{:S(2)}) async-start(), calls=%async_computation.18 | async-start | bytes 2162688 | tf_op jit(solution)/shard_map/reduce_scatter | solution.py:263
  1487.2 272.4 %reduce-scatter.15.cloned.1.call-start = ((), (), s32[]{:S(2)}) async-start(), calls=%async_computation.19 | async-start | bytes 2162688 | tf_op jit(solution)/shard_map/reduce_scatter | solution.py:264
  1489.7 451.6 %reduce-scatter.11.cloned.1.call-start = ((), (), s32[]{:S(2)}) async-start(), calls=%async_computation.17 | async-start | bytes 17301504 | tf_op jit(solution)/shard_map/reduce_scatter | solution.py:262
  1503.5 625.2 %reduce-scatter.17.cloned.1.call-start = ((), (), s32[]{:S(2)}) async-start(), calls=%async_computation.20 | async-start | bytes 17301504 | tf_op jit(solution)/shard_map/reduce_scatter | solution.py:265
  1515.4 1102.8 %reduce-scatter.19.cloned.1.call-start = ((), (), s32[]{:S(2)}) async-start(), calls=%async_computation.21 | async-start | bytes 47579136 | tf_op jit(solution)/shard_map/reduce_scatter | solution.py:267
  1538.0 1576.2 %reduce-scatter.21.cloned.1.call-start = ((), (), s32[]{:S(2)}) async-start(), calls=%async_computation.22 | async-start | bytes 47579136 | tf_op jit(solution)/shard_map/reduce_scatter | solution.py:268
  1559.0 2051.1 %reduce-scatter.23.cloned.1.call-start = ((), (), s32[]{:S(2)}) async-start(), calls=%async_computation.23 | async-start | bytes 47579136 | tf_op jit(solution)/shard_map/reduce_scatter | solution.py:269
  (41 other events, 531.4 us)
Sparse Core Ops, SparseCore 0:
  10.9 56.3 all-gather.10
  70.2 52.5 all-gather.16
  125.3 27.1 all-gather.12
  154.8 27.8 all-gather.26
  185.4 77.4 all-gather.14
  265.6 76.0 all-gather.18
  344.6 143.1 all-gather.20
  490.6 142.7 all-gather.22
  636.3 142.7 all-gather.24
  1434.0 49.4 reduce-scatter.8
  1487.4 136.7 reduce-scatter.12
  1626.8 132.7 reduce-scatter.14
  1762.6 178.6 reduce-scatter.10
  1944.1 184.5 reduce-scatter.16
  2131.5 486.6 reduce-scatter.18
  2621.1 493.0 reduce-scatter.20
  3117.0 493.0 reduce-scatter.22
where the time goes:
time: 3640 us; the launch traced here: 3620 us
  waiting for transfers between devices  2220 us (61%)
  matrix products  1070 us (29%)
  other arithmetic  153 us (4%)
  blocking collectives  90.8 us (2%)
  local copies, waits for them, and re-layouts  65.5 us (2%)
    reduce_scatter x1, waiting for transfers between devices, body(): lax.psum_scatter(down_term, ('dp', 'ctx'), scatter_dimension=0, tiled=True)  496 us
    reduce_scatter x1, waiting for transfers between devices, body(): lax.psum_scatter(up_term, ('dp', 'ctx'), scatter_dimension=0, tiled=True)  496 us
    reduce_scatter x1, waiting for transfers between devices, body(): lax.psum_scatter(gate_term, ('dp', 'ctx'), scatter_dimension=0, tiled=True)  490 us
    reduce_scatter x1, waiting for transfers between devices, body(): lax.psum_scatter(merge_term, ('dp', 'ctx'), scatter_dimension=0, tiled=True)  187 us
    reduce_scatter x1, waiting for transfers between devices, body(): lax.psum_scatter(query_term, ('dp', 'ctx'), scatter_dimension=0, tiled=True)  182 us
    dot_general x8, matrix products, back_step(): jnp.einsum('shgqd,skhd->shgqk', grad_heads, value_part, preferred_element...  158 us
    dot_general x8, matrix products, one_step(): jnp.einsum('shgqk,skhd->shgqd', probs.astype(jnp.bfloat16), value_part, p...  152 us
    reduce_sum x8, other arithmetic, one_step(): weight_sum = weight_sum * decay + jnp.sum(probs, -1)  122 us
  transfers between devices with their start and end apart: 17, of which 13 were waited for; matrix products, arithmetic and copies ran while one was open for 17% of the time, Pallas kernels for 0%

commit v1 on v0

v1 whole, which is shorter than its diff:
```python
import functools

import jax
import jax.numpy as jnp
from jax import lax
from jax.experimental import pallas as pl
from jax.experimental.pallas import tpu as pltpu
from jax.sharding import PartitionSpec as P

HD = 64
EPS = 1e-05
WIDE = 128
MASKED = -1e30
SCALE = HD**-0.5
LOG2E = 1.4426950408889634
TO_LOG2 = SCALE * LOG2E
BOTH = ("dp", "ctx")
F32 = jnp.float32
BF16 = jnp.bfloat16
NT = (((1,), (1,)), ((), ()))
NN = (((1,), (0,)), ((), ()))


def mm(left, right, dims):
    return lax.dot_general(left, right, dims, preferred_element_type=F32)


def later_in_run(keys, rows):
    run = rows // 2
    key = lax.broadcasted_iota(jnp.int32, (keys, rows), 0)
    query = lax.broadcasted_iota(jnp.int32, (keys, rows), 1)
    return (key > query) & ((key // run) == (query // run))


def attend_kernel(own_ref, qx_ref, kx_ref, vt_ref, o_ref, lse_ref, turned, *, pair):
    heads, rows, _ = qx_ref.shape
    kv_heads, length, _ = kx_ref.shape
    groups = heads // kv_heads
    own = own_ref[0]
    blocks = length // rows

    def scores(head, group, start):
        return mm(kx_ref[group, pl.ds(start, rows), :], qx_ref[head], NT) * TO_LOG2

    def weigh(probs, group, start):
        return mm(vt_ref[group, :, pl.ds(start, rows)], probs.astype(BF16), NN)

    def some_heads(index, _):
        members = [index * pair + i for i in range(pair)]
        group = members[0] // groups
        start = pl.multiple_of(own * rows, rows)
        blocked = later_in_run(rows, rows)
        state = []
        for head in members:
            s = jnp.where(blocked, MASKED, scores(head, group, start))
            top = jnp.max(s, 0, keepdims=True)
            state.append((top, weigh(jnp.exp2(s - top), group, start)))

        def step(j, state):
            start = pl.multiple_of(lax.rem(own + j, blocks) * rows, rows)
            raw = [scores(head, group, start) for head in members]
            result = []
            for (top, total), s in zip(state, raw):
                new_top = jnp.maximum(top, jnp.max(s, 0, keepdims=True))
                probs = jnp.exp2(s - new_top)
                result.append(
                    (new_top, total * jnp.exp2(top - new_top) + weigh(probs, group, start))
                )
            return result

        state = lax.fori_loop(1, blocks, step, state, unroll=True)
        for i, (head, (top, total)) in enumerate(zip(members, state)):
            weight_sum = total[HD : HD + 1, :]
            turned[i * HD : (i + 1) * HD, :] = total[:HD] / weight_sum
            lse_ref[pl.ds(head, 1), :] = top + jnp.log2(weight_sum)
        column = pl.multiple_of(index * (pair * HD), pair * HD)
        o_ref[:, pl.ds(column, pair * HD)] = turned[...].T
        return 0

    lax.fori_loop(0, heads // pair, some_heads, 0)


def attend(own, qx, kx, vt):
    heads, rows, _ = qx.shape
    length = kx.shape[1]
    pair = 2
    return pl.pallas_call(
        functools.partial(attend_kernel, pair=pair),
        out_shape=(
            jax.ShapeDtypeStruct((rows, heads * HD), F32),
            jax.ShapeDtypeStruct((heads, rows), F32),
        ),
        in_specs=[pl.BlockSpec(memory_space=pltpu.SMEM)]
        + [pl.BlockSpec(memory_space=pltpu.VMEM)] * 3,
        out_specs=(pl.BlockSpec(memory_space=pltpu.VMEM),) * 2,
        scratch_shapes=[pltpu.VMEM((pair * HD, rows), F32)],
        compiler_params=pltpu.CompilerParams(vmem_limit_bytes=48 << 20),
        cost_estimate=pl.CostEstimate(
            flops=16 * heads * rows * length * HD,
            bytes_accessed=2 * (qx.size + kx.size + vt.size) + 4 * rows * heads * HD,
            transcendentals=heads * rows * length,
        ),
        name="attend",
    )(own, qx, kx, vt)


def attend_back_kernel(own_ref, qx_ref, gx_ref, kx_ref, kt_ref, vx_ref, dq_ref, dkv_ref, *, pair):
    heads, rows, _ = qx_ref.shape
    kv_heads, length, _ = kx_ref.shape
    groups = heads // kv_heads
    own = own_ref[0]
    blocks = length // rows

    def kv_head(group, _):
        def block(index, diagonal):
            start = pl.multiple_of(index * rows, rows)

            def some_heads(i, sums):
                key_sum, value_sum = sums
                members = [group * groups + i * pair + t for t in range(pair)]
                key = kx_ref[group, pl.ds(start, rows), :]
                value = vx_ref[group, pl.ds(start, rows), :]
                key_turned = kt_ref[group, :, pl.ds(start, rows)]
                probs = [jnp.exp2(mm(key, qx_ref[h], NT) * TO_LOG2) for h in members]
                if diagonal:
                    blocked = later_in_run(rows, rows)
                    probs = [jnp.where(blocked, 0.0, p) for p in probs]
                slopes = [mm(value, gx_ref[h], NT) for h in members]
                grads = [(p * s).astype(BF16) for p, s in zip(probs, slopes)]
                for h, p, g in zip(members, probs, grads):
                    value_sum = value_sum + mm(p.astype(BF16), gx_ref[h], NN)
                    key_sum = key_sum + mm(g, qx_ref[h], NN)
                    term = mm(key_turned, g, NN)
                    dq_ref[h] = term if diagonal else dq_ref[h] + term
                return key_sum, value_sum

            zero = jnp.zeros((rows, WIDE), F32)
            key_sum, value_sum = lax.fori_loop(0, groups // pair, some_heads, (zero, zero))
            joined = jnp.concatenate([key_sum[:, :HD] * SCALE, value_sum[:, :HD]], 1)
            column = pl.multiple_of(group * WIDE, WIDE)
            dkv_ref[pl.ds(start, rows), pl.ds(column, WIDE)] = joined.astype(BF16)

        block(own, True)

        def rest(j, _):
            block(lax.rem(own + j, blocks), False)
            return 0

        lax.fori_loop(1, blocks, rest, 0)
        return 0

    lax.fori_loop(0, kv_heads, kv_head, 0)


def attend_back(own, qx, gx, kx, kt, vx):
    heads, rows, _ = qx.shape
    kv_heads, length, _ = kx.shape
    return pl.pallas_call(
        functools.partial(attend_back_kernel, pair=4),
        out_shape=(
            jax.ShapeDtypeStruct((heads, HD, rows), F32),
            jax.ShapeDtypeStruct((length, kv_heads * WIDE), BF16),
        ),
        in_specs=[pl.BlockSpec(memory_space=pltpu.SMEM)]
        + [pl.BlockSpec(memory_space=pltpu.VMEM)] * 5,
        out_specs=(pl.BlockSpec(memory_space=pltpu.VMEM),) * 2,
        compiler_params=pltpu.CompilerParams(vmem_limit_bytes=56 << 20),
        cost_estimate=pl.CostEstimate(
            flops=40 * heads * rows * length * HD,
            bytes_accessed=2 * (qx.size + gx.size + kx.size + kt.size + vx.size)
            + 4 * rows * heads * HD
            + 2 * length * kv_heads * WIDE,
            transcendentals=heads * rows * length,
        ),
        name="attend_back",
    )(own, qx, gx, kx, kt, vx)


def angles(positions, head_dim):
    half = head_dim // 2
    freq = 10000.0 ** (-(jnp.arange(half, dtype=F32) * 2.0 / head_dim))
    turned = positions.astype(F32)[..., None] * freq
    return (jnp.cos(turned)[:, None, :], jnp.sin(turned)[:, None, :])


def rotate(values, cosine, sine):
    half = values.shape[-1] // 2
    first = values[..., :half]
    second = values[..., half:]
    return jnp.concatenate([first * cosine - second * sine, second * cosine + first * sine], -1)


def normalize(rows):
    factor = lax.rsqrt(jnp.mean(rows * rows, -1, keepdims=True) + EPS)
    return (rows * factor, factor)


def norm_back(upstream, normed, factor, gain):
    scaled = upstream * gain
    inner = jnp.mean(scaled * normed, -1, keepdims=True)
    return (factor * (scaled - normed * inner), jnp.sum(upstream * normed, 0))


def rounded(values):
    return lax.reduce_precision(values, 8, 7)


def three_parts(values):
    high = rounded(values)
    middle = rounded(values - high)
    low = values - high - middle
    return jnp.stack([high, middle, low], -1).astype(BF16)


def widen(main, extra):
    pad = WIDE - main.shape[-1] - extra.shape[-1]
    return jnp.concatenate(
        [main, extra, jnp.zeros(main.shape[:-1] + (pad,), main.dtype)], -1
    )


def gather(piece):
    return lax.all_gather(piece, BOTH, axis=0, tiled=True)


def ctx_major(columns, n_dp, n_ctx):
    rows, width = columns.shape
    return (
        columns.reshape(rows, n_dp, n_ctx, width // (n_dp * n_ctx))
        .transpose(0, 2, 1, 3)
        .reshape(rows, width)
    )


def scatter(term):
    part = lax.psum_scatter(term, "ctx", scatter_dimension=0, tiled=True)
    return lax.psum_scatter(part, "dp", scatter_dimension=0, tiled=True).astype(F32)


def outer(left, right):
    return lax.dot_general(
        left, right, (((0,), (0,)), ((), ())), preferred_element_type=F32
    ).astype(BF16)


def body(
    n_dp,
    n_ctx,
    layer_in,
    positions,
    attn_gain,
    query_proj,
    key_proj,
    value_proj,
    merge_proj,
    ffn_gain,
    gate_proj,
    up_proj,
    down_proj,
    out_grad,
):
    _, rows, model = layer_in.shape
    kv_width = key_proj.shape[1]
    kv_heads = kv_width // HD
    width = query_proj.shape[1]
    heads = width // HD
    run = rows // 2
    positions = positions[0]
    own = lax.axis_index("ctx")
    own_ref = own.astype(jnp.int32).reshape(1)
    gains = jnp.stack([attn_gain, ffn_gain], -1)
    first_weights = gather(
        jnp.concatenate(
            [query_proj, key_proj, value_proj, widen(gains, gains[:, :0])], 1
        )
    )
    all_pos = lax.all_gather(positions, "ctx", axis=0, tiled=True)
    merge_all = gather(merge_proj)
    gate_all = gather(gate_proj)
    up_all = gather(up_proj)
    down_all = gather(down_proj)
    attn_all = first_weights[:, : width + 2 * kv_width]
    gain_one = first_weights[:, width + 2 * kv_width].astype(F32)
    gain_two = first_weights[:, width + 2 * kv_width + 1].astype(F32)

    cosine, sine = angles(positions, HD)
    rows_in = layer_in.reshape(rows, model).astype(F32)
    normed_one, factor_one = normalize(rows_in)
    first_in = (normed_one * gain_one).astype(BF16)
    raw = mm(first_in, attn_all, NN)
    queries = rotate(raw[:, :width].reshape(rows, heads, HD), cosine, sine).astype(BF16)
    keys = rotate(raw[:, width : width + kv_width].reshape(rows, kv_heads, HD), cosine, sine)
    keys = keys.astype(BF16).reshape(rows, kv_width)
    values = raw[:, width + kv_width :].astype(BF16)
    all_kv = lax.all_gather(jnp.concatenate([keys, values], 1), "ctx", axis=0, tiled=True)
    length = all_kv.shape[0]
    all_keys = all_kv[:, :kv_width].reshape(length, kv_heads, HD)
    all_values = all_kv[:, kv_width:].reshape(length, kv_heads, HD)

    run_starts = positions[::run]
    hidden_keys = all_pos[:, None] >= run_starts[None, :] + run
    bias = jnp.where(hidden_keys, MASKED, 0.0).astype(BF16)
    ones = jnp.ones((length, 3), BF16)
    key_extra = jnp.concatenate([bias, ones], 1)[None]
    kx = widen(
        all_keys.transpose(1, 0, 2), jnp.broadcast_to(key_extra, (kv_heads, length, 5))
    )
    kt = all_keys.transpose(1, 2, 0)
    vx = widen(
        all_values.transpose(1, 0, 2), jnp.broadcast_to(ones[None], (kv_heads, length, 3))
    )
    vt = jnp.concatenate(
        [
            all_values.transpose(1, 2, 0),
            jnp.ones((kv_heads, 1, length), BF16),
            jnp.zeros((kv_heads, 15, length), BF16),
        ],
        1,
    )
    queries = queries.transpose(1, 0, 2)
    in_run = (jnp.arange(rows)[:, None] // run == jnp.arange(2)[None, :]).astype(BF16)
    in_run = jnp.broadcast_to(in_run[None], (heads, rows, 2))
    attended, log_sum = attend(own_ref, widen(queries, in_run), kx, vt)

    mixed = attended.astype(BF16)
    middle = rows_in + mm(mixed, merge_all, NN)
    normed_two, factor_two = normalize(middle)
    second_in = (normed_two * gain_two).astype(BF16)
    gate = mm(second_in, gate_all, NN)
    lift = mm(second_in, up_all, NN)
    sigma = jax.nn.sigmoid(gate)
    activated = gate * sigma
    hidden = (activated * lift).astype(BF16)
    result = middle + mm(hidden, down_all, NN)
    layer_out = result.astype(BF16).reshape(layer_in.shape)

    grad_rows = out_grad.reshape(rows, model)
    down_share = scatter(outer(ctx_major(hidden, n_dp, n_ctx), grad_rows))
    grad_hidden = mm(grad_rows, down_all, NT)
    grad_gate = (grad_hidden * lift * sigma * (1.0 + gate * (1.0 - sigma))).astype(BF16)
    grad_lift = (grad_hidden * activated).astype(BF16)
    second_major = ctx_major(second_in, n_dp, n_ctx)
    gate_share = scatter(outer(second_major, grad_gate))
    up_share = scatter(outer(second_major, grad_lift))
    grad_second = mm(grad_gate, gate_all, NT) + mm(grad_lift, up_all, NT)
    grad_norm_two, gain_two_term = norm_back(grad_second, normed_two, factor_two, gain_two)
    grad_middle = grad_rows.astype(F32) + grad_norm_two
    grad_branch = grad_middle.astype(BF16)
    merge_share = scatter(outer(ctx_major(mixed, n_dp, n_ctx), grad_branch))
    grad_mixed = mm(grad_branch, merge_all, NT).astype(BF16)
    delta = jnp.sum((grad_mixed.astype(F32) * attended).reshape(rows, heads, HD), -1)
    grad_heads = grad_mixed.reshape(rows, heads, HD).transpose(1, 0, 2)
    gx = widen(grad_heads, three_parts(-delta.T))
    qx = widen(queries, jnp.concatenate([in_run, three_parts(log_sum * (-1.0 / TO_LOG2))], -1))
    dq, dkv = attend_back(own_ref, qx, gx, kx, kt, vx)
    dkv = lax.psum_scatter(dkv, "ctx", scatter_dimension=0, tiled=True).astype(F32)
    dkv = dkv.reshape(rows, kv_heads, 2, HD)
    grad_query = rotate(dq.transpose(2, 0, 1) * SCALE, cosine, -sine)
    grad_query = grad_query.reshape(rows, width).astype(BF16)
    grad_key = rotate(dkv[:, :, 0], cosine, -sine).reshape(rows, kv_width).astype(BF16)
    grad_value = dkv[:, :, 1].reshape(rows, kv_width).astype(BF16)
    grads = jnp.concatenate([grad_query, grad_key, grad_value], 1)
    grad_first = mm(grads, attn_all, NT)
    grad_norm_one, gain_one_term = norm_back(grad_first, normed_one, factor_one, gain_one)
    input_grad = (grad_middle + grad_norm_one).astype(BF16).reshape(layer_in.shape)
    gain_terms = jnp.stack([gain_one_term, gain_two_term], -1)
    gain_terms = ctx_major(gain_terms.T, n_dp, n_ctx).T.astype(BF16)
    first_major = ctx_major(first_in, n_dp, n_ctx)
    first_share = scatter(
        jnp.concatenate([outer(first_major, grads), widen(gain_terms, gain_terms[:, :0])], 1)
    )
    edge = width + kv_width
    return (
        layer_out,
        input_grad,
        first_share[:, edge + kv_width],
        first_share[:, :width],
        first_share[:, width:edge],
        first_share[:, edge : edge + kv_width],
        merge_share,
        first_share[:, edge + kv_width + 1],
        gate_share,
        up_share,
        down_share,
    )


def solution(mesh):
    acts = P("dp", "ctx", None)
    rows = P(BOTH, None)
    flat = P(BOTH)
    return jax.shard_map(
        functools.partial(body, mesh.shape["dp"], mesh.shape["ctx"]),
        mesh=mesh,
        in_specs=(acts, P("dp", "ctx"), flat, rows, rows, rows, rows, flat, rows, rows, rows, acts),
        out_specs=(acts, acts, flat, rows, rows, rows, rows, flat, rows, rows, rows),
        check_vma=False,
    )
```

time: 3640 us -> 1900 us (0.52)
  waiting for transfers between devices: 2220 us -> 1040 us
  matrix products: 1070 us -> 246 us
  Pallas kernels: 0 us -> 295 us
  local copies, waits for them, and re-layouts: 65.5 us -> 219 us
  other arithmetic: 153 us -> 67.9 us
  blocking collectives: 90.8 us -> 9.03 us
    reduce_scatter x8 -> x11, waiting for transfers between devices: 2000 us -> 688 us  [the longest x5 483 us: scatter(): part = lax.psum_scatter(term, 'ctx', scatter_dimension=0, tiled=True)]
    dot_general x77 -> x15, matrix products: 1070 us -> 246 us  [the longest x10 167 us: mm(): return lax.dot_general(left, right, dims, preferred_element_type=F32)]
    pallas_call x0 -> x2, Pallas kernels: none -> 295 us  [the longest x1 189 us: attend_back(): pl.pallas_call(functools.partial(attend_back_kernel, pair=4), out_shape=(...]
    all_gather x9 -> x6, waiting for transfers between devices: 214 us -> 351 us  [the longest x5 351 us: gather(): return lax.all_gather(piece, BOTH, axis=0, tiled=True)]
    reduce_sum x9 -> x1, other arithmetic: 126 us -> 2.8 us  [body(): jnp.sum((grad_mixed.astype(F32) * attended).reshape(rows, heads, HD), -1)]
    unnamed x2 -> x0, blocking collectives: 81.9 us -> none
    concatenate x0 -> x13, local copies, waits for them, and re-layouts: none -> 75.7 us  [the longest x7 51.7 us: widen(): jnp.concatenate([main, extra, jnp.zeros(main.shape[:-1] + (pad,), main.dt...]
  transfers between devices with their start and end apart: 17 -> 17, of which waited for: 13 -> 14; matrix products, arithmetic and copies ran while one was open for 17% -> 20% of each run, Pallas kernels for 0% -> 6%
where the time goes in v1:
time: 1900 us; the launch traced here: 1890 us
  waiting for transfers between devices  1040 us (55%)
  Pallas kernels  295 us (16%)
  matrix products  246 us (13%)
  local copies, waits for them, and re-layouts  219 us (12%)
  other arithmetic  67.9 us (4%)
    reduce_scatter x5, waiting for transfers between devices, scatter(): part = lax.psum_scatter(term, 'ctx', scatter_dimension=0, tiled=True)  483 us
    all_gather x5, waiting for transfers between devices, gather(): return lax.all_gather(piece, BOTH, axis=0, tiled=True)  351 us
    reduce_scatter x5, waiting for transfers between devices, scatter(): lax.psum_scatter(part, 'dp', scatter_dimension=0, tiled=True).astype(F32)  202 us
    pallas_call x1, Pallas kernels, attend_back(): pl.pallas_call(functools.partial(attend_back_kernel, pair=4), out_shape=(...  189 us
    dot_general x10, matrix products, mm(): return lax.dot_general(left, right, dims, preferred_element_type=F32)  167 us
    pallas_call x1, Pallas kernels, attend(): pl.pallas_call(functools.partial(attend_kernel, pair=pair), out_shape=(ja...  106 us
    dot_general x5, matrix products, outer(): lax.dot_general(left, right, (((0,), (0,)), ((), ())), preferred_element_...  78.6 us
    concatenate x7, local copies, waits for them, and re-layouts, widen(): jnp.concatenate([main, extra, jnp.zeros(main.shape[:-1] + (pad,), main.dt...  51.7 us
  transfers between devices with their start and end apart: 17, of which 14 were waited for; matrix products, arithmetic and copies ran while one was open for 20% of the time, Pallas kernels for 6%

profile of v1, /device:TPU:0, one launch (start us, length us, event | category | flops | bytes accessed | tf_op | source)
XLA Modules:
  0.0 1894.9 jit_solution(8253129187064577802)
XLA Ops:
  14.5 88.6 %all-gather.8.cloned.1.call-done = bf16[2048,2688]{1,0:T(8,128)(2,1)} async-done(((bf16[64,2688]{1,0:T(8,128)(2,1)}), bf16[2048,2688]{1,0:T(8,128)(2,1)}) %all-gather.8.cloned.1.call-update) | async-done | bytes 11010064 | tf_op jit(solution)/shard_map/all_gather | solution.py:223
  201.0 106.1 %attend.1 = (f32[512,2048]{1,0:T(8,128)}, f32[32,512]{1,0:T(8,128)S(1)}) custom-call(s32[1]{0:T(128)} %bitcast.1.own_ref, bf16[32,512,128]{2,1,0:T(8,128)(2,1)} %maximum_maximum_fusion.qx_ref, bf16[4,4096,128]{2,1,0:T(8,128)(2,1)} %copy.152.kx_ref, bf16[4,80,4096]{2,1,0:T(8,128)(2,1)S(1)} %maximum_maximum_fusion.3.vt_ref), custom_call_target="tpu_custom_call" | custom-call | flops 68719476736 | bytes 15204352 | tf_op jit(solution)/shard_map/attend/pallas_call | solution.py:87
  329.5 24.2 %concatenate.59.qx_ref = bf16[32,512,128]{2,1,0:T(8,128)(2,1)} concatenate(bf16[32,512,64]{2,1,0:T(8,128)(2,1)} %copy-done, bf16[32,512,2]{2,1,0:T(8,128)(2,1)} %copy-done.1, bf16[32,512,1]{2,1,0:T(8,128)(2,1)} %copy.153, bf16[32,512,1]{2,1,0:T(8,128)(2,1)} %copy.154, bf16[32,512,1]{2,1,0:T(8,128)(2,1)} %copy.155, bf16[32,512,59]{2,1,0:T(8,128)(2,1)} %broadcast_in_dim.75), dimensions={2} | concatenate | bytes 8388608 | tf_op jit(solution)/shard_map/concatenate | solution.py:217
  379.1 19.4 %fusion.36 = f32[512,5632]{1,0:T(8,128)} fusion(bf16[512,2048]{1,0:T(8,128)(2,1)S(1)} %multiply_convert_fusion.4, bf16[2048,5632]{1,0:T(8,128)(2,1)} %all-gather.14.cloned.1.call-done), kind=kOutput, calls=%fused_computation.111 | convolution fusion | flops 11811160064 | bytes 36700160 | tf_op jit(solution)/shard_map/dot_general | solution.py:25
  398.6 126.1 %all-gather.16.cloned.1.call-done = bf16[2048,5632]{1,0:T(8,128)(2,1)} async-done(((bf16[64,5632]{1,0:T(8,128)(2,1)}), bf16[2048,5632]{1,0:T(8,128)(2,1)}) %all-gather.16.cloned.1.call-update) | async-done | bytes 23068688 | tf_op jit(solution)/shard_map/all_gather | solution.py:223
  524.6 19.1 %fusion.37 = f32[512,5632]{1,0:T(8,128)} fusion(bf16[512,2048]{1,0:T(8,128)(2,1)S(1)} %multiply_convert_fusion.4, bf16[2048,5632]{1,0:T(8,128)(2,1)} %all-gather.16.cloned.1.call-done), kind=kOutput, calls=%fused_computation.112 | convolution fusion | flops 11811160064 | bytes 36700160 | tf_op jit(solution)/shard_map/dot_general | solution.py:25
  543.7 126.4 %all-gather.18.cloned.1.call-done = bf16[5632,2048]{1,0:T(8,128)(2,1)} async-done(((bf16[176,2048]{1,0:T(8,128)(2,1)}), bf16[5632,2048]{1,0:T(8,128)(2,1)}) %all-gather.18.cloned.1.call-update) | async-done | bytes 23068688 | tf_op jit(solution)/shard_map/all_gather | solution.py:223
  670.1 28.3 %multiply_convert_fusion = (bf16[512,5632]{1,0:T(8,128)(2,1)}, bf16[512,5632]{1,0:T(8,128)(2,1)}, bf16[512,5632]{1,0:T(8,128)(2,1)}) fusion(f32[512,5632]{1,0:T(8,128)} %fusion.36, f32[512,5632]{1,0:T(8,128)} %fusion.37, bf16[5632,2048]{1,0:T(8,128)(2,1)} %all-gather.18.cloned.1.call-done, bf16[1,512,2048]{2,1,0:T(8,128)(2,1)} %param.23), kind=kOutput, calls=%fused_computation.3 | convolution fusion | flops 11854413824 | bytes 65536000 | tf_op jit(solution)/shard_map/dot_general | solution.py:25
  698.4 19.6 %fusion.38 = f32[512,2048]{1,0:T(8,128)} fusion(bf16[512,5632]{1,0:T(8,128)(2,1)} %get-tuple-element.28, bf16[2048,5632]{1,0:T(8,128)(2,1)} %all-gather.14.cloned.1.call-done), kind=kOutput, calls=%fused_computation.113 | convolution fusion | flops 11811160064 | bytes 33030144 | tf_op jit(solution)/shard_map/dot_general | solution.py:25
  718.0 19.4 %multiply_reduce_fusion = (bf16[2048]{0:T(1024)(128)(2,1)}, f32[512]{0:T(512)S(1)}, f32[512,2048]{1,0:T(8,128)S(1)}) fusion(f32[512,2048]{1,0:T(8,128)} %copy-done.8, f32[512]{0:T(512)S(1)} %add_rsqrt_fusion, f32[2048]{0:T(1024)S(1)} %copy-done.20, f32[512,2048]{1,0:T(8,128)} %fusion.38, bf16[512,5632]{1,0:T(8,128)(2,1)} %get-tuple-element.27, ...), kind=kOutput, calls=%fused_computation.29 | convolution fusion | flops 11818498048 | bytes 41435136 | tf_op jit(solution)/shard_map/dot_general | solution.py:25
  778.7 20.8 %concatenate.60.gx_ref = bf16[32,512,128]{2,1,0:T(8,128)(2,1)} concatenate(bf16[32,512,64]{2,1,0:T(8,128)(2,1)} %bitcast.140, bf16[32,512,1]{2,1,0:T(8,128)(2,1)} %copy.159, bf16[32,512,1]{2,1,0:T(8,128)(2,1)} %copy.160, bf16[32,512,1]{2,1,0:T(8,128)(2,1)} %copy.161, bf16[32,512,61]{2,1,0:T(8,128)(2,1)} %broadcast_in_dim.76), dimensions={2} | concatenate | bytes 8388608 | tf_op jit(solution)/shard_map/concatenate | solution.py:217
  799.5 189.0 %attend_back.1 = (f32[32,64,512]{2,1,0:T(8,128)}, bf16[4096,512]{1,0:T(8,128)(2,1)}) custom-call(s32[1]{0:T(128)} %bitcast.1.own_ref, bf16[32,512,128]{2,1,0:T(8,128)(2,1)} %concatenate.59.qx_ref, bf16[32,512,128]{2,1,0:T(8,128)(2,1)} %concatenate.60.gx_ref, bf16[4,4096,128]{2,1,0:T(8,128)(2,1)} %copy.152.kx_ref, bf16[4,64,4096]{2,1,0:T(8,128)(2,1)} %bitcast.143, ...), custom_call_target="tpu_custom_call" | custom-call | flops 171798691840 | bytes 27262976 | tf_op jit(solution)/shard_map/attend_back/pallas_call | solution.py:158
  1088.7 19.5 %convolution_convert_fusion.2 = bf16[2048,5632]{1,0:T(8,128)(2,1)} fusion(bf16[512,2048]{0,1:T(8,128)(2,1)} %bitcast.152, bf16[512,5632]{1,0:T(8,128)(2,1)} %get-tuple-element.28), kind=kOutput, calls=%fused_computation.2 | convolution fusion | flops 11822694400 | bytes 30932992 | tf_op jit(solution)/shard_map/dot_general | solution.py:241
  1108.3 22.0 %convolution_convert_fusion.1 = bf16[2048,5632]{1,0:T(8,128)(2,1)} fusion(bf16[512,2048]{0,1:T(8,128)(2,1)} %bitcast.153, bf16[512,5632]{1,0:T(8,128)(2,1)} %get-tuple-element.27), kind=kOutput, calls=%fused_computation.1 | convolution fusion | flops 11822694400 | bytes 30932992 | tf_op jit(solution)/shard_map/dot_general | solution.py:241
  1145.3 19.6 %convolution_convert_fusion = bf16[5632,2048]{1,0:T(8,128)(2,1)} fusion(bf16[512,5632]{0,1:T(8,128)(2,1)} %bitcast.146, bf16[1,512,2048]{2,1,0:T(8,128)(2,1)} %param.23), kind=kOutput, calls=%fused_computation | convolution fusion | flops 11822694400 | bytes 30932992 | tf_op jit(solution)/shard_map/dot_general | solution.py:241
  1165.7 35.2 %reduce-scatter.14.cloned.1.call-done = bf16[256,2688]{1,0:T(8,128)(2,1)} async-done(((bf16[2048,2688]{1,0:T(8,128)(2,1)}), bf16[256,2688]{1,0:T(8,128)(2,1)}) %reduce-scatter.14.cloned.1.call-update) | async-done | bytes 1376272 | tf_op jit(solution)/shard_map/reduce_scatter | solution.py:236
  1201.0 149.4 %reduce-scatter.22.cloned.1.call-done = bf16[256,5632]{1,0:T(8,128)(2,1)} async-done(((bf16[2048,5632]{1,0:T(8,128)(2,1)}), bf16[256,5632]{1,0:T(8,128)(2,1)}) %reduce-scatter.22.cloned.1.call-update) | async-done | bytes 2883600 | tf_op jit(solution)/shard_map/reduce_scatter | solution.py:236
  1350.5 149.5 %reduce-scatter.26.cloned.1.call-done = bf16[256,5632]{1,0:T(8,128)(2,1)} async-done(((bf16[2048,5632]{1,0:T(8,128)(2,1)}), bf16[256,5632]{1,0:T(8,128)(2,1)}) %reduce-scatter.26.cloned.1.call-update) | async-done | bytes 2883600 | tf_op jit(solution)/shard_map/reduce_scatter | solution.py:236
  1500.0 149.3 %reduce-scatter.30.cloned.1.call-done = bf16[704,2048]{1,0:T(8,128)(2,1)} async-done(((bf16[5632,2048]{1,0:T(8,128)(2,1)}), bf16[704,2048]{1,0:T(8,128)(2,1)}) %reduce-scatter.30.cloned.1.call-update) | async-done | bytes 2883600 | tf_op jit(solution)/shard_map/reduce_scatter | solution.py:236
  1649.4 20.2 %fusion.6 = bf16[1,512,2048]{2,1,0:T(8,128)(2,1)} fusion(f32[512,2048]{1,0:T(8,128)} %copy-done.8, bf16[512,5632]{1,0:T(8,128)(2,1)} %get-tuple-element.29, bf16[5632,2048]{1,0:T(8,128)(2,1)} %all-gather.18.cloned.1.call-done), kind=kOutput, calls=%fused_computation.43 | convolution fusion | flops 11813257216 | bytes 35127296 | tf_op jit(solution)/shard_map/dot_general | solution.py:25
  1680.6 31.4 %reduce-scatter.16.cloned.1.call-done = bf16[64,2688]{1,0:T(8,128)(2,1)} async-done(((bf16[256,2688]{1,0:T(8,128)(2,1)}), bf16[64,2688]{1,0:T(8,128)(2,1)}) %reduce-scatter.16.cloned.1.call-update) | async-done | bytes 344080 | tf_op jit(solution)/shard_map/reduce_scatter | solution.py:237
  1716.9 52.3 %reduce-scatter.24.cloned.1.call-done = bf16[64,5632]{1,0:T(8,128)(2,1)} async-done(((bf16[256,5632]{1,0:T(8,128)(2,1)}), bf16[64,5632]{1,0:T(8,128)(2,1)}) %reduce-scatter.24.cloned.1.call-update) | async-done | bytes 720912 | tf_op jit(solution)/shard_map/reduce_scatter | solution.py:237
  1771.5 55.9 %reduce-scatter.28.cloned.1.call-done = bf16[64,5632]{1,0:T(8,128)(2,1)} async-done(((bf16[256,5632]{1,0:T(8,128)(2,1)}), bf16[64,5632]{1,0:T(8,128)(2,1)}) %reduce-scatter.28.cloned.1.call-update) | async-done | bytes 720912 | tf_op jit(solution)/shard_map/reduce_scatter | solution.py:237
  1829.8 55.9 %reduce-scatter.32.cloned.1.call-done = bf16[176,2048]{1,0:T(8,128)(2,1)} async-done(((bf16[704,2048]{1,0:T(8,128)(2,1)}), bf16[176,2048]{1,0:T(8,128)(2,1)}) %reduce-scatter.32.cloned.1.call-update) | async-done | bytes 720912 | tf_op jit(solution)/shard_map/reduce_scatter | solution.py:237
  (211 shorter events, 332.8 us)
Async XLA Ops:
  7.2 98.3 %copy-start.2 = (bf16[1,512,2048]{2,1,0:T(8,128)(2,1)S(1)}, bf16[1,512,2048]{2,1,0:T(8,128)(2,1)}, u32[]{:S(2)}) copy-start(bf16[1,512,2048]{2,1,0:T(8,128)(2,1)} %param.12) | copy-start | bytes 6291460
  7.2 96.0 %all-gather.8.cloned.1.call-start = ((), (), s32[]{:S(2)}) async-start(), calls=%async_computation.11 | async-start | bytes 11354112 | tf_op jit(solution)/shard_map/all_gather | solution.py:223
  10.7 164.7 %all-gather.10.cloned.1.call-start = ((), (), s32[]{:S(2)}) async-start(), calls=%async_computation.12 | async-start | bytes 4718592 | tf_op jit(solution)/shard_map/all_gather | solution.py:295
  13.6 100.3 %copy-start.23 = (f32[512]{0:T(512)}, f32[512]{0:T(512)S(1)}, u32[]{:S(2)}) copy-start(f32[512]{0:T(512)S(1)} %add_rsqrt_fusion.1) | copy-start | bytes 6148
  14.5 105.6 %copy-start.17 = (f32[512,32]{0,1:T(8,128)}, f32[512,32]{0,1:T(8,128)S(1)}, u32[]{:S(2)}) copy-start(f32[512,32]{0,1:T(8,128)S(1)} %get-tuple-element.54) | copy-start | bytes 196612
  117.6 236.2 %all-gather.12.cloned.1.call-start = ((), (), s32[]{:S(2)}) async-start(), calls=%async_computation.13 | async-start | bytes 8650752 | tf_op jit(solution)/shard_map/all_gather | solution.py:223
  118.3 260.8 %all-gather.14.cloned.1.call-start = ((), (), s32[]{:S(2)}) async-start(), calls=%async_computation.14 | async-start | bytes 23789568 | tf_op jit(solution)/shard_map/all_gather | solution.py:223
  118.9 405.8 %all-gather.16.cloned.1.call-start = ((), (), s32[]{:S(2)}) async-start(), calls=%async_computation.15 | async-start | bytes 23789568 | tf_op jit(solution)/shard_map/all_gather | solution.py:223
  119.5 550.7 %all-gather.18.cloned.1.call-start = ((), (), s32[]{:S(2)}) async-start(), calls=%async_computation.16 | async-start | bytes 23789568 | tf_op jit(solution)/shard_map/all_gather | solution.py:223
  120.0 918.1 %reduce-scatter.12.cloned.1.call-start = ((), (), s32[]{:S(2)}) async-start(), calls=%async_computation.17 | async-start | bytes 4718592 | tf_op jit(solution)/shard_map/reduce_scatter | solution.py:356
  120.2 37.6 %copy-start.15 = (f32[512,32]{1,0:T(8,128)}, f32[512,32]{1,0:T(8,128)S(1)}, u32[]{:S(2)}) copy-start(f32[512,32]{1,0:T(8,128)S(1)} %copy.145) | copy-start | bytes 196612
  364.2 160.5 %copy-start.10 = (bf16[512,2048]{1,0:T(8,128)(2,1)}, bf16[512,2048]{1,0:T(8,128)(2,1)S(1)}, u32[]{:S(2)}) copy-start(bf16[512,2048]{1,0:T(8,128)(2,1)S(1)} %multiply_convert_fusion.4) | copy-start | bytes 6291460
  988.5 176.5 %reduce-scatter.18.cloned.1.call-start = ((), (), s32[]{:S(2)}) async-start(), calls=%async_computation.20 | async-start | bytes 9437184 | tf_op jit(solution)/shard_map/reduce_scatter | solution.py:236
  1003.3 197.7 %reduce-scatter.14.cloned.1.call-start = ((), (), s32[]{:S(2)}) async-start(), calls=%async_computation.18 | async-start | bytes 12386304 | tf_op jit(solution)/shard_map/reduce_scatter | solution.py:236
  1081.2 269.2 %reduce-scatter.22.cloned.1.call-start = ((), (), s32[]{:S(2)}) async-start(), calls=%async_computation.22 | async-start | bytes 25952256 | tf_op jit(solution)/shard_map/reduce_scatter | solution.py:236
  1108.2 391.7 %reduce-scatter.26.cloned.1.call-start = ((), (), s32[]{:S(2)}) async-start(), calls=%async_computation.24 | async-start | bytes 25952256 | tf_op jit(solution)/shard_map/reduce_scatter | solution.py:236
  1130.3 519.0 %reduce-scatter.30.cloned.1.call-start = ((), (), s32[]{:S(2)}) async-start(), calls=%async_computation.26 | async-start | bytes 25952256 | tf_op jit(solution)/shard_map/reduce_scatter | solution.py:236
  1164.9 513.9 %reduce-scatter.20.cloned.1.call-start = ((), (), s32[]{:S(2)}) async-start(), calls=%async_computation.21 | async-start | bytes 1310720 | tf_op jit(solution)/shard_map/reduce_scatter | solution.py:237
  1165.7 546.3 %reduce-scatter.16.cloned.1.call-start = ((), (), s32[]{:S(2)}) async-start(), calls=%async_computation.19 | async-start | bytes 1720320 | tf_op jit(solution)/shard_map/reduce_scatter | solution.py:237
  1201.0 568.2 %reduce-scatter.24.cloned.1.call-start = ((), (), s32[]{:S(2)}) async-start(), calls=%async_computation.23 | async-start | bytes 3604480 | tf_op jit(solution)/shard_map/reduce_scatter | solution.py:237
  1350.4 477.0 %reduce-scatter.28.cloned.1.call-start = ((), (), s32[]{:S(2)}) async-start(), calls=%async_computation.25 | async-start | bytes 3604480 | tf_op jit(solution)/shard_map/reduce_scatter | solution.py:237
  1500.0 385.7 %reduce-scatter.32.cloned.1.call-start = ((), (), s32[]{:S(2)}) async-start(), calls=%async_computation.27 | async-start | bytes 3604480 | tf_op jit(solution)/shard_map/reduce_scatter | solution.py:237
  1649.4 20.2 %copy-start.6 = (f32[512,2048]{1,0:T(8,128)S(1)}, f32[512,2048]{1,0:T(8,128)}, u32[]{:S(2)}) copy-start(f32[512,2048]{1,0:T(8,128)} %copy-done.4) | copy-start | bytes 12582916
  1649.4 20.2 %copy-start.13 = (f32[512,2048]{1,0:T(8,128)S(1)}, f32[512,2048]{1,0:T(8,128)}, u32[]{:S(2)}) copy-start(f32[512,2048]{1,0:T(8,128)} %get-tuple-element.60) | copy-start | bytes 12582916
  (20 other events, 107.9 us)
Sparse Core Ops, SparseCore 0:
  11.5 91.6 all-gather.7
  117.7 35.1 all-gather.9
  155.7 77.4 all-gather.11
  235.9 143.1 all-gather.13
  381.8 142.7 all-gather.15
  527.3 142.7 all-gather.17
  988.6 49.4 reduce-scatter.11
  1042.0 71.2 reduce-scatter.17
  1116.9 84.0 reduce-scatter.13
  1204.4 145.9 reduce-scatter.21
  1354.0 145.8 reduce-scatter.25
  1503.4 145.8 reduce-scatter.29
  1651.6 27.1 reduce-scatter.19
  1681.1 30.8 reduce-scatter.15
  1714.1 55.0 reduce-scatter.23
  1771.4 56.0 reduce-scatter.27
  1829.6 56.0 reduce-scatter.31

commit v2 on v1

v2 whole, which is shorter than its diff:
```python
import functools

import jax
import jax.numpy as jnp
import numpy as np
from jax import lax
from jax.experimental import pallas as pl
from jax.experimental.pallas import tpu as pltpu
from jax.sharding import PartitionSpec as P

HD = 64
EPS = 1e-05
WIDE = 128
MASKED = -1e30
SCALE = HD**-0.5
LOG2E = 1.4426950408889634
TO_LOG2 = SCALE * LOG2E
F32 = jnp.float32
BF16 = jnp.bfloat16
NT = (((1,), (1,)), ((), ()))
NN = (((1,), (0,)), ((), ()))


def mm(left, right, dims):
    return lax.dot_general(left, right, dims, preferred_element_type=F32)


def same_run_later(keys, rows):
    run = rows // 2
    key = lax.broadcasted_iota(jnp.int32, (keys, rows), 0)
    query = lax.broadcasted_iota(jnp.int32, (keys, rows), 1)
    return (key > query) & ((key // run) == (query // run))


def split_heads(pair_ref, which, low_ref, high_ref):
    both = pair_ref[...]
    turned = pltpu.roll(both.astype(F32), HD, 1).astype(BF16)
    lane = lax.broadcasted_iota(jnp.int32, both.shape, 1)
    zero = jnp.zeros_like(both)
    first, second = (both, turned) if which == 0 else (turned, both)
    low_ref[...] = jnp.where(lane < HD, first, zero)
    high_ref[...] = jnp.where(lane < HD, zero, second)


def biased(scores, bias_ref, block, rows):
    run = rows // 2
    start = pl.multiple_of(block * rows, rows)
    parts = [
        scores[i * run : (i + 1) * run] + bias_ref[pl.ds(block * 2 + i, 1), :]
        for i in range(2)
    ]
    return jnp.concatenate(parts, 0)


def attend_kernel(own_ref, bias_ref, q_ref, kp_ref, vt_ref, o_ref, lse_ref, low, high, vx, turned, *, which, unroll):
    rows, width = q_ref.shape
    length = kp_ref.shape[0]
    own = own_ref[0]
    blocks = length // rows
    split_heads(kp_ref, which, low, high)
    vx[:HD, :] = vt_ref[...]
    top_row = lax.broadcasted_iota(jnp.int32, (16, length), 0) == 0
    vx[HD:, :] = top_row.astype(F32).astype(BF16)

    def scores(key, pair, block):
        start = pl.multiple_of(block * rows, rows)
        column = pl.multiple_of(pair * WIDE, WIDE)
        s = mm(key[pl.ds(start, rows), :], q_ref[:, pl.ds(column, WIDE)], NT) * TO_LOG2
        return biased(s, bias_ref, block, rows)

    def weigh(probs, block):
        start = pl.multiple_of(block * rows, rows)
        return mm(vx[:, pl.ds(start, rows)], probs.astype(BF16), NN)

    def one_pair(pair, _):
        blocked = same_run_later(rows, rows)
        state = []
        for key in (low, high):
            s = jnp.where(blocked, MASKED, scores(key, pair, own))
            top = jnp.max(s, 0, keepdims=True)
            state.append((top, weigh(jnp.exp2(s - top), own)))

        def step(j, state):
            block = lax.rem(own + j, blocks)
            raw = [scores(key, pair, block) for key in (low, high)]
            result = []
            for (top, total), s in zip(state, raw):
                new_top = jnp.maximum(top, jnp.max(s, 0, keepdims=True))
                probs = jnp.exp2(s - new_top)
                result.append((new_top, total * jnp.exp2(top - new_top) + weigh(probs, block)))
            return result

        state = lax.fori_loop(1, blocks, step, state, unroll=unroll)
        for i, (top, total) in enumerate(state):
            weight_sum = total[HD : HD + 1, :]
            turned[i * HD : (i + 1) * HD, :] = total[:HD] / weight_sum
            lse_ref[pl.ds(pair * 2 + i, 1), :] = top + jnp.log2(weight_sum)
        column = pl.multiple_of(pair * WIDE, WIDE)
        o_ref[:, pl.ds(column, WIDE)] = turned[...].T
        return 0

    lax.fori_loop(0, width // WIDE, one_pair, 0)


def attend(group, own, bias, q, kv, vt, unroll=True):
    rows, width = q.shape
    length = kv.shape[0]
    kv_heads = vt.shape[0] // HD
    mine = width // kv_heads
    heads = mine // HD
    return pl.pallas_call(
        functools.partial(attend_kernel, which=group % 2, unroll=unroll),
        grid=(1,),
        out_shape=(
            jax.ShapeDtypeStruct((rows, mine), F32),
            jax.ShapeDtypeStruct((heads, rows), F32),
        ),
        in_specs=[
            pl.BlockSpec(memory_space=pltpu.SMEM),
            pl.BlockSpec(bias.shape, lambda i: (0, 0)),
            pl.BlockSpec((rows, mine), lambda i: (0, group)),
            pl.BlockSpec((length, WIDE), lambda i: (0, group // 2)),
            pl.BlockSpec((HD, length), lambda i: (group, 0)),
        ],
        out_specs=(
            pl.BlockSpec((rows, mine), lambda i: (0, 0)),
            pl.BlockSpec((heads, rows), lambda i: (0, 0)),
        ),
        scratch_shapes=[
            pltpu.VMEM((length, WIDE), BF16),
            pltpu.VMEM((length, WIDE), BF16),
            pltpu.VMEM((HD + 16, length), BF16),
            pltpu.VMEM((WIDE, rows), F32),
        ],
        compiler_params=pltpu.CompilerParams(vmem_limit_bytes=40 << 20),
        cost_estimate=pl.CostEstimate(
            flops=16 * heads * rows * length * HD,
            bytes_accessed=2 * (rows * mine + 2 * length * WIDE) + 4 * rows * mine,
            transcendentals=heads * rows * length,
        ),
        name="attend",
    )(own, bias, q, kv, vt)


def attend_back_kernel(
    own_ref, bias_ref, lse_ref, o_ref, q_ref, g_ref, kp_ref, vp_ref, kt_ref,
    dq_ref, dkv_ref, k_low, k_high, v_low, v_high, dqt, delta_ref, *, which, unroll
):
    rows, width = q_ref.shape
    length = kp_ref.shape[0]
    own = own_ref[0]
    blocks = length // rows
    pairs = width // WIDE
    split_heads(kp_ref, which, k_low, k_high)
    split_heads(vp_ref, which, v_low, v_high)
    row = lax.broadcasted_iota(jnp.int32, (16, WIDE), 0)
    lane = lax.broadcasted_iota(jnp.int32, (16, WIDE), 1)
    chosen = (row == lane // HD).astype(F32).astype(BF16)
    for pair in range(pairs):
        column = pl.ds(pair * WIDE, WIDE)
        product = g_ref[:, column].astype(F32) * o_ref[:, column]
        main = product.astype(BF16)
        rest = (product - main.astype(F32)).astype(BF16)
        both = mm(chosen, main, NT) + mm(chosen, rest, NT)
        delta_ref[2 * pair : 2 * pair + 2, :] = both[:2]

    def block(index, diagonal):
        start = pl.multiple_of(index * rows, rows)

        def some_heads(i, sums):
            sums = list(sums)
            work = []
            for t in range(unroll):
                pair = i * unroll + t
                column = pl.multiple_of(pair * WIDE, WIDE)
                query = q_ref[:, pl.ds(column, WIDE)]
                grad = g_ref[:, pl.ds(column, WIDE)]
                for side, (key, value) in enumerate(((k_low, v_low), (k_high, v_high))):
                    head = pair * 2 + side
                    shift = -lse_ref[pl.ds(head, 1), :]
                    run = rows // 2
                    s = mm(key[pl.ds(start, rows), :], query, NT) * TO_LOG2
                    s = jnp.concatenate(
                        [
                            s[r * run : (r + 1) * run]
                            + (bias_ref[pl.ds(index * 2 + r, 1), :] + shift)
                            for r in range(2)
                        ],
                        0,
                    )
                    p = jnp.exp2(s)
                    if diagonal:
                        p = jnp.where(same_run_later(rows, rows), 0.0, p)
                    slope = mm(value[pl.ds(start, rows), :], grad, NT)
                    d = (p * (slope - delta_ref[pl.ds(head, 1), :])).astype(BF16)
                    work.append((side, pair, query, grad, p.astype(BF16), d))
            for side, pair, query, grad, p, d in work:
                sums[side] = sums[side] + mm(d, query, NN)
                sums[2 + side] = sums[2 + side] + mm(p, grad, NN)
                term = mm(kt_ref[:, pl.ds(start, rows)], d, NN)
                row = pl.multiple_of(pair * WIDE + side * HD, HD)
                if diagonal:
                    dqt[pl.ds(row, HD), :] = term
                else:
                    dqt[pl.ds(row, HD), :] += term
            return tuple(sums)

        zero = jnp.zeros((rows, WIDE), F32)
        sums = lax.fori_loop(0, pairs // unroll, some_heads, (zero,) * 4)
        lane = lax.broadcasted_iota(jnp.int32, (rows, WIDE), 1)
        key_sum = sums[0] + pltpu.roll(sums[1], HD, 1)
        value_sum = pltpu.roll(sums[2], HD, 1) + sums[3]
        dkv_ref[pl.ds(start, rows), :] = jnp.where(
            lane < HD, key_sum * SCALE, value_sum
        ).astype(BF16)

    block(own, True)

    def rest(j, _):
        block(lax.rem(own + j, blocks), False)
        return 0

    lax.fori_loop(1, blocks, rest, 0)
    for pair in range(pairs):
        dq_ref[:, pair * WIDE : (pair + 1) * WIDE] = (
            dqt[pair * WIDE : (pair + 1) * WIDE, :] * SCALE
        ).T


def attend_back(group, own, bias, lse, out, q, g, kv, kt, unroll=2):
    rows, width = q.shape
    length = kv.shape[0]
    kv_heads = kt.shape[0] // HD
    mine = width // kv_heads
    heads = mine // HD
    return pl.pallas_call(
        functools.partial(attend_back_kernel, which=group % 2, unroll=unroll),
        grid=(1,),
        out_shape=(
            jax.ShapeDtypeStruct((rows, mine), F32),
            jax.ShapeDtypeStruct((length, WIDE), BF16),
        ),
        in_specs=[
            pl.BlockSpec(memory_space=pltpu.SMEM),
            pl.BlockSpec(bias.shape, lambda i: (0, 0)),
            pl.BlockSpec((heads, rows), lambda i: (0, 0)),
            pl.BlockSpec((rows, mine), lambda i: (0, 0)),
            pl.BlockSpec((rows, mine), lambda i: (0, group)),
            pl.BlockSpec((rows, mine), lambda i: (0, group)),
            pl.BlockSpec((length, WIDE), lambda i: (0, group // 2)),
            pl.BlockSpec((length, WIDE), lambda i: (0, kv_heads // 2 + group // 2)),
            pl.BlockSpec((HD, length), lambda i: (group, 0)),
        ],
        out_specs=(
            pl.BlockSpec((rows, mine), lambda i: (0, 0)),
            pl.BlockSpec((length, WIDE), lambda i: (0, 0)),
        ),
        scratch_shapes=[pltpu.VMEM((length, WIDE), BF16)] * 4
        + [pltpu.VMEM((mine, rows), F32), pltpu.VMEM((heads, rows), F32)],
        compiler_params=pltpu.CompilerParams(vmem_limit_bytes=48 << 20),
        cost_estimate=pl.CostEstimate(
            flops=40 * heads * rows * length * HD,
            bytes_accessed=2 * (2 * rows * mine + 4 * length * WIDE) + 4 * rows * mine,
            transcendentals=heads * rows * length,
        ),
        name="attend_back",
    )(own, bias, lse, out, q, g, kv, kv, kt)


def turn_pairs(x, cosine, sine):
    lane = lax.broadcasted_iota(jnp.int32, x.shape, 1)
    swapped = jnp.where(
        lane % HD < HD // 2, pltpu.roll(x, WIDE - HD // 2, 1), pltpu.roll(x, HD // 2, 1)
    )
    return x * cosine + swapped * sine


def rotate_kernel(cos_ref, sin_ref, raw_ref, q_ref, kv_ref, *, kv_width):
    cosine, sine = cos_ref[...], sin_ref[...]
    width = q_ref.shape[1]
    for at in range(0, width, WIDE):
        q_ref[:, at : at + WIDE] = turn_pairs(raw_ref[:, at : at + WIDE], cosine, sine).astype(BF16)
    for at in range(0, kv_width, WIDE):
        column = slice(width + at, width + at + WIDE)
        kv_ref[:, at : at + WIDE] = turn_pairs(raw_ref[:, column], cosine, sine).astype(BF16)
    kv_ref[:, kv_width:] = raw_ref[:, width + kv_width :].astype(BF16)


def rotated(raw, cosine, sine, kv_width):
    rows, total = raw.shape
    return pl.pallas_call(
        functools.partial(rotate_kernel, kv_width=kv_width),
        out_shape=(
            jax.ShapeDtypeStruct((rows, total - 2 * kv_width), BF16),
            jax.ShapeDtypeStruct((rows, 2 * kv_width), BF16),
        ),
        in_specs=[pl.BlockSpec(memory_space=pltpu.VMEM)] * 3,
        out_specs=(pl.BlockSpec(memory_space=pltpu.VMEM),) * 2,
        compiler_params=pltpu.CompilerParams(vmem_limit_bytes=32 << 20),
        cost_estimate=pl.CostEstimate(
            flops=8 * raw.size, bytes_accessed=6 * raw.size, transcendentals=0
        ),
        name="rotated",
    )(cosine, sine, raw)


def unrotate_kernel(cos_ref, sin_ref, *refs, kv_heads):
    cosine, sine = cos_ref[...], -sin_ref[...]
    dqs, dkvs, out_ref = refs[:kv_heads], refs[kv_heads : 2 * kv_heads], refs[-1]
    mine = dqs[0].shape[1]
    lane = lax.broadcasted_iota(jnp.int32, cosine.shape, 1)
    for group in range(kv_heads):
        for at in range(0, mine, WIDE):
            turned = turn_pairs(dqs[group][:, at : at + WIDE], cosine, sine)
            out_ref[:, group * mine + at : group * mine + at + WIDE] = turned.astype(BF16)
    base = kv_heads * mine
    for i in range(kv_heads // 2):
        first, second = dkvs[2 * i][...].astype(F32), dkvs[2 * i + 1][...].astype(F32)
        keys = jnp.where(lane < HD, first, pltpu.roll(second, HD, 1))
        values = jnp.where(lane < HD, pltpu.roll(first, HD, 1), second)
        at = base + i * WIDE
        out_ref[:, at : at + WIDE] = turn_pairs(keys, cosine, sine).astype(BF16)
        at = base + kv_heads * HD + i * WIDE
        out_ref[:, at : at + WIDE] = values.astype(BF16)


def unrotated(dqs, dkvs, cosine, sine):
    rows, mine = dqs[0].shape
    kv_heads = len(dqs)
    total = kv_heads * (mine + 2 * HD)
    return pl.pallas_call(
        functools.partial(unrotate_kernel, kv_heads=kv_heads),
        out_shape=jax.ShapeDtypeStruct((rows, total), BF16),
        in_specs=[pl.BlockSpec(memory_space=pltpu.VMEM)] * (2 + 2 * kv_heads),
        out_specs=pl.BlockSpec(memory_space=pltpu.VMEM),
        compiler_params=pltpu.CompilerParams(vmem_limit_bytes=32 << 20),
        cost_estimate=pl.CostEstimate(
            flops=8 * rows * total, bytes_accessed=6 * rows * total, transcendentals=0
        ),
        name="unrotated",
    )(cosine, sine, *dqs, *dkvs)


BOTH = ("dp", "ctx")


class Grid:
    def __init__(self, n_dp, n_ctx):
        self.n_dp, self.n_a, self.n_b = n_dp, 2, n_ctx // 4
        self.n_ctx = n_ctx
        self.own = lax.axis_index("ctx").astype(jnp.int32)
        self.a = self.own // (2 * self.n_b)
        self.b = (self.own // 2) % self.n_b
        self.c = self.own % 2

    def size(self, axis):
        return {"a": self.n_a, "b": self.n_b, "c": 2}[axis]

    def next(self, values, axis):
        pairs = []
        for i in range(self.n_ctx):
            a, b, c = i // (2 * self.n_b), (i // 2) % self.n_b, i % 2
            if axis == "a":
                a = (a + 1) % self.n_a
            elif axis == "b":
                b = (b + 1) % self.n_b
            else:
                c = 1 - c
            pairs.append((i, (a * self.n_b + b) * 2 + c))
        return lax.ppermute(values, "ctx", pairs)

    def block_order(self, half_axes, core_major):
        half = self.n_dp // 2
        rows = []
        for core in range(2):
            for h, (first, second) in enumerate(half_axes):
                for i in range(self.size(first)):
                    for j in range(self.size(second)):
                        for d in range(half):
                            near = {first: i, second: j}
                            rows.append((core, h, near["a"], near["b"], h * half + d))
        rows = np.array(rows, np.int32)
        a = (self.a - rows[:, 2]) % self.n_a
        b = (self.b - rows[:, 3]) % self.n_b
        c = (self.c - rows[:, 0]) % 2
        return ((rows[:, 4] * self.n_a + a) * self.n_b + b) * 2 + c


HALVES = (("b", "a"), ("a", "b"))


def turn_kernel(order_ref, x_ref, o_ref, held, *, blk):
    tokens, width = x_ref.shape
    for i in range(width // WIDE):
        held[i * WIDE : (i + 1) * WIDE, :] = x_ref[:, i * WIDE : (i + 1) * WIDE].T

    def move(i, _):
        source = pl.multiple_of(order_ref[i] * blk, blk)
        target = pl.multiple_of(i * blk, blk)
        o_ref[pl.ds(target, blk), :] = held[pl.ds(source, blk), :]
        return 0

    lax.fori_loop(0, width // blk, move, 0)


def turned(x, order):
    tokens, width = x.shape
    blk = width // order.shape[0]
    if blk % 16:
        blocks = jnp.take(x.T.reshape(order.shape[0], blk, tokens), order, axis=0)
        return blocks.reshape(width, tokens)
    return pl.pallas_call(
        functools.partial(turn_kernel, blk=blk),
        out_shape=jax.ShapeDtypeStruct((width, tokens), x.dtype),
        in_specs=[
            pl.BlockSpec(memory_space=pltpu.SMEM),
            pl.BlockSpec(memory_space=pltpu.VMEM),
        ],
        out_specs=pl.BlockSpec(memory_space=pltpu.VMEM),
        scratch_shapes=[pltpu.VMEM((width, tokens), x.dtype)],
        compiler_params=pltpu.CompilerParams(vmem_limit_bytes=32 << 20),
        cost_estimate=pl.CostEstimate(flops=0, bytes_accessed=4 * x.size, transcendentals=0),
        name="turned",
    )(order, x)


def reduce_term(grid, left, right, extra=None):
    rows = left.shape[0]
    mine = rows // 2

    def term(start, size):
        part = mm(left[start : start + size], right, NN)
        if extra is not None:
            part = jnp.concatenate([part, extra[start : start + size].astype(F32)], 1)
        return part

    (arrived,) = yield [grid.next(term(mine, mine).astype(BF16), "c")]
    held = []
    for h, axes in enumerate(HALVES):
        start = h * (mine // 2)
        count = grid.size(axes[0])
        size = mine // 2 // count
        held.append(
            [
                (term(at, size) + arrived[at : at + size].astype(F32)).astype(BF16)
                for at in range(start, start + count * size, size)
            ]
        )
    for step in range(2):
        totals = [None, None]
        counts = [grid.size(axes[step]) for axes in HALVES]
        for k in range(1, max(counts)):
            live = [h for h in range(2) if k < counts[h]]
            sent = [
                grid.next(held[h][1] if k == 1 else totals[h], HALVES[h][step]) for h in live
            ]
            came = yield sent
            for h, part in zip(live, came):
                own = held[h][(k + 1) % counts[h]]
                totals[h] = (part.astype(F32) + own.astype(F32)).astype(BF16)
        if step == 0:
            held = []
            for h, total in enumerate(totals):
                count = grid.size(HALVES[h][1])
                size = total.shape[0] // count
                held.append([total[j * size : (j + 1) * size] for j in range(count)])
    joined = jnp.concatenate(totals, 0)
    (share,) = yield [lax.psum_scatter(joined, "dp", scatter_dimension=0, tiled=True)]
    return share.astype(F32)


def place_kernel(order_ref, *refs, sources, slots):
    pieces = refs[: -(3 + 1)]
    out_ref, held, in_sem, out_sem = refs[-4:]
    count = len(sources)

    def fetch(i):
        piece, place = sources[i]
        return pltpu.make_async_copy(
            pieces[piece].at[place], held.at[i % slots], in_sem.at[i % slots]
        )

    def store(i):
        return pltpu.make_async_copy(
            held.at[i % slots], out_ref.at[order_ref[i]], out_sem.at[i % slots]
        )

    ahead = slots // 2
    for i in range(min(ahead, count)):
        fetch(i).start()
    for i in range(count):
        fetch(i).wait()
        store(i).start()
        later = i + ahead
        if later < count:
            if later >= slots:
                store(later - slots).wait()
            fetch(later).start()
    for i in range(max(0, count - slots), count):
        store(i).wait()


def placed(order, pieces):
    blk, width = pieces[0].shape[-2:]
    flat = [p.reshape((-1, blk, width)) for p in pieces]
    sources = [(n, j) for n, p in enumerate(flat) for j in range(p.shape[0])]
    slots = 8
    whole = pl.pallas_call(
        functools.partial(place_kernel, sources=sources, slots=slots),
        out_shape=jax.ShapeDtypeStruct((len(sources), blk, width), flat[0].dtype),
        in_specs=[pl.BlockSpec(memory_space=pltpu.SMEM)]
        + [pl.BlockSpec(memory_space=pl.ANY)] * len(flat),
        out_specs=pl.BlockSpec(memory_space=pl.ANY),
        scratch_shapes=[
            pltpu.VMEM((slots, blk, width), flat[0].dtype),
            pltpu.SemaphoreType.DMA((slots,)),
            pltpu.SemaphoreType.DMA((slots,)),
        ],
        compiler_params=pltpu.CompilerParams(vmem_limit_bytes=16 << 20),
        cost_estimate=pl.CostEstimate(
            flops=0, bytes_accessed=4 * len(sources) * blk * width, transcendentals=0
        ),
        name="placed",
    )(order, *flat)
    return whole.reshape(len(sources) * blk, width)


def gather_weight(grid, weight, order):
    (column,) = yield [lax.all_gather(weight, "dp", axis=0)]
    half = grid.n_dp // 2
    parts = [column[:half], column[half:]]
    steps = [[parts[0]], [parts[1]]]
    for stage in (1, 0):
        counts = [grid.size(axes[stage]) for axes in HALVES]
        for k in range(1, max(counts)):
            live = [h for h in range(2) if k < counts[h]]
            came = yield [grid.next(steps[h][-1], HALVES[h][stage]) for h in live]
            for h, part in zip(live, came):
                steps[h].append(part)
        if stage == 1:
            steps = [[jnp.stack(s)] for s in steps]
    near = steps[0] + steps[1]
    far = yield [grid.next(piece, "c") for piece in near]
    return placed(order, near + list(far))


class Chain:
    def __init__(self, generator):
        self.generator, self.done, self.result = generator, False, None
        self.flight = next(generator)

    def advance(self, arrived):
        try:
            self.flight = self.generator.send(arrived)
        except StopIteration as stop:
            self.done, self.result, self.flight = True, stop.value, []


def meet(main, *chains):
    chains = [c for c in chains if not c.done]
    main, flights = lax.optimization_barrier((main, [list(c.flight) for c in chains]))
    for chain, flight in zip(chains, flights):
        chain.advance(flight)
    return main


def finish(chain):
    while not chain.done:
        chain.advance(chain.flight)
    return chain.result


def angles(positions):
    lane = jnp.arange(WIDE)
    freq = 10000.0 ** (-((lane % (HD // 2)).astype(F32) * 2.0 / HD))
    turn = positions.astype(F32)[:, None] * freq[None, :]
    sign = jnp.where(lane % HD < HD // 2, -1.0, 1.0)
    return jnp.cos(turn), jnp.sin(turn) * sign[None, :]


def normalize(rows):
    factor = lax.rsqrt(jnp.mean(rows * rows, -1, keepdims=True) + EPS)
    return (rows * factor, factor)


def norm_back(upstream, normed, factor, gain):
    scaled = upstream * gain
    inner = jnp.mean(scaled * normed, -1, keepdims=True)
    return (factor * (scaled - normed * inner), jnp.sum(upstream * normed, 0))


def body(
    n_dp,
    n_ctx,
    layer_in,
    positions,
    attn_gain,
    query_proj,
    key_proj,
    value_proj,
    merge_proj,
    ffn_gain,
    gate_proj,
    up_proj,
    down_proj,
    out_grad,
):
    _, rows, model = layer_in.shape
    kv_width = key_proj.shape[1]
    kv_heads = kv_width // HD
    width = query_proj.shape[1]
    heads = width // HD
    run = rows // 2
    positions = positions[0]
    grid = Grid(n_dp, n_ctx)
    own = grid.own.reshape(1)
    order = grid.block_order(HALVES, True)

    gains = jnp.stack([attn_gain, ffn_gain], -1)
    gains = jnp.concatenate([gains, jnp.zeros((gains.shape[0], WIDE - 2), BF16)], 1)
    packed = jnp.concatenate([query_proj, key_proj, value_proj, gains], 1)
    first_chain = Chain(gather_weight(grid, packed, order))
    (gate_proj,) = meet((gate_proj,))
    gate_chain = Chain(gather_weight(grid, gate_proj, order))
    merge_chain = Chain(gather_weight(grid, merge_proj, order))
    up_chain = Chain(gather_weight(grid, up_proj, order))
    down_chain = Chain(gather_weight(grid, down_proj, order))
    all_pos = lax.all_gather(positions[::run], "ctx", axis=0, tiled=True)
    cosine, sine = angles(positions)
    rows_in = layer_in.reshape(rows, model).astype(F32)
    normed_one, factor_one = normalize(rows_in)
    first_weights = finish(first_chain)
    attn_all = first_weights[:, : width + 2 * kv_width]
    gain_one = first_weights[:, width + 2 * kv_width].astype(F32)
    gain_two = first_weights[:, width + 2 * kv_width + 1].astype(F32)

    first_in = (normed_one * gain_one).astype(BF16)
    raw = mm(first_in, attn_all, NN)
    raw = meet(raw, gate_chain)
    queries, own_kv = rotated(raw, cosine, sine, kv_width)
    all_kv = lax.all_gather(own_kv, "ctx", axis=0, tiled=True)
    turned_kv = all_kv.T
    kt, vt = turned_kv[:kv_width], turned_kv[kv_width:]
    later = all_pos[:, None] > jnp.repeat(positions[::run], run)[None, :]
    bias = jnp.where(later, MASKED, 0.0).astype(F32)

    queries, vt = meet((queries, vt), gate_chain, merge_chain)
    plan = (
        (merge_chain,),
        (gate_chain, up_chain),
        (merge_chain, up_chain),
        (gate_chain, merge_chain, down_chain),
    )
    outs, log_sums = [], []
    for group in range(kv_heads):
        out, log_sum = attend(group, own, bias, queries, all_kv, vt)
        queries, out = meet((queries, out), *plan[group % 4])
        outs.append(out)
        log_sums.append(log_sum)
    mixed = jnp.concatenate([out.astype(BF16) for out in outs], 1)
    merge_all = finish(merge_chain)
    gate_all = finish(gate_chain)
    middle = rows_in + mm(mixed, merge_all, NN)
    middle = meet(middle, up_chain)
    normed_two, factor_two = normalize(middle)
    second_in = (normed_two * gain_two).astype(BF16)
    gate = mm(second_in, gate_all, NN)
    gate = meet(gate, up_chain, down_chain)
    up_all = finish(up_chain)
    lift = mm(second_in, up_all, NN)
    sigma = jax.nn.sigmoid(gate)
    activated = gate * sigma
    hidden = (activated * lift).astype(BF16)
    hidden = meet(hidden, down_chain)
    down_all = finish(down_chain)
    grad_rows = out_grad.reshape(rows, model)

    down_chain = Chain(reduce_term(grid, turned(hidden, order), grad_rows))
    result = middle + mm(hidden, down_all, NN)
    layer_out = result.astype(BF16).reshape(layer_in.shape)
    grad_hidden = mm(grad_rows, down_all, NT)
    grad_gate = (grad_hidden * lift * sigma * (1.0 + gate * (1.0 - sigma))).astype(BF16)
    grad_lift = (grad_hidden * activated).astype(BF16)
    grad_gate, grad_lift, layer_out = meet((grad_gate, grad_lift, layer_out), down_chain)
    second_turned = turned(second_in, order)
    gate_chain = Chain(reduce_term(grid, second_turned, grad_gate))
    up_chain = Chain(reduce_term(grid, second_turned, grad_lift))
    grad_second = mm(grad_gate, gate_all, NT) + mm(grad_lift, up_all, NT)
    grad_second = meet(grad_second, gate_chain, up_chain)
    grad_norm_two, gain_two_term = norm_back(grad_second, normed_two, factor_two, gain_two)
    grad_middle = grad_rows.astype(F32) + grad_norm_two
    grad_branch = grad_middle.astype(BF16)
    merge_chain = Chain(reduce_term(grid, turned(mixed, order), grad_branch))
    grad_mixed = mm(grad_branch, merge_all, NT).astype(BF16)
    grad_mixed = meet(grad_mixed, down_chain, merge_chain)
    plan = (
        (down_chain, gate_chain),
        (up_chain, gate_chain, merge_chain),
        (up_chain, merge_chain),
        (),
    )
    dqs, dkvs = [], []
    for group in range(kv_heads):
        dq, dkv = attend_back(
            group, own, bias, log_sums[group], outs[group], queries, grad_mixed, all_kv, kt
        )
        dq, grad_mixed, dkv = meet((dq, grad_mixed, dkv), *plan[group % 4])
        dqs.append(dq)
        dkvs.append(lax.psum_scatter(dkv, "ctx", scatter_dimension=0, tiled=True))
    first_turned = turned(first_in, order)
    grads = unrotated(dqs, dkvs, cosine, sine)
    grad_first = mm(grads, attn_all, NT)
    grad_norm_one, gain_one_term = norm_back(grad_first, normed_one, factor_one, gain_one)
    gain_terms = jnp.stack([gain_one_term, gain_two_term], 0)
    gain_terms = jnp.concatenate([gain_terms, jnp.zeros((WIDE - 2, model), F32)], 0)
    first_chain = Chain(
        reduce_term(grid, first_turned, grads, turned(gain_terms.astype(BF16), order))
    )
    input_grad = (grad_middle + grad_norm_one).astype(BF16).reshape(layer_in.shape)
    first_share = finish(first_chain)
    merge_share, gate_share = finish(merge_chain), finish(gate_chain)
    up_share, down_share = finish(up_chain), finish(down_chain)
    edge = width + kv_width
    return (
        layer_out,
        input_grad,
        first_share[:, edge + kv_width],
        first_share[:, :width],
        first_share[:, width:edge],
        first_share[:, edge : edge + kv_width],
        merge_share,
        first_share[:, edge + kv_width + 1],
        gate_share,
        up_share,
        down_share,
    )


def solution(mesh):
    acts = P("dp", "ctx", None)
    rows = P(BOTH, None)
    flat = P(BOTH)
    return jax.shard_map(
        functools.partial(body, mesh.shape["dp"], mesh.shape["ctx"]),
        mesh=mesh,
        in_specs=(acts, P("dp", "ctx"), flat, rows, rows, rows, rows, flat, rows, rows, rows, acts),
        out_specs=(acts, acts, flat, rows, rows, rows, rows, flat, rows, rows, rows),
        check_vma=False,
    )
```

time: 1900 us -> 1470 us (0.77)
  waiting for transfers between devices: 1040 us -> 504 us
  local copies, waits for them, and re-layouts: 219 us -> 106 us
  Pallas kernels: 295 us -> 387 us
  matrix products: 246 us -> 294 us
  starting transfers between devices: 0.68 us -> 48.5 us
  other arithmetic: 67.9 us -> 94.7 us
    reduce_scatter x11 -> x9, waiting for transfers between devices: 688 us -> 142 us  [the longest x5 126 us: reduce_term(): lax.psum_scatter(joined, 'dp', scatter_dimension=0, tiled=True)]
    ppermute x0 -> x65, waiting for transfers between devices: none -> 266 us  [next(): return lax.ppermute(values, 'ctx', pairs)]
    all_gather x6, waiting for transfers between devices: 351 us -> 95.2 us  [the longest x5 61.3 us: gather_weight(): column, = (yield [lax.all_gather(weight, 'dp', axis=0)])]
    dot_general x10 -> x35, matrix products: 167 us -> 294 us  [mm(): return lax.dot_general(left, right, dims, preferred_element_type=F32)]
    pallas_call x2 -> x20, Pallas kernels: 295 us -> 387 us  [the longest x4 206 us: attend_back(): pl.pallas_call(functools.partial(attend_back_kernel, which=group % 2, unr...]
    dot_general x5 -> x0, matrix products: 78.6 us -> none  [outer(): lax.dot_general(left, right, (((0,), (0,)), ((), ())), preferred_element_...]
    concatenate x13 -> x2, local copies, waits for them, and re-layouts: 75.7 us -> 1.87 us  [the longest x1 1.79 us: body(): packed = jnp.concatenate([query_proj, key_proj, value_proj, gains], 1)]
    ppermute x0 -> x65, starting transfers between devices: none -> 47.9 us  [next(): return lax.ppermute(values, 'ctx', pairs)]
  transfers between devices with their start and end apart: 17 -> 80, of which waited for: 14 -> 30; matrix products, arithmetic and copies ran while one was open for 20% -> 28% of each run, Pallas kernels for 6% -> 26%
where the time goes in v2:
time: 1470 us; the launch traced here: 1460 us
  waiting for transfers between devices  504 us (34%)
  Pallas kernels  387 us (26%)
  matrix products  294 us (20%)
  local copies, waits for them, and re-layouts  106 us (7%)
  other arithmetic  94.7 us (6%)
  starting transfers between devices  48.5 us (3%)
  between operations  16.6 us (1%)
    dot_general x35, matrix products, mm(): return lax.dot_general(left, right, dims, preferred_element_type=F32)  294 us
    ppermute x65, waiting for transfers between devices, next(): return lax.ppermute(values, 'ctx', pairs)  266 us
    pallas_call x4, Pallas kernels, attend_back(): pl.pallas_call(functools.partial(attend_back_kernel, which=group % 2, unr...  206 us
    reduce_scatter x5, waiting for transfers between devices, reduce_term(): lax.psum_scatter(joined, 'dp', scatter_dimension=0, tiled=True)  126 us
    pallas_call x4, Pallas kernels, attend(): pl.pallas_call(functools.partial(attend_kernel, which=group % 2, unroll=u...  104 us
    pallas_call x5, Pallas kernels, placed(): pl.pallas_call(functools.partial(place_kernel, sources=sources, slots=slo...  64.8 us
    all_gather x5, waiting for transfers between devices, gather_weight(): column, = (yield [lax.all_gather(weight, 'dp', axis=0)])  61.3 us
    unnamed x297, local copies, waits for them, and re-layouts  58.7 us
  transfers between devices with their start and end apart: 80, of which 30 were waited for; matrix products, arithmetic and copies ran while one was open for 28% of the time, Pallas kernels for 26%

profile of v2, /device:TPU:0, one launch (start us, length us, event | category | flops | bytes accessed | tf_op | source)
XLA Modules:
  0.0 1458.4 jit_solution(16493855243891983183)
XLA Ops:
  10.6 36.6 %all-gather.14.cloned.1.call-done = bf16[256,2688]{1,0:T(8,128)(2,1)} async-done(((bf16[64,2688]{1,0:T(8,128)(2,1)}), bf16[256,2688]{1,0:T(8,128)(2,1)}) %all-gather.14.cloned.1.call-update) | async-done | bytes 1376272 | tf_op jit(solution)/shard_map/all_gather | solution.py:529
  69.2 26.7 %collective-permute-done.1 = bf16[2,2,64,2688]{3,2,1,0:T(8,128)(2,1)} collective-permute-done((bf16[2,2,64,2688]{3,2,1,0:T(8,128)(2,1)S(1)}, bf16[2,2,64,2688]{3,2,1,0:T(8,128)(2,1)}, u32[]{:S(2)}, u32[]{:S(2)}) %collective-permute-start.1) | collective-permute-done | bytes 1376288 | tf_op jit(solution)/shard_map/ppermute | solution.py:370
  153.3 33.9 %all-gather.12.cloned.1.call-done = bf16[4096,512]{0,1:T(8,128)(2,1)} async-done(((bf16[512,512]{0,1:T(8,128)(2,1)}), bf16[4096,512]{0,1:T(8,128)(2,1)}) %all-gather.12.cloned.1.call-update) | async-done | bytes 4194320 | tf_op jit(solution)/shard_map/all_gather | solution.py:641
  191.9 24.7 %all-gather.18.cloned.1.call-done = bf16[256,2048]{1,0:T(8,128)(2,1)} async-done(((bf16[64,2048]{1,0:T(8,128)(2,1)}), bf16[256,2048]{1,0:T(8,128)(2,1)}) %all-gather.18.cloned.1.call-update) | async-done | bytes 1048592 | tf_op jit(solution)/shard_map/all_gather | solution.py:529
  239.8 25.7 %attend.4 = (f32[512,512]{1,0:T(8,128)S(1)}, f32[8,512]{1,0:T(8,128)S(1)}) custom-call(s32[1]{0:T(128)} %bitcast.24.own_ref, f32[16,512]{1,0:T(8,128)S(1)} %compare_select_fusion.bias_ref, bf16[512,2048]{1,0:T(8,128)(2,1)S(1)} %copy-done.62, bf16[4096,512]{1,0:T(8,128)(2,1)S(1)} %copy-done.13, bf16[256,4096]{1,0:T(8,128)(2,1)S(1)} %copy-done.25), custom_call_target="tpu_custom_call" | custom-call | flops 17179869184 | bytes 3670016 | tf_op jit(solution)/shard_map/attend/pallas_call | solution.py:111
  266.5 25.9 %attend.5 = (f32[512,512]{1,0:T(8,128)S(1)}, f32[8,512]{1,0:T(8,128)S(1)}) custom-call(s32[1]{0:T(128)} %bitcast.24.own_ref, f32[16,512]{1,0:T(8,128)S(1)} %compare_select_fusion.bias_ref, bf16[512,2048]{1,0:T(8,128)(2,1)S(1)} %copy-done.62, bf16[4096,512]{1,0:T(8,128)(2,1)S(1)} %copy-done.13, bf16[256,4096]{1,0:T(8,128)(2,1)S(1)} %copy-done.25), custom_call_target="tpu_custom_call" | custom-call | flops 17179869184 | bytes 3670016 | tf_op jit(solution)/shard_map/attend/pallas_call | solution.py:111
  327.9 28.5 %collective-permute-done.15 = bf16[2,2,64,2048]{3,2,1,0:T(8,128)(2,1)} collective-permute-done((bf16[2,2,64,2048]{3,2,1,0:T(8,128)(2,1)}, bf16[2,2,64,2048]{3,2,1,0:T(8,128)(2,1)}, u32[]{:S(2)}, u32[]{:S(2)}) %collective-permute-start.15) | collective-permute-done | bytes 1048608 | tf_op jit(solution)/shard_map/ppermute | solution.py:370
  361.6 26.0 %attend.6 = (f32[512,512]{1,0:T(8,128)S(1)}, f32[8,512]{1,0:T(8,128)S(1)}) custom-call(s32[1]{0:T(128)} %bitcast.24.own_ref, f32[16,512]{1,0:T(8,128)S(1)} %compare_select_fusion.bias_ref, bf16[512,2048]{1,0:T(8,128)(2,1)S(1)} %copy-done.63, bf16[4096,512]{1,0:T(8,128)(2,1)S(1)} %copy-done.14, bf16[256,4096]{1,0:T(8,128)(2,1)S(1)} %copy-done.26), custom_call_target="tpu_custom_call" | custom-call | flops 17179869184 | bytes 3670016 | tf_op jit(solution)/shard_map/attend/pallas_call | solution.py:111
  404.8 26.1 %attend.7 = (f32[512,512]{1,0:T(8,128)S(1)}, f32[8,512]{1,0:T(8,128)S(1)}) custom-call(s32[1]{0:T(128)} %bitcast.24.own_ref, f32[16,512]{1,0:T(8,128)S(1)} %compare_select_fusion.bias_ref, bf16[512,2048]{1,0:T(8,128)(2,1)S(1)} %copy-done.64, bf16[4096,512]{1,0:T(8,128)(2,1)S(1)} %copy-done.14, bf16[256,4096]{1,0:T(8,128)(2,1)S(1)} %copy-done.26), custom_call_target="tpu_custom_call" | custom-call | flops 17179869184 | bytes 3670016 | tf_op jit(solution)/shard_map/attend/pallas_call | solution.py:111
  474.7 19.2 %fusion.108 = f32[512,5632]{1,0:T(8,128)} fusion(bf16[512,2048]{1,0:T(8,128)(2,1)S(1)} %multiply_convert_fusion.1.x_ref, bf16[2048,5632]{1,0:T(8,128)(2,1)} %bitcast.207), kind=kOutput, calls=%fused_computation.214 | convolution fusion | flops 11811160064 | bytes 36700160 | tf_op jit(solution)/shard_map/dot_general | solution.py:25
  529.2 22.7 %multiply_convert_fusion = (bf16[512,5632]{1,0:T(8,128)(2,1)}, f32[512,5632]{1,0:T(8,128)}) fusion(f32[512,5632]{1,0:T(8,128)} %fusion.108, bf16[512,2048]{1,0:T(8,128)(2,1)} %copy-done.3, bf16[2048,5632]{1,0:T(8,128)(2,1)} %bitcast.209), kind=kOutput, calls=%fused_computation.6 | convolution fusion | flops 11828461568 | bytes 54001664 | tf_op jit(solution)/shard_map/dot_general | solution.py:25
  551.9 20.8 %collective-permute-done.34 = bf16[2,2,176,2048]{3,2,1,0:T(8,128)(2,1)} collective-permute-done((bf16[2,2,176,2048]{3,2,1,0:T(8,128)(2,1)S(1)}, bf16[2,2,176,2048]{3,2,1,0:T(8,128)(2,1)}, u32[]{:S(2)}, u32[]{:S(2)}) %collective-permute-start.34) | collective-permute-done | bytes 2883616 | tf_op jit(solution)/shard_map/ppermute | solution.py:370
  657.5 43.2 %fusion.3 = (bf16[512,5632]{1,0:T(8,128)(2,1)}, bf16[512,5632]{1,0:T(8,128)(2,1)}) fusion(f32[512,5632]{1,0:T(8,128)} %fusion.108, f32[512,5632]{1,0:T(8,128)} %get-tuple-element.258, bf16[5632,2048]{1,0:T(8,128)(2,1)} %bitcast.212, bf16[1,512,2048]{2,1,0:T(8,128)(2,1)S(1)} %copy-done.72), kind=kOutput, calls=%fused_computation.5 | convolution fusion | flops 11848646656 | bytes 59768832 | tf_op jit(solution)/shard_map/dot_general | solution.py:25
  743.6 19.6 %fusion.109 = f32[512,2048]{1,0:T(8,128)} fusion(bf16[512,5632]{1,0:T(8,128)(2,1)} %get-tuple-element.164, bf16[2048,5632]{1,0:T(8,128)(2,1)} %bitcast.210), kind=kOutput, calls=%fused_computation.215 | convolution fusion | flops 11811160064 | bytes 33030144 | tf_op jit(solution)/shard_map/dot_general | solution.py:25
  763.2 20.7 %convolution_add_fusion.8 = f32[512,2048]{1,0:T(8,128)} fusion(f32[512,2048]{1,0:T(8,128)} %fusion.109, bf16[512,5632]{1,0:T(8,128)(2,1)} %get-tuple-element.163, bf16[2048,5632]{1,0:T(8,128)(2,1)} %bitcast.208), kind=kOutput, calls=%fused_computation.70 | convolution fusion | flops 11812208640 | bytes 37224448 | tf_op jit(solution)/shard_map/dot_general | solution.py:25
  843.5 50.7 %attend_back.4 = (f32[512,512]{1,0:T(8,128)S(1)}, bf16[4096,128]{1,0:T(8,128)(2,1)S(1)}) custom-call(s32[1]{0:T(128)} %bitcast.24.own_ref, f32[16,512]{1,0:T(8,128)S(1)} %compare_select_fusion.bias_ref, f32[8,512]{1,0:T(8,128)S(1)} %get-tuple-element.166.lse_ref, f32[512,512]{1,0:T(8,128)S(1)} %copy-done.51, bf16[512,2048]{1,0:T(8,128)(2,1)S(1)} %copy-done.65, ...), custom_call_target="tpu_custom_call" | custom-call | flops 42949672960 | bytes 6291456 | tf_op jit(solution)/shard_map/attend_back/pallas_call | solution.py:236
  907.9 58.9 %collective-permute-done.47 = bf16[352,2048]{1,0:T(8,128)(2,1)} collective-permute-done((bf16[352,2048]{1,0:T(8,128)(2,1)}, bf16[352,2048]{1,0:T(8,128)(2,1)}, u32[]{:S(2)}, u32[]{:S(2)}) %collective-permute-start.47) | collective-permute-done | bytes 1441824 | tf_op jit(solution)/shard_map/ppermute | solution.py:370
  987.7 51.6 %attend_back.5 = (f32[512,512]{1,0:T(8,128)S(1)}, bf16[4096,128]{1,0:T(8,128)(2,1)}) custom-call(s32[1]{0:T(128)} %bitcast.24.own_ref, f32[16,512]{1,0:T(8,128)S(1)} %copy-done.60, f32[8,512]{1,0:T(8,128)S(1)} %get-tuple-element.176.lse_ref, f32[512,512]{1,0:T(8,128)S(1)} %copy-done.44, bf16[512,2048]{1,0:T(8,128)(2,1)S(1)} %copy-done.66, ...), custom_call_target="tpu_custom_call" | custom-call | flops 42949672960 | bytes 6291456 | tf_op jit(solution)/shard_map/attend_back/pallas_call | solution.py:236
  1066.5 51.8 %attend_back.6 = (f32[512,512]{1,0:T(8,128)S(1)}, bf16[4096,128]{1,0:T(8,128)(2,1)}) custom-call(s32[1]{0:T(128)} %bitcast.24.own_ref, f32[16,512]{1,0:T(8,128)S(1)} %copy-done.60, f32[8,512]{1,0:T(8,128)S(1)} %get-tuple-element.185.lse_ref, f32[512,512]{1,0:T(8,128)S(1)} %copy-done.46, bf16[512,2048]{1,0:T(8,128)(2,1)S(1)} %copy-done.67, ...), custom_call_target="tpu_custom_call" | custom-call | flops 42949672960 | bytes 6291456 | tf_op jit(solution)/shard_map/attend_back/pallas_call | solution.py:236
  1120.9 51.6 %attend_back.7 = (f32[512,512]{1,0:T(8,128)S(1)}, bf16[4096,128]{1,0:T(8,128)(2,1)}) custom-call(s32[1]{0:T(128)} %bitcast.24.own_ref, f32[16,512]{1,0:T(8,128)S(1)} %copy-done.60, f32[8,512]{1,0:T(8,128)S(1)} %get-tuple-element.194.lse_ref, f32[512,512]{1,0:T(8,128)S(1)} %copy-done.49, bf16[512,2048]{1,0:T(8,128)(2,1)S(1)} %copy-done.68, ...), custom_call_target="tpu_custom_call" | custom-call | flops 42949672960 | bytes 6291456 | tf_op jit(solution)/shard_map/attend_back/pallas_call | solution.py:236
  1255.6 26.5 %collective-permute-done.61 = bf16[256,2688]{1,0:T(8,128)(2,1)S(1)} collective-permute-done((bf16[256,2688]{1,0:T(8,128)(2,1)S(1)}, bf16[256,2688]{1,0:T(8,128)(2,1)S(1)}, u32[]{:S(2)}, u32[]{:S(2)}) %collective-permute-start.61) | collective-permute-done | bytes 1376288 | tf_op jit(solution)/shard_map/ppermute | solution.py:370
  1315.7 38.3 %reduce-scatter.22.cloned.1.call-done = bf16[64,5632]{1,0:T(8,128)(2,1)} async-done(((bf16[256,5632]{1,0:T(8,128)(2,1)}), bf16[64,5632]{1,0:T(8,128)(2,1)}) %reduce-scatter.22.cloned.1.call-update) | async-done | bytes 720912 | tf_op jit(solution)/shard_map/reduce_scatter | solution.py:468
  1356.3 56.0 %reduce-scatter.24.cloned.1.call-done = bf16[64,5632]{1,0:T(8,128)(2,1)} async-done(((bf16[256,5632]{1,0:T(8,128)(2,1)}), bf16[64,5632]{1,0:T(8,128)(2,1)}) %reduce-scatter.24.cloned.1.call-update) | async-done | bytes 720912 | tf_op jit(solution)/shard_map/reduce_scatter | solution.py:468
  1414.6 32.1 %reduce-scatter.18.cloned.1.call-done = bf16[64,2688]{1,0:T(8,128)(2,1)} async-done(((bf16[256,2688]{1,0:T(8,128)(2,1)}), bf16[64,2688]{1,0:T(8,128)(2,1)}) %reduce-scatter.18.cloned.1.call-update) | async-done | bytes 344080 | tf_op jit(solution)/shard_map/reduce_scatter | solution.py:468
  (600 shorter events, 624.1 us)
Async XLA Ops:
  10.6 119.8 %all-gather.16.cloned.1.call-start = ((), (), s32[]{:S(2)}) async-start(), calls=%async_computation.20 | async-start | bytes 3604480 | tf_op jit(solution)/shard_map/all_gather | solution.py:529
  68.6 118.5 %all-gather.12.cloned.1.call-start = ((), (), s32[]{:S(2)}) async-start(), calls=%async_computation.9 | async-start | bytes 4718592 | tf_op jit(solution)/shard_map/all_gather | solution.py:641
  137.2 156.1 %all-gather.20.cloned.1.call-start = ((), (), s32[]{:S(2)}) async-start(), calls=%async_computation.22 | async-start | bytes 3604480 | tf_op jit(solution)/shard_map/all_gather | solution.py:529
  138.9 296.2 %all-gather.22.cloned.1.call-start = ((), (), s32[]{:S(2)}) async-start(), calls=%async_computation.23 | async-start | bytes 3604480 | tf_op jit(solution)/shard_map/all_gather | solution.py:529
  309.3 883.9 %reduce-scatter.10.cloned.1.call-start = ((), (), s32[]{:S(2)}) async-start(), calls=%async_computation.10 | async-start | bytes 1179648 | tf_op jit(solution)/shard_map/reduce_scatter | solution.py:709
  311.0 86.8 %collective-permute-start.20 = (bf16[2,2,64,5632]{3,2,1,0:T(8,128)(2,1)}, bf16[2,2,64,5632]{3,2,1,0:T(8,128)(2,1)S(1)}, u32[]{:S(2)}, u32[]{:S(2)}) collective-permute-start(bf16[2,2,64,5632]{3,2,1,0:T(8,128)(2,1)} %pad_maximum_fusion.2), channel_id=1, source_target_pairs={{0,1},{1,0},{2,3},{3,2},{4,5},{5,4},{6,7},{7,6},{8,9},{9,8},{10,11... | collective-permute-start | bytes 8650760 | tf_op jit(solution)/shard_map/ppermute | solution.py:370
  590.0 110.7 %collective-permute-start.40 = (bf16[2816,2048]{1,0:T(8,128)(2,1)}, bf16[2816,2048]{1,0:T(8,128)(2,1)}, u32[]{:S(2)}, u32[]{:S(2)}) collective-permute-start(bf16[2816,2048]{1,0:T(8,128)(2,1)} %convolution_convert_fusion.2), channel_id=1, source_target_pairs={{0,1},{1,0},{2,3},{3,2},{4,5},{5,4},{6,7},{7,6},{8,9},{9,8},{10,11... | collective-permute-start | bytes 34603016 | tf_op jit(solution)/shard_map/ppermute | solution.py:370
  737.2 92.6 %collective-permute-start.43 = (bf16[704,2048]{1,0:T(8,128)(2,1)}, bf16[704,2048]{1,0:T(8,128)(2,1)}, u32[]{:S(2)}, u32[]{:S(2)}) collective-permute-start(bf16[704,2048]{1,0:T(8,128)(2,1)} %add_convert_fusion.9), channel_id=1, source_target_pairs={{0,2},{1,3},{2,0},{3,1},{4,6},{5,7},{6,4},{7,5},{8,10},{9,11},{10,... | collective-permute-start | bytes 8650760 | tf_op jit(solution)/shard_map/ppermute | solution.py:370
  743.1 87.4 %collective-permute-start.44 = (bf16[704,2048]{1,0:T(8,128)(2,1)}, bf16[704,2048]{1,0:T(8,128)(2,1)}, u32[]{:S(2)}, u32[]{:S(2)}) collective-permute-start(bf16[704,2048]{1,0:T(8,128)(2,1)} %add_convert_fusion.8), channel_id=1, source_target_pairs={{0,4},{1,5},{2,6},{3,7},{4,0},{5,1},{6,2},{7,3},{8,12},{9,13},{10,... | collective-permute-start | bytes 8650760 | tf_op jit(solution)/shard_map/ppermute | solution.py:370
  808.5 92.2 %collective-permute-start.48 = (bf16[256,5632]{1,0:T(8,128)(2,1)}, bf16[256,5632]{1,0:T(8,128)(2,1)}, u32[]{:S(2)}, u32[]{:S(2)}) collective-permute-start(bf16[256,5632]{1,0:T(8,128)(2,1)} %fusion.9), channel_id=1, source_target_pairs={{0,2},{1,3},{2,0},{3,1},{4,6},{5,7},{6,4},{7,5},{8,10},{9,11},{10,... | collective-permute-start | bytes 8650760 | tf_op jit(solution)/shard_map/ppermute | solution.py:370
  810.0 91.5 %collective-permute-start.49 = (bf16[256,5632]{1,0:T(8,128)(2,1)}, bf16[256,5632]{1,0:T(8,128)(2,1)}, u32[]{:S(2)}, u32[]{:S(2)}) collective-permute-start(bf16[256,5632]{1,0:T(8,128)(2,1)} %fusion.10), channel_id=1, source_target_pairs={{0,4},{1,5},{2,6},{3,7},{4,0},{5,1},{6,2},{7,3},{8,12},{9,13},{10,... | collective-permute-start | bytes 8650760 | tf_op jit(solution)/shard_map/ppermute | solution.py:370
  829.9 154.9 %collective-permute-start.50 = (bf16[256,5632]{1,0:T(8,128)(2,1)}, bf16[256,5632]{1,0:T(8,128)(2,1)}, u32[]{:S(2)}, u32[]{:S(2)}) collective-permute-start(bf16[256,5632]{1,0:T(8,128)(2,1)} %fusion.11), channel_id=1, source_target_pairs={{0,2},{1,3},{2,0},{3,1},{4,6},{5,7},{6,4},{7,5},{8,10},{9,11},{10,... | collective-permute-start | bytes 8650760 | tf_op jit(solution)/shard_map/ppermute | solution.py:370
  842.1 124.7 %collective-permute-start.47 = (bf16[352,2048]{1,0:T(8,128)(2,1)}, bf16[352,2048]{1,0:T(8,128)(2,1)}, u32[]{:S(2)}, u32[]{:S(2)}) collective-permute-start(bf16[352,2048]{1,0:T(8,128)(2,1)} %slice.367), channel_id=1, source_target_pairs={{0,2},{1,3},{2,0},{3,1},{4,6},{5,7},{6,4},{7,5},{8,10},{9,11},{10,... | collective-permute-start | bytes 4325384 | tf_op jit(solution)/shard_map/ppermute | solution.py:370
  900.8 139.6 %collective-permute-start.51 = (bf16[256,5632]{1,0:T(8,128)(2,1)}, bf16[256,5632]{1,0:T(8,128)(2,1)}, u32[]{:S(2)}, u32[]{:S(2)}) collective-permute-start(bf16[256,5632]{1,0:T(8,128)(2,1)} %fusion.12), channel_id=1, source_target_pairs={{0,4},{1,5},{2,6},{3,7},{4,0},{5,1},{6,2},{7,3},{8,12},{9,13},{10,... | collective-permute-start | bytes 8650760 | tf_op jit(solution)/shard_map/ppermute | solution.py:370
  901.5 138.8 %collective-permute-start.54 = (bf16[256,2048]{1,0:T(8,128)(2,1)}, bf16[256,2048]{1,0:T(8,128)(2,1)}, u32[]{:S(2)}, u32[]{:S(2)}) collective-permute-start(bf16[256,2048]{1,0:T(8,128)(2,1)} %add_convert_fusion.24), channel_id=1, source_target_pairs={{0,2},{1,3},{2,0},{3,1},{4,6},{5,7},{6,4},{7,5},{8,10},{9,11},{10,... | collective-permute-start | bytes 3145736 | tf_op jit(solution)/shard_map/ppermute | solution.py:370
  906.5 133.8 %collective-permute-start.55 = (bf16[256,2048]{1,0:T(8,128)(2,1)}, bf16[256,2048]{1,0:T(8,128)(2,1)}, u32[]{:S(2)}, u32[]{:S(2)}) collective-permute-start(bf16[256,2048]{1,0:T(8,128)(2,1)} %add_convert_fusion.23), channel_id=1, source_target_pairs={{0,4},{1,5},{2,6},{3,7},{4,0},{5,1},{6,2},{7,3},{8,12},{9,13},{10,... | collective-permute-start | bytes 3145736 | tf_op jit(solution)/shard_map/ppermute | solution.py:370
  984.7 208.6 %reduce-scatter.12.cloned.1.call-start = ((), (), s32[]{:S(2)}) async-start(), calls=%async_computation.11 | async-start | bytes 1179648 | tf_op jit(solution)/shard_map/reduce_scatter | solution.py:709
  1064.8 128.5 %reduce-scatter.14.cloned.1.call-start = ((), (), s32[]{:S(2)}) async-start(), calls=%async_computation.12 | async-start | bytes 1179648 | tf_op jit(solution)/shard_map/reduce_scatter | solution.py:709
  1119.3 89.7 %reduce-scatter.16.cloned.1.call-start = ((), (), s32[]{:S(2)}) async-start(), calls=%async_computation.13 | async-start | bytes 1179648 | tf_op jit(solution)/shard_map/reduce_scatter | solution.py:709
  1173.5 138.0 %reduce-scatter.20.cloned.1.call-start = ((), (), s32[]{:S(2)}) async-start(), calls=%async_computation.15 | async-start | bytes 1310720 | tf_op jit(solution)/shard_map/reduce_scatter | solution.py:468
  1177.0 136.3 %reduce-scatter.26.cloned.1.call-start = ((), (), s32[]{:S(2)}) async-start(), calls=%async_computation.18 | async-start | bytes 3604480 | tf_op jit(solution)/shard_map/reduce_scatter | solution.py:468
  1183.5 170.5 %reduce-scatter.22.cloned.1.call-start = ((), (), s32[]{:S(2)}) async-start(), calls=%async_computation.16 | async-start | bytes 3604480 | tf_op jit(solution)/shard_map/reduce_scatter | solution.py:468
  1193.2 219.1 %reduce-scatter.24.cloned.1.call-start = ((), (), s32[]{:S(2)}) async-start(), calls=%async_computation.17 | async-start | bytes 3604480 | tf_op jit(solution)/shard_map/reduce_scatter | solution.py:468
  1243.6 203.1 %reduce-scatter.18.cloned.1.call-start = ((), (), s32[]{:S(2)}) async-start(), calls=%async_computation.14 | async-start | bytes 1720320 | tf_op jit(solution)/shard_map/reduce_scatter | solution.py:468
  (201 other events, 5399.3 us)
Sparse Core Ops, SparseCore 0:
  10.7 36.5 all-gather.13
  68.7 57.5 all-gather.15
  136.8 50.3 all-gather.11
  188.6 27.9 all-gather.17
  217.9 58.6 all-gather.19
  309.5 57.1 all-gather.21
  984.8 39.5 reduce-scatter.9
  1064.9 38.7 reduce-scatter.11
  1119.4 35.2 reduce-scatter.13
  1173.6 35.2 reduce-scatter.15
  1211.2 27.1 reduce-scatter.19
  1240.7 54.8 reduce-scatter.25
  1297.9 56.0 reduce-scatter.21
  1356.3 56.0 reduce-scatter.23
  1414.6 32.0 reduce-scatter.17

commit v3 on v2

--- a/solution.py
+++ b/solution.py
@@ -52,10 +52,11 @@
     return jnp.concatenate(parts, 0)
 
 
-def attend_kernel(own_ref, bias_ref, q_ref, kp_ref, vt_ref, o_ref, lse_ref, low, high, vx, turned, *, which, unroll):
+def attend_kernel(
+    bias_ref, q_ref, kp_ref, vt_ref, o_ref, lse_ref, low, high, vx, turned, *, which, places
+):
     rows, width = q_ref.shape
     length = kp_ref.shape[0]
-    own = own_ref[0]
     blocks = length // rows
     split_heads(kp_ref, which, low, high)
     vx[:HD, :] = vt_ref[...]
@@ -69,19 +70,18 @@
         return biased(s, bias_ref, block, rows)
 
     def weigh(probs, block):
-        start = pl.multiple_of(block * rows, rows)
-        return mm(vx[:, pl.ds(start, rows)], probs.astype(BF16), NN)
+        start = places[block] * rows
+        return mm(vx[:, start : start + rows], probs.astype(BF16), NN)
 
     def one_pair(pair, _):
         blocked = same_run_later(rows, rows)
         state = []
         for key in (low, high):
-            s = jnp.where(blocked, MASKED, scores(key, pair, own))
+            s = jnp.where(blocked, MASKED, scores(key, pair, 0))
             top = jnp.max(s, 0, keepdims=True)
-            state.append((top, weigh(jnp.exp2(s - top), own)))
-
-        def step(j, state):
-            block = lax.rem(own + j, blocks)
+            state.append((top, weigh(jnp.exp2(s - top), 0)))
+
+        def step(block, state):
             raw = [scores(key, pair, block) for key in (low, high)]
             result = []
             for (top, total), s in zip(state, raw):
@@ -90,7 +90,8 @@
                 result.append((new_top, total * jnp.exp2(top - new_top) + weigh(probs, block)))
             return result
 
-        state = lax.fori_loop(1, blocks, step, state, unroll=unroll)
+        for block in range(1, blocks):
+            state = step(block, state)
         for i, (top, total) in enumerate(state):
             weight_sum = total[HD : HD + 1, :]
             turned[i * HD : (i + 1) * HD, :] = total[:HD] / weight_sum
@@ -102,21 +103,20 @@
     lax.fori_loop(0, width // WIDE, one_pair, 0)
 
 
-def attend(group, own, bias, q, kv, vt, unroll=True):
+def attend(group, places, bias, q, keys, vt):
     rows, width = q.shape
-    length = kv.shape[0]
+    length = keys.shape[0]
     kv_heads = vt.shape[0] // HD
     mine = width // kv_heads
     heads = mine // HD
     return pl.pallas_call(
-        functools.partial(attend_kernel, which=group % 2, unroll=unroll),
+        functools.partial(attend_kernel, which=group % 2, places=places),
         grid=(1,),
         out_shape=(
             jax.ShapeDtypeStruct((rows, mine), F32),
             jax.ShapeDtypeStruct((heads, rows), F32),
         ),
         in_specs=[
-            pl.BlockSpec(memory_space=pltpu.SMEM),
             pl.BlockSpec(bias.shape, lambda i: (0, 0)),
             pl.BlockSpec((rows, mine), lambda i: (0, group)),
             pl.BlockSpec((length, WIDE), lambda i: (0, group // 2)),
@@ -139,16 +139,15 @@
             transcendentals=heads * rows * length,
         ),
         name="attend",
-    )(own, bias, q, kv, vt)
+    )(bias, q, keys, vt)
 
 
 def attend_back_kernel(
-    own_ref, bias_ref, lse_ref, o_ref, q_ref, g_ref, kp_ref, vp_ref, kt_ref,
+    order_ref, place_ref, bias_ref, lse_ref, o_ref, q_ref, g_ref, kp_ref, vp_ref, kt_ref,
     dq_ref, dkv_ref, k_low, k_high, v_low, v_high, dqt, delta_ref, *, which, unroll
 ):
     rows, width = q_ref.shape
     length = kp_ref.shape[0]
-    own = own_ref[0]
     blocks = length // rows
     pairs = width // WIDE
     split_heads(kp_ref, which, k_low, k_high)
@@ -166,6 +165,7 @@
 
     def block(index, diagonal):
         start = pl.multiple_of(index * rows, rows)
+        value_start = pl.multiple_of(place_ref[index] * rows, rows)
 
         def some_heads(i, sums):
             sums = list(sums)
@@ -191,7 +191,7 @@
                     p = jnp.exp2(s)
                     if diagonal:
                         p = jnp.where(same_run_later(rows, rows), 0.0, p)
-                    slope = mm(value[pl.ds(start, rows), :], grad, NT)
+                    slope = mm(value[pl.ds(value_start, rows), :], grad, NT)
                     d = (p * (slope - delta_ref[pl.ds(head, 1), :])).astype(BF16)
                     work.append((side, pair, query, grad, p.astype(BF16), d))
             for side, pair, query, grad, p, d in work:
@@ -210,14 +210,15 @@
         lane = lax.broadcasted_iota(jnp.int32, (rows, WIDE), 1)
         key_sum = sums[0] + pltpu.roll(sums[1], HD, 1)
         value_sum = pltpu.roll(sums[2], HD, 1) + sums[3]
-        dkv_ref[pl.ds(start, rows), :] = jnp.where(
+        place = pl.multiple_of(order_ref[index] * rows, rows)
+        dkv_ref[pl.ds(place, rows), :] = jnp.where(
             lane < HD, key_sum * SCALE, value_sum
         ).astype(BF16)
 
-    block(own, True)
+    block(0, True)
 
     def rest(j, _):
-        block(lax.rem(own + j, blocks), False)
+        block(j, False)
         return 0
 
     lax.fori_loop(1, blocks, rest, 0)
@@ -227,9 +228,9 @@
         ).T
 
 
-def attend_back(group, own, bias, lse, out, q, g, kv, kt, unroll=2):
+def attend_back(group, order, places, bias, lse, out, q, g, keys, values, kt, unroll=2):
     rows, width = q.shape
-    length = kv.shape[0]
+    length = keys.shape[0]
     kv_heads = kt.shape[0] // HD
     mine = width // kv_heads
     heads = mine // HD
@@ -242,13 +243,14 @@
         ),
         in_specs=[
             pl.BlockSpec(memory_space=pltpu.SMEM),
+            pl.BlockSpec(memory_space=pltpu.SMEM),
             pl.BlockSpec(bias.shape, lambda i: (0, 0)),
             pl.BlockSpec((heads, rows), lambda i: (0, 0)),
             pl.BlockSpec((rows, mine), lambda i: (0, 0)),
             pl.BlockSpec((rows, mine), lambda i: (0, group)),
             pl.BlockSpec((rows, mine), lambda i: (0, group)),
             pl.BlockSpec((length, WIDE), lambda i: (0, group // 2)),
-            pl.BlockSpec((length, WIDE), lambda i: (0, kv_heads // 2 + group // 2)),
+            pl.BlockSpec((length, WIDE), lambda i: (0, group // 2)),
             pl.BlockSpec((HD, length), lambda i: (group, 0)),
         ],
         out_specs=(
@@ -264,7 +266,7 @@
             transcendentals=heads * rows * length,
         ),
         name="attend_back",
-    )(own, bias, lse, out, q, g, kv, kv, kt)
+    )(order, jnp.array(places, jnp.int32), bias, lse, out, q, g, keys, values, kt)
 
 
 def turn_pairs(x, cosine, sine):
@@ -304,41 +306,45 @@
     )(cosine, sine, raw)
 
 
-def unrotate_kernel(cos_ref, sin_ref, *refs, kv_heads):
+def unrotate_queries_kernel(cos_ref, sin_ref, *refs):
     cosine, sine = cos_ref[...], -sin_ref[...]
-    dqs, dkvs, out_ref = refs[:kv_heads], refs[kv_heads : 2 * kv_heads], refs[-1]
-    mine = dqs[0].shape[1]
+    out_ref = refs[-1]
+    mine = refs[0].shape[1]
+    for n, ref in enumerate(refs[:-1]):
+        for at in range(0, mine, WIDE):
+            turned = turn_pairs(ref[:, at : at + WIDE], cosine, sine)
+            out_ref[:, n * mine + at : n * mine + at + WIDE] = turned.astype(BF16)
+
+
+def unrotate_keys_kernel(cos_ref, sin_ref, *refs):
+    cosine, sine = cos_ref[...], -sin_ref[...]
+    out_ref = refs[-1]
+    count = len(refs) - 1
     lane = lax.broadcasted_iota(jnp.int32, cosine.shape, 1)
-    for group in range(kv_heads):
-        for at in range(0, mine, WIDE):
-            turned = turn_pairs(dqs[group][:, at : at + WIDE], cosine, sine)
-            out_ref[:, group * mine + at : group * mine + at + WIDE] = turned.astype(BF16)
-    base = kv_heads * mine
-    for i in range(kv_heads // 2):
-        first, second = dkvs[2 * i][...].astype(F32), dkvs[2 * i + 1][...].astype(F32)
+    for i in range(count // 2):
+        first, second = refs[2 * i][...].astype(F32), refs[2 * i + 1][...].astype(F32)
         keys = jnp.where(lane < HD, first, pltpu.roll(second, HD, 1))
         values = jnp.where(lane < HD, pltpu.roll(first, HD, 1), second)
-        at = base + i * WIDE
+        at = i * WIDE
         out_ref[:, at : at + WIDE] = turn_pairs(keys, cosine, sine).astype(BF16)
-        at = base + kv_heads * HD + i * WIDE
+        at = count * HD + i * WIDE
         out_ref[:, at : at + WIDE] = values.astype(BF16)
 
 
-def unrotated(dqs, dkvs, cosine, sine):
-    rows, mine = dqs[0].shape
-    kv_heads = len(dqs)
-    total = kv_heads * (mine + 2 * HD)
+def unrotated(kernel, parts, cosine, sine):
+    rows, mine = parts[0].shape
+    total = len(parts) * mine
     return pl.pallas_call(
-        functools.partial(unrotate_kernel, kv_heads=kv_heads),
+        kernel,
         out_shape=jax.ShapeDtypeStruct((rows, total), BF16),
-        in_specs=[pl.BlockSpec(memory_space=pltpu.VMEM)] * (2 + 2 * kv_heads),
+        in_specs=[pl.BlockSpec(memory_space=pltpu.VMEM)] * (2 + len(parts)),
         out_specs=pl.BlockSpec(memory_space=pltpu.VMEM),
         compiler_params=pltpu.CompilerParams(vmem_limit_bytes=32 << 20),
         cost_estimate=pl.CostEstimate(
             flops=8 * rows * total, bytes_accessed=6 * rows * total, transcendentals=0
         ),
         name="unrotated",
-    )(cosine, sine, *dqs, *dkvs)
+    )(cosine, sine, *parts)
 
 
 BOTH = ("dp", "ctx")
@@ -348,15 +354,21 @@
     def __init__(self, n_dp, n_ctx):
         self.n_dp, self.n_a, self.n_b = n_dp, 2, n_ctx // 4
         self.n_ctx = n_ctx
-        self.own = lax.axis_index("ctx").astype(jnp.int32)
-        self.a = self.own // (2 * self.n_b)
-        self.b = (self.own // 2) % self.n_b
-        self.c = self.own % 2
+        self.ring = [0, 1, 3, 2] if n_dp == 4 else list(range(n_dp))
+        own = lax.axis_index("ctx").astype(jnp.int32)
+        self.a = own // (2 * self.n_b)
+        self.b = (own // 2) % self.n_b
+        self.c = own % 2
+        places = np.argsort(np.array(self.ring)).astype(np.int32)
+        self.d = jnp.asarray(places)[lax.axis_index("dp")]
 
     def size(self, axis):
-        return {"a": self.n_a, "b": self.n_b, "c": 2}[axis]
+        return {"a": self.n_a, "b": self.n_b, "c": 2, "d": self.n_dp}[axis]
 
     def next(self, values, axis):
+        if axis == "d":
+            around = self.ring[1:] + self.ring[:1]
+            return lax.ppermute(values, "dp", list(zip(self.ring, around)))
         pairs = []
         for i in range(self.n_ctx):
             a, b, c = i // (2 * self.n_b), (i // 2) % self.n_b, i % 2
@@ -369,21 +381,47 @@
             pairs.append((i, (a * self.n_b + b) * 2 + c))
         return lax.ppermute(values, "ctx", pairs)
 
-    def block_order(self, half_axes, core_major):
+    def natural(self, rows):
+        rows = np.array(rows, np.int32)
+        a = (self.a - rows[:, 2]) % self.n_a
+        b = (self.b - rows[:, 3]) % self.n_b
+        c = (self.c - rows[:, 0]) % 2
+        return ((rows[:, 1] * self.n_a + a) * self.n_b + b) * 2 + c
+
+    def block_order(self):
         half = self.n_dp // 2
         rows = []
         for core in range(2):
-            for h, (first, second) in enumerate(half_axes):
+            for h, (first, second) in enumerate(HALVES):
                 for i in range(self.size(first)):
                     for j in range(self.size(second)):
                         for d in range(half):
                             near = {first: i, second: j}
-                            rows.append((core, h, near["a"], near["b"], h * half + d))
-        rows = np.array(rows, np.int32)
-        a = (self.a - rows[:, 2]) % self.n_a
-        b = (self.b - rows[:, 3]) % self.n_b
-        c = (self.c - rows[:, 0]) % 2
-        return ((rows[:, 4] * self.n_a + a) * self.n_b + b) * 2 + c
+                            rows.append((core, h * half + d, near["a"], near["b"]))
+        return self.natural(rows)
+
+    def ring_order(self):
+        rows, hops = [], []
+        for core in range(2):
+            for d in range(self.n_dp):
+                for b in range(self.n_b):
+                    for a in range(self.n_a):
+                        rows.append((core, 0, a, b))
+                        hops.append(d)
+        place = jnp.asarray(np.array(self.ring, np.int32))[
+            (self.d - np.array(hops, np.int32)) % self.n_dp
+        ]
+        return self.natural(rows) + place * self.n_ctx
+
+    def ctx_order(self):
+        rows = [
+            (c, 0, a, b) for c in range(2) for b in range(self.n_b) for a in range(self.n_a)
+        ]
+        return self.natural(rows)
+
+    def value_places(self):
+        cells = [(c, b, a) for c in range(2) for b in range(self.n_b) for a in range(self.n_a)]
+        return tuple((c * self.n_a + a) * self.n_b + b for c, b, a in cells)
 
 
 HALVES = (("b", "a"), ("a", "b"))
@@ -544,6 +582,61 @@
     return placed(order, near + list(far))
 
 
+def gather_ring(grid, weight):
+    part = weight
+    for axis in ("a", "b"):
+        steps = [part]
+        for _ in range(grid.size(axis) - 1):
+            (came,) = yield [grid.next(steps[-1], axis)]
+            steps.append(came)
+        part = jnp.stack(steps)
+    near, far = [part], []
+    for _ in range(grid.n_dp - 1):
+        came, other = yield [grid.next(near[-1], "d"), grid.next(near[-1], "c")]
+        near.append(came)
+        far.append(other)
+    (other,) = yield [grid.next(near[-1], "c")]
+    return placed(grid.ring_order(), near + far + [other])
+
+
+def reduce_ring(grid, left, right):
+    mine = left.shape[0] // 2
+    (arrived,) = yield [grid.next(mm(left[mine:], right, NN).astype(BF16), "c")]
+    size = mine // grid.n_dp
+    held = [
+        (mm(left[at : at + size], right, NN) + arrived[at : at + size].astype(F32)).astype(BF16)
+        for at in range(0, mine, size)
+    ]
+    for axis in ("d", "b", "a"):
+        count = grid.size(axis)
+        total = held[1]
+        for k in range(1, count):
+            (came,) = yield [grid.next(total, axis)]
+            total = (came.astype(F32) + held[(k + 1) % count].astype(F32)).astype(BF16)
+        following = {"d": grid.n_b, "b": grid.n_a, "a": 1}[axis]
+        size = total.shape[0] // following
+        held = [total[at : at + size] for at in range(0, total.shape[0], size)]
+    return held[0].astype(F32)
+
+
+def gather_keys(grid, own):
+    width = own.shape[1] // 2
+    steps = [[own[:, :width]], [own[:, width:]]]
+    for stage in (1, 0):
+        counts = [grid.size(axes[stage]) for axes in HALVES]
+        for k in range(1, max(counts)):
+            live = [h for h in range(2) if k < counts[h]]
+            came = yield [grid.next(steps[h][-1], HALVES[h][stage]) for h in live]
+            for h, part in zip(live, came):
+                steps[h].append(part)
+        steps = [[jnp.stack(s)] for s in steps]
+    near = [s[0] for s in steps]
+    far = yield [grid.next(part, "c") for part in near]
+    return tuple(
+        jnp.stack([one, two]).reshape(-1, width) for one, two in zip(near, far)
+    )
+
+
 class Chain:
     def __init__(self, generator):
         self.generator, self.done, self.result = generator, False, None
@@ -609,26 +702,25 @@
     kv_width = key_proj.shape[1]
     kv_heads = kv_width // HD
     width = query_proj.shape[1]
-    heads = width // HD
     run = rows // 2
     positions = positions[0]
     grid = Grid(n_dp, n_ctx)
-    own = grid.own.reshape(1)
-    order = grid.block_order(HALVES, True)
+    order, ring_order, ctx_order = grid.block_order(), grid.ring_order(), grid.ctx_order()
+    places = grid.value_places()
 
     gains = jnp.stack([attn_gain, ffn_gain], -1)
     gains = jnp.concatenate([gains, jnp.zeros((gains.shape[0], WIDE - 2), BF16)], 1)
     packed = jnp.concatenate([query_proj, key_proj, value_proj, gains], 1)
     first_chain = Chain(gather_weight(grid, packed, order))
-    (gate_proj,) = meet((gate_proj,))
-    gate_chain = Chain(gather_weight(grid, gate_proj, order))
-    merge_chain = Chain(gather_weight(grid, merge_proj, order))
-    up_chain = Chain(gather_weight(grid, up_proj, order))
-    down_chain = Chain(gather_weight(grid, down_proj, order))
+    down_chain = Chain(gather_ring(grid, down_proj))
     all_pos = lax.all_gather(positions[::run], "ctx", axis=0, tiled=True)
     cosine, sine = angles(positions)
     rows_in = layer_in.reshape(rows, model).astype(F32)
     normed_one, factor_one = normalize(rows_in)
+    all_pos, merge_proj, factor_one = meet((all_pos, merge_proj, factor_one), first_chain, down_chain)
+    merge_chain = Chain(gather_weight(grid, merge_proj, order))
+    gate_proj = meet(gate_proj, first_chain)
+    gate_chain = Chain(gather_weight(grid, gate_proj, order))
     first_weights = finish(first_chain)
     attn_all = first_weights[:, : width + 2 * kv_width]
     gain_one = first_weights[:, width + 2 * kv_width].astype(F32)
@@ -636,34 +728,37 @@
 
     first_in = (normed_one * gain_one).astype(BF16)
     raw = mm(first_in, attn_all, NN)
-    raw = meet(raw, gate_chain)
+    raw, up_proj = meet((raw, up_proj), merge_chain)
+    up_chain = Chain(gather_weight(grid, up_proj, order))
     queries, own_kv = rotated(raw, cosine, sine, kv_width)
-    all_kv = lax.all_gather(own_kv, "ctx", axis=0, tiled=True)
-    turned_kv = all_kv.T
-    kt, vt = turned_kv[:kv_width], turned_kv[kv_width:]
-    later = all_pos[:, None] > jnp.repeat(positions[::run], run)[None, :]
+    kv_chain = Chain(gather_keys(grid, own_kv))
+    later = all_pos.reshape(n_ctx, 2)[ctx_order].reshape(2 * n_ctx, 1)
+    later = later > jnp.repeat(positions[::run], run)[None, :]
     bias = jnp.where(later, MASKED, 0.0).astype(F32)
-
-    queries, vt = meet((queries, vt), gate_chain, merge_chain)
+    bias = meet(bias, kv_chain, gate_chain, merge_chain)
+    bias = meet(bias, kv_chain)
+    all_keys, all_values = finish(kv_chain)
+    kt, vt = all_keys.T, all_values.T
+
     plan = (
+        (gate_chain, merge_chain, up_chain, down_chain),
         (merge_chain,),
-        (gate_chain, up_chain),
-        (merge_chain, up_chain),
-        (gate_chain, merge_chain, down_chain),
+        (),
+        (gate_chain, up_chain, down_chain),
     )
     outs, log_sums = [], []
     for group in range(kv_heads):
-        out, log_sum = attend(group, own, bias, queries, all_kv, vt)
+        out, log_sum = attend(group, places, bias, queries, all_keys, vt)
         queries, out = meet((queries, out), *plan[group % 4])
         outs.append(out)
         log_sums.append(log_sum)
     mixed = jnp.concatenate([out.astype(BF16) for out in outs], 1)
     merge_all = finish(merge_chain)
-    gate_all = finish(gate_chain)
     middle = rows_in + mm(mixed, merge_all, NN)
-    middle = meet(middle, up_chain)
     normed_two, factor_two = normalize(middle)
     second_in = (normed_two * gain_two).astype(BF16)
+    second_in = meet(second_in, gate_chain)
+    gate_all = finish(gate_chain)
     gate = mm(second_in, gate_all, NN)
     gate = meet(gate, up_chain, down_chain)
     up_all = finish(up_chain)
@@ -671,65 +766,79 @@
     sigma = jax.nn.sigmoid(gate)
     activated = gate * sigma
     hidden = (activated * lift).astype(BF16)
+    grad_rows = out_grad.reshape(rows, model)
+    down_sum = Chain(reduce_ring(grid, turned(hidden, ring_order), grad_rows))
     hidden = meet(hidden, down_chain)
     down_all = finish(down_chain)
-    grad_rows = out_grad.reshape(rows, model)
-
-    down_chain = Chain(reduce_term(grid, turned(hidden, order), grad_rows))
     result = middle + mm(hidden, down_all, NN)
     layer_out = result.astype(BF16).reshape(layer_in.shape)
+    layer_out = meet(layer_out, down_sum)
     grad_hidden = mm(grad_rows, down_all, NT)
     grad_gate = (grad_hidden * lift * sigma * (1.0 + gate * (1.0 - sigma))).astype(BF16)
     grad_lift = (grad_hidden * activated).astype(BF16)
-    grad_gate, grad_lift, layer_out = meet((grad_gate, grad_lift, layer_out), down_chain)
     second_turned = turned(second_in, order)
-    gate_chain = Chain(reduce_term(grid, second_turned, grad_gate))
-    up_chain = Chain(reduce_term(grid, second_turned, grad_lift))
+    gate_sum = Chain(reduce_term(grid, second_turned, grad_gate))
+    up_sum = Chain(reduce_term(grid, second_turned, grad_lift))
     grad_second = mm(grad_gate, gate_all, NT) + mm(grad_lift, up_all, NT)
-    grad_second = meet(grad_second, gate_chain, up_chain)
+    grad_second = meet(grad_second, gate_sum, up_sum, down_sum)
     grad_norm_two, gain_two_term = norm_back(grad_second, normed_two, factor_two, gain_two)
     grad_middle = grad_rows.astype(F32) + grad_norm_two
     grad_branch = grad_middle.astype(BF16)
-    merge_chain = Chain(reduce_term(grid, turned(mixed, order), grad_branch))
+    merge_sum = Chain(reduce_term(grid, turned(mixed, order), grad_branch))
     grad_mixed = mm(grad_branch, merge_all, NT).astype(BF16)
-    grad_mixed = meet(grad_mixed, down_chain, merge_chain)
+    grad_mixed = meet(grad_mixed, merge_sum)
+    first_turned = turned(first_in, order)
     plan = (
-        (down_chain, gate_chain),
-        (up_chain, gate_chain, merge_chain),
-        (up_chain, merge_chain),
-        (),
+        (down_sum, gate_sum),
+        (up_sum, merge_sum),
+        (down_sum, gate_sum),
+        (merge_sum, up_sum, down_sum),
     )
-    dqs, dkvs = [], []
+    dqs, shares, dkv_parts, early = [], [], [], None
     for group in range(kv_heads):
         dq, dkv = attend_back(
-            group, own, bias, log_sums[group], outs[group], queries, grad_mixed, all_kv, kt
+            group, ctx_order, places, bias, log_sums[group], outs[group], queries, grad_mixed,
+            all_keys, all_values, kt,
         )
-        dq, grad_mixed, dkv = meet((dq, grad_mixed, dkv), *plan[group % 4])
+        flying = dkv_parts[-1:]
+        (dq, grad_mixed, dkv, flying) = meet((dq, grad_mixed, dkv, flying), *plan[group % 4])
+        dkv_parts[-1:] = flying
         dqs.append(dq)
-        dkvs.append(lax.psum_scatter(dkv, "ctx", scatter_dimension=0, tiled=True))
-    first_turned = turned(first_in, order)
-    grads = unrotated(dqs, dkvs, cosine, sine)
-    grad_first = mm(grads, attn_all, NT)
+        dkv_parts.append(lax.psum_scatter(dkv, "ctx", scatter_dimension=0, tiled=True))
+        if group == kv_heads - 2:
+            early_grads = unrotated(unrotate_queries_kernel, dqs, cosine, sine)
+            early = Chain(reduce_term(grid, first_turned, early_grads))
+            grad_mixed = meet(grad_mixed, early)
+    split = early_grads.shape[1]
+    late_grads = unrotated(unrotate_queries_kernel, dqs[-1:], cosine, sine)
+    late = Chain(reduce_term(grid, first_turned, late_grads))
+    grad_first = mm(early_grads, attn_all[:, :split], NT)
+    grad_first = grad_first + mm(late_grads, attn_all[:, split:width], NT)
+    grad_first, dkv_parts = meet((grad_first, dkv_parts), early, late, gate_sum, down_sum)
+    kv_grads = unrotated(unrotate_keys_kernel, dkv_parts, cosine, sine)
+    grad_first = grad_first + mm(kv_grads, attn_all[:, width:], NT)
     grad_norm_one, gain_one_term = norm_back(grad_first, normed_one, factor_one, gain_one)
     gain_terms = jnp.stack([gain_one_term, gain_two_term], 0)
     gain_terms = jnp.concatenate([gain_terms, jnp.zeros((WIDE - 2, model), F32)], 0)
-    first_chain = Chain(
-        reduce_term(grid, first_turned, grads, turned(gain_terms.astype(BF16), order))
+    last = Chain(
+        reduce_term(grid, first_turned, kv_grads, turned(gain_terms.astype(BF16), order))
     )
     input_grad = (grad_middle + grad_norm_one).astype(BF16).reshape(layer_in.shape)
-    first_share = finish(first_chain)
-    merge_share, gate_share = finish(merge_chain), finish(gate_chain)
-    up_share, down_share = finish(up_chain), finish(down_chain)
-    edge = width + kv_width
+    input_grad = meet(input_grad, last, early, late, merge_sum, up_sum)
+    while not last.done:
+        input_grad = meet(input_grad, last, early, late)
+    early_share, late_share, last_share = finish(early), finish(late), finish(last)
+    merge_share, gate_share = finish(merge_sum), finish(gate_sum)
+    up_share, down_share = finish(up_sum), finish(down_sum)
     return (
         layer_out,
         input_grad,
-        first_share[:, edge + kv_width],
-        first_share[:, :width],
-        first_share[:, width:edge],
-        first_share[:, edge : edge + kv_width],
+        last_share[:, 2 * kv_width],
+        jnp.concatenate([early_share, late_share], 1),
+        last_share[:, :kv_width],
+        last_share[:, kv_width : 2 * kv_width],
         merge_share,
-        first_share[:, edge + kv_width + 1],
+        last_share[:, 2 * kv_width + 1],
         gate_share,
         up_share,
         down_share,

time: 1470 us -> 1470 us (level)
  waiting for transfers between devices: 504 us -> 447 us
  other arithmetic: 94.7 us -> 134 us
  matrix products: 294 us -> 312 us
  local copies, waits for them, and re-layouts: 106 us -> 88.8 us
  starting transfers between devices: 48.5 us -> 63.7 us
    ppermute x0 -> x6, waiting for transfers between devices: none -> 65.1 us  [next(): return lax.ppermute(values, 'dp', list(zip(self.ring, around)))]
    all_gather x5 -> x4, waiting for transfers between devices: 61.3 us -> 18.5 us  [gather_weight(): column, = (yield [lax.all_gather(weight, 'dp', axis=0)])]
    reduce_scatter x5, waiting for transfers between devices: 126 us -> 88.6 us  [reduce_term(): lax.psum_scatter(joined, 'dp', scatter_dimension=0, tiled=True)]
    all_gather x1 -> x0, waiting for transfers between devices: 33.9 us -> none  [body(): all_kv = lax.all_gather(own_kv, 'ctx', axis=0, tiled=True)]
    convert_element_type x0 -> x5, other arithmetic: none -> 23.4 us  [the longest x4 22.1 us: reduce_ring(): total = (came.astype(F32) + held[(k + 1) % count].astype(F32)).astype(BF16)]
    dot_general x35 -> x47, matrix products: 294 us -> 312 us  [mm(): return lax.dot_general(left, right, dims, preferred_element_type=F32)]
    reduce_scatter x4, waiting for transfers between devices: 15.6 us -> 0.03 us  [body(): lax.psum_scatter(dkv, 'ctx', scatter_dimension=0, tiled=True)]
    convert_element_type x13 -> x16, other arithmetic: 28.4 us -> 42.3 us  [reduce_term(): totals[h] = (part.astype(F32) + own.astype(F32)).astype(BF16)]
  transfers between devices with their start and end apart: 80 -> 97, of which waited for: 30 -> 39; matrix products, arithmetic and copies ran while one was open for 28% -> 31% of each run, Pallas kernels for 26% -> 26%
where the time goes in v3:
time: 1470 us; the launch traced here: 1460 us
  waiting for transfers between devices  447 us (30%)
  Pallas kernels  386 us (26%)
  matrix products  312 us (21%)
  other arithmetic  134 us (9%)
  local copies, waits for them, and re-layouts  88.8 us (6%)
  starting transfers between devices  63.7 us (4%)
  between operations  16.9 us (1%)
    dot_general x47, matrix products, mm(): return lax.dot_general(left, right, dims, preferred_element_type=F32)  312 us
    ppermute x77, waiting for transfers between devices, next(): return lax.ppermute(values, 'ctx', pairs)  261 us
    pallas_call x4, Pallas kernels, attend_back(): pl.pallas_call(functools.partial(attend_back_kernel, which=group % 2, unr...  205 us
    pallas_call x4, Pallas kernels, attend(): pl.pallas_call(functools.partial(attend_kernel, which=group % 2, places=p...  103 us
    reduce_scatter x5, waiting for transfers between devices, reduce_term(): lax.psum_scatter(joined, 'dp', scatter_dimension=0, tiled=True)  88.6 us
    ppermute x6, waiting for transfers between devices, next(): return lax.ppermute(values, 'dp', list(zip(self.ring, around)))  65.1 us
    pallas_call x5, Pallas kernels, placed(): pl.pallas_call(functools.partial(place_kernel, sources=sources, slots=slo...  64.8 us
    ppermute x77, starting transfers between devices, next(): return lax.ppermute(values, 'ctx', pairs)  59.4 us
  transfers between devices with their start and end apart: 97, of which 39 were waited for; matrix products, arithmetic and copies ran while one was open for 31% of the time, Pallas kernels for 26%

profile of v3, /device:TPU:0, one launch (start us, length us, event | category | flops | bytes accessed | tf_op | source)
XLA Modules:
  0.0 1462.8 jit_solution(8587083815697789388)
XLA Ops:
  69.7 27.2 %collective-permute-done.4 = bf16[2,2,64,2688]{3,2,1,0:T(8,128)(2,1)} collective-permute-done((bf16[2,2,64,2688]{3,2,1,0:T(8,128)(2,1)S(1)}, bf16[2,2,64,2688]{3,2,1,0:T(8,128)(2,1)}, u32[]{:S(2)}, u32[]{:S(2)}) %collective-permute-start.4) | collective-permute-done | bytes 1376288 | tf_op jit(solution)/shard_map/ppermute | solution.py:382
  191.0 25.6 %attend.4 = (f32[512,512]{1,0:T(8,128)S(1)}, f32[8,512]{1,0:T(8,128)S(1)}) custom-call(f32[16,512]{1,0:T(8,128)S(1)} %compare_select_fusion.bias_ref, bf16[512,2048]{1,0:T(8,128)(2,1)S(1)} %copy-done.60, bf16[4096,256]{1,0:T(8,128)(2,1)S(1)} %bitcast.223, bf16[256,4096]{1,0:T(8,128)(2,1)S(1)} %copy-done.23), custom_call_target="tpu_custom_call" | custom-call | flops 17179869184 | bytes 3670016 | tf_op jit(solution)/shard_map/attend/pallas_call | solution.py:112
  227.5 29.7 %collective-permute-done.18 = bf16[2,64,5632]{2,1,0:T(8,128)(2,1)} collective-permute-done((bf16[2,64,5632]{2,1,0:T(8,128)(2,1)}, bf16[2,64,5632]{2,1,0:T(8,128)(2,1)}, u32[]{:S(2)}, u32[]{:S(2)}) %collective-permute-start.18) | collective-permute-done | bytes 1441824 | tf_op jit(solution)/shard_map/ppermute | solution.py:382
  261.8 26.1 %attend.5 = (f32[512,512]{1,0:T(8,128)S(1)}, f32[8,512]{1,0:T(8,128)S(1)}) custom-call(f32[16,512]{1,0:T(8,128)S(1)} %compare_select_fusion.bias_ref, bf16[512,2048]{1,0:T(8,128)(2,1)S(1)} %copy-done.61, bf16[4096,256]{1,0:T(8,128)(2,1)S(1)} %bitcast.224, bf16[256,4096]{1,0:T(8,128)(2,1)S(1)} %copy-done.24), custom_call_target="tpu_custom_call" | custom-call | flops 17179869184 | bytes 3670016 | tf_op jit(solution)/shard_map/attend/pallas_call | solution.py:112
  301.4 25.8 %attend.6 = (f32[512,512]{1,0:T(8,128)S(1)}, f32[8,512]{1,0:T(8,128)S(1)}) custom-call(f32[16,512]{1,0:T(8,128)S(1)} %compare_select_fusion.bias_ref, bf16[512,2048]{1,0:T(8,128)(2,1)S(1)} %copy-done.62, bf16[4096,256]{1,0:T(8,128)(2,1)S(1)} %bitcast.230, bf16[256,4096]{1,0:T(8,128)(2,1)S(1)} %copy-done.25), custom_call_target="tpu_custom_call" | custom-call | flops 17179869184 | bytes 3670016 | tf_op jit(solution)/shard_map/attend/pallas_call | solution.py:112
  338.2 55.4 %collective-permute-done.29 = bf16[2,64,5632]{2,1,0:T(8,128)(2,1)} collective-permute-done((bf16[2,64,5632]{2,1,0:T(8,128)(2,1)}, bf16[2,64,5632]{2,1,0:T(8,128)(2,1)}, u32[]{:S(2)}, u32[]{:S(2)}) %collective-permute-start.29) | collective-permute-done | bytes 1441824 | tf_op jit(solution)/shard_map/ppermute | solution.py:382
  398.9 25.7 %attend.7 = (f32[512,512]{1,0:T(8,128)S(1)}, f32[8,512]{1,0:T(8,128)S(1)}) custom-call(f32[16,512]{1,0:T(8,128)S(1)} %compare_select_fusion.bias_ref, bf16[512,2048]{1,0:T(8,128)(2,1)S(1)} %copy-done.63, bf16[4096,256]{1,0:T(8,128)(2,1)S(1)} %bitcast.231, bf16[256,4096]{1,0:T(8,128)(2,1)S(1)} %copy-done.26), custom_call_target="tpu_custom_call" | custom-call | flops 17179869184 | bytes 3670016 | tf_op jit(solution)/shard_map/attend/pallas_call | solution.py:112
  462.4 19.9 %fusion.160 = f32[512,5632]{1,0:T(8,128)} fusion(bf16[512,2048]{1,0:T(8,128)(2,1)} %multiply_convert_fusion.1.x_ref, bf16[2048,5632]{1,0:T(8,128)(2,1)} %bitcast.247), kind=kOutput, calls=%fused_computation.311 | convolution fusion | flops 11811160064 | bytes 36700160 | tf_op jit(solution)/shard_map/dot_general | solution.py:25
  482.3 26.5 %collective-permute-done.37 = bf16[2,2,64,5632]{3,2,1,0:T(8,128)(2,1)} collective-permute-done((bf16[2,2,64,5632]{3,2,1,0:T(8,128)(2,1)}, bf16[2,2,64,5632]{3,2,1,0:T(8,128)(2,1)}, u32[]{:S(2)}, u32[]{:S(2)}) %collective-permute-start.37) | collective-permute-done | bytes 2883616 | tf_op jit(solution)/shard_map/ppermute | solution.py:382
  522.6 17.4 %placed.8 = bf16[32,64,5632]{2,1,0:T(8,128)(2,1)} custom-call(s32[32]{0:T(128)S(1)} %fusion.132.order_ref, bf16[4,64,5632]{2,1,0:T(8,128)(2,1)} %bitcast.76.refs_0_, bf16[4,64,5632]{2,1,0:T(8,128)(2,1)} %bitcast.77.refs_1_, bf16[4,64,5632]{2,1,0:T(8,128)(2,1)} %bitcast.78.refs_2_, bf16[4,64,5632]{2,1,0:T(8,128)(2,1)} %bitcast.79.refs_3_, ...), custom_call_target="tpu_custom_call" | custom-call | bytes 46137344 | tf_op jit(solution)/shard_map/placed/pallas_call | solution.py:546
  540.1 23.3 %multiply_convert_fusion = (bf16[512,5632]{1,0:T(8,128)(2,1)}, f32[512,5632]{1,0:T(8,128)}) fusion(f32[512,5632]{1,0:T(8,128)} %fusion.160, bf16[512,2048]{1,0:T(8,128)(2,1)} %multiply_convert_fusion.1.x_ref, bf16[2048,5632]{1,0:T(8,128)(2,1)} %bitcast.249), kind=kOutput, calls=%fused_computation.7 | convolution fusion | flops 11828461568 | bytes 54001664 | tf_op jit(solution)/shard_map/dot_general | solution.py:25
  563.4 19.1 %collective-permute-done.44 = bf16[2,2,176,2048]{3,2,1,0:T(8,128)(2,1)} collective-permute-done((bf16[2,2,176,2048]{3,2,1,0:T(8,128)(2,1)}, bf16[2,2,176,2048]{3,2,1,0:T(8,128)(2,1)}, u32[]{:S(2)}, u32[]{:S(2)}) %collective-permute-start.44) | collective-permute-done | bytes 2883616 | tf_op jit(solution)/shard_map/ppermute | solution.py:371
  629.4 43.2 %fusion.3 = (bf16[512,5632]{1,0:T(8,128)(2,1)}, bf16[512,5632]{1,0:T(8,128)(2,1)}) fusion(f32[512,5632]{1,0:T(8,128)} %fusion.160, f32[512,5632]{1,0:T(8,128)} %get-tuple-element.397, bf16[5632,2048]{1,0:T(8,128)(2,1)} %bitcast.251, bf16[1,512,2048]{2,1,0:T(8,128)(2,1)S(1)} %copy-done.71), kind=kOutput, calls=%fused_computation.6 | convolution fusion | flops 11848646656 | bytes 59768832 | tf_op jit(solution)/shard_map/dot_general | solution.py:25
  710.2 19.9 %fusion.161 = f32[512,2048]{1,0:T(8,128)} fusion(bf16[512,5632]{1,0:T(8,128)(2,1)} %get-tuple-element.341, bf16[2048,5632]{1,0:T(8,128)(2,1)} %bitcast.248), kind=kOutput, calls=%fused_computation.312 | convolution fusion | flops 11811160064 | bytes 33030144 | tf_op jit(solution)/shard_map/dot_general | solution.py:25
  730.1 19.9 %fusion.25 = bf16[1,512,2048]{2,1,0:T(8,128)(2,1)} fusion(f32[512,2048]{1,0:T(8,128)} %get-tuple-element.395, bf16[512,5632]{1,0:T(8,128)(2,1)} %get-tuple-element.211.x_ref, bf16[5632,2048]{1,0:T(8,128)(2,1)} %bitcast.252), kind=kOutput, calls=%fused_computation.79 | convolution fusion | flops 11813257216 | bytes 35127296 | tf_op jit(solution)/shard_map/dot_general | solution.py:25
  755.6 20.3 %fusion.159 = f32[512,2048]{1,0:T(8,128)} fusion(f32[512,2048]{1,0:T(8,128)} %fusion.161, bf16[512,5632]{1,0:T(8,128)(2,1)} %get-tuple-element.340, bf16[2048,5632]{1,0:T(8,128)(2,1)} %bitcast.250), kind=kOutput, calls=%fused_computation.310 | convolution fusion | flops 11812208640 | bytes 37224448 | tf_op jit(solution)/shard_map/dot_general | solution.py:25
  775.9 45.0 %collective-permute-done.50 = bf16[704,2048]{1,0:T(8,128)(2,1)} collective-permute-done((bf16[704,2048]{1,0:T(8,128)(2,1)}, bf16[704,2048]{1,0:T(8,128)(2,1)}, u32[]{:S(2)}, u32[]{:S(2)}) %collective-permute-start.50) | collective-permute-done | bytes 2883616 | tf_op jit(solution)/shard_map/ppermute | solution.py:371
  880.9 51.4 %attend_back.4 = (f32[512,512]{1,0:T(8,128)S(1)}, bf16[4096,128]{1,0:T(8,128)(2,1)}) custom-call(s32[8]{0:T(128)S(1)} %get-tuple-element.339.order_ref, s32[8]{0:T(128)S(1)} %copy-done.67, f32[16,512]{1,0:T(8,128)S(1)} %compare_select_fusion.bias_ref, f32[8,512]{1,0:T(8,128)S(1)} %get-tuple-element.220.lse_ref, f32[512,512]{1,0:T(8,128)S(1)} %copy-done.48, ...), custom_call_target="tpu_custom_call" | custom-call | flops 42949672960 | bytes 6291456 | tf_op jit(solution)/shard_map/attend_back/pallas_call | solution.py:237
  933.3 37.5 %collective-permute-done.53 = bf16[256,5632]{1,0:T(8,128)(2,1)} collective-permute-done((bf16[256,5632]{1,0:T(8,128)(2,1)}, bf16[256,5632]{1,0:T(8,128)(2,1)}, u32[]{:S(2)}, u32[]{:S(2)}) %collective-permute-start.53) | collective-permute-done | bytes 2883616 | tf_op jit(solution)/shard_map/ppermute | solution.py:382
  988.5 51.6 %attend_back.5 = (f32[512,512]{1,0:T(8,128)S(1)}, bf16[4096,128]{1,0:T(8,128)(2,1)}) custom-call(s32[8]{0:T(128)S(1)} %get-tuple-element.339.order_ref, s32[8]{0:T(128)S(1)} %copy-done.67, f32[16,512]{1,0:T(8,128)S(1)} %compare_select_fusion.bias_ref, f32[8,512]{1,0:T(8,128)S(1)} %get-tuple-element.228.lse_ref, f32[512,512]{1,0:T(8,128)S(1)} %copy-done.46, ...), custom_call_target="tpu_custom_call" | custom-call | flops 42949672960 | bytes 6291456 | tf_op jit(solution)/shard_map/attend_back/pallas_call | solution.py:237
  1057.5 51.1 %attend_back.6 = (f32[512,512]{1,0:T(8,128)S(1)}, bf16[4096,128]{1,0:T(8,128)(2,1)S(1)}) custom-call(s32[8]{0:T(128)S(1)} %get-tuple-element.339.order_ref, s32[8]{0:T(128)S(1)} %copy-done.67, f32[16,512]{1,0:T(8,128)S(1)} %compare_select_fusion.bias_ref, f32[8,512]{1,0:T(8,128)S(1)} %get-tuple-element.236.lse_ref, f32[512,512]{1,0:T(8,128)S(1)} %copy-done.44, ...), custom_call_target="tpu_custom_call" | custom-call | flops 42949672960 | bytes 6291456 | tf_op jit(solution)/shard_map/attend_back/pallas_call | solution.py:237
  1146.8 50.8 %attend_back.7 = (f32[512,512]{1,0:T(8,128)S(1)}, bf16[4096,128]{1,0:T(8,128)(2,1)S(1)}) custom-call(s32[8]{0:T(128)S(1)} %get-tuple-element.339.order_ref, s32[8]{0:T(128)S(1)} %copy-done.67, f32[16,512]{1,0:T(8,128)S(1)} %compare_select_fusion.bias_ref, f32[8,512]{1,0:T(8,128)S(1)} %get-tuple-element.245.lse_ref, f32[512,512]{1,0:T(8,128)S(1)} %copy-done.42, ...), custom_call_target="tpu_custom_call" | custom-call | flops 42949672960 | bytes 6291456 | tf_op jit(solution)/shard_map/attend_back/pallas_call | solution.py:237
  1268.4 27.6 %reduce-scatter.21.cloned.1.call-done = bf16[64,5632]{1,0:T(8,128)(2,1)} async-done(((bf16[256,5632]{1,0:T(8,128)(2,1)}), bf16[64,5632]{1,0:T(8,128)(2,1)}) %reduce-scatter.21.cloned.1.call-update) | async-done | bytes 720912 | tf_op jit(solution)/shard_map/reduce_scatter | solution.py:506
  1335.5 47.6 %reduce-scatter.25.cloned.1.call-done = bf16[64,5632]{1,0:T(8,128)(2,1)} async-done(((bf16[256,5632]{1,0:T(8,128)(2,1)}), bf16[64,5632]{1,0:T(8,128)(2,1)}) %reduce-scatter.25.cloned.1.call-update) | async-done | bytes 720912 | tf_op jit(solution)/shard_map/reduce_scatter | solution.py:506
  (730 shorter events, 658.2 us)
Async XLA Ops:
  10.6 121.0 %all-gather.11.cloned.1.call-start = ((), (), s32[]{:S(2)}) async-start(), calls=%async_computation.20 | async-start | bytes 1310720 | tf_op jit(solution)/shard_map/all_gather | solution.py:567
  99.7 157.5 %all-gather.15.cloned.1.call-start = ((), (), s32[]{:S(2)}) async-start(), calls=%async_computation.22 | async-start | bytes 3604480 | tf_op jit(solution)/shard_map/all_gather | solution.py:567
  146.1 901.9 %reduce-scatter.13.cloned.1.call-start = ((), (), s32[]{:S(2)}) async-start(), calls=%async_computation.10 | async-start | bytes 1179648 | tf_op jit(solution)/shard_map/reduce_scatter | solution.py:807
  289.9 136.3 %collective-permute-start.31 = (bf16[2,2,176,2048]{3,2,1,0:T(8,128)(2,1)S(1)}, bf16[2,2,176,2048]{3,2,1,0:T(8,128)(2,1)}, u32[]{:S(2)}, u32[]{:S(2)}) collective-permute-start(bf16[2,2,176,2048]{3,2,1,0:T(8,128)(2,1)S(1)} %pad_maximum_fusion.2), channel_id=1, source_target_pairs={{0,1},{1,0},{2,3},{3,2},{4,5},{5,4},{6,7},{7,6},{8,9},{9,8},{10,11... | collective-permute-start | bytes 8650760 | tf_op jit(solution)/shard_map/ppermute | solution.py:382
  296.8 129.9 %collective-permute-start.30 = (bf16[2,2,176,2048]{3,2,1,0:T(8,128)(2,1)S(1)}, bf16[2,2,176,2048]{3,2,1,0:T(8,128)(2,1)}, u32[]{:S(2)}, u32[]{:S(2)}) collective-permute-start(bf16[2,2,176,2048]{3,2,1,0:T(8,128)(2,1)S(1)} %pad_maximum_fusion.2), channel_id=1, source_target_pairs={{0,8},{8,24},{24,16},{16,0},{1,9},{9,25},{25,17},{17,1},{2,10},{10... | collective-permute-start | bytes 8650760 | tf_op jit(solution)/shard_map/ppermute | solution.py:371
  296.9 129.9 %collective-permute-start.27 = (bf16[2,2,64,5632]{3,2,1,0:T(8,128)(2,1)S(1)}, bf16[2,2,64,5632]{3,2,1,0:T(8,128)(2,1)}, u32[]{:S(2)}, u32[]{:S(2)}) collective-permute-start(bf16[2,2,64,5632]{3,2,1,0:T(8,128)(2,1)S(1)} %pad_maximum_fusion.1), channel_id=1, source_target_pairs={{0,4},{1,5},{2,6},{3,7},{4,0},{5,1},{6,2},{7,3},{8,12},{9,13},{10,... | collective-permute-start | bytes 8650760 | tf_op jit(solution)/shard_map/ppermute | solution.py:382
  298.5 128.3 %collective-permute-start.26 = (bf16[2,2,64,5632]{3,2,1,0:T(8,128)(2,1)S(1)}, bf16[2,2,64,5632]{3,2,1,0:T(8,128)(2,1)}, u32[]{:S(2)}, u32[]{:S(2)}) collective-permute-start(bf16[2,2,64,5632]{3,2,1,0:T(8,128)(2,1)S(1)} %pad_maximum_fusion), channel_id=1, source_target_pairs={{0,2},{1,3},{2,0},{3,1},{4,6},{5,7},{6,4},{7,5},{8,10},{9,11},{10,... | collective-permute-start | bytes 8650760 | tf_op jit(solution)/shard_map/ppermute | solution.py:382
  300.0 93.6 %collective-permute-start.29 = (bf16[2,64,5632]{2,1,0:T(8,128)(2,1)}, bf16[2,64,5632]{2,1,0:T(8,128)(2,1)}, u32[]{:S(2)}, u32[]{:S(2)}) collective-permute-start(bf16[2,64,5632]{2,1,0:T(8,128)(2,1)} %get-tuple-element.352), channel_id=1, source_target_pairs={{0,2},{1,3},{2,0},{3,1},{4,6},{5,7},{6,4},{7,5},{8,10},{9,11},{10,... | collective-permute-start | bytes 4325384 | tf_op jit(solution)/shard_map/ppermute | solution.py:382
  600.2 149.8 %collective-permute-start.47 = (bf16[2816,2048]{1,0:T(8,128)(2,1)}, bf16[2816,2048]{1,0:T(8,128)(2,1)}, u32[]{:S(2)}, u32[]{:S(2)}) collective-permute-start(bf16[2816,2048]{1,0:T(8,128)(2,1)} %convolution_convert_fusion.2), channel_id=1, source_target_pairs={{0,1},{1,0},{2,3},{3,2},{4,5},{5,4},{6,7},{7,6},{8,9},{9,8},{10,11... | collective-permute-start | bytes 34603016 | tf_op jit(solution)/shard_map/ppermute | solution.py:382
  843.9 202.5 %collective-permute-start.55 = (bf16[256,5632]{1,0:T(8,128)(2,1)}, bf16[256,5632]{1,0:T(8,128)(2,1)}, u32[]{:S(2)}, u32[]{:S(2)}) collective-permute-start(bf16[256,5632]{1,0:T(8,128)(2,1)} %add_convert_fusion.13), channel_id=1, source_target_pairs={{0,2},{1,3},{2,0},{3,1},{4,6},{5,7},{6,4},{7,5},{8,10},{9,11},{10,... | collective-permute-start | bytes 8650760 | tf_op jit(solution)/shard_map/ppermute | solution.py:382
  845.4 202.5 %collective-permute-start.56 = (bf16[256,5632]{1,0:T(8,128)(2,1)}, bf16[256,5632]{1,0:T(8,128)(2,1)}, u32[]{:S(2)}, u32[]{:S(2)}) collective-permute-start(bf16[256,5632]{1,0:T(8,128)(2,1)} %add_convert_fusion.12), channel_id=1, source_target_pairs={{0,4},{1,5},{2,6},{3,7},{4,0},{5,1},{6,2},{7,3},{8,12},{9,13},{10,... | collective-permute-start | bytes 8650760 | tf_op jit(solution)/shard_map/ppermute | solution.py:382
  852.2 118.6 %collective-permute-start.53 = (bf16[256,5632]{1,0:T(8,128)(2,1)}, bf16[256,5632]{1,0:T(8,128)(2,1)}, u32[]{:S(2)}, u32[]{:S(2)}) collective-permute-start(bf16[256,5632]{1,0:T(8,128)(2,1)} %add_convert_fusion.15), channel_id=1, source_target_pairs={{0,2},{1,3},{2,0},{3,1},{4,6},{5,7},{6,4},{7,5},{8,10},{9,11},{10,... | collective-permute-start | bytes 8650760 | tf_op jit(solution)/shard_map/ppermute | solution.py:382
  857.9 114.1 %collective-permute-start.54 = (bf16[256,5632]{1,0:T(8,128)(2,1)}, bf16[256,5632]{1,0:T(8,128)(2,1)}, u32[]{:S(2)}, u32[]{:S(2)}) collective-permute-start(bf16[256,5632]{1,0:T(8,128)(2,1)} %add_convert_fusion.14), channel_id=1, source_target_pairs={{0,4},{1,5},{2,6},{3,7},{4,0},{5,1},{6,2},{7,3},{8,12},{9,13},{10,... | collective-permute-start | bytes 8650760 | tf_op jit(solution)/shard_map/ppermute | solution.py:382
  874.8 97.2 %collective-permute-start.52 = (bf16[704,2048]{1,0:T(8,128)(2,1)}, bf16[704,2048]{1,0:T(8,128)(2,1)}, u32[]{:S(2)}, u32[]{:S(2)}) collective-permute-start(bf16[704,2048]{1,0:T(8,128)(2,1)} %add_convert_fusion.16), channel_id=1, source_target_pairs={{0,8},{8,24},{24,16},{16,0},{1,9},{9,25},{25,17},{17,1},{2,10},{10... | collective-permute-start | bytes 8650760 | tf_op jit(solution)/shard_map/ppermute | solution.py:371
  972.0 139.5 %reduce-scatter.15.cloned.1.call-start = ((), (), s32[]{:S(2)}) async-start(), calls=%async_computation.11 | async-start | bytes 1179648 | tf_op jit(solution)/shard_map/reduce_scatter | solution.py:807
  988.1 122.5 %collective-permute-start.60 = (bf16[128,5632]{1,0:T(8,128)(2,1)}, bf16[128,5632]{1,0:T(8,128)(2,1)}, u32[]{:S(2)}, u32[]{:S(2)}) collective-permute-start(bf16[128,5632]{1,0:T(8,128)(2,1)} %slice.448), channel_id=1, source_target_pairs={{0,4},{1,5},{2,6},{3,7},{4,0},{5,1},{6,2},{7,3},{8,12},{9,13},{10,... | collective-permute-start | bytes 4325384 | tf_op jit(solution)/shard_map/ppermute | solution.py:382
  1048.9 152.6 %reduce-scatter.17.cloned.1.call-start = ((), (), s32[]{:S(2)}) async-start(), calls=%async_computation.12 | async-start | bytes 1179648 | tf_op jit(solution)/shard_map/reduce_scatter | solution.py:807
  1055.3 144.3 %collective-permute-start.63 = (bf16[128,2048]{1,0:T(8,128)(2,1)}, bf16[128,2048]{1,0:T(8,128)(2,1)}, u32[]{:S(2)}, u32[]{:S(2)}) collective-permute-start(bf16[128,2048]{1,0:T(8,128)(2,1)} %slice.454), channel_id=1, source_target_pairs={{0,4},{1,5},{2,6},{3,7},{4,0},{5,1},{6,2},{7,3},{8,12},{9,13},{10,... | collective-permute-start | bytes 1572872 | tf_op jit(solution)/shard_map/ppermute | solution.py:382
  1056.9 142.8 %collective-permute-start.64 = (bf16[128,2048]{1,0:T(8,128)(2,1)}, bf16[128,2048]{1,0:T(8,128)(2,1)}, u32[]{:S(2)}, u32[]{:S(2)}) collective-permute-start(bf16[128,2048]{1,0:T(8,128)(2,1)} %slice.456), channel_id=1, source_target_pairs={{0,2},{1,3},{2,0},{3,1},{4,6},{5,7},{6,4},{7,5},{8,10},{9,11},{10,... | collective-permute-start | bytes 1572872 | tf_op jit(solution)/shard_map/ppermute | solution.py:382
  1133.0 135.4 %reduce-scatter.19.cloned.1.call-start = ((), (), s32[]{:S(2)}) async-start(), calls=%async_computation.13 | async-start | bytes 1179648 | tf_op jit(solution)/shard_map/reduce_scatter | solution.py:807
  1201.5 94.5 %reduce-scatter.21.cloned.1.call-start = ((), (), s32[]{:S(2)}) async-start(), calls=%async_computation.14 | async-start | bytes 3604480 | tf_op jit(solution)/shard_map/reduce_scatter | solution.py:506
  1205.7 124.9 %reduce-scatter.23.cloned.1.call-start = ((), (), s32[]{:S(2)}) async-start(), calls=%async_computation.15 | async-start | bytes 1310720 | tf_op jit(solution)/shard_map/reduce_scatter | solution.py:506
  1221.4 161.7 %reduce-scatter.25.cloned.1.call-start = ((), (), s32[]{:S(2)}) async-start(), calls=%async_computation.16 | async-start | bytes 3604480 | tf_op jit(solution)/shard_map/reduce_scatter | solution.py:506
  1226.0 183.8 %reduce-scatter.27.cloned.1.call-start = ((), (), s32[]{:S(2)}) async-start(), calls=%async_computation.17 | async-start | bytes 983040 | tf_op jit(solution)/shard_map/reduce_scatter | solution.py:506
  (243 other events, 5925.1 us)
Sparse Core Ops, SparseCore 0:
  10.7 36.5 all-gather.8
  69.2 26.7 all-gather.10
  99.9 58.2 all-gather.12
  159.6 57.8 all-gather.14
  972.2 39.2 reduce-scatter.12
  1048.1 39.9 reduce-scatter.14
  1133.1 39.1 reduce-scatter.16
  1201.6 35.1 reduce-scatter.18
  1239.1 56.8 reduce-scatter.20
  1298.8 26.9 reduce-scatter.22
  1328.2 54.8 reduce-scatter.24
  1386.6 23.1 reduce-scatter.26
  1412.7 18.8 reduce-scatter.28
  1434.7 18.2 reduce-scatter.30

commit v4 on v3

--- a/solution.py
+++ b/solution.py
@@ -15,6 +15,7 @@
 SCALE = HD**-0.5
 LOG2E = 1.4426950408889634
 TO_LOG2 = SCALE * LOG2E
+BRIEF = pl.CostEstimate(flops=1 << 20, bytes_accessed=1 << 16, transcendentals=0)
 F32 = jnp.float32
 BF16 = jnp.bfloat16
 NT = (((1,), (1,)), ((), ()))
@@ -133,17 +134,13 @@
             pltpu.VMEM((WIDE, rows), F32),
         ],
         compiler_params=pltpu.CompilerParams(vmem_limit_bytes=40 << 20),
-        cost_estimate=pl.CostEstimate(
-            flops=16 * heads * rows * length * HD,
-            bytes_accessed=2 * (rows * mine + 2 * length * WIDE) + 4 * rows * mine,
-            transcendentals=heads * rows * length,
-        ),
+        cost_estimate=BRIEF,
         name="attend",
     )(bias, q, keys, vt)
 
 
 def attend_back_kernel(
-    order_ref, place_ref, bias_ref, lse_ref, o_ref, q_ref, g_ref, kp_ref, vp_ref, kt_ref,
+    place_ref, bias_ref, lse_ref, o_ref, q_ref, g_ref, kp_ref, vp_ref, kt_ref,
     dq_ref, dkv_ref, k_low, k_high, v_low, v_high, dqt, delta_ref, *, which, unroll
 ):
     rows, width = q_ref.shape
@@ -210,8 +207,7 @@
         lane = lax.broadcasted_iota(jnp.int32, (rows, WIDE), 1)
         key_sum = sums[0] + pltpu.roll(sums[1], HD, 1)
         value_sum = pltpu.roll(sums[2], HD, 1) + sums[3]
-        place = pl.multiple_of(order_ref[index] * rows, rows)
-        dkv_ref[pl.ds(place, rows), :] = jnp.where(
+        dkv_ref[pl.ds(start, rows), :] = jnp.where(
             lane < HD, key_sum * SCALE, value_sum
         ).astype(BF16)
 
@@ -228,7 +224,7 @@
         ).T
 
 
-def attend_back(group, order, places, bias, lse, out, q, g, keys, values, kt, unroll=2):
+def attend_back(group, places, bias, lse, out, q, g, keys, values, kt, unroll=2):
     rows, width = q.shape
     length = keys.shape[0]
     kv_heads = kt.shape[0] // HD
@@ -242,7 +238,6 @@
             jax.ShapeDtypeStruct((length, WIDE), BF16),
         ),
         in_specs=[
-            pl.BlockSpec(memory_space=pltpu.SMEM),
             pl.BlockSpec(memory_space=pltpu.SMEM),
             pl.BlockSpec(bias.shape, lambda i: (0, 0)),
             pl.BlockSpec((heads, rows), lambda i: (0, 0)),
@@ -260,13 +255,9 @@
         scratch_shapes=[pltpu.VMEM((length, WIDE), BF16)] * 4
         + [pltpu.VMEM((mine, rows), F32), pltpu.VMEM((heads, rows), F32)],
         compiler_params=pltpu.CompilerParams(vmem_limit_bytes=48 << 20),
-        cost_estimate=pl.CostEstimate(
-            flops=40 * heads * rows * length * HD,
-            bytes_accessed=2 * (2 * rows * mine + 4 * length * WIDE) + 4 * rows * mine,
-            transcendentals=heads * rows * length,
-        ),
+        cost_estimate=BRIEF,
         name="attend_back",
-    )(order, jnp.array(places, jnp.int32), bias, lse, out, q, g, keys, values, kt)
+    )(jnp.array(places, jnp.int32), bias, lse, out, q, g, keys, values, kt)
 
 
 def turn_pairs(x, cosine, sine):
@@ -388,17 +379,23 @@
         c = (self.c - rows[:, 0]) % 2
         return ((rows[:, 1] * self.n_a + a) * self.n_b + b) * 2 + c
 
-    def block_order(self):
+    def block_order(self, around):
         half = self.n_dp // 2
-        rows = []
+        rows, hops = [], []
         for core in range(2):
             for h, (first, second) in enumerate(HALVES):
                 for i in range(self.size(first)):
                     for j in range(self.size(second)):
                         for d in range(half):
                             near = {first: i, second: j}
-                            rows.append((core, h * half + d, near["a"], near["b"]))
-        return self.natural(rows)
+                            at = h * half + d
+                            rows.append((core, 0 if around else at, near["a"], near["b"]))
+                            hops.append(at)
+        return self.natural(rows) + (self.around(hops) * self.n_ctx if around else 0)
+
+    def around(self, hops):
+        ring = jnp.asarray(np.array(self.ring, np.int32))
+        return ring[(self.d - np.array(hops, np.int32)) % self.n_dp]
 
     def ring_order(self):
         rows, hops = [], []
@@ -408,10 +405,7 @@
                     for a in range(self.n_a):
                         rows.append((core, 0, a, b))
                         hops.append(d)
-        place = jnp.asarray(np.array(self.ring, np.int32))[
-            (self.d - np.array(hops, np.int32)) % self.n_dp
-        ]
-        return self.natural(rows) + place * self.n_ctx
+        return self.natural(rows) + self.around(hops) * self.n_ctx
 
     def ctx_order(self):
         rows = [
@@ -462,7 +456,7 @@
     )(order, x)
 
 
-def reduce_term(grid, left, right, extra=None):
+def reduce_term(grid, left, right, extra=None, around=False):
     rows = left.shape[0]
     mine = rows // 2
 
@@ -502,9 +496,19 @@
                 count = grid.size(HALVES[h][1])
                 size = total.shape[0] // count
                 held.append([total[j * size : (j + 1) * size] for j in range(count)])
-    joined = jnp.concatenate(totals, 0)
-    (share,) = yield [lax.psum_scatter(joined, "dp", scatter_dimension=0, tiled=True)]
-    return share.astype(F32)
+    if not around:
+        joined = jnp.concatenate(totals, 0)
+        (share,) = yield [lax.psum_scatter(joined, "dp", scatter_dimension=0, tiled=True)]
+        return share.astype(F32)
+    half = grid.n_dp // 2
+    size = totals[0].shape[0] // half
+    held = [t[at : at + size] for t in totals for at in range(0, half * size, size)]
+    total = held[1]
+    for k in range(1, grid.n_dp):
+        (came,) = yield [grid.next(total, "d")]
+        total = came.astype(F32) + held[(k + 1) % grid.n_dp].astype(F32)
+        total = total if k == grid.n_dp - 1 else total.astype(BF16)
+    return total
 
 
 def place_kernel(order_ref, *refs, sources, slots):
@@ -563,10 +567,17 @@
     return whole.reshape(len(sources) * blk, width)
 
 
-def gather_weight(grid, weight, order):
-    (column,) = yield [lax.all_gather(weight, "dp", axis=0)]
+def gather_weight(grid, weight, around=False):
     half = grid.n_dp // 2
-    parts = [column[:half], column[half:]]
+    if around:
+        column = [weight]
+        for _ in range(grid.n_dp - 1):
+            (came,) = yield [grid.next(column[-1], "d")]
+            column.append(came)
+        parts = [jnp.stack(column[:half]), jnp.stack(column[half:])]
+    else:
+        (column,) = yield [lax.all_gather(weight, "dp", axis=0)]
+        parts = [column[:half], column[half:]]
     steps = [[parts[0]], [parts[1]]]
     for stage in (1, 0):
         counts = [grid.size(axes[stage]) for axes in HALVES]
@@ -577,9 +588,9 @@
                 steps[h].append(part)
         if stage == 1:
             steps = [[jnp.stack(s)] for s in steps]
-    near = steps[0] + steps[1]
-    far = yield [grid.next(piece, "c") for piece in near]
-    return placed(order, near + list(far))
+    near = jnp.concatenate([p.reshape((-1,) + p.shape[-2:]) for p in steps[0] + steps[1]], 0)
+    (far,) = yield [grid.next(near, "c")]
+    return placed(grid.block_order(around), [near, far])
 
 
 def gather_ring(grid, weight):
@@ -591,11 +602,19 @@
             steps.append(came)
         part = jnp.stack(steps)
     near, far = [part], []
-    for _ in range(grid.n_dp - 1):
-        came, other = yield [grid.next(near[-1], "d"), grid.next(near[-1], "c")]
-        near.append(came)
-        far.append(other)
-    (other,) = yield [grid.next(near[-1], "c")]
+    waiting = [part]
+    for k in range(grid.n_dp - 1):
+        sent = [grid.next(near[-1], "d")]
+        early = k == grid.n_dp - 2
+        if early:
+            sent.append(grid.next(jnp.stack(waiting[:-1]), "c"))
+            waiting = waiting[-1:]
+        came = yield sent
+        if early:
+            far.append(came[1])
+        near.append(came[0])
+        waiting.append(came[0])
+    (other,) = yield [grid.next(jnp.stack(waiting), "c")]
     return placed(grid.ring_order(), near + far + [other])
 
 
@@ -637,6 +656,21 @@
     )
 
 
+def reduce_keys(grid, terms):
+    mine = terms.shape[0] // 2
+    (came,) = yield [grid.next(terms[mine:], "c")]
+    total = (terms[:mine].astype(F32) + came.astype(F32)).astype(BF16)
+    for axis in ("b", "a"):
+        count = grid.size(axis)
+        size = total.shape[0] // count
+        held = [total[at : at + size] for at in range(0, count * size, size)]
+        total = held[1]
+        for k in range(1, count):
+            (came,) = yield [grid.next(total, axis)]
+            total = (came.astype(F32) + held[(k + 1) % count].astype(F32)).astype(BF16)
+    return total
+
+
 class Chain:
     def __init__(self, generator):
         self.generator, self.done, self.result = generator, False, None
@@ -654,6 +688,13 @@
     main, flights = lax.optimization_barrier((main, [list(c.flight) for c in chains]))
     for chain, flight in zip(chains, flights):
         chain.advance(flight)
+    return main
+
+
+def settle(main, *chains):
+    main, flights = lax.optimization_barrier((main, [list(c.flight) for c in chains]))
+    for chain, flight in zip(chains, flights):
+        chain.flight = flight
     return main
 
 
@@ -705,128 +746,147 @@
     run = rows // 2
     positions = positions[0]
     grid = Grid(n_dp, n_ctx)
-    order, ring_order, ctx_order = grid.block_order(), grid.ring_order(), grid.ctx_order()
+    order, sum_order = grid.block_order(False), grid.block_order(True)
+    ring_order, ctx_order = grid.ring_order(), grid.ctx_order()
     places = grid.value_places()
 
     gains = jnp.stack([attn_gain, ffn_gain], -1)
     gains = jnp.concatenate([gains, jnp.zeros((gains.shape[0], WIDE - 2), BF16)], 1)
     packed = jnp.concatenate([query_proj, key_proj, value_proj, gains], 1)
-    first_chain = Chain(gather_weight(grid, packed, order))
-    down_chain = Chain(gather_ring(grid, down_proj))
+    down_chain = Chain(gather_weight(grid, down_proj))
+    first_chain = Chain(gather_weight(grid, packed, True))
+    up_chain = Chain(gather_ring(grid, up_proj))
     all_pos = lax.all_gather(positions[::run], "ctx", axis=0, tiled=True)
     cosine, sine = angles(positions)
     rows_in = layer_in.reshape(rows, model).astype(F32)
     normed_one, factor_one = normalize(rows_in)
-    all_pos, merge_proj, factor_one = meet((all_pos, merge_proj, factor_one), first_chain, down_chain)
-    merge_chain = Chain(gather_weight(grid, merge_proj, order))
-    gate_proj = meet(gate_proj, first_chain)
-    gate_chain = Chain(gather_weight(grid, gate_proj, order))
+    all_pos, gate_proj = meet((all_pos, gate_proj), first_chain, up_chain)
+    gate_chain = Chain(gather_weight(grid, gate_proj))
+    factor_one, merge_proj = meet((factor_one, merge_proj), first_chain)
+    merge_chain = Chain(gather_weight(grid, merge_proj))
+    cosine, sine = meet((cosine, sine), first_chain)
+    cosine = meet(cosine, first_chain, down_chain)
     first_weights = finish(first_chain)
+    first_weights = meet(first_weights, down_chain, up_chain)
+    first_weights = settle(first_weights, gate_chain)
     attn_all = first_weights[:, : width + 2 * kv_width]
     gain_one = first_weights[:, width + 2 * kv_width].astype(F32)
     gain_two = first_weights[:, width + 2 * kv_width + 1].astype(F32)
 
     first_in = (normed_one * gain_one).astype(BF16)
     raw = mm(first_in, attn_all, NN)
-    raw, up_proj = meet((raw, up_proj), merge_chain)
-    up_chain = Chain(gather_weight(grid, up_proj, order))
     queries, own_kv = rotated(raw, cosine, sine, kv_width)
     kv_chain = Chain(gather_keys(grid, own_kv))
     later = all_pos.reshape(n_ctx, 2)[ctx_order].reshape(2 * n_ctx, 1)
     later = later > jnp.repeat(positions[::run], run)[None, :]
     bias = jnp.where(later, MASKED, 0.0).astype(F32)
-    bias = meet(bias, kv_chain, gate_chain, merge_chain)
     bias = meet(bias, kv_chain)
+    bias = meet(bias, kv_chain)
+    bias = settle(bias, merge_chain)
+    bias = meet(bias, kv_chain, gate_chain)
     all_keys, all_values = finish(kv_chain)
     kt, vt = all_keys.T, all_values.T
 
+    grad_rows = out_grad.reshape(rows, model)
     plan = (
-        (gate_chain, merge_chain, up_chain, down_chain),
-        (merge_chain,),
-        (),
-        (gate_chain, up_chain, down_chain),
+        (down_chain, gate_chain, up_chain),
+        (down_chain, merge_chain),
+        (gate_chain, merge_chain, up_chain),
+        (gate_chain, merge_chain),
     )
     outs, log_sums = [], []
     for group in range(kv_heads):
         out, log_sum = attend(group, places, bias, queries, all_keys, vt)
-        queries, out = meet((queries, out), *plan[group % 4])
+        queries, out, grad_rows = meet((queries, out, grad_rows), *plan[group % 4])
+        if group == 1:
+            down_all = finish(down_chain)
+            grad_hidden = mm(grad_rows, down_all, NT)
+            queries, grad_hidden = lax.optimization_barrier((queries, grad_hidden))
         outs.append(out)
         log_sums.append(log_sum)
     mixed = jnp.concatenate([out.astype(BF16) for out in outs], 1)
-    merge_all = finish(merge_chain)
+    gate_all, merge_all = finish(gate_chain), finish(merge_chain)
     middle = rows_in + mm(mixed, merge_all, NN)
     normed_two, factor_two = normalize(middle)
     second_in = (normed_two * gain_two).astype(BF16)
-    second_in = meet(second_in, gate_chain)
-    gate_all = finish(gate_chain)
     gate = mm(second_in, gate_all, NN)
-    gate = meet(gate, up_chain, down_chain)
+    gate = meet(gate, up_chain)
     up_all = finish(up_chain)
     lift = mm(second_in, up_all, NN)
     sigma = jax.nn.sigmoid(gate)
     activated = gate * sigma
     hidden = (activated * lift).astype(BF16)
-    grad_rows = out_grad.reshape(rows, model)
-    down_sum = Chain(reduce_ring(grid, turned(hidden, ring_order), grad_rows))
-    hidden = meet(hidden, down_chain)
-    down_all = finish(down_chain)
-    result = middle + mm(hidden, down_all, NN)
-    layer_out = result.astype(BF16).reshape(layer_in.shape)
-    layer_out = meet(layer_out, down_sum)
-    grad_hidden = mm(grad_rows, down_all, NT)
     grad_gate = (grad_hidden * lift * sigma * (1.0 + gate * (1.0 - sigma))).astype(BF16)
     grad_lift = (grad_hidden * activated).astype(BF16)
+    hidden, grad_gate, grad_lift = lax.optimization_barrier((hidden, grad_gate, grad_lift))
     second_turned = turned(second_in, order)
     gate_sum = Chain(reduce_term(grid, second_turned, grad_gate))
     up_sum = Chain(reduce_term(grid, second_turned, grad_lift))
-    grad_second = mm(grad_gate, gate_all, NT) + mm(grad_lift, up_all, NT)
-    grad_second = meet(grad_second, gate_sum, up_sum, down_sum)
+    down_sum = Chain(reduce_ring(grid, turned(hidden, ring_order), grad_rows))
+    grad_second = mm(grad_gate, gate_all, NT)
+    grad_second, grad_lift, hidden = meet((grad_second, grad_lift, hidden), gate_sum)
+    grad_second = grad_second + mm(grad_lift, up_all, NT)
+    result = middle + mm(hidden, down_all, NN)
+    layer_out = result.astype(BF16).reshape(layer_in.shape)
     grad_norm_two, gain_two_term = norm_back(grad_second, normed_two, factor_two, gain_two)
     grad_middle = grad_rows.astype(F32) + grad_norm_two
     grad_branch = grad_middle.astype(BF16)
-    merge_sum = Chain(reduce_term(grid, turned(mixed, order), grad_branch))
     grad_mixed = mm(grad_branch, merge_all, NT).astype(BF16)
-    grad_mixed = meet(grad_mixed, merge_sum)
-    first_turned = turned(first_in, order)
-    plan = (
-        (down_sum, gate_sum),
-        (up_sum, merge_sum),
-        (down_sum, gate_sum),
-        (merge_sum, up_sum, down_sum),
+    grad_mixed, layer_out, grad_branch = meet(
+        (grad_mixed, layer_out, grad_branch), down_sum, up_sum
     )
-    dqs, shares, dkv_parts, early = [], [], [], None
+    first_turned = turned(first_in, sum_order)
+    mixed_turned = turned(mixed, order)
+
+    dqs, dkvs = [], []
     for group in range(kv_heads):
         dq, dkv = attend_back(
-            group, ctx_order, places, bias, log_sums[group], outs[group], queries, grad_mixed,
+            group, places, bias, log_sums[group], outs[group], queries, grad_mixed,
             all_keys, all_values, kt,
         )
-        flying = dkv_parts[-1:]
-        (dq, grad_mixed, dkv, flying) = meet((dq, grad_mixed, dkv, flying), *plan[group % 4])
-        dkv_parts[-1:] = flying
         dqs.append(dq)
-        dkv_parts.append(lax.psum_scatter(dkv, "ctx", scatter_dimension=0, tiled=True))
-        if group == kv_heads - 2:
+        dkvs.append(dkv)
+        if group == kv_heads - 4:
+            grad_mixed, dkv, grad_branch = meet(
+                (grad_mixed, dkv, grad_branch), gate_sum, down_sum
+            )
+        elif group == kv_heads - 3:
+            grad_mixed, dkv, grad_branch = meet(
+                (grad_mixed, dkv, grad_branch), gate_sum, up_sum, down_sum
+            )
+            merge_sum = Chain(reduce_term(grid, mixed_turned, grad_branch))
+        elif group == kv_heads - 2:
             early_grads = unrotated(unrotate_queries_kernel, dqs, cosine, sine)
-            early = Chain(reduce_term(grid, first_turned, early_grads))
-            grad_mixed = meet(grad_mixed, early)
+            grad_mixed, early_grads, dkvs = meet(
+                (grad_mixed, early_grads, dkvs), up_sum, merge_sum, down_sum
+            )
+            early = Chain(reduce_term(grid, first_turned, early_grads, around=True))
+            keys_sum = Chain(reduce_keys(grid, jnp.concatenate(dkvs, 1)))
+    dq, dkv = meet((dq, dkv), gate_sum, merge_sum, down_sum, early, keys_sum)
+    last_keys = Chain(reduce_keys(grid, dkv))
+    late_grads = unrotated(unrotate_queries_kernel, dqs[-1:], cosine, sine)
     split = early_grads.shape[1]
-    late_grads = unrotated(unrotate_queries_kernel, dqs[-1:], cosine, sine)
-    late = Chain(reduce_term(grid, first_turned, late_grads))
     grad_first = mm(early_grads, attn_all[:, :split], NT)
+    grad_first = meet(grad_first, last_keys, keys_sum)
     grad_first = grad_first + mm(late_grads, attn_all[:, split:width], NT)
-    grad_first, dkv_parts = meet((grad_first, dkv_parts), early, late, gate_sum, down_sum)
+    late = Chain(reduce_term(grid, first_turned, late_grads, around=True))
+    grad_first = meet(grad_first, last_keys, keys_sum, early, merge_sum)
+    grad_first = meet(grad_first, last_keys, up_sum, down_sum)
+    wide = finish(keys_sum)
+    dkv_parts = [wide[:, at : at + WIDE] for at in range(0, wide.shape[1], WIDE)]
+    dkv_parts.append(finish(last_keys))
     kv_grads = unrotated(unrotate_keys_kernel, dkv_parts, cosine, sine)
     grad_first = grad_first + mm(kv_grads, attn_all[:, width:], NT)
     grad_norm_one, gain_one_term = norm_back(grad_first, normed_one, factor_one, gain_one)
     gain_terms = jnp.stack([gain_one_term, gain_two_term], 0)
     gain_terms = jnp.concatenate([gain_terms, jnp.zeros((WIDE - 2, model), F32)], 0)
-    last = Chain(
-        reduce_term(grid, first_turned, kv_grads, turned(gain_terms.astype(BF16), order))
-    )
+    gain_terms = meet(gain_terms, early, late, down_sum)
+    gain_columns = turned(gain_terms.astype(BF16), sum_order)
+    last = Chain(reduce_term(grid, first_turned, kv_grads, gain_columns, around=True))
     input_grad = (grad_middle + grad_norm_one).astype(BF16).reshape(layer_in.shape)
-    input_grad = meet(input_grad, last, early, late, merge_sum, up_sum)
-    while not last.done:
-        input_grad = meet(input_grad, last, early, late)
+    waiting = (last, late, early, down_sum)
+    while not all(c.done for c in waiting):
+        input_grad = meet(input_grad, *waiting)
     early_share, late_share, last_share = finish(early), finish(late), finish(last)
     merge_share, gate_share = finish(merge_sum), finish(gate_sum)
     up_share, down_share = finish(up_sum), finish(down_sum)

time: 1470 us -> 1360 us (0.925)
  waiting for transfers between devices: 447 us -> 312 us
  starting transfers between devices: 63.7 us -> 96.5 us
  other arithmetic: 134 us -> 151 us
  matrix products: 312 us -> 296 us
    ppermute x77 -> x69, waiting for transfers between devices: 261 us -> 169 us  [next(): return lax.ppermute(values, 'ctx', pairs)]
    reduce_scatter x5 -> x3, waiting for transfers between devices: 88.6 us -> 0.04 us  [reduce_term(): lax.psum_scatter(joined, 'dp', scatter_dimension=0, tiled=True)]
    ppermute x6 -> x18, waiting for transfers between devices: 65.1 us -> 137 us  [next(): return lax.ppermute(values, 'dp', list(zip(self.ring, around)))]
    ppermute x6 -> x18, starting transfers between devices: 2.67 us -> 38.5 us  [next(): return lax.ppermute(values, 'dp', list(zip(self.ring, around)))]
    convert_element_type x0 -> x13, other arithmetic: none -> 21.2 us  [the longest x1 13.3 us: body(): grad_lift = (grad_hidden * activated).astype(BF16)]
    convert_element_type x4 -> x1, other arithmetic: 22.1 us -> 2.02 us  [reduce_ring(): total = (came.astype(F32) + held[(k + 1) % count].astype(F32)).astype(BF16)]
    concatenate x0 -> x4, other arithmetic: none -> 18.8 us  [gather_weight(): jnp.concatenate([p.reshape((-1,) + p.shape[-2:]) for p in steps[0] + step...]
    dot_general x47, matrix products: 312 us -> 296 us  [mm(): return lax.dot_general(left, right, dims, preferred_element_type=F32)]
  transfers between devices with their start and end apart: 97 -> 93, of which waited for: 39 -> 32; matrix products, arithmetic and copies ran while one was open for 31% -> 30% of each run, Pallas kernels for 26% -> 27%
where the time goes in v4:
time: 1360 us; the launch traced here: 1350 us
  Pallas kernels  382 us (28%)
  waiting for transfers between devices  312 us (23%)
  matrix products  296 us (22%)
  other arithmetic  151 us (11%)
  starting transfers between devices  96.5 us (7%)
  local copies, waits for them, and re-layouts  91.3 us (7%)
  between operations  17.3 us (1%)
    dot_general x47, matrix products, mm(): return lax.dot_general(left, right, dims, preferred_element_type=F32)  296 us
    pallas_call x4, Pallas kernels, attend_back(): pl.pallas_call(functools.partial(attend_back_kernel, which=group % 2, unr...  204 us
    ppermute x69, waiting for transfers between devices, next(): return lax.ppermute(values, 'ctx', pairs)  169 us
    ppermute x18, waiting for transfers between devices, next(): return lax.ppermute(values, 'dp', list(zip(self.ring, around)))  137 us
    pallas_call x4, Pallas kernels, attend(): pl.pallas_call(functools.partial(attend_kernel, which=group % 2, places=p...  103 us
    pallas_call x5, Pallas kernels, placed(): pl.pallas_call(functools.partial(place_kernel, sources=sources, slots=slo...  61.8 us
    ppermute x69, starting transfers between devices, next(): return lax.ppermute(values, 'ctx', pairs)  57.5 us
    ppermute x18, starting transfers between devices, next(): return lax.ppermute(values, 'dp', list(zip(self.ring, around)))  38.5 us
  transfers between devices with their start and end apart: 93, of which 32 were waited for; matrix products, arithmetic and copies ran while one was open for 30% of the time, Pallas kernels for 27%

profile of v4, /device:TPU:0, one launch (start us, length us, event | category | flops | bytes accessed | tf_op | source)
XLA Modules:
  0.0 1352.7 jit_solution(8977034878570586078)
XLA Ops:
  34.0 20.3 %collective-permute-done.2 = bf16[64,2688]{1,0:T(8,128)(2,1)S(1)} collective-permute-done((bf16[64,2688]{1,0:T(8,128)(2,1)S(1)}, bf16[64,2688]{1,0:T(8,128)(2,1)S(1)}, u32[]{:S(2)}, u32[]{:S(2)}) %collective-permute-start.2) | collective-permute-done | bytes 344096 | tf_op jit(solution)/shard_map/ppermute | solution.py:362
  61.0 20.0 %collective-permute-done.3 = bf16[64,2688]{1,0:T(8,128)(2,1)S(1)} collective-permute-done((bf16[64,2688]{1,0:T(8,128)(2,1)S(1)}, bf16[64,2688]{1,0:T(8,128)(2,1)S(1)}, u32[]{:S(2)}, u32[]{:S(2)}) %collective-permute-start.3) | collective-permute-done | bytes 344096 | tf_op jit(solution)/shard_map/ppermute | solution.py:362
  98.1 23.3 %collective-permute-done.7 = bf16[2,2,64,2688]{3,2,1,0:T(8,128)(2,1)S(1)} collective-permute-done((bf16[2,2,64,2688]{3,2,1,0:T(8,128)(2,1)S(1)}, bf16[2,2,64,2688]{3,2,1,0:T(8,128)(2,1)S(1)}, u32[]{:S(2)}, u32[]{:S(2)}) %collective-permute-start.7) | collective-permute-done | bytes 1376288 | tf_op jit(solution)/shard_map/ppermute | solution.py:373
  169.2 26.5 %collective-permute-done.10 = bf16[2,176,2048]{2,1,0:T(8,128)(2,1)S(1)} collective-permute-done((bf16[2,176,2048]{2,1,0:T(8,128)(2,1)}, bf16[2,176,2048]{2,1,0:T(8,128)(2,1)S(1)}, u32[]{:S(2)}, u32[]{:S(2)}) %collective-permute-start.10) | collective-permute-done | bytes 1441824 | tf_op jit(solution)/shard_map/ppermute | solution.py:373
  285.6 25.6 %attend.4 = (f32[512,512]{1,0:T(8,128)S(1)}, f32[8,512]{1,0:T(8,128)S(1)}) custom-call(f32[16,512]{1,0:T(8,128)S(1)} %compare_select_fusion.bias_ref, bf16[512,2048]{1,0:T(8,128)(2,1)S(1)} %copy-done.2, bf16[4096,256]{1,0:T(8,128)(2,1)S(1)} %bitcast.176, bf16[256,4096]{1,0:T(8,128)(2,1)S(1)} %copy-done.6), custom_call_target="tpu_custom_call" | custom-call | flops 1048576 | bytes 65536 | tf_op jit(solution)/shard_map/attend/pallas_call | solution.py:113
  331.4 22.2 %collective-permute-done.20 = bf16[2,64,5632]{2,1,0:T(8,128)(2,1)} collective-permute-done((bf16[2,64,5632]{2,1,0:T(8,128)(2,1)}, bf16[2,64,5632]{2,1,0:T(8,128)(2,1)}, u32[]{:S(2)}, u32[]{:S(2)}) %collective-permute-start.20) | collective-permute-done | bytes 1441824 | tf_op jit(solution)/shard_map/ppermute | solution.py:373
  371.4 25.9 %attend.5 = (f32[512,512]{1,0:T(8,128)S(1)}, f32[8,512]{1,0:T(8,128)S(1)}) custom-call(f32[16,512]{1,0:T(8,128)S(1)} %compare_select_fusion.bias_ref, bf16[512,2048]{1,0:T(8,128)(2,1)S(1)} %copy-done.2, bf16[4096,256]{1,0:T(8,128)(2,1)S(1)} %bitcast.177, bf16[256,4096]{1,0:T(8,128)(2,1)S(1)} %copy-done.6), custom_call_target="tpu_custom_call" | custom-call | flops 1048576 | bytes 65536 | tf_op jit(solution)/shard_map/attend/pallas_call | solution.py:113
  401.0 15.2 %placed.6 = bf16[32,176,2048]{2,1,0:T(8,128)(2,1)} custom-call(s32[32]{0:T(128)S(1)} %get-tuple-element.369.order_ref, bf16[16,176,2048]{2,1,0:T(8,128)(2,1)S(1)} %pad_maximum_fusion.refs_0_, bf16[16,176,2048]{2,1,0:T(8,128)(2,1)} %collective-permute-done.23.refs_1_), custom_call_target="tpu_custom_call" | custom-call | bytes 46137344 | tf_op jit(solution)/shard_map/placed/pallas_call | solution.py:550
  416.1 19.8 %fusion.140 = f32[512,5632]{1,0:T(8,128)} fusion(bf16[512,2048]{1,0:T(8,128)(2,1)} %bitcast.222, bf16[5632,2048]{1,0:T(8,128)(2,1)} %bitcast.210), kind=kOutput, calls=%fused_computation.329 | convolution fusion | flops 11811160064 | bytes 36700160 | tf_op jit(solution)/shard_map/dot_general | solution.py:26
  439.1 25.8 %attend.6 = (f32[512,512]{1,0:T(8,128)S(1)}, f32[8,512]{1,0:T(8,128)S(1)}) custom-call(f32[16,512]{1,0:T(8,128)S(1)} %compare_select_fusion.bias_ref, bf16[512,2048]{1,0:T(8,128)(2,1)S(1)} %copy-done.3, bf16[4096,256]{1,0:T(8,128)(2,1)S(1)} %bitcast.178, bf16[256,4096]{1,0:T(8,128)(2,1)S(1)} %copy-done.7), custom_call_target="tpu_custom_call" | custom-call | flops 1048576 | bytes 65536 | tf_op jit(solution)/shard_map/attend/pallas_call | solution.py:113
  475.9 25.5 %attend.7 = (f32[512,512]{1,0:T(8,128)S(1)}, f32[8,512]{1,0:T(8,128)S(1)}) custom-call(f32[16,512]{1,0:T(8,128)S(1)} %compare_select_fusion.bias_ref, bf16[512,2048]{1,0:T(8,128)(2,1)S(1)} %copy-done.3, bf16[4096,256]{1,0:T(8,128)(2,1)S(1)} %bitcast.179, bf16[256,4096]{1,0:T(8,128)(2,1)S(1)} %copy-done.7), custom_call_target="tpu_custom_call" | custom-call | flops 1048576 | bytes 65536 | tf_op jit(solution)/shard_map/attend/pallas_call | solution.py:113
  517.1 15.3 %placed.8 = bf16[32,64,5632]{2,1,0:T(8,128)(2,1)} custom-call(s32[32]{0:T(128)S(1)} %get-tuple-element.369.order_ref, bf16[16,64,5632]{2,1,0:T(8,128)(2,1)S(1)} %pad_maximum_fusion.1.refs_0_, bf16[16,64,5632]{2,1,0:T(8,128)(2,1)} %collective-permute-done.29.refs_1_), custom_call_target="tpu_custom_call" | custom-call | bytes 46137344 | tf_op jit(solution)/shard_map/placed/pallas_call | solution.py:550
  544.9 19.1 %fusion.141 = f32[512,5632]{1,0:T(8,128)} fusion(bf16[512,2048]{1,0:T(8,128)(2,1)S(1)} %multiply_convert_fusion.3.x_ref, bf16[2048,5632]{1,0:T(8,128)(2,1)} %bitcast.212), kind=kOutput, calls=%fused_computation.330 | convolution fusion | flops 11811160064 | bytes 36700160 | tf_op jit(solution)/shard_map/dot_general | solution.py:26
  591.2 15.4 %placed.9 = bf16[32,64,5632]{2,1,0:T(8,128)(2,1)} custom-call(s32[32]{0:T(128)S(1)} %get-tuple-element.367.order_ref, bf16[4,64,5632]{2,1,0:T(8,128)(2,1)} %bitcast.76.refs_0_, bf16[4,64,5632]{2,1,0:T(8,128)(2,1)} %bitcast.77.refs_1_, bf16[4,64,5632]{2,1,0:T(8,128)(2,1)} %bitcast.78.refs_2_, bf16[4,64,5632]{2,1,0:T(8,128)(2,1)} %bitcast.79.refs_3_, ...), custom_call_target="tpu_custom_call" | custom-call | bytes 46137344 | tf_op jit(solution)/shard_map/placed/pallas_call | solution.py:550
  606.6 19.4 %fusion.142 = f32[512,5632]{1,0:T(8,128)} fusion(bf16[512,2048]{1,0:T(8,128)(2,1)S(1)} %multiply_convert_fusion.3.x_ref, bf16[2048,5632]{1,0:T(8,128)(2,1)} %bitcast.214), kind=kOutput, calls=%fused_computation.331 | convolution fusion | flops 11811160064 | bytes 36700160 | tf_op jit(solution)/shard_map/dot_general | solution.py:26
  669.9 19.6 %fusion.143 = f32[512,2048]{1,0:T(8,128)} fusion(bf16[512,5632]{1,0:T(8,128)(2,1)} %copy-done.55, bf16[2048,5632]{1,0:T(8,128)(2,1)} %bitcast.213), kind=kOutput, calls=%fused_computation.332 | convolution fusion | flops 11811160064 | bytes 33030144 | tf_op jit(solution)/shard_map/dot_general | solution.py:26
  689.5 19.7 %multiply_reduce_fusion = (f32[2048]{0:T(1024)}, f32[512]{0:T(512)S(1)}, f32[512,2048]{1,0:T(8,128)S(1)}) fusion(f32[512,2048]{1,0:T(8,128)} %copy-done.61, f32[512]{0:T(512)S(1)} %add_rsqrt_fusion, f32[512,2048]{1,0:T(8,128)} %fusion.143, f32[2048]{0:T(1024)S(1)} %bitcast.249, bf16[512,5632]{1,0:T(8,128)(2,1)} %copy-done.54, bf16[2048,5632]{1,0:T(8,128)(2,1)} %bitcast.215), kind=kOutput, calls=%fused_computation.53 | convolution fusion | flops 11818498048 | bytes 41439232 | tf_op jit(solution)/shard_map/dot_general | solution.py:26
  736.9 17.5 %fusion.18 = bf16[1,512,2048]{2,1,0:T(8,128)(2,1)} fusion(f32[512,2048]{1,0:T(8,128)S(1)} %copy-done.62, bf16[512,5632]{1,0:T(8,128)(2,1)S(1)} %bitcast.191, bf16[5632,2048]{1,0:T(8,128)(2,1)} %bitcast.211), kind=kOutput, calls=%fused_computation.80 | convolution fusion | flops 11813257216 | bytes 35127296 | tf_op jit(solution)/shard_map/dot_general | solution.py:26
  794.8 50.8 %attend_back.4 = (f32[512,512]{1,0:T(8,128)S(1)}, bf16[4096,128]{1,0:T(8,128)(2,1)S(1)}) custom-call(s32[8]{0:T(128)S(1)} %copy-done.52, f32[16,512]{1,0:T(8,128)S(1)} %compare_select_fusion.bias_ref, f32[8,512]{1,0:T(8,128)S(1)} %get-tuple-element.252.lse_ref, f32[512,512]{1,0:T(8,128)S(1)} %copy-done.30, bf16[512,2048]{1,0:T(8,128)(2,1)S(1)} %copy-done.4, ...), custom_call_target="tpu_custom_call" | custom-call | flops 1048576 | bytes 65536 | tf_op jit(solution)/shard_map/attend_back/pallas_call | solution.py:233
  879.9 50.9 %attend_back.5 = (f32[512,512]{1,0:T(8,128)S(1)}, bf16[4096,128]{1,0:T(8,128)(2,1)S(1)}) custom-call(s32[8]{0:T(128)S(1)} %copy-done.52, f32[16,512]{1,0:T(8,128)S(1)} %compare_select_fusion.bias_ref, f32[8,512]{1,0:T(8,128)S(1)} %get-tuple-element.259.lse_ref, f32[512,512]{1,0:T(8,128)S(1)} %get-tuple-element.232.o_ref, bf16[512,2048]{1,0:T(8,128)(2,1)S(1)} %copy-done.4, ...), custom_call_target="tpu_custom_call" | custom-call | flops 1048576 | bytes 65536 | tf_op jit(solution)/shard_map/attend_back/pallas_call | solution.py:233
  961.8 51.2 %attend_back.6 = (f32[512,512]{1,0:T(8,128)S(1)}, bf16[4096,128]{1,0:T(8,128)(2,1)S(1)}) custom-call(s32[8]{0:T(128)S(1)} %copy-done.52, f32[16,512]{1,0:T(8,128)S(1)} %compare_select_fusion.bias_ref, f32[8,512]{1,0:T(8,128)S(1)} %get-tuple-element.269.lse_ref, f32[512,512]{1,0:T(8,128)S(1)} %copy-done.27, bf16[512,2048]{1,0:T(8,128)(2,1)S(1)} %copy-done.4, ...), custom_call_target="tpu_custom_call" | custom-call | flops 1048576 | bytes 65536 | tf_op jit(solution)/shard_map/attend_back/pallas_call | solution.py:233
  1014.9 53.8 %collective-permute-done.50 = bf16[704,2048]{1,0:T(8,128)(2,1)} collective-permute-done((bf16[704,2048]{1,0:T(8,128)(2,1)}, bf16[704,2048]{1,0:T(8,128)(2,1)}, u32[]{:S(2)}, u32[]{:S(2)}) %collective-permute-start.50) | collective-permute-done | bytes 2883616 | tf_op jit(solution)/shard_map/ppermute | solution.py:362
  1099.0 51.0 %attend_back.7 = (f32[512,512]{1,0:T(8,128)S(1)}, bf16[4096,128]{1,0:T(8,128)(2,1)S(1)}) custom-call(s32[8]{0:T(128)S(1)} %copy-done.52, f32[16,512]{1,0:T(8,128)S(1)} %compare_select_fusion.bias_ref, f32[8,512]{1,0:T(8,128)S(1)} %get-tuple-element.277.lse_ref, f32[512,512]{1,0:T(8,128)S(1)} %copy-done.25, bf16[512,2048]{1,0:T(8,128)(2,1)S(1)} %copy-done.4, ...), custom_call_target="tpu_custom_call" | custom-call | flops 1048576 | bytes 65536 | tf_op jit(solution)/shard_map/attend_back/pallas_call | solution.py:233
  1190.7 14.8 %collective-permute-done.62 = bf16[128,2048]{1,0:T(8,128)(2,1)S(1)} collective-permute-done((bf16[128,2048]{1,0:T(8,128)(2,1)S(1)}, bf16[128,2048]{1,0:T(8,128)(2,1)S(1)}, u32[]{:S(2)}, u32[]{:S(2)}) %collective-permute-start.62) | collective-permute-done | bytes 524320 | tf_op jit(solution)/shard_map/ppermute | solution.py:373
  (707 shorter events, 686.5 us)
Async XLA Ops:
  7.2 88.7 %all-gather.7.cloned.1.call-start = ((), (), s32[]{:S(2)}) async-start(), calls=%async_computation.6 | async-start | bytes 3604480 | tf_op jit(solution)/shard_map/all_gather | solution.py:579
  7.9 187.7 %all-gather.9.cloned.1.call-start = ((), (), s32[]{:S(2)}) async-start(), calls=%async_computation.7 | async-start | bytes 3604480 | tf_op jit(solution)/shard_map/all_gather | solution.py:579
  127.1 144.1 %all-gather.11.cloned.1.call-start = ((), (), s32[]{:S(2)}) async-start(), calls=%async_computation.8 | async-start | bytes 1310720 | tf_op jit(solution)/shard_map/all_gather | solution.py:579
  240.0 926.3 %reduce-scatter.4.cloned.1.call-start = ((), (), s32[]{:S(2)}) async-start(), calls=%async_computation.3 | async-start | bytes 3604480 | tf_op jit(solution)/shard_map/reduce_scatter | solution.py:501
  275.8 77.8 %collective-permute-start.20 = (bf16[2,64,5632]{2,1,0:T(8,128)(2,1)}, bf16[2,64,5632]{2,1,0:T(8,128)(2,1)}, u32[]{:S(2)}, u32[]{:S(2)}) collective-permute-start(bf16[2,64,5632]{2,1,0:T(8,128)(2,1)} %get-tuple-element.386), channel_id=1, source_target_pairs={{0,4},{1,5},{2,6},{3,7},{4,0},{5,1},{6,2},{7,3},{8,12},{9,13},{10,... | collective-permute-start | bytes 4325384 | tf_op jit(solution)/shard_map/ppermute | solution.py:373
  363.9 101.0 %collective-permute-start.24 = (bf16[2,2,64,5632]{3,2,1,0:T(8,128)(2,1)}, bf16[2,2,64,5632]{3,2,1,0:T(8,128)(2,1)}, u32[]{:S(2)}, u32[]{:S(2)}) collective-permute-start(bf16[2,2,64,5632]{3,2,1,0:T(8,128)(2,1)} %pad_maximum_fusion.9), channel_id=1, source_target_pairs={{0,2},{1,3},{2,0},{3,1},{4,6},{5,7},{6,4},{7,5},{8,10},{9,11},{10,... | collective-permute-start | bytes 8650760 | tf_op jit(solution)/shard_map/ppermute | solution.py:373
  368.6 96.3 %collective-permute-start.25 = (bf16[2,2,64,5632]{3,2,1,0:T(8,128)(2,1)}, bf16[2,2,64,5632]{3,2,1,0:T(8,128)(2,1)}, u32[]{:S(2)}, u32[]{:S(2)}) collective-permute-start(bf16[2,2,64,5632]{3,2,1,0:T(8,128)(2,1)} %pad_maximum_fusion.10), channel_id=1, source_target_pairs={{0,4},{1,5},{2,6},{3,7},{4,0},{5,1},{6,2},{7,3},{8,12},{9,13},{10,... | collective-permute-start | bytes 8650760 | tf_op jit(solution)/shard_map/ppermute | solution.py:373
  369.7 95.3 %collective-permute-start.28 = (bf16[2,2,64,5632]{3,2,1,0:T(8,128)(2,1)}, bf16[2,2,64,5632]{3,2,1,0:T(8,128)(2,1)}, u32[]{:S(2)}, u32[]{:S(2)}) collective-permute-start(bf16[2,2,64,5632]{3,2,1,0:T(8,128)(2,1)} %collective-permute-done.22), channel_id=1, source_target_pairs={{0,8},{8,24},{24,16},{16,0},{1,9},{9,25},{25,17},{17,1},{2,10},{10... | collective-permute-start | bytes 8650760 | tf_op jit(solution)/shard_map/ppermute | solution.py:362
  660.5 93.9 %collective-permute-start.37 = (bf16[2816,2048]{1,0:T(8,128)(2,1)}, bf16[2816,2048]{1,0:T(8,128)(2,1)}, u32[]{:S(2)}, u32[]{:S(2)}) collective-permute-start(bf16[2816,2048]{1,0:T(8,128)(2,1)} %convolution_convert_fusion.1), channel_id=1, source_target_pairs={{0,1},{1,0},{2,3},{3,2},{4,5},{5,4},{6,7},{7,6},{8,9},{9,8},{10,11... | collective-permute-start | bytes 34603016 | tf_op jit(solution)/shard_map/ppermute | solution.py:373
  669.7 84.7 %collective-permute-start.38 = (bf16[1024,5632]{1,0:T(8,128)(2,1)}, bf16[1024,5632]{1,0:T(8,128)(2,1)}, u32[]{:S(2)}, u32[]{:S(2)}) collective-permute-start(bf16[1024,5632]{1,0:T(8,128)(2,1)} %convolution_convert_fusion), channel_id=1, source_target_pairs={{0,1},{1,0},{2,3},{3,2},{4,5},{5,4},{6,7},{7,6},{8,9},{9,8},{10,11... | collective-permute-start | bytes 34603016 | tf_op jit(solution)/shard_map/ppermute | solution.py:373
  754.4 91.3 %collective-permute-start.39 = (bf16[256,5632]{1,0:T(8,128)(2,1)}, bf16[256,5632]{1,0:T(8,128)(2,1)}, u32[]{:S(2)}, u32[]{:S(2)}) collective-permute-start(bf16[256,5632]{1,0:T(8,128)(2,1)} %add_convert_fusion.18), channel_id=1, source_target_pairs={{0,2},{1,3},{2,0},{3,1},{4,6},{5,7},{6,4},{7,5},{8,10},{9,11},{10,... | collective-permute-start | bytes 8650760 | tf_op jit(solution)/shard_map/ppermute | solution.py:373
  755.9 89.8 %collective-permute-start.40 = (bf16[256,5632]{1,0:T(8,128)(2,1)}, bf16[256,5632]{1,0:T(8,128)(2,1)}, u32[]{:S(2)}, u32[]{:S(2)}) collective-permute-start(bf16[256,5632]{1,0:T(8,128)(2,1)} %add_convert_fusion.17), channel_id=1, source_target_pairs={{0,4},{1,5},{2,6},{3,7},{4,0},{5,1},{6,2},{7,3},{8,12},{9,13},{10,... | collective-permute-start | bytes 8650760 | tf_op jit(solution)/shard_map/ppermute | solution.py:373
  762.8 82.9 %collective-permute-start.41 = (bf16[704,2048]{1,0:T(8,128)(2,1)}, bf16[704,2048]{1,0:T(8,128)(2,1)}, u32[]{:S(2)}, u32[]{:S(2)}) collective-permute-start(bf16[704,2048]{1,0:T(8,128)(2,1)} %add_convert_fusion.16), channel_id=1, source_target_pairs={{0,8},{8,24},{24,16},{16,0},{1,9},{9,25},{25,17},{17,1},{2,10},{10... | collective-permute-start | bytes 8650760 | tf_op jit(solution)/shard_map/ppermute | solution.py:362
  787.8 143.1 %collective-permute-start.44 = (bf16[256,5632]{1,0:T(8,128)(2,1)}, bf16[256,5632]{1,0:T(8,128)(2,1)}, u32[]{:S(2)}, u32[]{:S(2)}) collective-permute-start(bf16[256,5632]{1,0:T(8,128)(2,1)} %add_convert_fusion.11), channel_id=1, source_target_pairs={{0,2},{1,3},{2,0},{3,1},{4,6},{5,7},{6,4},{7,5},{8,10},{9,11},{10,... | collective-permute-start | bytes 8650760 | tf_op jit(solution)/shard_map/ppermute | solution.py:373
  793.9 137.1 %collective-permute-start.45 = (bf16[256,5632]{1,0:T(8,128)(2,1)}, bf16[256,5632]{1,0:T(8,128)(2,1)}, u32[]{:S(2)}, u32[]{:S(2)}) collective-permute-start(bf16[256,5632]{1,0:T(8,128)(2,1)} %add_convert_fusion.10), channel_id=1, source_target_pairs={{0,4},{1,5},{2,6},{3,7},{4,0},{5,1},{6,2},{7,3},{8,12},{9,13},{10,... | collective-permute-start | bytes 8650760 | tf_op jit(solution)/shard_map/ppermute | solution.py:373
  853.5 77.5 %collective-permute-start.46 = (bf16[704,2048]{1,0:T(8,128)(2,1)}, bf16[704,2048]{1,0:T(8,128)(2,1)}, u32[]{:S(2)}, u32[]{:S(2)}) collective-permute-start(bf16[704,2048]{1,0:T(8,128)(2,1)} %add_convert_fusion.8), channel_id=1, source_target_pairs={{0,8},{8,24},{24,16},{16,0},{1,9},{9,25},{25,17},{17,1},{2,10},{10... | collective-permute-start | bytes 8650760 | tf_op jit(solution)/shard_map/ppermute | solution.py:362
  949.8 118.9 %collective-permute-start.49 = (bf16[1024,2048]{1,0:T(8,128)(2,1)}, bf16[1024,2048]{1,0:T(8,128)(2,1)}, u32[]{:S(2)}, u32[]{:S(2)}) collective-permute-start(bf16[1024,2048]{1,0:T(8,128)(2,1)} %convolution_convert_fusion.4), channel_id=1, source_target_pairs={{0,1},{1,0},{2,3},{3,2},{4,5},{5,4},{6,7},{7,6},{8,9},{9,8},{10,11... | collective-permute-start | bytes 12582920 | tf_op jit(solution)/shard_map/ppermute | solution.py:373
  956.4 112.3 %collective-permute-start.50 = (bf16[704,2048]{1,0:T(8,128)(2,1)}, bf16[704,2048]{1,0:T(8,128)(2,1)}, u32[]{:S(2)}, u32[]{:S(2)}) collective-permute-start(bf16[704,2048]{1,0:T(8,128)(2,1)} %add_convert_fusion.2), channel_id=1, source_target_pairs={{0,8},{8,24},{24,16},{16,0},{1,9},{9,25},{25,17},{17,1},{2,10},{10... | collective-permute-start | bytes 8650760 | tf_op jit(solution)/shard_map/ppermute | solution.py:362
  960.5 278.9 %reduce-scatter.6.cloned.1.call-start = ((), (), s32[]{:S(2)}) async-start(), calls=%async_computation.4 | async-start | bytes 3604480 | tf_op jit(solution)/shard_map/reduce_scatter | solution.py:501
  1074.9 91.3 %collective-permute-start.51 = (bf16[256,2048]{1,0:T(8,128)(2,1)}, bf16[256,2048]{1,0:T(8,128)(2,1)}, u32[]{:S(2)}, u32[]{:S(2)}) collective-permute-start(bf16[256,2048]{1,0:T(8,128)(2,1)} %fusion.19), channel_id=1, source_target_pairs={{0,2},{1,3},{2,0},{3,1},{4,6},{5,7},{6,4},{7,5},{8,10},{9,11},{10,... | collective-permute-start | bytes 3145736 | tf_op jit(solution)/shard_map/ppermute | solution.py:373
  1076.0 90.3 %collective-permute-start.52 = (bf16[256,2048]{1,0:T(8,128)(2,1)}, bf16[256,2048]{1,0:T(8,128)(2,1)}, u32[]{:S(2)}, u32[]{:S(2)}) collective-permute-start(bf16[256,2048]{1,0:T(8,128)(2,1)} %fusion.20), channel_id=1, source_target_pairs={{0,4},{1,5},{2,6},{3,7},{4,0},{5,1},{6,2},{7,3},{8,12},{9,13},{10,... | collective-permute-start | bytes 3145736 | tf_op jit(solution)/shard_map/ppermute | solution.py:373
  1083.2 83.1 %collective-permute-start.53 = (bf16[352,2048]{1,0:T(8,128)(2,1)}, bf16[352,2048]{1,0:T(8,128)(2,1)}, u32[]{:S(2)}, u32[]{:S(2)}) collective-permute-start(bf16[352,2048]{1,0:T(8,128)(2,1)} %slice.560), channel_id=1, source_target_pairs={{0,2},{1,3},{2,0},{3,1},{4,6},{5,7},{6,4},{7,5},{8,10},{9,11},{10,... | collective-permute-start | bytes 4325384 | tf_op jit(solution)/shard_map/ppermute | solution.py:373
  1088.5 77.8 %collective-permute-start.54 = (bf16[1024,1536]{1,0:T(8,128)(2,1)}, bf16[1024,1536]{1,0:T(8,128)(2,1)}, u32[]{:S(2)}, u32[]{:S(2)}) collective-permute-start(bf16[1024,1536]{1,0:T(8,128)(2,1)} %convolution_convert_fusion.3), channel_id=1, source_target_pairs={{0,1},{1,0},{2,3},{3,2},{4,5},{5,4},{6,7},{7,6},{8,9},{9,8},{10,11... | collective-permute-start | bytes 9437192 | tf_op jit(solution)/shard_map/ppermute | solution.py:373
  1097.7 203.3 %reduce-scatter.8.cloned.1.call-start = ((), (), s32[]{:S(2)}) async-start(), calls=%async_computation.5 | async-start | bytes 1310720 | tf_op jit(solution)/shard_map/reduce_scatter | solution.py:501
  (225 other events, 4573.4 us)
Sparse Core Ops, SparseCore 0:
  9.6 76.3 all-gather.6
  127.2 60.7 all-gather.8
  240.1 31.0 all-gather.10
  960.6 98.4 reduce-scatter.3
  1097.8 53.6 reduce-scatter.5
  1233.4 24.5 reduce-scatter.7

commit v5 on v4

--- a/solution.py
+++ b/solution.py
@@ -746,71 +746,70 @@
     run = rows // 2
     positions = positions[0]
     grid = Grid(n_dp, n_ctx)
-    order, sum_order = grid.block_order(False), grid.block_order(True)
+    order = grid.block_order(False)
     ring_order, ctx_order = grid.ring_order(), grid.ctx_order()
     places = grid.value_places()
 
     gains = jnp.stack([attn_gain, ffn_gain], -1)
     gains = jnp.concatenate([gains, jnp.zeros((gains.shape[0], WIDE - 2), BF16)], 1)
     packed = jnp.concatenate([query_proj, key_proj, value_proj, gains], 1)
+    packed, down_proj, gate_proj, merge_proj = lax.optimization_barrier(
+        (packed, down_proj, gate_proj, merge_proj)
+    )
+    first_chain = Chain(gather_weight(grid, packed))
     down_chain = Chain(gather_weight(grid, down_proj))
-    first_chain = Chain(gather_weight(grid, packed, True))
+    gate_chain = Chain(gather_weight(grid, gate_proj))
+    merge_chain = Chain(gather_weight(grid, merge_proj))
     up_chain = Chain(gather_ring(grid, up_proj))
     all_pos = lax.all_gather(positions[::run], "ctx", axis=0, tiled=True)
     cosine, sine = angles(positions)
     rows_in = layer_in.reshape(rows, model).astype(F32)
     normed_one, factor_one = normalize(rows_in)
-    all_pos, gate_proj = meet((all_pos, gate_proj), first_chain, up_chain)
-    gate_chain = Chain(gather_weight(grid, gate_proj))
-    factor_one, merge_proj = meet((factor_one, merge_proj), first_chain)
-    merge_chain = Chain(gather_weight(grid, merge_proj))
-    cosine, sine = meet((cosine, sine), first_chain)
-    cosine = meet(cosine, first_chain, down_chain)
+    all_pos, factor_one, cosine = meet((all_pos, factor_one, cosine), first_chain, up_chain)
     first_weights = finish(first_chain)
-    first_weights = meet(first_weights, down_chain, up_chain)
-    first_weights = settle(first_weights, gate_chain)
     attn_all = first_weights[:, : width + 2 * kv_width]
     gain_one = first_weights[:, width + 2 * kv_width].astype(F32)
     gain_two = first_weights[:, width + 2 * kv_width + 1].astype(F32)
 
     first_in = (normed_one * gain_one).astype(BF16)
+    first_in = meet(first_in, down_chain)
     raw = mm(first_in, attn_all, NN)
     queries, own_kv = rotated(raw, cosine, sine, kv_width)
     kv_chain = Chain(gather_keys(grid, own_kv))
     later = all_pos.reshape(n_ctx, 2)[ctx_order].reshape(2 * n_ctx, 1)
     later = later > jnp.repeat(positions[::run], run)[None, :]
     bias = jnp.where(later, MASKED, 0.0).astype(F32)
+    bias = meet(bias, kv_chain, down_chain, up_chain)
     bias = meet(bias, kv_chain)
-    bias = meet(bias, kv_chain)
-    bias = settle(bias, merge_chain)
     bias = meet(bias, kv_chain, gate_chain)
     all_keys, all_values = finish(kv_chain)
     kt, vt = all_keys.T, all_values.T
 
     grad_rows = out_grad.reshape(rows, model)
     plan = (
+        (),
         (down_chain, gate_chain, up_chain),
         (down_chain, merge_chain),
         (gate_chain, merge_chain, up_chain),
-        (gate_chain, merge_chain),
     )
     outs, log_sums = [], []
     for group in range(kv_heads):
         out, log_sum = attend(group, places, bias, queries, all_keys, vt)
         queries, out, grad_rows = meet((queries, out, grad_rows), *plan[group % 4])
-        if group == 1:
+        if group == 2:
             down_all = finish(down_chain)
             grad_hidden = mm(grad_rows, down_all, NT)
             queries, grad_hidden = lax.optimization_barrier((queries, grad_hidden))
         outs.append(out)
         log_sums.append(log_sum)
     mixed = jnp.concatenate([out.astype(BF16) for out in outs], 1)
+    mixed = meet(mixed, gate_chain, merge_chain)
     gate_all, merge_all = finish(gate_chain), finish(merge_chain)
     middle = rows_in + mm(mixed, merge_all, NN)
     normed_two, factor_two = normalize(middle)
     second_in = (normed_two * gain_two).astype(BF16)
+    second_in = meet(second_in, up_chain)
     gate = mm(second_in, gate_all, NN)
-    gate = meet(gate, up_chain)
     up_all = finish(up_chain)
     lift = mm(second_in, up_all, NN)
     sigma = jax.nn.sigmoid(gate)
@@ -824,18 +823,14 @@
     up_sum = Chain(reduce_term(grid, second_turned, grad_lift))
     down_sum = Chain(reduce_ring(grid, turned(hidden, ring_order), grad_rows))
     grad_second = mm(grad_gate, gate_all, NT)
-    grad_second, grad_lift, hidden = meet((grad_second, grad_lift, hidden), gate_sum)
+    grad_second, grad_lift = meet((grad_second, grad_lift), gate_sum)
     grad_second = grad_second + mm(grad_lift, up_all, NT)
-    result = middle + mm(hidden, down_all, NN)
-    layer_out = result.astype(BF16).reshape(layer_in.shape)
     grad_norm_two, gain_two_term = norm_back(grad_second, normed_two, factor_two, gain_two)
     grad_middle = grad_rows.astype(F32) + grad_norm_two
     grad_branch = grad_middle.astype(BF16)
     grad_mixed = mm(grad_branch, merge_all, NT).astype(BF16)
-    grad_mixed, layer_out, grad_branch = meet(
-        (grad_mixed, layer_out, grad_branch), down_sum, up_sum
-    )
-    first_turned = turned(first_in, sum_order)
+    grad_mixed, grad_branch = meet((grad_mixed, grad_branch), down_sum, up_sum)
+    first_turned = turned(first_in, order)
     mixed_turned = turned(mixed, order)
 
     dqs, dkvs = [], []
@@ -847,31 +842,25 @@
         dqs.append(dq)
         dkvs.append(dkv)
         if group == kv_heads - 4:
-            grad_mixed, dkv, grad_branch = meet(
-                (grad_mixed, dkv, grad_branch), gate_sum, down_sum
-            )
+            grad_mixed, dkv = meet((grad_mixed, dkv), gate_sum, down_sum)
         elif group == kv_heads - 3:
-            grad_mixed, dkv, grad_branch = meet(
-                (grad_mixed, dkv, grad_branch), gate_sum, up_sum, down_sum
-            )
+            grad_mixed, dkv, grad_branch = meet((grad_mixed, dkv, grad_branch), gate_sum, up_sum)
             merge_sum = Chain(reduce_term(grid, mixed_turned, grad_branch))
         elif group == kv_heads - 2:
-            early_grads = unrotated(unrotate_queries_kernel, dqs, cosine, sine)
-            grad_mixed, early_grads, dkvs = meet(
-                (grad_mixed, early_grads, dkvs), up_sum, merge_sum, down_sum
-            )
-            early = Chain(reduce_term(grid, first_turned, early_grads, around=True))
+            grad_mixed, dkvs = meet((grad_mixed, dkvs), up_sum, merge_sum, gate_sum)
             keys_sum = Chain(reduce_keys(grid, jnp.concatenate(dkvs, 1)))
-    dq, dkv = meet((dq, dkv), gate_sum, merge_sum, down_sum, early, keys_sum)
+    dqs, dkv, hidden = meet((dqs, dkv, hidden), merge_sum, keys_sum, up_sum)
     last_keys = Chain(reduce_keys(grid, dkv))
-    late_grads = unrotated(unrotate_queries_kernel, dqs[-1:], cosine, sine)
-    split = early_grads.shape[1]
-    grad_first = mm(early_grads, attn_all[:, :split], NT)
+    query_grads = unrotated(unrotate_queries_kernel, dqs, cosine, sine)
+    query_sum = Chain(reduce_term(grid, first_turned, query_grads))
+    grad_first = mm(query_grads, attn_all[:, :width], NT)
+    grad_first, hidden = meet(
+        (grad_first, hidden), last_keys, keys_sum, query_sum, merge_sum, down_sum
+    )
+    result = middle + mm(hidden, down_all, NN)
+    layer_out = result.astype(BF16).reshape(layer_in.shape)
     grad_first = meet(grad_first, last_keys, keys_sum)
-    grad_first = grad_first + mm(late_grads, attn_all[:, split:width], NT)
-    late = Chain(reduce_term(grid, first_turned, late_grads, around=True))
-    grad_first = meet(grad_first, last_keys, keys_sum, early, merge_sum)
-    grad_first = meet(grad_first, last_keys, up_sum, down_sum)
+    grad_first, layer_out = meet((grad_first, layer_out), last_keys, query_sum)
     wide = finish(keys_sum)
     dkv_parts = [wide[:, at : at + WIDE] for at in range(0, wide.shape[1], WIDE)]
     dkv_parts.append(finish(last_keys))
@@ -880,21 +869,20 @@
     grad_norm_one, gain_one_term = norm_back(grad_first, normed_one, factor_one, gain_one)
     gain_terms = jnp.stack([gain_one_term, gain_two_term], 0)
     gain_terms = jnp.concatenate([gain_terms, jnp.zeros((WIDE - 2, model), F32)], 0)
-    gain_terms = meet(gain_terms, early, late, down_sum)
-    gain_columns = turned(gain_terms.astype(BF16), sum_order)
-    last = Chain(reduce_term(grid, first_turned, kv_grads, gain_columns, around=True))
+    gain_columns = turned(gain_terms.astype(BF16), order)
+    last = Chain(reduce_term(grid, first_turned, kv_grads, gain_columns))
     input_grad = (grad_middle + grad_norm_one).astype(BF16).reshape(layer_in.shape)
-    waiting = (last, late, early, down_sum)
-    while not all(c.done for c in waiting):
-        input_grad = meet(input_grad, *waiting)
-    early_share, late_share, last_share = finish(early), finish(late), finish(last)
+    input_grad = meet(input_grad, last, query_sum)
+    input_grad = meet(input_grad, last, down_sum)
+    input_grad = meet(input_grad, last, down_sum)
+    query_share, last_share = finish(query_sum), finish(last)
     merge_share, gate_share = finish(merge_sum), finish(gate_sum)
     up_share, down_share = finish(up_sum), finish(down_sum)
     return (
         layer_out,
         input_grad,
         last_share[:, 2 * kv_width],
-        jnp.concatenate([early_share, late_share], 1),
+        query_share,
         last_share[:, :kv_width],
         last_share[:, kv_width : 2 * kv_width],
         merge_share,

time: 1360 us -> 1390 us (1.022)
  waiting for transfers between devices: 312 us -> 375 us
  starting transfers between devices: 96.5 us -> 72 us
  other arithmetic: 151 us -> 134 us
    unnamed x321, local copies, waits for them, and re-layouts: 37.2 us -> 63.3 us
    ppermute x18 -> x6, starting transfers between devices: 38.5 us -> 13 us  [next(): return lax.ppermute(values, 'dp', list(zip(self.ring, around)))]
    ppermute x69 -> x64, waiting for transfers between devices: 169 us -> 192 us  [next(): return lax.ppermute(values, 'ctx', pairs)]
    ppermute x18 -> x6, waiting for transfers between devices: 137 us -> 156 us  [next(): return lax.ppermute(values, 'dp', list(zip(self.ring, around)))]
    convert_element_type x7 -> x0, other arithmetic: 16.1 us -> none  [the longest x1 13.3 us: body(): grad_lift = (grad_hidden * activated).astype(BF16)]
    optimization_barrier x1 -> x0, local copies, waits for them, and re-layouts: 14.7 us -> none  [settle(): lax.optimization_barrier((main, [list(c.flight) for c in chains]))]
    dot_general x47 -> x41, matrix products: 296 us -> 288 us  [mm(): return lax.dot_general(left, right, dims, preferred_element_type=F32)]
    ppermute x69 -> x64, starting transfers between devices: 57.5 us -> 57.7 us  [next(): return lax.ppermute(values, 'ctx', pairs)]
  transfers between devices with their start and end apart: 93 -> 79, of which waited for: 32 -> 26; matrix products, arithmetic and copies ran while one was open for 30% -> 26% of each run, Pallas kernels for 27% -> 27%
where the time goes in v5:
time: 1390 us; the launch traced here: 1380 us
  Pallas kernels  385 us (28%)
  waiting for transfers between devices  375 us (27%)
  matrix products  288 us (21%)
  other arithmetic  134 us (10%)
  local copies, waits for them, and re-layouts  99.1 us (7%)
  starting transfers between devices  72 us (5%)
  between operations  16.8 us (1%)
    dot_general x41, matrix products, mm(): return lax.dot_general(left, right, dims, preferred_element_type=F32)  288 us
    pallas_call x4, Pallas kernels, attend_back(): pl.pallas_call(functools.partial(attend_back_kernel, which=group % 2, unr...  204 us
    ppermute x64, waiting for transfers between devices, next(): return lax.ppermute(values, 'ctx', pairs)  192 us
    ppermute x6, waiting for transfers between devices, next(): return lax.ppermute(values, 'dp', list(zip(self.ring, around)))  156 us
    pallas_call x4, Pallas kernels, attend(): pl.pallas_call(functools.partial(attend_kernel, which=group % 2, places=p...  103 us
    pallas_call x5, Pallas kernels, placed(): pl.pallas_call(functools.partial(place_kernel, sources=sources, slots=slo...  64.6 us
    unnamed x321, local copies, waits for them, and re-layouts  63.3 us
    ppermute x64, starting transfers between devices, next(): return lax.ppermute(values, 'ctx', pairs)  57.7 us
  transfers between devices with their start and end apart: 79, of which 26 were waited for; matrix products, arithmetic and copies ran while one was open for 26% of the time, Pallas kernels for 27%

profile of v5, /device:TPU:0, one launch (start us, length us, event | category | flops | bytes accessed | tf_op | source)
XLA Modules:
  0.0 1382.7 jit_solution(6073228737922531059)
XLA Ops:
  51.8 13.5 collective-permute-done.3
  69.8 26.3 %collective-permute-done.4 = bf16[2,2,64,2688]{3,2,1,0:T(8,128)(2,1)} collective-permute-done((bf16[2,2,64,2688]{3,2,1,0:T(8,128)(2,1)S(1)}, bf16[2,2,64,2688]{3,2,1,0:T(8,128)(2,1)}, u32[]{:S(2)}, u32[]{:S(2)}) %collective-permute-start.4) | collective-permute-done | bytes 1376288 | tf_op jit(solution)/shard_map/ppermute | solution.py:373
  154.6 22.3 %collective-permute-done.6 = bf16[512,256]{1,0:T(8,128)(2,1)S(1)} collective-permute-done((bf16[512,256]{1,0:T(8,128)(2,1)S(1)}, bf16[512,256]{1,0:T(8,128)(2,1)S(1)}, u32[]{:S(2)}, u32[]{:S(2)}) %collective-permute-start.6) | collective-permute-done | bytes 262176 | tf_op jit(solution)/shard_map/ppermute | solution.py:373
  222.0 25.6 %attend.4 = (f32[512,512]{1,0:T(8,128)S(1)}, f32[8,512]{1,0:T(8,128)S(1)}) custom-call(f32[16,512]{1,0:T(8,128)S(1)} %compare_select_fusion.bias_ref, bf16[512,2048]{1,0:T(8,128)(2,1)S(1)} %copy-done.2, bf16[4096,256]{1,0:T(8,128)(2,1)S(1)} %bitcast.167, bf16[256,4096]{1,0:T(8,128)(2,1)S(1)} %copy-done.6), custom_call_target="tpu_custom_call" | custom-call | flops 1048576 | bytes 65536 | tf_op jit(solution)/shard_map/attend/pallas_call | solution.py:113
  248.6 26.1 %attend.5 = (f32[512,512]{1,0:T(8,128)S(1)}, f32[8,512]{1,0:T(8,128)S(1)}) custom-call(f32[16,512]{1,0:T(8,128)S(1)} %compare_select_fusion.bias_ref, bf16[512,2048]{1,0:T(8,128)(2,1)S(1)} %copy-done.2, bf16[4096,256]{1,0:T(8,128)(2,1)S(1)} %bitcast.168, bf16[256,4096]{1,0:T(8,128)(2,1)S(1)} %copy-done.6), custom_call_target="tpu_custom_call" | custom-call | flops 1048576 | bytes 65536 | tf_op jit(solution)/shard_map/attend/pallas_call | solution.py:113
  274.8 21.9 %collective-permute-done.17 = bf16[2,64,5632]{2,1,0:T(8,128)(2,1)} collective-permute-done((bf16[2,64,5632]{2,1,0:T(8,128)(2,1)}, bf16[2,64,5632]{2,1,0:T(8,128)(2,1)}, u32[]{:S(2)}, u32[]{:S(2)}) %collective-permute-start.17) | collective-permute-done | bytes 1441824 | tf_op jit(solution)/shard_map/ppermute | solution.py:373
  318.2 25.8 %attend.6 = (f32[512,512]{1,0:T(8,128)S(1)}, f32[8,512]{1,0:T(8,128)S(1)}) custom-call(f32[16,512]{1,0:T(8,128)S(1)} %compare_select_fusion.bias_ref, bf16[512,2048]{1,0:T(8,128)(2,1)S(1)} %copy-done.3, bf16[4096,256]{1,0:T(8,128)(2,1)S(1)} %bitcast.169, bf16[256,4096]{1,0:T(8,128)(2,1)S(1)} %copy-done.7), custom_call_target="tpu_custom_call" | custom-call | flops 1048576 | bytes 65536 | tf_op jit(solution)/shard_map/attend/pallas_call | solution.py:113
  346.3 17.4 %placed.6 = bf16[32,176,2048]{2,1,0:T(8,128)(2,1)} custom-call(s32[32]{0:T(128)S(1)} %fusion.103.order_ref, bf16[16,176,2048]{2,1,0:T(8,128)(2,1)} %pad_maximum_fusion.refs_0_, bf16[16,176,2048]{2,1,0:T(8,128)(2,1)} %collective-permute-done.20.refs_1_), custom_call_target="tpu_custom_call" | custom-call | bytes 46137344 | tf_op jit(solution)/shard_map/placed/pallas_call | solution.py:550
  369.3 19.7 %fusion.126 = f32[512,5632]{1,0:T(8,128)} fusion(bf16[512,2048]{1,0:T(8,128)(2,1)} %bitcast.215, bf16[5632,2048]{1,0:T(8,128)(2,1)} %bitcast.200), kind=kOutput, calls=%fused_computation.289 | convolution fusion | flops 11811160064 | bytes 36700160 | tf_op jit(solution)/shard_map/dot_general | solution.py:26
  392.2 25.8 %attend.7 = (f32[512,512]{1,0:T(8,128)S(1)}, f32[8,512]{1,0:T(8,128)S(1)}) custom-call(f32[16,512]{1,0:T(8,128)S(1)} %compare_select_fusion.bias_ref, bf16[512,2048]{1,0:T(8,128)(2,1)S(1)} %copy-done.4, bf16[4096,256]{1,0:T(8,128)(2,1)S(1)} %bitcast.170, bf16[256,4096]{1,0:T(8,128)(2,1)S(1)} %copy-done.8), custom_call_target="tpu_custom_call" | custom-call | flops 1048576 | bytes 65536 | tf_op jit(solution)/shard_map/attend/pallas_call | solution.py:113
  433.9 22.0 %collective-permute-done.27 = bf16[2,2,64,2048]{3,2,1,0:T(8,128)(2,1)S(1)} collective-permute-done((bf16[2,2,64,2048]{3,2,1,0:T(8,128)(2,1)S(1)}, bf16[2,2,64,2048]{3,2,1,0:T(8,128)(2,1)S(1)}, u32[]{:S(2)}, u32[]{:S(2)}) %collective-permute-start.27) | collective-permute-done | bytes 1048608 | tf_op jit(solution)/shard_map/ppermute | solution.py:373
  491.9 89.6 %collective-permute-done.30 = bf16[2,2,64,5632]{3,2,1,0:T(8,128)(2,1)} collective-permute-done((bf16[2,2,64,5632]{3,2,1,0:T(8,128)(2,1)}, bf16[2,2,64,5632]{3,2,1,0:T(8,128)(2,1)}, u32[]{:S(2)}, u32[]{:S(2)}) %collective-permute-start.30) | collective-permute-done | bytes 2883616 | tf_op jit(solution)/shard_map/ppermute | solution.py:362
  610.3 15.5 %placed.9 = bf16[32,64,5632]{2,1,0:T(8,128)(2,1)} custom-call(s32[32]{0:T(128)S(1)} %get-tuple-element.332.order_ref, bf16[4,64,5632]{2,1,0:T(8,128)(2,1)} %bitcast.73.refs_0_, bf16[4,64,5632]{2,1,0:T(8,128)(2,1)} %bitcast.74.refs_1_, bf16[4,64,5632]{2,1,0:T(8,128)(2,1)} %bitcast.75.refs_2_, bf16[4,64,5632]{2,1,0:T(8,128)(2,1)} %bitcast.76.refs_3_, ...), custom_call_target="tpu_custom_call" | custom-call | bytes 46137344 | tf_op jit(solution)/shard_map/placed/pallas_call | solution.py:550
  625.7 19.1 %fusion.127 = f32[512,5632]{1,0:T(8,128)} fusion(bf16[512,2048]{1,0:T(8,128)(2,1)S(1)} %multiply_convert_fusion.3.x_ref, bf16[2048,5632]{1,0:T(8,128)(2,1)} %bitcast.204), kind=kOutput, calls=%fused_computation.290 | convolution fusion | flops 11811160064 | bytes 36700160 | tf_op jit(solution)/shard_map/dot_general | solution.py:26
  644.8 28.8 %multiply_convert_fusion = (bf16[512,5632]{1,0:T(8,128)(2,1)}, bf16[512,5632]{1,0:T(8,128)(2,1)}, bf16[512,5632]{1,0:T(8,128)(2,1)}) fusion(f32[512,5632]{1,0:T(8,128)} %fusion.126, f32[512,5632]{1,0:T(8,128)} %fusion.127, bf16[512,2048]{1,0:T(8,128)(2,1)} %copy-done.14, bf16[2048,5632]{1,0:T(8,128)(2,1)} %bitcast.202), kind=kOutput, calls=%fused_computation.3 | convolution fusion | flops 11854413824 | bytes 65536000 | tf_op jit(solution)/shard_map/dot_general | solution.py:26
  706.4 19.7 %fusion.128 = f32[512,2048]{1,0:T(8,128)} fusion(bf16[512,5632]{1,0:T(8,128)(2,1)} %get-tuple-element.215, bf16[2048,5632]{1,0:T(8,128)(2,1)} %bitcast.203), kind=kOutput, calls=%fused_computation.291 | convolution fusion | flops 11811160064 | bytes 33030144 | tf_op jit(solution)/shard_map/dot_general | solution.py:26
  726.0 19.9 %multiply_reduce_fusion = (bf16[2048]{0:T(1024)(128)(2,1)S(1)}, f32[512]{0:T(512)S(1)}, f32[512,2048]{1,0:T(8,128)}) fusion(f32[512,2048]{1,0:T(8,128)} %copy-done.63, f32[512]{0:T(512)S(1)} %copy-done.127, f32[512,2048]{1,0:T(8,128)} %fusion.128, f32[2048]{0:T(1024)S(1)} %bitcast.238, bf16[512,5632]{1,0:T(8,128)(2,1)} %get-tuple-element.218, ...), kind=kOutput, calls=%fused_computation.53 | convolution fusion | flops 11818498048 | bytes 41435136 | tf_op jit(solution)/shard_map/dot_general | solution.py:26
  808.8 50.8 %attend_back.4 = (f32[512,512]{1,0:T(8,128)S(1)}, bf16[4096,128]{1,0:T(8,128)(2,1)S(1)}) custom-call(s32[8]{0:T(128)S(1)} %copy-done.57, f32[16,512]{1,0:T(8,128)S(1)} %compare_select_fusion.bias_ref, f32[8,512]{1,0:T(8,128)S(1)} %get-tuple-element.172.lse_ref, f32[512,512]{1,0:T(8,128)S(1)} %copy-done.34, bf16[512,2048]{1,0:T(8,128)(2,1)S(1)} %copy-done.5, ...), custom_call_target="tpu_custom_call" | custom-call | flops 1048576 | bytes 65536 | tf_op jit(solution)/shard_map/attend_back/pallas_call | solution.py:233
  871.1 51.1 %attend_back.5 = (f32[512,512]{1,0:T(8,128)S(1)}, bf16[4096,128]{1,0:T(8,128)(2,1)S(1)}) custom-call(s32[8]{0:T(128)S(1)} %copy-done.57, f32[16,512]{1,0:T(8,128)S(1)} %compare_select_fusion.bias_ref, f32[8,512]{1,0:T(8,128)S(1)} %get-tuple-element.222.lse_ref, f32[512,512]{1,0:T(8,128)S(1)} %copy-done.31, bf16[512,2048]{1,0:T(8,128)(2,1)S(1)} %copy-done.5, ...), custom_call_target="tpu_custom_call" | custom-call | flops 1048576 | bytes 65536 | tf_op jit(solution)/shard_map/attend_back/pallas_call | solution.py:233
  961.9 51.1 %attend_back.6 = (f32[512,512]{1,0:T(8,128)S(1)}, bf16[4096,128]{1,0:T(8,128)(2,1)S(1)}) custom-call(s32[8]{0:T(128)S(1)} %copy-done.57, f32[16,512]{1,0:T(8,128)S(1)} %compare_select_fusion.bias_ref, f32[8,512]{1,0:T(8,128)S(1)} %get-tuple-element.228.lse_ref, f32[512,512]{1,0:T(8,128)S(1)} %get-tuple-element.200.o_ref, bf16[512,2048]{1,0:T(8,128)(2,1)S(1)} %copy-done.5, ...), custom_call_target="tpu_custom_call" | custom-call | flops 1048576 | bytes 65536 | tf_op jit(solution)/shard_map/attend_back/pallas_call | solution.py:233
  1036.4 51.0 %attend_back.7 = (f32[512,512]{1,0:T(8,128)S(1)}, bf16[4096,128]{1,0:T(8,128)(2,1)S(1)}) custom-call(s32[8]{0:T(128)S(1)} %copy-done.57, f32[16,512]{1,0:T(8,128)S(1)} %compare_select_fusion.bias_ref, f32[8,512]{1,0:T(8,128)S(1)} %get-tuple-element.236.lse_ref, f32[512,512]{1,0:T(8,128)S(1)} %copy-done.28, bf16[512,2048]{1,0:T(8,128)(2,1)S(1)} %copy-done.5, ...), custom_call_target="tpu_custom_call" | custom-call | flops 1048576 | bytes 65536 | tf_op jit(solution)/shard_map/attend_back/pallas_call | solution.py:233
  1118.5 53.6 %collective-permute-done.54 = bf16[704,2048]{1,0:T(8,128)(2,1)S(1)} collective-permute-done((bf16[704,2048]{1,0:T(8,128)(2,1)S(1)}, bf16[704,2048]{1,0:T(8,128)(2,1)S(1)}, u32[]{:S(2)}, u32[]{:S(2)}) %collective-permute-start.54) | collective-permute-done | bytes 2883616 | tf_op jit(solution)/shard_map/ppermute | solution.py:362
  1198.4 18.3 %fusion.18 = bf16[1,512,2048]{2,1,0:T(8,128)(2,1)} fusion(f32[512,2048]{1,0:T(8,128)} %copy-done.63, bf16[512,5632]{1,0:T(8,128)(2,1)S(1)} %bitcast.190, bf16[5632,2048]{1,0:T(8,128)(2,1)} %bitcast.201), kind=kOutput, calls=%fused_computation.76 | convolution fusion | flops 11813257216 | bytes 35127296 | tf_op jit(solution)/shard_map/dot_general | solution.py:26
  1323.4 24.9 %collective-permute-done.67 = bf16[128,640]{0,1:T(8,128)(2,1)S(1)} collective-permute-done((bf16[128,640]{0,1:T(8,128)(2,1)S(1)}, bf16[128,640]{0,1:T(8,128)(2,1)S(1)}, u32[]{:S(2)}, u32[]{:S(2)}) %collective-permute-start.67) | collective-permute-done | bytes 163872 | tf_op jit(solution)/shard_map/ppermute | solution.py:373
  (661 shorter events, 626.1 us)
Async XLA Ops:
  10.6 121.4 %all-gather.11.cloned.1.call-start = ((), (), s32[]{:S(2)}) async-start(), calls=%async_computation.10 | async-start | bytes 3604480 | tf_op jit(solution)/shard_map/all_gather | solution.py:579
  69.7 138.3 %all-gather.13.cloned.1.call-start = ((), (), s32[]{:S(2)}) async-start(), calls=%async_computation.11 | async-start | bytes 3604480 | tf_op jit(solution)/shard_map/all_gather | solution.py:579
  104.3 241.9 %all-gather.15.cloned.1.call-start = ((), (), s32[]{:S(2)}) async-start(), calls=%async_computation.12 | async-start | bytes 1310720 | tf_op jit(solution)/shard_map/all_gather | solution.py:579
  186.2 88.6 %collective-permute-start.15 = (bf16[2,2,176,2048]{3,2,1,0:T(8,128)(2,1)}, bf16[2,2,176,2048]{3,2,1,0:T(8,128)(2,1)}, u32[]{:S(2)}, u32[]{:S(2)}) collective-permute-start(bf16[2,2,176,2048]{3,2,1,0:T(8,128)(2,1)} %pad_maximum_fusion.6), channel_id=1, source_target_pairs={{0,2},{1,3},{2,0},{3,1},{4,6},{5,7},{6,4},{7,5},{8,10},{9,11},{10,... | collective-permute-start | bytes 8650760 | tf_op jit(solution)/shard_map/ppermute | solution.py:373
  212.7 84.0 %collective-permute-start.17 = (bf16[2,64,5632]{2,1,0:T(8,128)(2,1)}, bf16[2,64,5632]{2,1,0:T(8,128)(2,1)}, u32[]{:S(2)}, u32[]{:S(2)}) collective-permute-start(bf16[2,64,5632]{2,1,0:T(8,128)(2,1)} %get-tuple-element.348), channel_id=1, source_target_pairs={{0,4},{1,5},{2,6},{3,7},{4,0},{5,1},{6,2},{7,3},{8,12},{9,13},{10,... | collective-permute-start | bytes 4325384 | tf_op jit(solution)/shard_map/ppermute | solution.py:373
  213.9 82.8 %collective-permute-start.18 = (bf16[2,64,5632]{2,1,0:T(8,128)(2,1)}, bf16[2,64,5632]{2,1,0:T(8,128)(2,1)}, u32[]{:S(2)}, u32[]{:S(2)}) collective-permute-start(bf16[2,64,5632]{2,1,0:T(8,128)(2,1)} %get-tuple-element.347), channel_id=1, source_target_pairs={{0,2},{1,3},{2,0},{3,1},{4,6},{5,7},{6,4},{7,5},{8,10},{9,11},{10,... | collective-permute-start | bytes 4325384 | tf_op jit(solution)/shard_map/ppermute | solution.py:373
  307.6 707.4 %reduce-scatter.8.cloned.1.call-start = ((), (), s32[]{:S(2)}) async-start(), calls=%async_computation.5 | async-start | bytes 3604480 | tf_op jit(solution)/shard_map/reduce_scatter | solution.py:501
  311.4 106.5 %collective-permute-start.21 = (bf16[2,2,64,5632]{3,2,1,0:T(8,128)(2,1)}, bf16[2,2,64,5632]{3,2,1,0:T(8,128)(2,1)}, u32[]{:S(2)}, u32[]{:S(2)}) collective-permute-start(bf16[2,2,64,5632]{3,2,1,0:T(8,128)(2,1)} %pad_maximum_fusion.9), channel_id=1, source_target_pairs={{0,2},{1,3},{2,0},{3,1},{4,6},{5,7},{6,4},{7,5},{8,10},{9,11},{10,... | collective-permute-start | bytes 8650760 | tf_op jit(solution)/shard_map/ppermute | solution.py:373
  316.1 101.9 %collective-permute-start.22 = (bf16[2,2,64,5632]{3,2,1,0:T(8,128)(2,1)}, bf16[2,2,64,5632]{3,2,1,0:T(8,128)(2,1)}, u32[]{:S(2)}, u32[]{:S(2)}) collective-permute-start(bf16[2,2,64,5632]{3,2,1,0:T(8,128)(2,1)} %pad_maximum_fusion.10), channel_id=1, source_target_pairs={{0,4},{1,5},{2,6},{3,7},{4,0},{5,1},{6,2},{7,3},{8,12},{9,13},{10,... | collective-permute-start | bytes 8650760 | tf_op jit(solution)/shard_map/ppermute | solution.py:373
  316.6 101.4 %collective-permute-start.25 = (bf16[2,2,64,5632]{3,2,1,0:T(8,128)(2,1)}, bf16[2,2,64,5632]{3,2,1,0:T(8,128)(2,1)}, u32[]{:S(2)}, u32[]{:S(2)}) collective-permute-start(bf16[2,2,64,5632]{3,2,1,0:T(8,128)(2,1)} %collective-permute-done.19), channel_id=1, source_target_pairs={{0,8},{8,24},{24,16},{16,0},{1,9},{9,25},{25,17},{17,1},{2,10},{10... | collective-permute-start | bytes 8650760 | tf_op jit(solution)/shard_map/ppermute | solution.py:362
  469.4 112.0 %collective-permute-start.30 = (bf16[2,2,64,5632]{3,2,1,0:T(8,128)(2,1)}, bf16[2,2,64,5632]{3,2,1,0:T(8,128)(2,1)}, u32[]{:S(2)}, u32[]{:S(2)}) collective-permute-start(bf16[2,2,64,5632]{3,2,1,0:T(8,128)(2,1)} %collective-permute-done.25), channel_id=1, source_target_pairs={{0,8},{8,24},{24,16},{16,0},{1,9},{9,25},{25,17},{17,1},{2,10},{10... | collective-permute-start | bytes 8650760 | tf_op jit(solution)/shard_map/ppermute | solution.py:362
  696.6 75.9 %collective-permute-start.34 = (bf16[2816,2048]{1,0:T(8,128)(2,1)}, bf16[2816,2048]{1,0:T(8,128)(2,1)}, u32[]{:S(2)}, u32[]{:S(2)}) collective-permute-start(bf16[2816,2048]{1,0:T(8,128)(2,1)} %convolution_convert_fusion.1), channel_id=1, source_target_pairs={{0,1},{1,0},{2,3},{3,2},{4,5},{5,4},{6,7},{7,6},{8,9},{9,8},{10,11... | collective-permute-start | bytes 34603016 | tf_op jit(solution)/shard_map/ppermute | solution.py:373
  772.5 87.2 %collective-permute-start.36 = (bf16[256,5632]{1,0:T(8,128)(2,1)}, bf16[256,5632]{1,0:T(8,128)(2,1)}, u32[]{:S(2)}, u32[]{:S(2)}) collective-permute-start(bf16[256,5632]{1,0:T(8,128)(2,1)} %add_convert_fusion.18), channel_id=1, source_target_pairs={{0,2},{1,3},{2,0},{3,1},{4,6},{5,7},{6,4},{7,5},{8,10},{9,11},{10,... | collective-permute-start | bytes 8650760 | tf_op jit(solution)/shard_map/ppermute | solution.py:373
  772.9 86.7 %collective-permute-start.37 = (bf16[256,5632]{1,0:T(8,128)(2,1)}, bf16[256,5632]{1,0:T(8,128)(2,1)}, u32[]{:S(2)}, u32[]{:S(2)}) collective-permute-start(bf16[256,5632]{1,0:T(8,128)(2,1)} %add_convert_fusion.17), channel_id=1, source_target_pairs={{0,4},{1,5},{2,6},{3,7},{4,0},{5,1},{6,2},{7,3},{8,12},{9,13},{10,... | collective-permute-start | bytes 8650760 | tf_op jit(solution)/shard_map/ppermute | solution.py:373
  780.0 79.7 %collective-permute-start.38 = (bf16[704,2048]{1,0:T(8,128)(2,1)}, bf16[704,2048]{1,0:T(8,128)(2,1)}, u32[]{:S(2)}, u32[]{:S(2)}) collective-permute-start(bf16[704,2048]{1,0:T(8,128)(2,1)} %add_convert_fusion.16), channel_id=1, source_target_pairs={{0,8},{8,24},{24,16},{16,0},{1,9},{9,25},{25,17},{17,1},{2,10},{10... | collective-permute-start | bytes 8650760 | tf_op jit(solution)/shard_map/ppermute | solution.py:362
  801.7 120.6 %collective-permute-start.41 = (bf16[256,5632]{1,0:T(8,128)(2,1)}, bf16[256,5632]{1,0:T(8,128)(2,1)}, u32[]{:S(2)}, u32[]{:S(2)}) collective-permute-start(bf16[256,5632]{1,0:T(8,128)(2,1)} %add_convert_fusion.11), channel_id=1, source_target_pairs={{0,2},{1,3},{2,0},{3,1},{4,6},{5,7},{6,4},{7,5},{8,10},{9,11},{10,... | collective-permute-start | bytes 8650760 | tf_op jit(solution)/shard_map/ppermute | solution.py:373
  808.6 113.7 %collective-permute-start.42 = (bf16[256,5632]{1,0:T(8,128)(2,1)}, bf16[256,5632]{1,0:T(8,128)(2,1)}, u32[]{:S(2)}, u32[]{:S(2)}) collective-permute-start(bf16[256,5632]{1,0:T(8,128)(2,1)} %add_convert_fusion.10), channel_id=1, source_target_pairs={{0,4},{1,5},{2,6},{3,7},{4,0},{5,1},{6,2},{7,3},{8,12},{9,13},{10,... | collective-permute-start | bytes 8650760 | tf_op jit(solution)/shard_map/ppermute | solution.py:373
  935.3 154.1 %reduce-scatter.10.cloned.1.call-start = ((), (), s32[]{:S(2)}) async-start(), calls=%async_computation.6 | async-start | bytes 3604480 | tf_op jit(solution)/shard_map/reduce_scatter | solution.py:501
  1021.3 334.2 %reduce-scatter.14.cloned.1.call-start = ((), (), s32[]{:S(2)}) async-start(), calls=%async_computation.8 | async-start | bytes 1310720 | tf_op jit(solution)/shard_map/reduce_scatter | solution.py:501
  1101.0 87.4 %collective-permute-start.51 = (bf16[1024,2048]{1,0:T(8,128)(2,1)}, bf16[1024,2048]{1,0:T(8,128)(2,1)}, u32[]{:S(2)}, u32[]{:S(2)}) collective-permute-start(bf16[1024,2048]{1,0:T(8,128)(2,1)} %convolution_convert_fusion.3), channel_id=1, source_target_pairs={{0,1},{1,0},{2,3},{3,2},{4,5},{5,4},{6,7},{7,6},{8,9},{9,8},{10,11... | collective-permute-start | bytes 12582920 | tf_op jit(solution)/shard_map/ppermute | solution.py:373
  1110.7 76.8 %collective-permute-start.50 = (bf16[1024,384]{1,0:T(8,128)(2,1)S(1)}, bf16[1024,384]{1,0:T(8,128)(2,1)S(1)}, u32[]{:S(2)}, u32[]{:S(2)}) collective-permute-start(bf16[1024,384]{1,0:T(8,128)(2,1)S(1)} %slice.476), channel_id=1, source_target_pairs={{0,2},{1,3},{2,0},{3,1},{4,6},{5,7},{6,4},{7,5},{8,10},{9,11},{10,... | collective-permute-start | bytes 2359304 | tf_op jit(solution)/shard_map/ppermute | solution.py:373
  1225.4 80.4 %collective-permute-start.65 = (bf16[704,2048]{1,0:T(8,128)(2,1)}, bf16[704,2048]{1,0:T(8,128)(2,1)}, u32[]{:S(2)}, u32[]{:S(2)}) collective-permute-start(bf16[704,2048]{1,0:T(8,128)(2,1)} %add_convert_fusion.2), channel_id=1, source_target_pairs={{0,8},{8,24},{24,16},{16,0},{1,9},{9,25},{25,17},{17,1},{2,10},{10... | collective-permute-start | bytes 8650760 | tf_op jit(solution)/shard_map/ppermute | solution.py:362
  1228.0 129.2 %reduce-scatter.12.cloned.1.call-start = ((), (), s32[]{:S(2)}) async-start(), calls=%async_computation.7 | async-start | bytes 1310720 | tf_op jit(solution)/shard_map/reduce_scatter | solution.py:501
  1287.4 82.8 %reduce-scatter.16.cloned.1.call-start = ((), (), s32[]{:S(2)}) async-start(), calls=%async_computation.13 | async-start | bytes 409600
  (209 other events, 4691.7 us)
Sparse Core Ops, SparseCore 0:
  10.7 36.5 all-gather.8
  69.8 57.5 all-gather.10
  129.0 57.8 all-gather.12
  307.7 38.5 all-gather.14
  935.4 58.9 reduce-scatter.7
  1021.4 57.4 reduce-scatter.9
  1228.1 43.4 reduce-scatter.13
  1287.6 50.0 reduce-scatter.11
  1349.4 20.7 reduce-scatter.15

commit v6 on v5

--- a/solution.py
+++ b/solution.py
@@ -766,6 +766,7 @@
     rows_in = layer_in.reshape(rows, model).astype(F32)
     normed_one, factor_one = normalize(rows_in)
     all_pos, factor_one, cosine = meet((all_pos, factor_one, cosine), first_chain, up_chain)
+    factor_one = meet(factor_one, first_chain, up_chain)
     first_weights = finish(first_chain)
     attn_all = first_weights[:, : width + 2 * kv_width]
     gain_one = first_weights[:, width + 2 * kv_width].astype(F32)
@@ -788,13 +789,15 @@
     grad_rows = out_grad.reshape(rows, model)
     plan = (
         (),
-        (down_chain, gate_chain, up_chain),
-        (down_chain, merge_chain),
+        (down_chain, merge_chain, up_chain),
+        (down_chain, merge_chain, gate_chain),
         (gate_chain, merge_chain, up_chain),
     )
     outs, log_sums = [], []
     for group in range(kv_heads):
         out, log_sum = attend(group, places, bias, queries, all_keys, vt)
+        if group < 2:
+            out = settle(out, (merge_chain, gate_chain)[group])
         queries, out, grad_rows = meet((queries, out, grad_rows), *plan[group % 4])
         if group == 2:
             down_all = finish(down_chain)
@@ -803,12 +806,13 @@
         outs.append(out)
         log_sums.append(log_sum)
     mixed = jnp.concatenate([out.astype(BF16) for out in outs], 1)
-    mixed = meet(mixed, gate_chain, merge_chain)
-    gate_all, merge_all = finish(gate_chain), finish(merge_chain)
+    mixed = meet(mixed, merge_chain)
+    merge_all = finish(merge_chain)
     middle = rows_in + mm(mixed, merge_all, NN)
     normed_two, factor_two = normalize(middle)
     second_in = (normed_two * gain_two).astype(BF16)
-    second_in = meet(second_in, up_chain)
+    second_in = meet(second_in, gate_chain, up_chain)
+    gate_all = finish(gate_chain)
     gate = mm(second_in, gate_all, NN)
     up_all = finish(up_chain)
     lift = mm(second_in, up_all, NN)
@@ -844,23 +848,25 @@
         if group == kv_heads - 4:
             grad_mixed, dkv = meet((grad_mixed, dkv), gate_sum, down_sum)
         elif group == kv_heads - 3:
-            grad_mixed, dkv, grad_branch = meet((grad_mixed, dkv, grad_branch), gate_sum, up_sum)
+            grad_mixed, dkv, grad_branch = meet(
+                (grad_mixed, dkv, grad_branch), gate_sum, up_sum, down_sum
+            )
             merge_sum = Chain(reduce_term(grid, mixed_turned, grad_branch))
         elif group == kv_heads - 2:
-            grad_mixed, dkvs = meet((grad_mixed, dkvs), up_sum, merge_sum, gate_sum)
+            grad_mixed, dkvs = meet((grad_mixed, dkvs), up_sum, merge_sum, down_sum)
             keys_sum = Chain(reduce_keys(grid, jnp.concatenate(dkvs, 1)))
-    dqs, dkv, hidden = meet((dqs, dkv, hidden), merge_sum, keys_sum, up_sum)
+    dqs, dkv, hidden = meet((dqs, dkv, hidden), merge_sum, keys_sum, gate_sum, down_sum)
     last_keys = Chain(reduce_keys(grid, dkv))
     query_grads = unrotated(unrotate_queries_kernel, dqs, cosine, sine)
+    grad_first = mm(query_grads, attn_all[:, :width], NT)
+    grad_first, query_grads, hidden = meet(
+        (grad_first, query_grads, hidden), last_keys, keys_sum, merge_sum, down_sum
+    )
     query_sum = Chain(reduce_term(grid, first_turned, query_grads))
-    grad_first = mm(query_grads, attn_all[:, :width], NT)
-    grad_first, hidden = meet(
-        (grad_first, hidden), last_keys, keys_sum, query_sum, merge_sum, down_sum
-    )
     result = middle + mm(hidden, down_all, NN)
     layer_out = result.astype(BF16).reshape(layer_in.shape)
-    grad_first = meet(grad_first, last_keys, keys_sum)
-    grad_first, layer_out = meet((grad_first, layer_out), last_keys, query_sum)
+    grad_first, layer_out = meet((grad_first, layer_out), last_keys, keys_sum, query_sum)
+    grad_first = meet(grad_first, last_keys)
     wide = finish(keys_sum)
     dkv_parts = [wide[:, at : at + WIDE] for at in range(0, wide.shape[1], WIDE)]
     dkv_parts.append(finish(last_keys))
@@ -872,9 +878,9 @@
     gain_columns = turned(gain_terms.astype(BF16), order)
     last = Chain(reduce_term(grid, first_turned, kv_grads, gain_columns))
     input_grad = (grad_middle + grad_norm_one).astype(BF16).reshape(layer_in.shape)
-    input_grad = meet(input_grad, last, query_sum)
-    input_grad = meet(input_grad, last, down_sum)
-    input_grad = meet(input_grad, last, down_sum)
+    input_grad = meet(input_grad, last, query_sum, up_sum)
+    input_grad = meet(input_grad, last, query_sum, merge_sum)
+    input_grad = meet(input_grad, last)
     query_share, last_share = finish(query_sum), finish(last)
     merge_share, gate_share = finish(merge_sum), finish(gate_sum)
     up_share, down_share = finish(up_sum), finish(down_sum)

time: 1390 us -> 1370 us (0.986)
  waiting for transfers between devices: 375 us -> 347 us
  local copies, waits for them, and re-layouts: 99.1 us -> 81.7 us
    ppermute x64, waiting for transfers between devices: 192 us -> 164 us  [next(): return lax.ppermute(values, 'ctx', pairs)]
    reduce_scatter x4, waiting for transfers between devices: 0.04 us -> 24.8 us  [reduce_term(): lax.psum_scatter(joined, 'dp', scatter_dimension=0, tiled=True)]
    unnamed x321 -> x293, local copies, waits for them, and re-layouts: 63.3 us -> 38.8 us
    ppermute x6, waiting for transfers between devices: 156 us -> 133 us  [next(): return lax.ppermute(values, 'dp', list(zip(self.ring, around)))]
  transfers between devices with their start and end apart: 79 -> 79, of which waited for: 26 -> 23; matrix products, arithmetic and copies ran while one was open for 26% -> 29% of each run, Pallas kernels for 27% -> 26%
where the time goes in v6:
time: 1370 us; the launch traced here: 1360 us
  Pallas kernels  390 us (28%)
  waiting for transfers between devices  347 us (25%)
  matrix products  292 us (21%)
  other arithmetic  143 us (10%)
  local copies, waits for them, and re-layouts  81.7 us (6%)
  starting transfers between devices  78.3 us (6%)
  between operations  16.7 us (1%)
    dot_general x41, matrix products, mm(): return lax.dot_general(left, right, dims, preferred_element_type=F32)  292 us
    pallas_call x4, Pallas kernels, attend_back(): pl.pallas_call(functools.partial(attend_back_kernel, which=group % 2, unr...  204 us
    ppermute x64, waiting for transfers between devices, next(): return lax.ppermute(values, 'ctx', pairs)  164 us
    ppermute x6, waiting for transfers between devices, next(): return lax.ppermute(values, 'dp', list(zip(self.ring, around)))  133 us
    pallas_call x4, Pallas kernels, attend(): pl.pallas_call(functools.partial(attend_kernel, which=group % 2, places=p...  103 us
    pallas_call x5, Pallas kernels, placed(): pl.pallas_call(functools.partial(place_kernel, sources=sources, slots=slo...  69.2 us
    ppermute x64, starting transfers between devices, next(): return lax.ppermute(values, 'ctx', pairs)  59 us
    unnamed x293, local copies, waits for them, and re-layouts  38.8 us
  transfers between devices with their start and end apart: 79, of which 23 were waited for; matrix products, arithmetic and copies ran while one was open for 29% of the time, Pallas kernels for 26%

profile of v6, /device:TPU:0, one launch (start us, length us, event | category | flops | bytes accessed | tf_op | source)
XLA Modules:
  0.0 1362.7 jit_solution(738348238632022968)
XLA Ops:
  66.6 29.4 %collective-permute-done.2 = bf16[2,64,2688]{2,1,0:T(8,128)(2,1)S(1)} collective-permute-done((bf16[2,64,2688]{2,1,0:T(8,128)(2,1)S(1)}, bf16[2,64,2688]{2,1,0:T(8,128)(2,1)S(1)}, u32[]{:S(2)}, u32[]{:S(2)}) %collective-permute-start.2) | collective-permute-done | bytes 688160 | tf_op jit(solution)/shard_map/ppermute | solution.py:373
  99.4 27.2 %collective-permute-done.5 = bf16[2,2,64,2688]{3,2,1,0:T(8,128)(2,1)} collective-permute-done((bf16[2,2,64,2688]{3,2,1,0:T(8,128)(2,1)S(1)}, bf16[2,2,64,2688]{3,2,1,0:T(8,128)(2,1)}, u32[]{:S(2)}, u32[]{:S(2)}) %collective-permute-start.5) | collective-permute-done | bytes 1376288 | tf_op jit(solution)/shard_map/ppermute | solution.py:373
  188.1 76.6 %collective-permute-done.11 = bf16[2,2,64,5632]{3,2,1,0:T(8,128)(2,1)} collective-permute-done((bf16[2,2,64,5632]{3,2,1,0:T(8,128)(2,1)S(1)}, bf16[2,2,64,5632]{3,2,1,0:T(8,128)(2,1)}, u32[]{:S(2)}, u32[]{:S(2)}) %collective-permute-start.11) | collective-permute-done | bytes 2883616 | tf_op jit(solution)/shard_map/ppermute | solution.py:362
  307.9 25.6 %attend.4 = (f32[512,512]{1,0:T(8,128)S(1)}, f32[8,512]{1,0:T(8,128)S(1)}) custom-call(f32[16,512]{1,0:T(8,128)S(1)} %compare_select_fusion.bias_ref, bf16[512,2048]{1,0:T(8,128)(2,1)S(1)} %copy-done.2, bf16[4096,256]{1,0:T(8,128)(2,1)S(1)} %bitcast.167, bf16[256,4096]{1,0:T(8,128)(2,1)S(1)} %copy-done.7), custom_call_target="tpu_custom_call" | custom-call | flops 1048576 | bytes 65536 | tf_op jit(solution)/shard_map/attend/pallas_call | solution.py:113
  337.6 25.8 %attend.5 = (f32[512,512]{1,0:T(8,128)S(1)}, f32[8,512]{1,0:T(8,128)S(1)}) custom-call(f32[16,512]{1,0:T(8,128)S(1)} %compare_select_fusion.bias_ref, bf16[512,2048]{1,0:T(8,128)(2,1)S(1)} %copy-done.3, bf16[4096,256]{1,0:T(8,128)(2,1)S(1)} %bitcast.168, bf16[256,4096]{1,0:T(8,128)(2,1)S(1)} %copy-done.8), custom_call_target="tpu_custom_call" | custom-call | flops 1048576 | bytes 65536 | tf_op jit(solution)/shard_map/attend/pallas_call | solution.py:113
  364.4 23.3 %collective-permute-done.16 = bf16[2,64,5632]{2,1,0:T(8,128)(2,1)} collective-permute-done((bf16[2,64,5632]{2,1,0:T(8,128)(2,1)}, bf16[2,64,5632]{2,1,0:T(8,128)(2,1)}, u32[]{:S(2)}, u32[]{:S(2)}) %collective-permute-start.16) | collective-permute-done | bytes 1441824 | tf_op jit(solution)/shard_map/ppermute | solution.py:373
  403.4 25.9 %attend.6 = (f32[512,512]{1,0:T(8,128)S(1)}, f32[8,512]{1,0:T(8,128)S(1)}) custom-call(f32[16,512]{1,0:T(8,128)S(1)} %compare_select_fusion.bias_ref, bf16[512,2048]{1,0:T(8,128)(2,1)S(1)} %copy-done.4, bf16[4096,256]{1,0:T(8,128)(2,1)S(1)} %bitcast.169, bf16[256,4096]{1,0:T(8,128)(2,1)S(1)} %copy-done.9), custom_call_target="tpu_custom_call" | custom-call | flops 1048576 | bytes 65536 | tf_op jit(solution)/shard_map/attend/pallas_call | solution.py:113
  438.3 15.0 %placed.6 = bf16[32,176,2048]{2,1,0:T(8,128)(2,1)} custom-call(s32[32]{0:T(128)S(1)} %fusion.103.order_ref, bf16[16,176,2048]{2,1,0:T(8,128)(2,1)S(1)} %pad_maximum_fusion.refs_0_, bf16[16,176,2048]{2,1,0:T(8,128)(2,1)} %collective-permute-done.21.refs_1_), custom_call_target="tpu_custom_call" | custom-call | bytes 46137344 | tf_op jit(solution)/shard_map/placed/pallas_call | solution.py:550
  457.6 20.1 %fusion.126 = f32[512,5632]{1,0:T(8,128)} fusion(bf16[512,2048]{1,0:T(8,128)(2,1)} %bitcast.214, bf16[5632,2048]{1,0:T(8,128)(2,1)} %bitcast.198), kind=kOutput, calls=%fused_computation.289 | convolution fusion | flops 11811160064 | bytes 36700160 | tf_op jit(solution)/shard_map/dot_general | solution.py:26
  480.9 25.6 %attend.7 = (f32[512,512]{1,0:T(8,128)S(1)}, f32[8,512]{1,0:T(8,128)S(1)}) custom-call(f32[16,512]{1,0:T(8,128)S(1)} %compare_select_fusion.bias_ref, bf16[512,2048]{1,0:T(8,128)(2,1)S(1)} %copy-done.5, bf16[4096,256]{1,0:T(8,128)(2,1)S(1)} %bitcast.170, bf16[256,4096]{1,0:T(8,128)(2,1)S(1)} %copy-done.10), custom_call_target="tpu_custom_call" | custom-call | flops 1048576 | bytes 65536 | tf_op jit(solution)/shard_map/attend/pallas_call | solution.py:113
  576.0 17.4 %placed.9 = bf16[32,64,5632]{2,1,0:T(8,128)(2,1)} custom-call(s32[32]{0:T(128)S(1)} %get-tuple-element.358.order_ref, bf16[4,64,5632]{2,1,0:T(8,128)(2,1)S(1)} %bitcast.182, bf16[4,64,5632]{2,1,0:T(8,128)(2,1)} %bitcast.76.refs_1_, bf16[4,64,5632]{2,1,0:T(8,128)(2,1)} %bitcast.77.refs_2_, bf16[4,64,5632]{2,1,0:T(8,128)(2,1)} %bitcast.78.refs_3_, ...), custom_call_target="tpu_custom_call" | custom-call | bytes 46137344 | tf_op jit(solution)/shard_map/placed/pallas_call | solution.py:550
  593.4 19.0 %fusion.127 = f32[512,5632]{1,0:T(8,128)} fusion(bf16[512,2048]{1,0:T(8,128)(2,1)S(1)} %multiply_convert_fusion.3.x_ref, bf16[2048,5632]{1,0:T(8,128)(2,1)} %bitcast.200), kind=kOutput, calls=%fused_computation.290 | convolution fusion | flops 11811160064 | bytes 36700160 | tf_op jit(solution)/shard_map/dot_general | solution.py:26
  612.5 17.4 %placed.8 = bf16[32,64,5632]{2,1,0:T(8,128)(2,1)} custom-call(s32[32]{0:T(128)S(1)} %fusion.103.order_ref, bf16[16,64,5632]{2,1,0:T(8,128)(2,1)} %pad_maximum_fusion.1.refs_0_, bf16[16,64,5632]{2,1,0:T(8,128)(2,1)} %collective-permute-done.31.refs_1_), custom_call_target="tpu_custom_call" | custom-call | bytes 46137344 | tf_op jit(solution)/shard_map/placed/pallas_call | solution.py:550
  629.9 29.3 %multiply_convert_fusion = (bf16[512,5632]{1,0:T(8,128)(2,1)}, bf16[512,5632]{1,0:T(8,128)(2,1)}, bf16[512,5632]{1,0:T(8,128)(2,1)}) fusion(f32[512,5632]{1,0:T(8,128)} %fusion.126, f32[512,5632]{1,0:T(8,128)} %fusion.127, bf16[512,2048]{1,0:T(8,128)(2,1)} %copy-done.15, bf16[2048,5632]{1,0:T(8,128)(2,1)} %bitcast.202), kind=kOutput, calls=%fused_computation.3 | convolution fusion | flops 11854413824 | bytes 65536000 | tf_op jit(solution)/shard_map/dot_general | solution.py:26
  691.7 19.5 %fusion.128 = f32[512,2048]{1,0:T(8,128)} fusion(bf16[512,5632]{1,0:T(8,128)(2,1)} %get-tuple-element.238, bf16[2048,5632]{1,0:T(8,128)(2,1)} %bitcast.203), kind=kOutput, calls=%fused_computation.291 | convolution fusion | flops 11811160064 | bytes 33030144 | tf_op jit(solution)/shard_map/dot_general | solution.py:26
  711.2 19.9 %multiply_reduce_fusion = (bf16[2048]{0:T(1024)(128)(2,1)S(1)}, f32[512]{0:T(512)S(1)}, f32[512,2048]{1,0:T(8,128)}) fusion(f32[512,2048]{1,0:T(8,128)} %copy-done.58, f32[512]{0:T(512)S(1)} %copy-done.115, f32[512,2048]{1,0:T(8,128)} %fusion.128, f32[2048]{0:T(1024)S(1)} %bitcast.236, bf16[512,5632]{1,0:T(8,128)(2,1)} %get-tuple-element.241, ...), kind=kOutput, calls=%fused_computation.53 | convolution fusion | flops 11818498048 | bytes 41435136 | tf_op jit(solution)/shard_map/dot_general | solution.py:26
  764.5 15.8 %collective-permute-start.38 = (bf16[704,2048]{1,0:T(8,128)(2,1)}, bf16[704,2048]{1,0:T(8,128)(2,1)}, u32[]{:S(2)}, u32[]{:S(2)}) collective-permute-start(bf16[704,2048]{1,0:T(8,128)(2,1)} %add_convert_fusion.16), channel_id=1, source_target_pairs={{0,8},{8,24},{24,16},{16,0},{1,9},{9,25},{25,17},{17,1},{2,10},{10... | collective-permute-start | bytes 8650760 | tf_op jit(solution)/shard_map/ppermute | solution.py:362
  807.0 51.2 %attend_back.4 = (f32[512,512]{1,0:T(8,128)S(1)}, bf16[4096,128]{1,0:T(8,128)(2,1)S(1)}) custom-call(s32[8]{0:T(128)S(1)} %copy-done.54, f32[16,512]{1,0:T(8,128)S(1)} %compare_select_fusion.bias_ref, f32[8,512]{1,0:T(8,128)S(1)} %get-tuple-element.189.lse_ref, f32[512,512]{1,0:T(8,128)S(1)} %copy-done.33, bf16[512,2048]{1,0:T(8,128)(2,1)S(1)} %copy-done.6, ...), custom_call_target="tpu_custom_call" | custom-call | flops 1048576 | bytes 65536 | tf_op jit(solution)/shard_map/attend_back/pallas_call | solution.py:233
  892.6 50.9 %attend_back.5 = (f32[512,512]{1,0:T(8,128)S(1)}, bf16[4096,128]{1,0:T(8,128)(2,1)S(1)}) custom-call(s32[8]{0:T(128)S(1)} %copy-done.54, f32[16,512]{1,0:T(8,128)S(1)} %compare_select_fusion.bias_ref, f32[8,512]{1,0:T(8,128)S(1)} %get-tuple-element.245.lse_ref, f32[512,512]{1,0:T(8,128)S(1)} %copy-done.31, bf16[512,2048]{1,0:T(8,128)(2,1)S(1)} %copy-done.6, ...), custom_call_target="tpu_custom_call" | custom-call | flops 1048576 | bytes 65536 | tf_op jit(solution)/shard_map/attend_back/pallas_call | solution.py:233
  974.4 51.0 %attend_back.6 = (f32[512,512]{1,0:T(8,128)S(1)}, bf16[4096,128]{1,0:T(8,128)(2,1)S(1)}) custom-call(s32[8]{0:T(128)S(1)} %copy-done.54, f32[16,512]{1,0:T(8,128)S(1)} %compare_select_fusion.bias_ref, f32[8,512]{1,0:T(8,128)S(1)} %get-tuple-element.251.lse_ref, f32[512,512]{1,0:T(8,128)S(1)} %copy-done.29, bf16[512,2048]{1,0:T(8,128)(2,1)S(1)} %copy-done.6, ...), custom_call_target="tpu_custom_call" | custom-call | flops 1048576 | bytes 65536 | tf_op jit(solution)/shard_map/attend_back/pallas_call | solution.py:233
  1025.5 56.0 %collective-permute-done.47 = bf16[704,2048]{1,0:T(8,128)(2,1)} collective-permute-done((bf16[704,2048]{1,0:T(8,128)(2,1)}, bf16[704,2048]{1,0:T(8,128)(2,1)}, u32[]{:S(2)}, u32[]{:S(2)}) %collective-permute-start.47) | collective-permute-done | bytes 2883616 | tf_op jit(solution)/shard_map/ppermute | solution.py:362
  1105.9 51.1 %attend_back.7 = (f32[512,512]{1,0:T(8,128)S(1)}, bf16[4096,128]{1,0:T(8,128)(2,1)S(1)}) custom-call(s32[8]{0:T(128)S(1)} %copy-done.54, f32[16,512]{1,0:T(8,128)S(1)} %compare_select_fusion.bias_ref, f32[8,512]{1,0:T(8,128)S(1)} %get-tuple-element.260.lse_ref, f32[512,512]{1,0:T(8,128)S(1)} %get-tuple-element.225.o_ref, bf16[512,2048]{1,0:T(8,128)(2,1)S(1)} %copy-done.6, ...), custom_call_target="tpu_custom_call" | custom-call | flops 1048576 | bytes 65536 | tf_op jit(solution)/shard_map/attend_back/pallas_call | solution.py:233
  1210.4 18.1 %fusion.18 = bf16[1,512,2048]{2,1,0:T(8,128)(2,1)} fusion(f32[512,2048]{1,0:T(8,128)} %copy-done.58, bf16[512,5632]{1,0:T(8,128)(2,1)S(1)} %bitcast.188, bf16[5632,2048]{1,0:T(8,128)(2,1)} %bitcast.199), kind=kOutput, calls=%fused_computation.76 | convolution fusion | flops 11813257216 | bytes 35127296 | tf_op jit(solution)/shard_map/dot_general | solution.py:26
  1329.3 24.8 %reduce-scatter.14.cloned.1.call-done = bf16[64,2048]{1,0:T(8,128)(2,1)} async-done(((bf16[256,2048]{1,0:T(8,128)(2,1)}), bf16[64,2048]{1,0:T(8,128)(2,1)}) %reduce-scatter.14.cloned.1.call-update) | async-done | bytes 262160 | tf_op jit(solution)/shard_map/reduce_scatter | solution.py:501
  (633 shorter events, 610.0 us)
Async XLA Ops:
  10.6 153.8 %all-gather.11.cloned.1.call-start = ((), (), s32[]{:S(2)}) async-start(), calls=%async_computation.10 | async-start | bytes 3604480 | tf_op jit(solution)/shard_map/all_gather | solution.py:579
  99.4 194.7 %all-gather.13.cloned.1.call-start = ((), (), s32[]{:S(2)}) async-start(), calls=%async_computation.11 | async-start | bytes 3604480 | tf_op jit(solution)/shard_map/all_gather | solution.py:579
  133.1 201.3 %all-gather.15.cloned.1.call-start = ((), (), s32[]{:S(2)}) async-start(), calls=%async_computation.12 | async-start | bytes 1310720 | tf_op jit(solution)/shard_map/all_gather | solution.py:579
  138.4 126.3 %collective-permute-start.11 = (bf16[2,2,64,5632]{3,2,1,0:T(8,128)(2,1)S(1)}, bf16[2,2,64,5632]{3,2,1,0:T(8,128)(2,1)}, u32[]{:S(2)}, u32[]{:S(2)}) collective-permute-start(bf16[2,2,64,5632]{3,2,1,0:T(8,128)(2,1)S(1)} %get-tuple-element.370), channel_id=1, source_target_pairs={{0,8},{8,24},{24,16},{16,0},{1,9},{9,25},{25,17},{17,1},{2,10},{10... | collective-permute-start | bytes 8650760 | tf_op jit(solution)/shard_map/ppermute | solution.py:362
  169.3 95.4 %collective-permute-start.9 = (bf16[2,176,2048]{2,1,0:T(8,128)(2,1)}, bf16[2,176,2048]{2,1,0:T(8,128)(2,1)}, u32[]{:S(2)}, u32[]{:S(2)}) collective-permute-start(bf16[2,176,2048]{2,1,0:T(8,128)(2,1)} %get-tuple-element.378), channel_id=1, source_target_pairs={{0,4},{1,5},{2,6},{3,7},{4,0},{5,1},{6,2},{7,3},{8,12},{9,13},{10,... | collective-permute-start | bytes 4325384 | tf_op jit(solution)/shard_map/ppermute | solution.py:373
  171.9 92.8 %collective-permute-start.10 = (bf16[2,176,2048]{2,1,0:T(8,128)(2,1)}, bf16[2,176,2048]{2,1,0:T(8,128)(2,1)}, u32[]{:S(2)}, u32[]{:S(2)}) collective-permute-start(bf16[2,176,2048]{2,1,0:T(8,128)(2,1)} %get-tuple-element.377), channel_id=1, source_target_pairs={{0,2},{1,3},{2,0},{3,1},{4,6},{5,7},{6,4},{7,5},{8,10},{9,11},{10,... | collective-permute-start | bytes 4325384 | tf_op jit(solution)/shard_map/ppermute | solution.py:373
  285.2 873.9 %reduce-scatter.8.cloned.1.call-start = ((), (), s32[]{:S(2)}) async-start(), calls=%async_computation.5 | async-start | bytes 3604480 | tf_op jit(solution)/shard_map/reduce_scatter | solution.py:501
  288.6 99.1 %collective-permute-start.18 = (bf16[2,2,176,2048]{3,2,1,0:T(8,128)(2,1)}, bf16[2,2,176,2048]{3,2,1,0:T(8,128)(2,1)}, u32[]{:S(2)}, u32[]{:S(2)}) collective-permute-start(bf16[2,2,176,2048]{3,2,1,0:T(8,128)(2,1)} %pad_maximum_fusion.7), channel_id=1, source_target_pairs={{0,2},{1,3},{2,0},{3,1},{4,6},{5,7},{6,4},{7,5},{8,10},{9,11},{10,... | collective-permute-start | bytes 8650760 | tf_op jit(solution)/shard_map/ppermute | solution.py:373
  292.4 95.3 %collective-permute-start.19 = (bf16[2,2,176,2048]{3,2,1,0:T(8,128)(2,1)}, bf16[2,2,176,2048]{3,2,1,0:T(8,128)(2,1)}, u32[]{:S(2)}, u32[]{:S(2)}) collective-permute-start(bf16[2,2,176,2048]{3,2,1,0:T(8,128)(2,1)} %pad_maximum_fusion.8), channel_id=1, source_target_pairs={{0,4},{1,5},{2,6},{3,7},{4,0},{5,1},{6,2},{7,3},{8,12},{9,13},{10,... | collective-permute-start | bytes 8650760 | tf_op jit(solution)/shard_map/ppermute | solution.py:373
  293.9 93.8 %collective-permute-start.20 = (bf16[2,2,64,5632]{3,2,1,0:T(8,128)(2,1)}, bf16[2,2,64,5632]{3,2,1,0:T(8,128)(2,1)}, u32[]{:S(2)}, u32[]{:S(2)}) collective-permute-start(bf16[2,2,64,5632]{3,2,1,0:T(8,128)(2,1)} %collective-permute-done.11), channel_id=1, source_target_pairs={{0,8},{8,24},{24,16},{16,0},{1,9},{9,25},{25,17},{17,1},{2,10},{10... | collective-permute-start | bytes 8650760 | tf_op jit(solution)/shard_map/ppermute | solution.py:362
  298.7 89.1 %collective-permute-start.16 = (bf16[2,64,5632]{2,1,0:T(8,128)(2,1)}, bf16[2,64,5632]{2,1,0:T(8,128)(2,1)}, u32[]{:S(2)}, u32[]{:S(2)}) collective-permute-start(bf16[2,64,5632]{2,1,0:T(8,128)(2,1)} %get-tuple-element.374), channel_id=1, source_target_pairs={{0,4},{1,5},{2,6},{3,7},{4,0},{5,1},{6,2},{7,3},{8,12},{9,13},{10,... | collective-permute-start | bytes 4325384 | tf_op jit(solution)/shard_map/ppermute | solution.py:373
  299.2 88.5 %collective-permute-start.17 = (bf16[2,64,5632]{2,1,0:T(8,128)(2,1)}, bf16[2,64,5632]{2,1,0:T(8,128)(2,1)}, u32[]{:S(2)}, u32[]{:S(2)}) collective-permute-start(bf16[2,64,5632]{2,1,0:T(8,128)(2,1)} %get-tuple-element.373), channel_id=1, source_target_pairs={{0,2},{1,3},{2,0},{3,1},{4,6},{5,7},{6,4},{7,5},{8,10},{9,11},{10,... | collective-permute-start | bytes 4325384 | tf_op jit(solution)/shard_map/ppermute | solution.py:373
  403.4 103.0 %collective-permute-start.28 = (bf16[2,2,64,5632]{3,2,1,0:T(8,128)(2,1)}, bf16[2,2,64,5632]{3,2,1,0:T(8,128)(2,1)}, u32[]{:S(2)}, u32[]{:S(2)}) collective-permute-start(bf16[2,2,64,5632]{3,2,1,0:T(8,128)(2,1)} %collective-permute-done.20), channel_id=1, source_target_pairs={{0,8},{8,24},{24,16},{16,0},{1,9},{9,25},{25,17},{17,1},{2,10},{10... | collective-permute-start | bytes 8650760 | tf_op jit(solution)/shard_map/ppermute | solution.py:362
  432.9 90.2 %collective-permute-start.24 = (bf16[2,2,64,5632]{3,2,1,0:T(8,128)(2,1)}, bf16[2,2,64,5632]{3,2,1,0:T(8,128)(2,1)}, u32[]{:S(2)}, u32[]{:S(2)}) collective-permute-start(bf16[2,2,64,5632]{3,2,1,0:T(8,128)(2,1)} %pad_maximum_fusion.9), channel_id=1, source_target_pairs={{0,2},{1,3},{2,0},{3,1},{4,6},{5,7},{6,4},{7,5},{8,10},{9,11},{10,... | collective-permute-start | bytes 8650760 | tf_op jit(solution)/shard_map/ppermute | solution.py:373
  757.2 101.0 %collective-permute-start.36 = (bf16[256,5632]{1,0:T(8,128)(2,1)}, bf16[256,5632]{1,0:T(8,128)(2,1)}, u32[]{:S(2)}, u32[]{:S(2)}) collective-permute-start(bf16[256,5632]{1,0:T(8,128)(2,1)} %add_convert_fusion.18), channel_id=1, source_target_pairs={{0,2},{1,3},{2,0},{3,1},{4,6},{5,7},{6,4},{7,5},{8,10},{9,11},{10,... | collective-permute-start | bytes 8650760 | tf_op jit(solution)/shard_map/ppermute | solution.py:373
  758.6 99.6 %collective-permute-start.37 = (bf16[256,5632]{1,0:T(8,128)(2,1)}, bf16[256,5632]{1,0:T(8,128)(2,1)}, u32[]{:S(2)}, u32[]{:S(2)}) collective-permute-start(bf16[256,5632]{1,0:T(8,128)(2,1)} %add_convert_fusion.17), channel_id=1, source_target_pairs={{0,4},{1,5},{2,6},{3,7},{4,0},{5,1},{6,2},{7,3},{8,12},{9,13},{10,... | collective-permute-start | bytes 8650760 | tf_op jit(solution)/shard_map/ppermute | solution.py:373
  764.5 93.7 %collective-permute-start.38 = (bf16[704,2048]{1,0:T(8,128)(2,1)}, bf16[704,2048]{1,0:T(8,128)(2,1)}, u32[]{:S(2)}, u32[]{:S(2)}) collective-permute-start(bf16[704,2048]{1,0:T(8,128)(2,1)} %add_convert_fusion.16), channel_id=1, source_target_pairs={{0,8},{8,24},{24,16},{16,0},{1,9},{9,25},{25,17},{17,1},{2,10},{10... | collective-permute-start | bytes 8650760 | tf_op jit(solution)/shard_map/ppermute | solution.py:362
  799.8 143.7 %collective-permute-start.41 = (bf16[256,5632]{1,0:T(8,128)(2,1)}, bf16[256,5632]{1,0:T(8,128)(2,1)}, u32[]{:S(2)}, u32[]{:S(2)}) collective-permute-start(bf16[256,5632]{1,0:T(8,128)(2,1)} %add_convert_fusion.11), channel_id=1, source_target_pairs={{0,2},{1,3},{2,0},{3,1},{4,6},{5,7},{6,4},{7,5},{8,10},{9,11},{10,... | collective-permute-start | bytes 8650760 | tf_op jit(solution)/shard_map/ppermute | solution.py:373
  806.7 136.8 %collective-permute-start.42 = (bf16[256,5632]{1,0:T(8,128)(2,1)}, bf16[256,5632]{1,0:T(8,128)(2,1)}, u32[]{:S(2)}, u32[]{:S(2)}) collective-permute-start(bf16[256,5632]{1,0:T(8,128)(2,1)} %add_convert_fusion.10), channel_id=1, source_target_pairs={{0,4},{1,5},{2,6},{3,7},{4,0},{5,1},{6,2},{7,3},{8,12},{9,13},{10,... | collective-permute-start | bytes 8650760 | tf_op jit(solution)/shard_map/ppermute | solution.py:373
  962.6 118.8 %collective-permute-start.46 = (bf16[1024,2048]{1,0:T(8,128)(2,1)}, bf16[1024,2048]{1,0:T(8,128)(2,1)}, u32[]{:S(2)}, u32[]{:S(2)}) collective-permute-start(bf16[1024,2048]{1,0:T(8,128)(2,1)} %convolution_convert_fusion.4), channel_id=1, source_target_pairs={{0,1},{1,0},{2,3},{3,2},{4,5},{5,4},{6,7},{7,6},{8,9},{9,8},{10,11... | collective-permute-start | bytes 12582920 | tf_op jit(solution)/shard_map/ppermute | solution.py:373
  969.1 112.3 %collective-permute-start.47 = (bf16[704,2048]{1,0:T(8,128)(2,1)}, bf16[704,2048]{1,0:T(8,128)(2,1)}, u32[]{:S(2)}, u32[]{:S(2)}) collective-permute-start(bf16[704,2048]{1,0:T(8,128)(2,1)} %add_convert_fusion.2), channel_id=1, source_target_pairs={{0,8},{8,24},{24,16},{16,0},{1,9},{9,25},{25,17},{17,1},{2,10},{10... | collective-permute-start | bytes 8650760 | tf_op jit(solution)/shard_map/ppermute | solution.py:362
  973.1 294.2 %reduce-scatter.10.cloned.1.call-start = ((), (), s32[]{:S(2)}) async-start(), calls=%async_computation.6 | async-start | bytes 3604480 | tf_op jit(solution)/shard_map/reduce_scatter | solution.py:501
  1105.9 178.4 %reduce-scatter.12.cloned.1.call-start = ((), (), s32[]{:S(2)}) async-start(), calls=%async_computation.7 | async-start | bytes 1310720 | tf_op jit(solution)/shard_map/reduce_scatter | solution.py:501
  1229.6 96.7 %reduce-scatter.16.cloned.1.call-start = ((), (), s32[]{:S(2)}) async-start(), calls=%async_computation.13 | async-start | bytes 409600
  (195 other events, 4118.4 us)
Sparse Core Ops, SparseCore 0:
  10.8 36.5 all-gather.8
  99.5 64.8 all-gather.10
  166.0 97.4 all-gather.12
  285.3 38.0 all-gather.14
  973.2 98.8 reduce-scatter.7
  1106.0 54.8 reduce-scatter.9
  1229.8 25.9 reduce-scatter.11
  1307.3 18.9 reduce-scatter.15
  1328.7 25.3 reduce-scatter.13

commit v7 on v6

--- a/solution.py
+++ b/solution.py
@@ -605,10 +605,10 @@
     waiting = [part]
     for k in range(grid.n_dp - 1):
         sent = [grid.next(near[-1], "d")]
-        early = k == grid.n_dp - 2
+        early = k == grid.n_dp // 2 - 1
         if early:
-            sent.append(grid.next(jnp.stack(waiting[:-1]), "c"))
-            waiting = waiting[-1:]
+            sent.append(grid.next(jnp.stack(waiting), "c"))
+            waiting = []
         came = yield sent
         if early:
             far.append(came[1])
@@ -683,18 +683,14 @@
             self.done, self.result, self.flight = True, stop.value, []
 
 
-def meet(main, *chains):
+def meet(main, *chains, hold=()):
     chains = [c for c in chains if not c.done]
-    main, flights = lax.optimization_barrier((main, [list(c.flight) for c in chains]))
-    for chain, flight in zip(chains, flights):
-        chain.advance(flight)
-    return main
-
-
-def settle(main, *chains):
-    main, flights = lax.optimization_barrier((main, [list(c.flight) for c in chains]))
-    for chain, flight in zip(chains, flights):
+    both = chains + [c for c in hold if not c.done]
+    main, flights = lax.optimization_barrier((main, [list(c.flight) for c in both]))
+    for i, (chain, flight) in enumerate(zip(both, flights)):
         chain.flight = flight
+        if i < len(chains):
+            chain.advance(flight)
     return main
 
 
@@ -746,7 +742,7 @@
     run = rows // 2
     positions = positions[0]
     grid = Grid(n_dp, n_ctx)
-    order = grid.block_order(False)
+    order, sum_order = grid.block_order(False), grid.block_order(True)
     ring_order, ctx_order = grid.ring_order(), grid.ctx_order()
     places = grid.value_places()
 
@@ -766,7 +762,6 @@
     rows_in = layer_in.reshape(rows, model).astype(F32)
     normed_one, factor_one = normalize(rows_in)
     all_pos, factor_one, cosine = meet((all_pos, factor_one, cosine), first_chain, up_chain)
-    factor_one = meet(factor_one, first_chain, up_chain)
     first_weights = finish(first_chain)
     attn_all = first_weights[:, : width + 2 * kv_width]
     gain_one = first_weights[:, width + 2 * kv_width].astype(F32)
@@ -780,42 +775,42 @@
     later = all_pos.reshape(n_ctx, 2)[ctx_order].reshape(2 * n_ctx, 1)
     later = later > jnp.repeat(positions[::run], run)[None, :]
     bias = jnp.where(later, MASKED, 0.0).astype(F32)
-    bias = meet(bias, kv_chain, down_chain, up_chain)
     bias = meet(bias, kv_chain)
-    bias = meet(bias, kv_chain, gate_chain)
+    bias = meet(bias, kv_chain)
+    bias = meet(bias, kv_chain, down_chain, up_chain, gate_chain)
     all_keys, all_values = finish(kv_chain)
     kt, vt = all_keys.T, all_values.T
 
     grad_rows = out_grad.reshape(rows, model)
     plan = (
-        (),
-        (down_chain, merge_chain, up_chain),
-        (down_chain, merge_chain, gate_chain),
-        (gate_chain, merge_chain, up_chain),
+        ((), ()),
+        ((up_chain,), ()),
+        ((down_chain, merge_chain), (gate_chain,)),
+        ((down_chain, merge_chain, gate_chain, up_chain), ()),
     )
     outs, log_sums = [], []
     for group in range(kv_heads):
         out, log_sum = attend(group, places, bias, queries, all_keys, vt)
-        if group < 2:
-            out = settle(out, (merge_chain, gate_chain)[group])
-        queries, out, grad_rows = meet((queries, out, grad_rows), *plan[group % 4])
-        if group == 2:
-            down_all = finish(down_chain)
-            grad_hidden = mm(grad_rows, down_all, NT)
-            queries, grad_hidden = lax.optimization_barrier((queries, grad_hidden))
+        on, hold = plan[group % 4]
+        queries, out, grad_rows = meet((queries, out, grad_rows), *on, hold=hold)
         outs.append(out)
         log_sums.append(log_sum)
+    down_all = finish(down_chain)
+    grad_hidden = mm(grad_rows, down_all, NT)
+    outs, grad_hidden = meet((outs, grad_hidden), merge_chain)
     mixed = jnp.concatenate([out.astype(BF16) for out in outs], 1)
     mixed = meet(mixed, merge_chain)
     merge_all = finish(merge_chain)
     middle = rows_in + mm(mixed, merge_all, NN)
     normed_two, factor_two = normalize(middle)
     second_in = (normed_two * gain_two).astype(BF16)
-    second_in = meet(second_in, gate_chain, up_chain)
+    second_in = meet(second_in, up_chain)
+    second_in = meet(second_in, gate_chain)
+    up_all = finish(up_chain)
+    lift = mm(second_in, up_all, NN)
+    lift = meet(lift, gate_chain)
     gate_all = finish(gate_chain)
     gate = mm(second_in, gate_all, NN)
-    up_all = finish(up_chain)
-    lift = mm(second_in, up_all, NN)
     sigma = jax.nn.sigmoid(gate)
     activated = gate * sigma
     hidden = (activated * lift).astype(BF16)
@@ -849,23 +844,19 @@
             grad_mixed, dkv = meet((grad_mixed, dkv), gate_sum, down_sum)
         elif group == kv_heads - 3:
             grad_mixed, dkv, grad_branch = meet(
-                (grad_mixed, dkv, grad_branch), gate_sum, up_sum, down_sum
+                (grad_mixed, dkv, grad_branch), up_sum, down_sum, hold=(gate_sum,)
             )
             merge_sum = Chain(reduce_term(grid, mixed_turned, grad_branch))
         elif group == kv_heads - 2:
-            grad_mixed, dkvs = meet((grad_mixed, dkvs), up_sum, merge_sum, down_sum)
+            grad_mixed, dkvs = meet((grad_mixed, dkvs), gate_sum, up_sum, merge_sum, down_sum)
             keys_sum = Chain(reduce_keys(grid, jnp.concatenate(dkvs, 1)))
-    dqs, dkv, hidden = meet((dqs, dkv, hidden), merge_sum, keys_sum, gate_sum, down_sum)
+    dqs, dkv = meet((dqs, dkv), keys_sum, gate_sum, down_sum, hold=(merge_sum,))
     last_keys = Chain(reduce_keys(grid, dkv))
     query_grads = unrotated(unrotate_queries_kernel, dqs, cosine, sine)
+    query_sum = Chain(reduce_term(grid, first_turned, query_grads))
     grad_first = mm(query_grads, attn_all[:, :width], NT)
-    grad_first, query_grads, hidden = meet(
-        (grad_first, query_grads, hidden), last_keys, keys_sum, merge_sum, down_sum
-    )
-    query_sum = Chain(reduce_term(grid, first_turned, query_grads))
-    result = middle + mm(hidden, down_all, NN)
-    layer_out = result.astype(BF16).reshape(layer_in.shape)
-    grad_first, layer_out = meet((grad_first, layer_out), last_keys, keys_sum, query_sum)
+    grad_first = meet(grad_first, last_keys, keys_sum, query_sum, down_sum)
+    grad_first = meet(grad_first, last_keys, keys_sum, merge_sum)
     grad_first = meet(grad_first, last_keys)
     wide = finish(keys_sum)
     dkv_parts = [wide[:, at : at + WIDE] for at in range(0, wide.shape[1], WIDE)]
@@ -875,12 +866,16 @@
     grad_norm_one, gain_one_term = norm_back(grad_first, normed_one, factor_one, gain_one)
     gain_terms = jnp.stack([gain_one_term, gain_two_term], 0)
     gain_terms = jnp.concatenate([gain_terms, jnp.zeros((WIDE - 2, model), F32)], 0)
-    gain_columns = turned(gain_terms.astype(BF16), order)
-    last = Chain(reduce_term(grid, first_turned, kv_grads, gain_columns))
+    gain_columns = turned(gain_terms.astype(BF16), sum_order)
+    last_turned = turned(first_in, sum_order)
+    last = Chain(reduce_term(grid, last_turned, kv_grads, gain_columns, around=True))
+    grad_norm_one, hidden = meet((grad_norm_one, hidden), last, query_sum, merge_sum, up_sum)
+    result = middle + mm(hidden, down_all, NN)
+    layer_out = result.astype(BF16).reshape(layer_in.shape)
     input_grad = (grad_middle + grad_norm_one).astype(BF16).reshape(layer_in.shape)
-    input_grad = meet(input_grad, last, query_sum, up_sum)
-    input_grad = meet(input_grad, last, query_sum, merge_sum)
-    input_grad = meet(input_grad, last)
+    layer_out, input_grad = meet((layer_out, input_grad), last, query_sum)
+    while not last.done:
+        input_grad = meet(input_grad, last)
     query_share, last_share = finish(query_sum), finish(last)
     merge_share, gate_share = finish(merge_sum), finish(gate_sum)
     up_share, down_share = finish(up_sum), finish(down_sum)

time: 1370 us -> 1320 us (0.964)
  starting transfers between devices: 78.3 us -> 61.6 us
  waiting for transfers between devices: 347 us -> 331 us
    ppermute x6 -> x9, waiting for transfers between devices: 133 us -> 99.1 us  [next(): return lax.ppermute(values, 'dp', list(zip(self.ring, around)))]
    all_gather x4, waiting for transfers between devices: 14.2 us -> 45 us  [gather_weight(): column, = (yield [lax.all_gather(weight, 'dp', axis=0)])]
    reduce_scatter x4, waiting for transfers between devices: 24.8 us -> 6.16 us  [reduce_term(): lax.psum_scatter(joined, 'dp', scatter_dimension=0, tiled=True)]
    ppermute x64, waiting for transfers between devices: 164 us -> 180 us  [next(): return lax.ppermute(values, 'ctx', pairs)]
    unnamed x293 -> x331, local copies, waits for them, and re-layouts: 38.8 us -> 41.3 us
  transfers between devices with their start and end apart: 79 -> 81, of which waited for: 23 -> 30; matrix products, arithmetic and copies ran while one was open for 29% -> 28% of each run, Pallas kernels for 26% -> 27%
where the time goes in v7:
time: 1320 us
  Pallas kernels  388 us (29%)
  waiting for transfers between devices  331 us (25%)
  matrix products  285 us (22%)
  other arithmetic  144 us (11%)
  local copies, waits for them, and re-layouts  75.8 us (6%)
  starting transfers between devices  61.6 us (5%)
  between operations  17.5 us (1%)
  blocking collectives  13.5 us (1%)
    dot_general x41, matrix products, mm(): return lax.dot_general(left, right, dims, preferred_element_type=F32)  285 us
    pallas_call x4, Pallas kernels, attend_back(): pl.pallas_call(functools.partial(attend_back_kernel, which=group % 2, unr...  204 us
    ppermute x64, waiting for transfers between devices, next(): return lax.ppermute(values, 'ctx', pairs)  180 us
    pallas_call x4, Pallas kernels, attend(): pl.pallas_call(functools.partial(attend_kernel, which=group % 2, places=p...  103 us
    ppermute x9, waiting for transfers between devices, next(): return lax.ppermute(values, 'dp', list(zip(self.ring, around)))  99.1 us
    pallas_call x5, Pallas kernels, placed(): pl.pallas_call(functools.partial(place_kernel, sources=sources, slots=slo...  65.9 us
    ppermute x64, starting transfers between devices, next(): return lax.ppermute(values, 'ctx', pairs)  53.3 us
    all_gather x4, waiting for transfers between devices, gather_weight(): column, = (yield [lax.all_gather(weight, 'dp', axis=0)])  45 us
  transfers between devices with their start and end apart: 81, of which 30 were waited for; matrix products, arithmetic and copies ran while one was open for 28% of the time, Pallas kernels for 27%

profile of v7, /device:TPU:0, one launch (start us, length us, event | category | flops | bytes accessed | tf_op | source)
XLA Modules:
  0.0 1316.2 jit_solution(15450694494915526606)
XLA Ops:
  68.7 27.3 %collective-permute-done.4 = bf16[2,2,64,2688]{3,2,1,0:T(8,128)(2,1)S(1)} collective-permute-done((bf16[2,2,64,2688]{3,2,1,0:T(8,128)(2,1)S(1)}, bf16[2,2,64,2688]{3,2,1,0:T(8,128)(2,1)S(1)}, u32[]{:S(2)}, u32[]{:S(2)}) %collective-permute-start.4) | collective-permute-done | bytes 1376288 | tf_op jit(solution)/shard_map/ppermute | solution.py:373
  128.2 31.7 %all-gather.11.cloned.1.call-done = bf16[704,2048]{1,0:T(8,128)(2,1)} async-done(((bf16[176,2048]{1,0:T(8,128)(2,1)}), bf16[704,2048]{1,0:T(8,128)(2,1)}) %all-gather.11.cloned.1.call-update) | async-done | bytes 2883600 | tf_op jit(solution)/shard_map/all_gather | solution.py:579
  189.7 35.4 %collective-permute-done.8 = bf16[2,512,256]{2,1,0:T(8,128)(2,1)S(1)} collective-permute-done((bf16[2,512,256]{2,1,0:T(8,128)(2,1)S(1)}, bf16[2,512,256]{2,1,0:T(8,128)(2,1)S(1)}, u32[]{:S(2)}, u32[]{:S(2)}) %collective-permute-start.8) | collective-permute-done | bytes 524320 | tf_op jit(solution)/shard_map/ppermute | solution.py:373
  228.7 25.9 %collective-permute-done.13 = bf16[2,176,2048]{2,1,0:T(8,128)(2,1)} collective-permute-done((bf16[2,176,2048]{2,1,0:T(8,128)(2,1)}, bf16[2,176,2048]{2,1,0:T(8,128)(2,1)}, u32[]{:S(2)}, u32[]{:S(2)}) %collective-permute-start.13) | collective-permute-done | bytes 1441824 | tf_op jit(solution)/shard_map/ppermute | solution.py:373
  279.6 25.6 %attend.4 = (f32[512,512]{1,0:T(8,128)S(1)}, f32[8,512]{1,0:T(8,128)S(1)}) custom-call(f32[16,512]{1,0:T(8,128)S(1)} %compare_select_fusion.bias_ref, bf16[512,2048]{1,0:T(8,128)(2,1)S(1)} %copy-done.2, bf16[4096,256]{1,0:T(8,128)(2,1)S(1)} %bitcast.166, bf16[256,4096]{1,0:T(8,128)(2,1)S(1)} %copy-done.5), custom_call_target="tpu_custom_call" | custom-call | flops 1048576 | bytes 65536 | tf_op jit(solution)/shard_map/attend/pallas_call | solution.py:113
  306.3 25.7 %attend.5 = (f32[512,512]{1,0:T(8,128)S(1)}, f32[8,512]{1,0:T(8,128)S(1)}) custom-call(f32[16,512]{1,0:T(8,128)S(1)} %compare_select_fusion.bias_ref, bf16[512,2048]{1,0:T(8,128)(2,1)S(1)} %copy-done.2, bf16[4096,256]{1,0:T(8,128)(2,1)S(1)} %bitcast.167, bf16[256,4096]{1,0:T(8,128)(2,1)S(1)} %copy-done.5), custom_call_target="tpu_custom_call" | custom-call | flops 1048576 | bytes 65536 | tf_op jit(solution)/shard_map/attend/pallas_call | solution.py:113
  333.0 25.6 %attend.6 = (f32[512,512]{1,0:T(8,128)S(1)}, f32[8,512]{1,0:T(8,128)S(1)}) custom-call(f32[16,512]{1,0:T(8,128)S(1)} %compare_select_fusion.bias_ref, bf16[512,2048]{1,0:T(8,128)(2,1)S(1)} %copy-done.2, bf16[4096,256]{1,0:T(8,128)(2,1)S(1)} %bitcast.168, bf16[256,4096]{1,0:T(8,128)(2,1)S(1)} %copy-done.5), custom_call_target="tpu_custom_call" | custom-call | flops 1048576 | bytes 65536 | tf_op jit(solution)/shard_map/attend/pallas_call | solution.py:113
  376.9 26.0 %attend.7 = (f32[512,512]{1,0:T(8,128)S(1)}, f32[8,512]{1,0:T(8,128)S(1)}) custom-call(f32[16,512]{1,0:T(8,128)S(1)} %compare_select_fusion.bias_ref, bf16[512,2048]{1,0:T(8,128)(2,1)S(1)} %copy-done.3, bf16[4096,256]{1,0:T(8,128)(2,1)S(1)} %bitcast.169, bf16[256,4096]{1,0:T(8,128)(2,1)S(1)} %copy-done.6), custom_call_target="tpu_custom_call" | custom-call | flops 1048576 | bytes 65536 | tf_op jit(solution)/shard_map/attend/pallas_call | solution.py:113
  402.9 36.6 %collective-permute-done.23 = bf16[2,2,64,5632]{3,2,1,0:T(8,128)(2,1)} collective-permute-done((bf16[2,2,64,5632]{3,2,1,0:T(8,128)(2,1)}, bf16[2,2,64,5632]{3,2,1,0:T(8,128)(2,1)}, u32[]{:S(2)}, u32[]{:S(2)}) %collective-permute-start.23) | collective-permute-done | bytes 2883616 | tf_op jit(solution)/shard_map/ppermute | solution.py:362
  439.5 15.0 %placed.6 = bf16[32,176,2048]{2,1,0:T(8,128)(2,1)} custom-call(s32[32]{0:T(128)S(1)} %get-tuple-element.420.order_ref, bf16[16,176,2048]{2,1,0:T(8,128)(2,1)S(1)} %pad_maximum_fusion.refs_0_, bf16[16,176,2048]{2,1,0:T(8,128)(2,1)} %collective-permute-done.20.refs_1_), custom_call_target="tpu_custom_call" | custom-call | bytes 46137344 | tf_op jit(solution)/shard_map/placed/pallas_call | solution.py:550
  457.7 19.7 %fusion.123 = f32[512,5632]{1,0:T(8,128)} fusion(bf16[512,2048]{1,0:T(8,128)(2,1)} %bitcast.211, bf16[5632,2048]{1,0:T(8,128)(2,1)} %bitcast.201), kind=kOutput, calls=%fused_computation.298 | convolution fusion | flops 11811160064 | bytes 36700160 | tf_op jit(solution)/shard_map/dot_general | solution.py:26
  515.4 36.2 %collective-permute-done.28 = bf16[2,2,64,5632]{3,2,1,0:T(8,128)(2,1)} collective-permute-done((bf16[2,2,64,5632]{3,2,1,0:T(8,128)(2,1)}, bf16[2,2,64,5632]{3,2,1,0:T(8,128)(2,1)}, u32[]{:S(2)}, u32[]{:S(2)}) %collective-permute-start.28) | collective-permute-done | bytes 2883616 | tf_op jit(solution)/shard_map/ppermute | solution.py:362
  574.3 17.1 %collective-permute-done.31 = bf16[2,2,2,64,5632]{4,3,2,1,0:T(8,128)(2,1)S(1)} collective-permute-done((bf16[2,2,2,64,5632]{4,3,2,1,0:T(8,128)(2,1)}, bf16[2,2,2,64,5632]{4,3,2,1,0:T(8,128)(2,1)S(1)}, u32[]{:S(2)}, u32[]{:S(2)}) %collective-permute-start.31) | collective-permute-done | bytes 5767200 | tf_op jit(solution)/shard_map/ppermute | solution.py:373
  596.4 15.5 %placed.8 = bf16[32,64,5632]{2,1,0:T(8,128)(2,1)} custom-call(s32[32]{0:T(128)S(1)} %get-tuple-element.419.order_ref, bf16[4,64,5632]{2,1,0:T(8,128)(2,1)} %bitcast.73.refs_0_, bf16[4,64,5632]{2,1,0:T(8,128)(2,1)} %bitcast.74.refs_1_, bf16[4,64,5632]{2,1,0:T(8,128)(2,1)} %bitcast.75.refs_2_, bf16[4,64,5632]{2,1,0:T(8,128)(2,1)} %bitcast.76.refs_3_, ...), custom_call_target="tpu_custom_call" | custom-call | bytes 46137344 | tf_op jit(solution)/shard_map/placed/pallas_call | solution.py:550
  611.9 19.6 %fusion.124 = f32[512,5632]{1,0:T(8,128)} fusion(bf16[512,2048]{1,0:T(8,128)(2,1)} %copy-done.12, bf16[2048,5632]{1,0:T(8,128)(2,1)} %bitcast.203), kind=kOutput, calls=%fused_computation.299 | convolution fusion | flops 11811160064 | bytes 36700160 | tf_op jit(solution)/shard_map/dot_general | solution.py:26
  646.6 19.8 %fusion.125 = f32[512,5632]{1,0:T(8,128)} fusion(bf16[512,2048]{1,0:T(8,128)(2,1)} %copy-done.12, bf16[2048,5632]{1,0:T(8,128)(2,1)} %bitcast.205), kind=kOutput, calls=%fused_computation.300 | convolution fusion | flops 11811160064 | bytes 36700160 | tf_op jit(solution)/shard_map/dot_general | solution.py:26
  710.6 19.6 %fusion.126 = f32[512,2048]{1,0:T(8,128)} fusion(bf16[512,5632]{1,0:T(8,128)(2,1)} %copy-done.60, bf16[2048,5632]{1,0:T(8,128)(2,1)} %bitcast.206), kind=kOutput, calls=%fused_computation.301 | convolution fusion | flops 11811160064 | bytes 33030144 | tf_op jit(solution)/shard_map/dot_general | solution.py:26
  730.3 20.1 %multiply_reduce_fusion = (bf16[2048]{0:T(1024)(128)(2,1)S(1)}, f32[512]{0:T(512)S(1)}, f32[512,2048]{1,0:T(8,128)}) fusion(f32[512,2048]{1,0:T(8,128)} %copy-done.64, f32[512]{0:T(512)S(1)} %copy-done.133, f32[512,2048]{1,0:T(8,128)} %fusion.126, f32[2048]{0:T(1024)S(1)} %bitcast.236, bf16[512,5632]{1,0:T(8,128)(2,1)} %copy-done.59, ...), kind=kOutput, calls=%fused_computation.53 | convolution fusion | flops 11818498048 | bytes 41435136 | tf_op jit(solution)/shard_map/dot_general | solution.py:26
  814.8 51.3 %attend_back.4 = (f32[512,512]{1,0:T(8,128)S(1)}, bf16[4096,128]{1,0:T(8,128)(2,1)S(1)}) custom-call(s32[8]{0:T(128)S(1)} %copy-done.57, f32[16,512]{1,0:T(8,128)S(1)} %compare_select_fusion.bias_ref, f32[8,512]{1,0:T(8,128)S(1)} %get-tuple-element.228.lse_ref, f32[512,512]{1,0:T(8,128)S(1)} %copy-done.30, bf16[512,2048]{1,0:T(8,128)(2,1)S(1)} %copy-done.4, ...), custom_call_target="tpu_custom_call" | custom-call | flops 1048576 | bytes 65536 | tf_op jit(solution)/shard_map/attend_back/pallas_call | solution.py:233
  891.9 51.0 %attend_back.5 = (f32[512,512]{1,0:T(8,128)S(1)}, bf16[4096,128]{1,0:T(8,128)(2,1)S(1)}) custom-call(s32[8]{0:T(128)S(1)} %copy-done.57, f32[16,512]{1,0:T(8,128)S(1)} %compare_select_fusion.bias_ref, f32[8,512]{1,0:T(8,128)S(1)} %get-tuple-element.249.lse_ref, f32[512,512]{1,0:T(8,128)S(1)} %copy-done.27, bf16[512,2048]{1,0:T(8,128)(2,1)S(1)} %copy-done.4, ...), custom_call_target="tpu_custom_call" | custom-call | flops 1048576 | bytes 65536 | tf_op jit(solution)/shard_map/attend_back/pallas_call | solution.py:233
  969.9 50.8 %attend_back.6 = (f32[512,512]{1,0:T(8,128)S(1)}, bf16[4096,128]{1,0:T(8,128)(2,1)S(1)}) custom-call(s32[8]{0:T(128)S(1)} %copy-done.57, f32[16,512]{1,0:T(8,128)S(1)} %compare_select_fusion.bias_ref, f32[8,512]{1,0:T(8,128)S(1)} %get-tuple-element.255.lse_ref, f32[512,512]{1,0:T(8,128)S(1)} %copy-done.24, bf16[512,2048]{1,0:T(8,128)(2,1)S(1)} %copy-done.4, ...), custom_call_target="tpu_custom_call" | custom-call | flops 1048576 | bytes 65536 | tf_op jit(solution)/shard_map/attend_back/pallas_call | solution.py:233
  1053.4 51.3 %attend_back.7 = (f32[512,512]{1,0:T(8,128)S(1)}, bf16[4096,128]{1,0:T(8,128)(2,1)S(1)}) custom-call(s32[8]{0:T(128)S(1)} %copy-done.57, f32[16,512]{1,0:T(8,128)S(1)} %compare_select_fusion.bias_ref, f32[8,512]{1,0:T(8,128)S(1)} %get-tuple-element.264.lse_ref, f32[512,512]{1,0:T(8,128)S(1)} %get-tuple-element.222.o_ref, bf16[512,2048]{1,0:T(8,128)(2,1)S(1)} %copy-done.4, ...), custom_call_target="tpu_custom_call" | custom-call | flops 1048576 | bytes 65536 | tf_op jit(solution)/shard_map/attend_back/pallas_call | solution.py:233
  1171.0 17.7 %collective-permute-done.58 = bf16[512,128]{1,0:T(8,128)(2,1)S(1)} collective-permute-done((bf16[512,128]{1,0:T(8,128)(2,1)S(1)}, bf16[512,128]{1,0:T(8,128)(2,1)S(1)}, u32[]{:S(2)}, u32[]{:S(2)}) %collective-permute-start.58) | collective-permute-done | bytes 131104 | tf_op jit(solution)/shard_map/ppermute | solution.py:373
  1214.0 19.9 %fusion.16 = bf16[1,512,2048]{2,1,0:T(8,128)(2,1)} fusion(f32[512,2048]{1,0:T(8,128)} %copy-done.64, bf16[512,5632]{1,0:T(8,128)(2,1)} %copy-done.7, bf16[5632,2048]{1,0:T(8,128)(2,1)} %bitcast.202), kind=kOutput, calls=%fused_computation.75 | convolution fusion | flops 11813257216 | bytes 35127296 | tf_op jit(solution)/shard_map/dot_general | solution.py:26
  (678 shorter events, 614.4 us)
Async XLA Ops:
  10.6 149.3 %all-gather.11.cloned.1.call-start = ((), (), s32[]{:S(2)}) async-start(), calls=%async_computation.9 | async-start | bytes 3604480 | tf_op jit(solution)/shard_map/all_gather | solution.py:579
  100.6 128.1 %all-gather.13.cloned.1.call-start = ((), (), s32[]{:S(2)}) async-start(), calls=%async_computation.10 | async-start | bytes 3604480 | tf_op jit(solution)/shard_map/all_gather | solution.py:579
  101.3 258.2 %all-gather.15.cloned.1.call-start = ((), (), s32[]{:S(2)}) async-start(), calls=%async_computation.11 | async-start | bytes 1310720 | tf_op jit(solution)/shard_map/all_gather | solution.py:579
  228.6 880.9 %reduce-scatter.5.cloned.1.call-start = ((), (), s32[]{:S(2)}) async-start(), calls=%async_computation.4 | async-start | bytes 3604480 | tf_op jit(solution)/shard_map/reduce_scatter | solution.py:501
  258.9 74.1 %collective-permute-start.15 = (bf16[2,2,64,5632]{3,2,1,0:T(8,128)(2,1)}, bf16[2,2,64,5632]{3,2,1,0:T(8,128)(2,1)}, u32[]{:S(2)}, u32[]{:S(2)}) collective-permute-start(bf16[2,2,64,5632]{3,2,1,0:T(8,128)(2,1)} %get-tuple-element.375), channel_id=1, source_target_pairs={{0,8},{8,24},{24,16},{16,0},{1,9},{9,25},{25,17},{17,1},{2,10},{10... | collective-permute-start | bytes 8650760 | tf_op jit(solution)/shard_map/ppermute | solution.py:362
  262.6 98.8 %collective-permute-start.16 = (bf16[2,2,176,2048]{3,2,1,0:T(8,128)(2,1)}, bf16[2,2,176,2048]{3,2,1,0:T(8,128)(2,1)}, u32[]{:S(2)}, u32[]{:S(2)}) collective-permute-start(bf16[2,2,176,2048]{3,2,1,0:T(8,128)(2,1)} %pad_maximum_fusion.7), channel_id=1, source_target_pairs={{0,2},{1,3},{2,0},{3,1},{4,6},{5,7},{6,4},{7,5},{8,10},{9,11},{10,... | collective-permute-start | bytes 8650760 | tf_op jit(solution)/shard_map/ppermute | solution.py:373
  267.5 93.9 %collective-permute-start.17 = (bf16[2,2,176,2048]{3,2,1,0:T(8,128)(2,1)}, bf16[2,2,176,2048]{3,2,1,0:T(8,128)(2,1)}, u32[]{:S(2)}, u32[]{:S(2)}) collective-permute-start(bf16[2,2,176,2048]{3,2,1,0:T(8,128)(2,1)} %pad_maximum_fusion.8), channel_id=1, source_target_pairs={{0,4},{1,5},{2,6},{3,7},{4,0},{5,1},{6,2},{7,3},{8,12},{9,13},{10,... | collective-permute-start | bytes 8650760 | tf_op jit(solution)/shard_map/ppermute | solution.py:373
  270.8 90.7 %collective-permute-start.18 = (bf16[2,64,5632]{2,1,0:T(8,128)(2,1)}, bf16[2,64,5632]{2,1,0:T(8,128)(2,1)}, u32[]{:S(2)}, u32[]{:S(2)}) collective-permute-start(bf16[2,64,5632]{2,1,0:T(8,128)(2,1)} %get-tuple-element.373), channel_id=1, source_target_pairs={{0,4},{1,5},{2,6},{3,7},{4,0},{5,1},{6,2},{7,3},{8,12},{9,13},{10,... | collective-permute-start | bytes 4325384 | tf_op jit(solution)/shard_map/ppermute | solution.py:373
  272.2 89.2 %collective-permute-start.19 = (bf16[2,64,5632]{2,1,0:T(8,128)(2,1)}, bf16[2,64,5632]{2,1,0:T(8,128)(2,1)}, u32[]{:S(2)}, u32[]{:S(2)}) collective-permute-start(bf16[2,64,5632]{2,1,0:T(8,128)(2,1)} %get-tuple-element.372), channel_id=1, source_target_pairs={{0,2},{1,3},{2,0},{3,1},{4,6},{5,7},{6,4},{7,5},{8,10},{9,11},{10,... | collective-permute-start | bytes 4325384 | tf_op jit(solution)/shard_map/ppermute | solution.py:373
  368.3 71.2 %collective-permute-start.20 = (bf16[16,176,2048]{2,1,0:T(8,128)(2,1)S(1)}, bf16[16,176,2048]{2,1,0:T(8,128)(2,1)}, u32[]{:S(2)}, u32[]{:S(2)}) collective-permute-start(bf16[16,176,2048]{2,1,0:T(8,128)(2,1)S(1)} %pad_maximum_fusion.refs_0_), channel_id=1, source_target_pairs={{0,1},{1,0},{2,3},{3,2},{4,5},{5,4},{6,7},{7,6},{8,9},{9,8},{10,11... | collective-permute-start | bytes 34603016 | tf_op jit(solution)/shard_map/ppermute | solution.py:373
  373.4 66.1 %collective-permute-start.24 = (bf16[2,2,2,64,5632]{4,3,2,1,0:T(8,128)(2,1)}, bf16[2,2,2,64,5632]{4,3,2,1,0:T(8,128)(2,1)}, u32[]{:S(2)}, u32[]{:S(2)}) collective-permute-start(bf16[2,2,2,64,5632]{4,3,2,1,0:T(8,128)(2,1)} %pad_maximum_fusion.2), channel_id=1, source_target_pairs={{0,1},{1,0},{2,3},{3,2},{4,5},{5,4},{6,7},{7,6},{8,9},{9,8},{10,11... | collective-permute-start | bytes 17301512 | tf_op jit(solution)/shard_map/ppermute | solution.py:373
  485.4 66.1 %collective-permute-start.28 = (bf16[2,2,64,5632]{3,2,1,0:T(8,128)(2,1)}, bf16[2,2,64,5632]{3,2,1,0:T(8,128)(2,1)}, u32[]{:S(2)}, u32[]{:S(2)}) collective-permute-start(bf16[2,2,64,5632]{3,2,1,0:T(8,128)(2,1)} %collective-permute-done.23), channel_id=1, source_target_pairs={{0,8},{8,24},{24,16},{16,0},{1,9},{9,25},{25,17},{17,1},{2,10},{10... | collective-permute-start | bytes 8650760 | tf_op jit(solution)/shard_map/ppermute | solution.py:362
  565.1 66.4 %collective-permute-start.32 = (bf16[16,64,5632]{2,1,0:T(8,128)(2,1)S(1)}, bf16[16,64,5632]{2,1,0:T(8,128)(2,1)}, u32[]{:S(2)}, u32[]{:S(2)}) collective-permute-start(bf16[16,64,5632]{2,1,0:T(8,128)(2,1)S(1)} %pad_maximum_fusion.1.refs_0_), channel_id=1, source_target_pairs={{0,1},{1,0},{2,3},{3,2},{4,5},{5,4},{6,7},{7,6},{8,9},{9,8},{10,11... | collective-permute-start | bytes 34603016 | tf_op jit(solution)/shard_map/ppermute | solution.py:373
  701.2 75.0 %collective-permute-start.34 = (bf16[2816,2048]{1,0:T(8,128)(2,1)}, bf16[2816,2048]{1,0:T(8,128)(2,1)}, u32[]{:S(2)}, u32[]{:S(2)}) collective-permute-start(bf16[2816,2048]{1,0:T(8,128)(2,1)} %convolution_convert_fusion.1), channel_id=1, source_target_pairs={{0,1},{1,0},{2,3},{3,2},{4,5},{5,4},{6,7},{7,6},{8,9},{9,8},{10,11... | collective-permute-start | bytes 34603016 | tf_op jit(solution)/shard_map/ppermute | solution.py:373
  776.2 89.9 %collective-permute-start.36 = (bf16[256,5632]{1,0:T(8,128)(2,1)}, bf16[256,5632]{1,0:T(8,128)(2,1)}, u32[]{:S(2)}, u32[]{:S(2)}) collective-permute-start(bf16[256,5632]{1,0:T(8,128)(2,1)} %add_convert_fusion.18), channel_id=1, source_target_pairs={{0,2},{1,3},{2,0},{3,1},{4,6},{5,7},{6,4},{7,5},{8,10},{9,11},{10,... | collective-permute-start | bytes 8650760 | tf_op jit(solution)/shard_map/ppermute | solution.py:373
  776.6 89.5 %collective-permute-start.37 = (bf16[256,5632]{1,0:T(8,128)(2,1)}, bf16[256,5632]{1,0:T(8,128)(2,1)}, u32[]{:S(2)}, u32[]{:S(2)}) collective-permute-start(bf16[256,5632]{1,0:T(8,128)(2,1)} %add_convert_fusion.17), channel_id=1, source_target_pairs={{0,4},{1,5},{2,6},{3,7},{4,0},{5,1},{6,2},{7,3},{8,12},{9,13},{10,... | collective-permute-start | bytes 8650760 | tf_op jit(solution)/shard_map/ppermute | solution.py:373
  782.6 83.5 %collective-permute-start.38 = (bf16[704,2048]{1,0:T(8,128)(2,1)}, bf16[704,2048]{1,0:T(8,128)(2,1)}, u32[]{:S(2)}, u32[]{:S(2)}) collective-permute-start(bf16[704,2048]{1,0:T(8,128)(2,1)} %add_convert_fusion.16), channel_id=1, source_target_pairs={{0,8},{8,24},{24,16},{16,0},{1,9},{9,25},{25,17},{17,1},{2,10},{10... | collective-permute-start | bytes 8650760 | tf_op jit(solution)/shard_map/ppermute | solution.py:362
  806.9 136.1 %collective-permute-start.39 = (bf16[256,5632]{1,0:T(8,128)(2,1)}, bf16[256,5632]{1,0:T(8,128)(2,1)}, u32[]{:S(2)}, u32[]{:S(2)}) collective-permute-start(bf16[256,5632]{1,0:T(8,128)(2,1)} %add_convert_fusion.15), channel_id=1, source_target_pairs={{0,2},{1,3},{2,0},{3,1},{4,6},{5,7},{6,4},{7,5},{8,10},{9,11},{10,... | collective-permute-start | bytes 8650760 | tf_op jit(solution)/shard_map/ppermute | solution.py:373
  813.3 129.7 %collective-permute-start.40 = (bf16[256,5632]{1,0:T(8,128)(2,1)}, bf16[256,5632]{1,0:T(8,128)(2,1)}, u32[]{:S(2)}, u32[]{:S(2)}) collective-permute-start(bf16[256,5632]{1,0:T(8,128)(2,1)} %add_convert_fusion.14), channel_id=1, source_target_pairs={{0,4},{1,5},{2,6},{3,7},{4,0},{5,1},{6,2},{7,3},{8,12},{9,13},{10,... | collective-permute-start | bytes 8650760 | tf_op jit(solution)/shard_map/ppermute | solution.py:373
  873.9 69.1 %collective-permute-start.41 = (bf16[704,2048]{1,0:T(8,128)(2,1)}, bf16[704,2048]{1,0:T(8,128)(2,1)}, u32[]{:S(2)}, u32[]{:S(2)}) collective-permute-start(bf16[704,2048]{1,0:T(8,128)(2,1)} %add_convert_fusion.12), channel_id=1, source_target_pairs={{0,8},{8,24},{24,16},{16,0},{1,9},{9,25},{25,17},{17,1},{2,10},{10... | collective-permute-start | bytes 8650760 | tf_op jit(solution)/shard_map/ppermute | solution.py:362
  947.4 77.2 %collective-permute-start.46 = (bf16[1024,2048]{1,0:T(8,128)(2,1)}, bf16[1024,2048]{1,0:T(8,128)(2,1)}, u32[]{:S(2)}, u32[]{:S(2)}) collective-permute-start(bf16[1024,2048]{1,0:T(8,128)(2,1)} %convolution_convert_fusion.4), channel_id=1, source_target_pairs={{0,1},{1,0},{2,3},{3,2},{4,5},{5,4},{6,7},{7,6},{8,9},{9,8},{10,11... | collective-permute-start | bytes 12582920 | tf_op jit(solution)/shard_map/ppermute | solution.py:373
  1028.6 185.3 %reduce-scatter.7.cloned.1.call-start = ((), (), s32[]{:S(2)}) async-start(), calls=%async_computation.5 | async-start | bytes 3604480 | tf_op jit(solution)/shard_map/reduce_scatter | solution.py:501
  1038.8 70.7 %collective-permute-start.48 = (bf16[2048,384]{1,0:T(8,128)(2,1)S(1)}, bf16[2048,384]{1,0:T(8,128)(2,1)}, u32[]{:S(2)}, u32[]{:S(2)}) collective-permute-start(bf16[2048,384]{1,0:T(8,128)(2,1)S(1)} %slice.505), channel_id=1, source_target_pairs={{0,1},{1,0},{2,3},{3,2},{4,5},{5,4},{6,7},{7,6},{8,9},{9,8},{10,11... | collective-permute-start | bytes 4718600 | tf_op jit(solution)/shard_map/ppermute | solution.py:373
  1124.3 175.1 %reduce-scatter.11.cloned.1.call-start = ((), (), s32[]{:S(2)}) async-start(), calls=%async_computation.7 | async-start | bytes 1310720 | tf_op jit(solution)/shard_map/reduce_scatter | solution.py:501
  (217 other events, 4282.4 us)
Sparse Core Ops, SparseCore 0:
  10.7 36.5 all-gather.8
  100.7 59.1 all-gather.10
  161.5 57.8 all-gather.12
  228.7 25.6 all-gather.14
  1028.7 54.5 reduce-scatter.4
  1124.4 54.8 reduce-scatter.6
  1250.4 27.5 reduce-scatter.10
  1280.4 26.9 reduce-scatter.8

commit v8 on v7

--- a/solution.py
+++ b/solution.py
@@ -605,10 +605,10 @@
     waiting = [part]
     for k in range(grid.n_dp - 1):
         sent = [grid.next(near[-1], "d")]
-        early = k == grid.n_dp // 2 - 1
+        early = k == grid.n_dp - 2
         if early:
-            sent.append(grid.next(jnp.stack(waiting), "c"))
-            waiting = []
+            sent.append(grid.next(jnp.stack(waiting[:-1]), "c"))
+            waiting = waiting[-1:]
         came = yield sent
         if early:
             far.append(came[1])
@@ -749,19 +749,19 @@
     gains = jnp.stack([attn_gain, ffn_gain], -1)
     gains = jnp.concatenate([gains, jnp.zeros((gains.shape[0], WIDE - 2), BF16)], 1)
     packed = jnp.concatenate([query_proj, key_proj, value_proj, gains], 1)
-    packed, down_proj, gate_proj, merge_proj = lax.optimization_barrier(
-        (packed, down_proj, gate_proj, merge_proj)
-    )
-    first_chain = Chain(gather_weight(grid, packed))
     down_chain = Chain(gather_weight(grid, down_proj))
     gate_chain = Chain(gather_weight(grid, gate_proj))
     merge_chain = Chain(gather_weight(grid, merge_proj))
+    first_chain = Chain(gather_weight(grid, packed, True))
     up_chain = Chain(gather_ring(grid, up_proj))
     all_pos = lax.all_gather(positions[::run], "ctx", axis=0, tiled=True)
     cosine, sine = angles(positions)
     rows_in = layer_in.reshape(rows, model).astype(F32)
     normed_one, factor_one = normalize(rows_in)
-    all_pos, factor_one, cosine = meet((all_pos, factor_one, cosine), first_chain, up_chain)
+    all_pos, factor_one = meet((all_pos, factor_one), first_chain, up_chain)
+    factor_one = meet(factor_one, first_chain)
+    cosine, sine = meet((cosine, sine), first_chain, up_chain)
+    cosine = meet(cosine, first_chain, down_chain)
     first_weights = finish(first_chain)
     attn_all = first_weights[:, : width + 2 * kv_width]
     gain_one = first_weights[:, width + 2 * kv_width].astype(F32)
@@ -777,27 +777,28 @@
     bias = jnp.where(later, MASKED, 0.0).astype(F32)
     bias = meet(bias, kv_chain)
     bias = meet(bias, kv_chain)
-    bias = meet(bias, kv_chain, down_chain, up_chain, gate_chain)
+    bias = meet(bias, kv_chain, gate_chain, up_chain)
     all_keys, all_values = finish(kv_chain)
     kt, vt = all_keys.T, all_values.T
 
     grad_rows = out_grad.reshape(rows, model)
     plan = (
         ((), ()),
-        ((up_chain,), ()),
-        ((down_chain, merge_chain), (gate_chain,)),
-        ((down_chain, merge_chain, gate_chain, up_chain), ()),
+        ((down_chain, merge_chain, up_chain), (gate_chain,)),
+        ((down_chain, merge_chain, gate_chain), ()),
+        ((merge_chain, gate_chain, up_chain), ()),
     )
     outs, log_sums = [], []
     for group in range(kv_heads):
         out, log_sum = attend(group, places, bias, queries, all_keys, vt)
         on, hold = plan[group % 4]
         queries, out, grad_rows = meet((queries, out, grad_rows), *on, hold=hold)
+        if group == 2:
+            down_all = finish(down_chain)
+            grad_hidden = mm(grad_rows, down_all, NT)
+            queries, grad_hidden = lax.optimization_barrier((queries, grad_hidden))
         outs.append(out)
         log_sums.append(log_sum)
-    down_all = finish(down_chain)
-    grad_hidden = mm(grad_rows, down_all, NT)
-    outs, grad_hidden = meet((outs, grad_hidden), merge_chain)
     mixed = jnp.concatenate([out.astype(BF16) for out in outs], 1)
     mixed = meet(mixed, merge_chain)
     merge_all = finish(merge_chain)
@@ -805,7 +806,6 @@
     normed_two, factor_two = normalize(middle)
     second_in = (normed_two * gain_two).astype(BF16)
     second_in = meet(second_in, up_chain)
-    second_in = meet(second_in, gate_chain)
     up_all = finish(up_chain)
     lift = mm(second_in, up_all, NN)
     lift = meet(lift, gate_chain)
@@ -850,13 +850,13 @@
         elif group == kv_heads - 2:
             grad_mixed, dkvs = meet((grad_mixed, dkvs), gate_sum, up_sum, merge_sum, down_sum)
             keys_sum = Chain(reduce_keys(grid, jnp.concatenate(dkvs, 1)))
-    dqs, dkv = meet((dqs, dkv), keys_sum, gate_sum, down_sum, hold=(merge_sum,))
+    dqs, dkv = meet((dqs, dkv), keys_sum, gate_sum, merge_sum, hold=(down_sum,))
     last_keys = Chain(reduce_keys(grid, dkv))
     query_grads = unrotated(unrotate_queries_kernel, dqs, cosine, sine)
     query_sum = Chain(reduce_term(grid, first_turned, query_grads))
     grad_first = mm(query_grads, attn_all[:, :width], NT)
-    grad_first = meet(grad_first, last_keys, keys_sum, query_sum, down_sum)
-    grad_first = meet(grad_first, last_keys, keys_sum, merge_sum)
+    grad_first = meet(grad_first, last_keys, keys_sum, query_sum, merge_sum)
+    grad_first = meet(grad_first, last_keys, keys_sum, down_sum)
     grad_first = meet(grad_first, last_keys)
     wide = finish(keys_sum)
     dkv_parts = [wide[:, at : at + WIDE] for at in range(0, wide.shape[1], WIDE)]
@@ -869,11 +869,14 @@
     gain_columns = turned(gain_terms.astype(BF16), sum_order)
     last_turned = turned(first_in, sum_order)
     last = Chain(reduce_term(grid, last_turned, kv_grads, gain_columns, around=True))
-    grad_norm_one, hidden = meet((grad_norm_one, hidden), last, query_sum, merge_sum, up_sum)
+    input_grad = (grad_middle + grad_norm_one).astype(BF16).reshape(layer_in.shape)
+    last.flight, input_grad = lax.optimization_barrier((last.flight, input_grad))
+    input_grad = meet(input_grad, last, query_sum, up_sum, down_sum)
+    input_grad, hidden = meet((input_grad, hidden), last, query_sum)
     result = middle + mm(hidden, down_all, NN)
     layer_out = result.astype(BF16).reshape(layer_in.shape)
-    input_grad = (grad_middle + grad_norm_one).astype(BF16).reshape(layer_in.shape)
-    layer_out, input_grad = meet((layer_out, input_grad), last, query_sum)
+    input_grad = meet(input_grad, last)
+    input_grad, layer_out = meet((input_grad, layer_out), last, merge_sum)
     while not last.done:
         input_grad = meet(input_grad, last)
     query_share, last_share = finish(query_sum), finish(last)

time: 1320 us -> 1250 us (0.947)
  waiting for transfers between devices: 331 us -> 253 us
  starting transfers between devices: 61.6 us -> 74.9 us
    ppermute x64, waiting for transfers between devices: 180 us -> 131 us  [next(): return lax.ppermute(values, 'ctx', pairs)]
    all_gather x4 -> x3, waiting for transfers between devices: 45 us -> 10.5 us  [gather_weight(): column, = (yield [lax.all_gather(weight, 'dp', axis=0)])]
    convert_element_type x1 -> x0, other arithmetic: 13.3 us -> none  [body(): grad_lift = (grad_hidden * activated).astype(BF16)]
    ppermute x9 -> x12, waiting for transfers between devices: 99.1 us -> 111 us  [next(): return lax.ppermute(values, 'dp', list(zip(self.ring, around)))]
    unnamed x331 -> x329, local copies, waits for them, and re-layouts: 41.3 us -> 40.3 us
  transfers between devices with their start and end apart: 81 -> 83, of which waited for: 30 -> 26; matrix products, arithmetic and copies ran while one was open for 28% -> 32% of each run, Pallas kernels for 27% -> 30%
where the time goes in v8:
time: 1250 us
  Pallas kernels  392 us (31%)
  matrix products  291 us (23%)
  waiting for transfers between devices  253 us (20%)
  other arithmetic  135 us (11%)
  local copies, waits for them, and re-layouts  75.6 us (6%)
  starting transfers between devices  74.9 us (6%)
  between operations  17.4 us (1%)
    dot_general x41, matrix products, mm(): return lax.dot_general(left, right, dims, preferred_element_type=F32)  291 us
    pallas_call x4, Pallas kernels, attend_back(): pl.pallas_call(functools.partial(attend_back_kernel, which=group % 2, unr...  204 us
    ppermute x64, waiting for transfers between devices, next(): return lax.ppermute(values, 'ctx', pairs)  131 us
    ppermute x12, waiting for transfers between devices, next(): return lax.ppermute(values, 'dp', list(zip(self.ring, around)))  111 us
    pallas_call x4, Pallas kernels, attend(): pl.pallas_call(functools.partial(attend_kernel, which=group % 2, places=p...  103 us
    pallas_call x5, Pallas kernels, placed(): pl.pallas_call(functools.partial(place_kernel, sources=sources, slots=slo...  69.4 us
    ppermute x64, starting transfers between devices, next(): return lax.ppermute(values, 'ctx', pairs)  54.2 us
    unnamed x329, local copies, waits for them, and re-layouts  40.3 us
  transfers between devices with their start and end apart: 83, of which 26 were waited for; matrix products, arithmetic and copies ran while one was open for 32% of the time, Pallas kernels for 30%

profile of v8, /device:TPU:0, one launch (start us, length us, event | category | flops | bytes accessed | tf_op | source)
XLA Modules:
  0.0 1245.9 jit_solution(10599933241059904001)
XLA Ops:
  39.6 19.4 %collective-permute-done.2 = bf16[64,2688]{1,0:T(8,128)(2,1)S(1)} collective-permute-done((bf16[64,2688]{1,0:T(8,128)(2,1)}, bf16[64,2688]{1,0:T(8,128)(2,1)S(1)}, u32[]{:S(2)}, u32[]{:S(2)}) %collective-permute-start.2) | collective-permute-done | bytes 344096 | tf_op jit(solution)/shard_map/ppermute | solution.py:362
  65.5 19.5 %collective-permute-done.3 = bf16[64,2688]{1,0:T(8,128)(2,1)S(1)} collective-permute-done((bf16[64,2688]{1,0:T(8,128)(2,1)S(1)}, bf16[64,2688]{1,0:T(8,128)(2,1)S(1)}, u32[]{:S(2)}, u32[]{:S(2)}) %collective-permute-start.3) | collective-permute-done | bytes 344096 | tf_op jit(solution)/shard_map/ppermute | solution.py:362
  103.5 21.0 %collective-permute-done.8 = bf16[2,2,64,2688]{3,2,1,0:T(8,128)(2,1)S(1)} collective-permute-done((bf16[2,2,64,2688]{3,2,1,0:T(8,128)(2,1)S(1)}, bf16[2,2,64,2688]{3,2,1,0:T(8,128)(2,1)S(1)}, u32[]{:S(2)}, u32[]{:S(2)}) %collective-permute-start.8) | collective-permute-done | bytes 1376288 | tf_op jit(solution)/shard_map/ppermute | solution.py:373
  232.9 19.4 %collective-permute-done.18 = bf16[2,2,64,5632]{3,2,1,0:T(8,128)(2,1)} collective-permute-done((bf16[2,2,64,5632]{3,2,1,0:T(8,128)(2,1)S(1)}, bf16[2,2,64,5632]{3,2,1,0:T(8,128)(2,1)}, u32[]{:S(2)}, u32[]{:S(2)}) %collective-permute-start.18) | collective-permute-done | bytes 2883616 | tf_op jit(solution)/shard_map/ppermute | solution.py:362
  266.1 25.6 %attend.4 = (f32[512,512]{1,0:T(8,128)S(1)}, f32[8,512]{1,0:T(8,128)S(1)}) custom-call(f32[16,512]{1,0:T(8,128)S(1)} %compare_select_fusion.bias_ref, bf16[512,2048]{1,0:T(8,128)(2,1)S(1)} %copy-done.2, bf16[4096,256]{1,0:T(8,128)(2,1)S(1)} %bitcast.169, bf16[256,4096]{1,0:T(8,128)(2,1)S(1)} %copy-done.6), custom_call_target="tpu_custom_call" | custom-call | flops 1048576 | bytes 65536 | tf_op jit(solution)/shard_map/attend/pallas_call | solution.py:113
  292.7 25.8 %attend.5 = (f32[512,512]{1,0:T(8,128)S(1)}, f32[8,512]{1,0:T(8,128)S(1)}) custom-call(f32[16,512]{1,0:T(8,128)S(1)} %compare_select_fusion.bias_ref, bf16[512,2048]{1,0:T(8,128)(2,1)S(1)} %copy-done.2, bf16[4096,256]{1,0:T(8,128)(2,1)S(1)} %bitcast.170, bf16[256,4096]{1,0:T(8,128)(2,1)S(1)} %copy-done.6), custom_call_target="tpu_custom_call" | custom-call | flops 1048576 | bytes 65536 | tf_op jit(solution)/shard_map/attend/pallas_call | solution.py:113
  319.6 15.6 %collective-permute-done.21 = bf16[2,2,64,5632]{3,2,1,0:T(8,128)(2,1)} collective-permute-done((bf16[2,2,64,5632]{3,2,1,0:T(8,128)(2,1)}, bf16[2,2,64,5632]{3,2,1,0:T(8,128)(2,1)}, u32[]{:S(2)}, u32[]{:S(2)}) %collective-permute-start.21) | collective-permute-done | bytes 2883616 | tf_op jit(solution)/shard_map/ppermute | solution.py:362
  349.2 26.1 %attend.6 = (f32[512,512]{1,0:T(8,128)S(1)}, f32[8,512]{1,0:T(8,128)S(1)}) custom-call(f32[16,512]{1,0:T(8,128)S(1)} %compare_select_fusion.bias_ref, bf16[512,2048]{1,0:T(8,128)(2,1)S(1)} %copy-done.3, bf16[4096,256]{1,0:T(8,128)(2,1)S(1)} %bitcast.171, bf16[256,4096]{1,0:T(8,128)(2,1)S(1)} %copy-done.7), custom_call_target="tpu_custom_call" | custom-call | flops 1048576 | bytes 65536 | tf_op jit(solution)/shard_map/attend/pallas_call | solution.py:113
  386.1 15.1 %placed.6 = bf16[32,176,2048]{2,1,0:T(8,128)(2,1)} custom-call(s32[32]{0:T(128)S(1)} %get-tuple-element.363.order_ref, bf16[16,176,2048]{2,1,0:T(8,128)(2,1)S(1)} %pad_maximum_fusion.refs_0_, bf16[16,176,2048]{2,1,0:T(8,128)(2,1)} %collective-permute-done.24.refs_1_), custom_call_target="tpu_custom_call" | custom-call | bytes 46137344 | tf_op jit(solution)/shard_map/placed/pallas_call | solution.py:550
  414.6 19.8 %fusion.127 = f32[512,5632]{1,0:T(8,128)} fusion(bf16[512,2048]{1,0:T(8,128)(2,1)} %bitcast.216, bf16[5632,2048]{1,0:T(8,128)(2,1)} %bitcast.200), kind=kOutput, calls=%fused_computation.301 | convolution fusion | flops 11811160064 | bytes 36700160 | tf_op jit(solution)/shard_map/dot_general | solution.py:26
  437.6 25.5 %attend.7 = (f32[512,512]{1,0:T(8,128)S(1)}, f32[8,512]{1,0:T(8,128)S(1)}) custom-call(f32[16,512]{1,0:T(8,128)S(1)} %compare_select_fusion.bias_ref, bf16[512,2048]{1,0:T(8,128)(2,1)S(1)} %copy-done.4, bf16[4096,256]{1,0:T(8,128)(2,1)S(1)} %bitcast.172, bf16[256,4096]{1,0:T(8,128)(2,1)S(1)} %copy-done.8), custom_call_target="tpu_custom_call" | custom-call | flops 1048576 | bytes 65536 | tf_op jit(solution)/shard_map/attend/pallas_call | solution.py:113
  523.7 17.4 %placed.8 = bf16[32,64,5632]{2,1,0:T(8,128)(2,1)} custom-call(s32[32]{0:T(128)S(1)} %get-tuple-element.361.order_ref, bf16[4,64,5632]{2,1,0:T(8,128)(2,1)S(1)} %bitcast.184, bf16[4,64,5632]{2,1,0:T(8,128)(2,1)} %bitcast.78.refs_1_, bf16[4,64,5632]{2,1,0:T(8,128)(2,1)} %bitcast.79.refs_2_, bf16[4,64,5632]{2,1,0:T(8,128)(2,1)} %bitcast.80.refs_3_, ...), custom_call_target="tpu_custom_call" | custom-call | bytes 46137344 | tf_op jit(solution)/shard_map/placed/pallas_call | solution.py:550
  541.1 19.2 %fusion.128 = f32[512,5632]{1,0:T(8,128)} fusion(bf16[512,2048]{1,0:T(8,128)(2,1)S(1)} %multiply_convert_fusion.3.x_ref, bf16[2048,5632]{1,0:T(8,128)(2,1)} %bitcast.202), kind=kOutput, calls=%fused_computation.302 | convolution fusion | flops 11811160064 | bytes 36700160 | tf_op jit(solution)/shard_map/dot_general | solution.py:26
  560.3 17.4 %placed.9 = bf16[32,64,5632]{2,1,0:T(8,128)(2,1)} custom-call(s32[32]{0:T(128)S(1)} %get-tuple-element.363.order_ref, bf16[16,64,5632]{2,1,0:T(8,128)(2,1)} %pad_maximum_fusion.1.refs_0_, bf16[16,64,5632]{2,1,0:T(8,128)(2,1)} %collective-permute-done.35.refs_1_), custom_call_target="tpu_custom_call" | custom-call | bytes 46137344 | tf_op jit(solution)/shard_map/placed/pallas_call | solution.py:550
  577.7 29.2 %multiply_convert_fusion = (bf16[512,5632]{1,0:T(8,128)(2,1)}, bf16[512,5632]{1,0:T(8,128)(2,1)}, bf16[512,5632]{1,0:T(8,128)(2,1)}) fusion(f32[512,5632]{1,0:T(8,128)} %fusion.127, f32[512,5632]{1,0:T(8,128)} %fusion.128, bf16[512,2048]{1,0:T(8,128)(2,1)} %copy-done.16, bf16[2048,5632]{1,0:T(8,128)(2,1)} %bitcast.204), kind=kOutput, calls=%fused_computation.3 | convolution fusion | flops 11854413824 | bytes 65536000 | tf_op jit(solution)/shard_map/dot_general | solution.py:26
  639.1 19.6 %fusion.129 = f32[512,2048]{1,0:T(8,128)} fusion(bf16[512,5632]{1,0:T(8,128)(2,1)} %get-tuple-element.243, bf16[2048,5632]{1,0:T(8,128)(2,1)} %bitcast.205), kind=kOutput, calls=%fused_computation.303 | convolution fusion | flops 11811160064 | bytes 33030144 | tf_op jit(solution)/shard_map/dot_general | solution.py:26
  658.7 19.8 %multiply_reduce_fusion.1 = (f32[512]{0:T(512)S(1)}, bf16[2048]{0:T(1024)(128)(2,1)S(1)}, f32[512,2048]{1,0:T(8,128)}) fusion(f32[512,2048]{1,0:T(8,128)} %copy-done.63, f32[2048]{0:T(1024)S(1)} %bitcast.242, f32[512]{0:T(512)S(1)} %copy-done.128, f32[512,2048]{1,0:T(8,128)} %fusion.129, bf16[512,5632]{1,0:T(8,128)(2,1)} %get-tuple-element.246, ...), kind=kOutput, calls=%fused_computation.56 | convolution fusion | flops 11818498048 | bytes 41435136 | tf_op jit(solution)/shard_map/dot_general | solution.py:26
  739.9 50.8 %attend_back.4 = (f32[512,512]{1,0:T(8,128)S(1)}, bf16[4096,128]{1,0:T(8,128)(2,1)S(1)}) custom-call(s32[8]{0:T(128)S(1)} %copy-done.59, f32[16,512]{1,0:T(8,128)S(1)} %compare_select_fusion.bias_ref, f32[8,512]{1,0:T(8,128)S(1)} %get-tuple-element.197.lse_ref, f32[512,512]{1,0:T(8,128)S(1)} %copy-done.32, bf16[512,2048]{1,0:T(8,128)(2,1)S(1)} %copy-done.5, ...), custom_call_target="tpu_custom_call" | custom-call | flops 1048576 | bytes 65536 | tf_op jit(solution)/shard_map/attend_back/pallas_call | solution.py:233
  816.9 51.3 %attend_back.5 = (f32[512,512]{1,0:T(8,128)S(1)}, bf16[4096,128]{1,0:T(8,128)(2,1)S(1)}) custom-call(s32[8]{0:T(128)S(1)} %copy-done.59, f32[16,512]{1,0:T(8,128)S(1)} %compare_select_fusion.bias_ref, f32[8,512]{1,0:T(8,128)S(1)} %get-tuple-element.250.lse_ref, f32[512,512]{1,0:T(8,128)S(1)} %copy-done.30, bf16[512,2048]{1,0:T(8,128)(2,1)S(1)} %copy-done.5, ...), custom_call_target="tpu_custom_call" | custom-call | flops 1048576 | bytes 65536 | tf_op jit(solution)/shard_map/attend_back/pallas_call | solution.py:233
  895.9 50.8 %attend_back.6 = (f32[512,512]{1,0:T(8,128)S(1)}, bf16[4096,128]{1,0:T(8,128)(2,1)S(1)}) custom-call(s32[8]{0:T(128)S(1)} %copy-done.59, f32[16,512]{1,0:T(8,128)S(1)} %compare_select_fusion.bias_ref, f32[8,512]{1,0:T(8,128)S(1)} %get-tuple-element.256.lse_ref, f32[512,512]{1,0:T(8,128)S(1)} %copy-done.28, bf16[512,2048]{1,0:T(8,128)(2,1)S(1)} %copy-done.5, ...), custom_call_target="tpu_custom_call" | custom-call | flops 1048576 | bytes 65536 | tf_op jit(solution)/shard_map/attend_back/pallas_call | solution.py:233
  975.5 51.3 %attend_back.7 = (f32[512,512]{1,0:T(8,128)S(1)}, bf16[4096,128]{1,0:T(8,128)(2,1)S(1)}) custom-call(s32[8]{0:T(128)S(1)} %copy-done.59, f32[16,512]{1,0:T(8,128)S(1)} %compare_select_fusion.bias_ref, f32[8,512]{1,0:T(8,128)S(1)} %get-tuple-element.265.lse_ref, f32[512,512]{1,0:T(8,128)S(1)} %get-tuple-element.229.o_ref, bf16[512,2048]{1,0:T(8,128)(2,1)S(1)} %copy-done.5, ...), custom_call_target="tpu_custom_call" | custom-call | flops 1048576 | bytes 65536 | tf_op jit(solution)/shard_map/attend_back/pallas_call | solution.py:233
  1102.2 20.0 %collective-permute-done.62 = bf16[512,128]{1,0:T(8,128)(2,1)S(1)} collective-permute-done((bf16[512,128]{1,0:T(8,128)(2,1)S(1)}, bf16[512,128]{1,0:T(8,128)(2,1)S(1)}, u32[]{:S(2)}, u32[]{:S(2)}) %collective-permute-start.62) | collective-permute-done | bytes 131104 | tf_op jit(solution)/shard_map/ppermute | solution.py:373
  1163.4 14.2 %collective-permute-done.67 = bf16[256,640]{0,1:T(8,128)(2,1)} collective-permute-done((bf16[256,640]{0,1:T(8,128)(2,1)}, bf16[256,640]{0,1:T(8,128)(2,1)}, u32[]{:S(2)}, u32[]{:S(2)}) %collective-permute-start.67) | collective-permute-done | bytes 327712 | tf_op jit(solution)/shard_map/ppermute | solution.py:373
  1180.9 19.3 %fusion.18 = bf16[1,512,2048]{2,1,0:T(8,128)(2,1)} fusion(f32[512,2048]{1,0:T(8,128)S(1)} %copy-done.65, bf16[512,5632]{1,0:T(8,128)(2,1)} %get-tuple-element.315.x_ref, bf16[5632,2048]{1,0:T(8,128)(2,1)} %bitcast.201), kind=kOutput, calls=%fused_computation.76 | convolution fusion | flops 11813257216 | bytes 35127296 | tf_op jit(solution)/shard_map/dot_general | solution.py:26
  (680 shorter events, 615.3 us)
Async XLA Ops:
  7.2 94.1 %all-gather.7.cloned.1.call-start = ((), (), s32[]{:S(2)}) async-start(), calls=%async_computation.8 | async-start | bytes 3604480 | tf_op jit(solution)/shard_map/all_gather | solution.py:579
  7.9 225.0 %all-gather.9.cloned.1.call-start = ((), (), s32[]{:S(2)}) async-start(), calls=%async_computation.9 | async-start | bytes 3604480 | tf_op jit(solution)/shard_map/all_gather | solution.py:579
  131.4 188.1 %all-gather.11.cloned.1.call-start = ((), (), s32[]{:S(2)}) async-start(), calls=%async_computation.10 | async-start | bytes 1310720 | tf_op jit(solution)/shard_map/all_gather | solution.py:579
  140.2 112.1 %collective-permute-start.18 = (bf16[2,2,64,5632]{3,2,1,0:T(8,128)(2,1)S(1)}, bf16[2,2,64,5632]{3,2,1,0:T(8,128)(2,1)}, u32[]{:S(2)}, u32[]{:S(2)}) collective-permute-start(bf16[2,2,64,5632]{3,2,1,0:T(8,128)(2,1)S(1)} %get-tuple-element.376), channel_id=1, source_target_pairs={{0,8},{8,24},{24,16},{16,0},{1,9},{9,25},{25,17},{17,1},{2,10},{10... | collective-permute-start | bytes 8650760 | tf_op jit(solution)/shard_map/ppermute | solution.py:362
  214.1 817.4 %reduce-scatter.5.cloned.1.call-start = ((), (), s32[]{:S(2)}) async-start(), calls=%async_computation.4 | async-start | bytes 3604480 | tf_op jit(solution)/shard_map/reduce_scatter | solution.py:501
  218.0 101.6 %collective-permute-start.19 = (bf16[2,2,176,2048]{3,2,1,0:T(8,128)(2,1)}, bf16[2,2,176,2048]{3,2,1,0:T(8,128)(2,1)}, u32[]{:S(2)}, u32[]{:S(2)}) collective-permute-start(bf16[2,2,176,2048]{3,2,1,0:T(8,128)(2,1)} %pad_maximum_fusion.7), channel_id=1, source_target_pairs={{0,2},{1,3},{2,0},{3,1},{4,6},{5,7},{6,4},{7,5},{8,10},{9,11},{10,... | collective-permute-start | bytes 8650760 | tf_op jit(solution)/shard_map/ppermute | solution.py:373
  221.5 98.0 %collective-permute-start.20 = (bf16[2,2,176,2048]{3,2,1,0:T(8,128)(2,1)}, bf16[2,2,176,2048]{3,2,1,0:T(8,128)(2,1)}, u32[]{:S(2)}, u32[]{:S(2)}) collective-permute-start(bf16[2,2,176,2048]{3,2,1,0:T(8,128)(2,1)} %pad_maximum_fusion.8), channel_id=1, source_target_pairs={{0,4},{1,5},{2,6},{3,7},{4,0},{5,1},{6,2},{7,3},{8,12},{9,13},{10,... | collective-permute-start | bytes 8650760 | tf_op jit(solution)/shard_map/ppermute | solution.py:373
  252.3 82.9 %collective-permute-start.21 = (bf16[2,2,64,5632]{3,2,1,0:T(8,128)(2,1)}, bf16[2,2,64,5632]{3,2,1,0:T(8,128)(2,1)}, u32[]{:S(2)}, u32[]{:S(2)}) collective-permute-start(bf16[2,2,64,5632]{3,2,1,0:T(8,128)(2,1)} %collective-permute-done.18), channel_id=1, source_target_pairs={{0,8},{8,24},{24,16},{16,0},{1,9},{9,25},{25,17},{17,1},{2,10},{10... | collective-permute-start | bytes 8650760 | tf_op jit(solution)/shard_map/ppermute | solution.py:362
  347.1 116.0 %collective-permute-start.32 = (bf16[2,2,2,64,5632]{4,3,2,1,0:T(8,128)(2,1)}, bf16[2,2,2,64,5632]{4,3,2,1,0:T(8,128)(2,1)}, u32[]{:S(2)}, u32[]{:S(2)}) collective-permute-start(bf16[2,2,2,64,5632]{4,3,2,1,0:T(8,128)(2,1)} %pad_maximum_fusion.2), channel_id=1, source_target_pairs={{0,1},{1,0},{2,3},{3,2},{4,5},{5,4},{6,7},{7,6},{8,9},{9,8},{10,11... | collective-permute-start | bytes 17301512 | tf_op jit(solution)/shard_map/ppermute | solution.py:373
  378.9 91.7 %collective-permute-start.29 = (bf16[2,2,64,5632]{3,2,1,0:T(8,128)(2,1)}, bf16[2,2,64,5632]{3,2,1,0:T(8,128)(2,1)}, u32[]{:S(2)}, u32[]{:S(2)}) collective-permute-start(bf16[2,2,64,5632]{3,2,1,0:T(8,128)(2,1)} %pad_maximum_fusion.9), channel_id=1, source_target_pairs={{0,2},{1,3},{2,0},{3,1},{4,6},{5,7},{6,4},{7,5},{8,10},{9,11},{10,... | collective-permute-start | bytes 8650760 | tf_op jit(solution)/shard_map/ppermute | solution.py:373
  384.1 86.4 %collective-permute-start.30 = (bf16[2,2,64,5632]{3,2,1,0:T(8,128)(2,1)}, bf16[2,2,64,5632]{3,2,1,0:T(8,128)(2,1)}, u32[]{:S(2)}, u32[]{:S(2)}) collective-permute-start(bf16[2,2,64,5632]{3,2,1,0:T(8,128)(2,1)} %pad_maximum_fusion.10), channel_id=1, source_target_pairs={{0,4},{1,5},{2,6},{3,7},{4,0},{5,1},{6,2},{7,3},{8,12},{9,13},{10,... | collective-permute-start | bytes 8650760 | tf_op jit(solution)/shard_map/ppermute | solution.py:373
  385.9 80.1 %collective-permute-start.27 = (bf16[2,2,64,2048]{3,2,1,0:T(8,128)(2,1)}, bf16[2,2,64,2048]{3,2,1,0:T(8,128)(2,1)}, u32[]{:S(2)}, u32[]{:S(2)}) collective-permute-start(bf16[2,2,64,2048]{3,2,1,0:T(8,128)(2,1)} %pad_maximum_fusion.22), channel_id=1, source_target_pairs={{0,2},{1,3},{2,0},{3,1},{4,6},{5,7},{6,4},{7,5},{8,10},{9,11},{10,... | collective-permute-start | bytes 3145736 | tf_op jit(solution)/shard_map/ppermute | solution.py:373
  480.8 79.4 %collective-permute-start.35 = (bf16[16,64,5632]{2,1,0:T(8,128)(2,1)}, bf16[16,64,5632]{2,1,0:T(8,128)(2,1)}, u32[]{:S(2)}, u32[]{:S(2)}) collective-permute-start(bf16[16,64,5632]{2,1,0:T(8,128)(2,1)} %pad_maximum_fusion.1.refs_0_), channel_id=1, source_target_pairs={{0,1},{1,0},{2,3},{3,2},{4,5},{5,4},{6,7},{7,6},{8,9},{9,8},{10,11... | collective-permute-start | bytes 34603016 | tf_op jit(solution)/shard_map/ppermute | solution.py:373
  629.5 75.0 %collective-permute-start.37 = (bf16[2816,2048]{1,0:T(8,128)(2,1)}, bf16[2816,2048]{1,0:T(8,128)(2,1)}, u32[]{:S(2)}, u32[]{:S(2)}) collective-permute-start(bf16[2816,2048]{1,0:T(8,128)(2,1)} %convolution_convert_fusion.1), channel_id=1, source_target_pairs={{0,1},{1,0},{2,3},{3,2},{4,5},{5,4},{6,7},{7,6},{8,9},{9,8},{10,11... | collective-permute-start | bytes 34603016 | tf_op jit(solution)/shard_map/ppermute | solution.py:373
  704.5 86.2 %collective-permute-start.39 = (bf16[256,5632]{1,0:T(8,128)(2,1)}, bf16[256,5632]{1,0:T(8,128)(2,1)}, u32[]{:S(2)}, u32[]{:S(2)}) collective-permute-start(bf16[256,5632]{1,0:T(8,128)(2,1)} %add_convert_fusion.18), channel_id=1, source_target_pairs={{0,2},{1,3},{2,0},{3,1},{4,6},{5,7},{6,4},{7,5},{8,10},{9,11},{10,... | collective-permute-start | bytes 8650760 | tf_op jit(solution)/shard_map/ppermute | solution.py:373
  705.0 85.7 %collective-permute-start.40 = (bf16[256,5632]{1,0:T(8,128)(2,1)}, bf16[256,5632]{1,0:T(8,128)(2,1)}, u32[]{:S(2)}, u32[]{:S(2)}) collective-permute-start(bf16[256,5632]{1,0:T(8,128)(2,1)} %add_convert_fusion.17), channel_id=1, source_target_pairs={{0,4},{1,5},{2,6},{3,7},{4,0},{5,1},{6,2},{7,3},{8,12},{9,13},{10,... | collective-permute-start | bytes 8650760 | tf_op jit(solution)/shard_map/ppermute | solution.py:373
  711.7 79.1 %collective-permute-start.41 = (bf16[704,2048]{1,0:T(8,128)(2,1)}, bf16[704,2048]{1,0:T(8,128)(2,1)}, u32[]{:S(2)}, u32[]{:S(2)}) collective-permute-start(bf16[704,2048]{1,0:T(8,128)(2,1)} %add_convert_fusion.16), channel_id=1, source_target_pairs={{0,8},{8,24},{24,16},{16,0},{1,9},{9,25},{25,17},{17,1},{2,10},{10... | collective-permute-start | bytes 8650760 | tf_op jit(solution)/shard_map/ppermute | solution.py:362
  732.7 135.5 %collective-permute-start.42 = (bf16[256,5632]{1,0:T(8,128)(2,1)}, bf16[256,5632]{1,0:T(8,128)(2,1)}, u32[]{:S(2)}, u32[]{:S(2)}) collective-permute-start(bf16[256,5632]{1,0:T(8,128)(2,1)} %add_convert_fusion.15), channel_id=1, source_target_pairs={{0,2},{1,3},{2,0},{3,1},{4,6},{5,7},{6,4},{7,5},{8,10},{9,11},{10,... | collective-permute-start | bytes 8650760 | tf_op jit(solution)/shard_map/ppermute | solution.py:373
  738.3 129.9 %collective-permute-start.43 = (bf16[256,5632]{1,0:T(8,128)(2,1)}, bf16[256,5632]{1,0:T(8,128)(2,1)}, u32[]{:S(2)}, u32[]{:S(2)}) collective-permute-start(bf16[256,5632]{1,0:T(8,128)(2,1)} %add_convert_fusion.14), channel_id=1, source_target_pairs={{0,4},{1,5},{2,6},{3,7},{4,0},{5,1},{6,2},{7,3},{8,12},{9,13},{10,... | collective-permute-start | bytes 8650760 | tf_op jit(solution)/shard_map/ppermute | solution.py:373
  872.7 77.2 %collective-permute-start.49 = (bf16[1024,2048]{1,0:T(8,128)(2,1)}, bf16[1024,2048]{1,0:T(8,128)(2,1)}, u32[]{:S(2)}, u32[]{:S(2)}) collective-permute-start(bf16[1024,2048]{1,0:T(8,128)(2,1)} %convolution_convert_fusion.4), channel_id=1, source_target_pairs={{0,1},{1,0},{2,3},{3,2},{4,5},{5,4},{6,7},{7,6},{8,9},{9,8},{10,11... | collective-permute-start | bytes 12582920 | tf_op jit(solution)/shard_map/ppermute | solution.py:373
  953.9 193.2 %reduce-scatter.7.cloned.1.call-start = ((), (), s32[]{:S(2)}) async-start(), calls=%async_computation.5 | async-start | bytes 3604480 | tf_op jit(solution)/shard_map/reduce_scatter | solution.py:501
  959.6 71.9 %collective-permute-start.51 = (bf16[2048,384]{1,0:T(8,128)(2,1)S(1)}, bf16[2048,384]{1,0:T(8,128)(2,1)}, u32[]{:S(2)}, u32[]{:S(2)}) collective-permute-start(bf16[2048,384]{1,0:T(8,128)(2,1)S(1)} %slice.498), channel_id=1, source_target_pairs={{0,1},{1,0},{2,3},{3,2},{4,5},{5,4},{6,7},{7,6},{8,9},{9,8},{10,11... | collective-permute-start | bytes 4718600 | tf_op jit(solution)/shard_map/ppermute | solution.py:373
  1043.8 161.7 %reduce-scatter.9.cloned.1.call-start = ((), (), s32[]{:S(2)}) async-start(), calls=%async_computation.6 | async-start | bytes 1310720 | tf_op jit(solution)/shard_map/reduce_scatter | solution.py:501
  1095.3 141.8 %reduce-scatter.11.cloned.1.call-start = ((), (), s32[]{:S(2)}) async-start(), calls=%async_computation.7 | async-start | bytes 1310720 | tf_op jit(solution)/shard_map/reduce_scatter | solution.py:501
  (218 other events, 4045.1 us)
Sparse Core Ops, SparseCore 0:
  9.6 76.3 all-gather.6
  131.5 101.3 all-gather.8
  234.5 61.2 all-gather.10
  954.0 54.8 reduce-scatter.4
  1043.9 54.5 reduce-scatter.6
  1100.7 26.9 reduce-scatter.8
  1203.9 30.7 reduce-scatter.10

commit v9 on v8

--- a/solution.py
+++ b/solution.py
@@ -605,10 +605,10 @@
     waiting = [part]
     for k in range(grid.n_dp - 1):
         sent = [grid.next(near[-1], "d")]
-        early = k == grid.n_dp - 2
+        early = k == grid.n_dp // 2 - 1
         if early:
-            sent.append(grid.next(jnp.stack(waiting[:-1]), "c"))
-            waiting = waiting[-1:]
+            sent.append(grid.next(jnp.stack(waiting), "c"))
+            waiting = []
         came = yield sent
         if early:
             far.append(came[1])
@@ -777,35 +777,33 @@
     bias = jnp.where(later, MASKED, 0.0).astype(F32)
     bias = meet(bias, kv_chain)
     bias = meet(bias, kv_chain)
-    bias = meet(bias, kv_chain, gate_chain, up_chain)
+    bias = meet(bias, kv_chain)
     all_keys, all_values = finish(kv_chain)
     kt, vt = all_keys.T, all_values.T
 
     grad_rows = out_grad.reshape(rows, model)
     plan = (
-        ((), ()),
+        ((gate_chain, up_chain), ()),
+        ((down_chain,), ()),
         ((down_chain, merge_chain, up_chain), (gate_chain,)),
-        ((down_chain, merge_chain, gate_chain), ()),
-        ((merge_chain, gate_chain, up_chain), ()),
+        ((merge_chain, gate_chain), ()),
     )
     outs, log_sums = [], []
     for group in range(kv_heads):
         out, log_sum = attend(group, places, bias, queries, all_keys, vt)
         on, hold = plan[group % 4]
         queries, out, grad_rows = meet((queries, out, grad_rows), *on, hold=hold)
-        if group == 2:
-            down_all = finish(down_chain)
-            grad_hidden = mm(grad_rows, down_all, NT)
-            queries, grad_hidden = lax.optimization_barrier((queries, grad_hidden))
         outs.append(out)
         log_sums.append(log_sum)
+    down_all = finish(down_chain)
+    grad_hidden = mm(grad_rows, down_all, NT)
+    outs, grad_hidden = meet((outs, grad_hidden), merge_chain, up_chain, hold=(gate_chain,))
     mixed = jnp.concatenate([out.astype(BF16) for out in outs], 1)
-    mixed = meet(mixed, merge_chain)
+    mixed = meet(mixed, merge_chain, gate_chain)
     merge_all = finish(merge_chain)
     middle = rows_in + mm(mixed, merge_all, NN)
     normed_two, factor_two = normalize(middle)
     second_in = (normed_two * gain_two).astype(BF16)
-    second_in = meet(second_in, up_chain)
     up_all = finish(up_chain)
     lift = mm(second_in, up_all, NN)
     lift = meet(lift, gate_chain)
@@ -855,9 +853,9 @@
     query_grads = unrotated(unrotate_queries_kernel, dqs, cosine, sine)
     query_sum = Chain(reduce_term(grid, first_turned, query_grads))
     grad_first = mm(query_grads, attn_all[:, :width], NT)
-    grad_first = meet(grad_first, last_keys, keys_sum, query_sum, merge_sum)
-    grad_first = meet(grad_first, last_keys, keys_sum, down_sum)
-    grad_first = meet(grad_first, last_keys)
+    grad_first = meet(grad_first, last_keys, keys_sum)
+    grad_first = meet(grad_first, last_keys, keys_sum, merge_sum)
+    grad_first = meet(grad_first, last_keys, query_sum, down_sum)
     wide = finish(keys_sum)
     dkv_parts = [wide[:, at : at + WIDE] for at in range(0, wide.shape[1], WIDE)]
     dkv_parts.append(finish(last_keys))

time: 1250 us -> 1370 us (1.096)
  waiting for transfers between devices: 253 us -> 348 us
  other arithmetic: 135 us -> 151 us
    ppermute x64, waiting for transfers between devices: 131 us -> 239 us  [next(): return lax.ppermute(values, 'ctx', pairs)]
    unnamed x329 -> x307, local copies, waits for them, and re-layouts: 40.3 us -> 49.3 us
  transfers between devices with their start and end apart: 83 -> 83, of which waited for: 26 -> 28; matrix products, arithmetic and copies ran while one was open for 32% -> 29% of each run, Pallas kernels for 30% -> 27%
where the time goes in v9:
time: 1370 us; the launch traced here: 1360 us
  Pallas kernels  387 us (28%)
  waiting for transfers between devices  348 us (25%)
  matrix products  284 us (21%)
  other arithmetic  151 us (11%)
  local copies, waits for them, and re-layouts  89.1 us (7%)
  starting transfers between devices  80.8 us (6%)
  between operations  17.2 us (1%)
    dot_general x41, matrix products, mm(): return lax.dot_general(left, right, dims, preferred_element_type=F32)  284 us
    ppermute x64, waiting for transfers between devices, next(): return lax.ppermute(values, 'ctx', pairs)  239 us
    pallas_call x4, Pallas kernels, attend_back(): pl.pallas_call(functools.partial(attend_back_kernel, which=group % 2, unr...  204 us
    pallas_call x4, Pallas kernels, attend(): pl.pallas_call(functools.partial(attend_kernel, which=group % 2, places=p...  103 us
    ppermute x12, waiting for transfers between devices, next(): return lax.ppermute(values, 'dp', list(zip(self.ring, around)))  99.3 us
    pallas_call x5, Pallas kernels, placed(): pl.pallas_call(functools.partial(place_kernel, sources=sources, slots=slo...  65.5 us
    ppermute x64, starting transfers between devices, next(): return lax.ppermute(values, 'ctx', pairs)  57.1 us
    unnamed x307, local copies, waits for them, and re-layouts  49.3 us
  transfers between devices with their start and end apart: 83, of which 28 were waited for; matrix products, arithmetic and copies ran while one was open for 29% of the time, Pallas kernels for 27%

profile of v9, /device:TPU:0, one launch (start us, length us, event | category | flops | bytes accessed | tf_op | source)
XLA Modules:
  0.0 1363.6 jit_solution(2945004097143413992)
XLA Ops:
  38.8 19.3 %collective-permute-done.2 = bf16[64,2688]{1,0:T(8,128)(2,1)S(1)} collective-permute-done((bf16[64,2688]{1,0:T(8,128)(2,1)S(1)}, bf16[64,2688]{1,0:T(8,128)(2,1)S(1)}, u32[]{:S(2)}, u32[]{:S(2)}) %collective-permute-start.2) | collective-permute-done | bytes 344096 | tf_op jit(solution)/shard_map/ppermute | solution.py:362
  65.0 20.2 %collective-permute-done.3 = bf16[64,2688]{1,0:T(8,128)(2,1)S(1)} collective-permute-done((bf16[64,2688]{1,0:T(8,128)(2,1)S(1)}, bf16[64,2688]{1,0:T(8,128)(2,1)S(1)}, u32[]{:S(2)}, u32[]{:S(2)}) %collective-permute-start.3) | collective-permute-done | bytes 344096 | tf_op jit(solution)/shard_map/ppermute | solution.py:362
  105.3 24.1 %collective-permute-done.8 = bf16[2,2,64,2688]{3,2,1,0:T(8,128)(2,1)S(1)} collective-permute-done((bf16[2,2,64,2688]{3,2,1,0:T(8,128)(2,1)S(1)}, bf16[2,2,64,2688]{3,2,1,0:T(8,128)(2,1)S(1)}, u32[]{:S(2)}, u32[]{:S(2)}) %collective-permute-start.8) | collective-permute-done | bytes 1376288 | tf_op jit(solution)/shard_map/ppermute | solution.py:373
  199.8 55.7 %collective-permute-done.12 = bf16[512,256]{1,0:T(8,128)(2,1)S(1)} collective-permute-done((bf16[512,256]{1,0:T(8,128)(2,1)S(1)}, bf16[512,256]{1,0:T(8,128)(2,1)S(1)}, u32[]{:S(2)}, u32[]{:S(2)}) %collective-permute-start.12) | collective-permute-done | bytes 262176 | tf_op jit(solution)/shard_map/ppermute | solution.py:373
  279.9 25.8 %attend.4 = (f32[512,512]{1,0:T(8,128)S(1)}, f32[8,512]{1,0:T(8,128)S(1)}) custom-call(f32[16,512]{1,0:T(8,128)S(1)} %compare_select_fusion.bias_ref, bf16[512,2048]{1,0:T(8,128)(2,1)S(1)} %copy-done.2, bf16[4096,256]{1,0:T(8,128)(2,1)S(1)} %bitcast.169, bf16[256,4096]{1,0:T(8,128)(2,1)S(1)} %copy-done.7), custom_call_target="tpu_custom_call" | custom-call | flops 1048576 | bytes 65536 | tf_op jit(solution)/shard_map/attend/pallas_call | solution.py:113
  309.9 25.6 %attend.5 = (f32[512,512]{1,0:T(8,128)S(1)}, f32[8,512]{1,0:T(8,128)S(1)}) custom-call(f32[16,512]{1,0:T(8,128)S(1)} %compare_select_fusion.bias_ref, bf16[512,2048]{1,0:T(8,128)(2,1)S(1)} %copy-done.3, bf16[4096,256]{1,0:T(8,128)(2,1)S(1)} %bitcast.170, bf16[256,4096]{1,0:T(8,128)(2,1)S(1)} %copy-done.8), custom_call_target="tpu_custom_call" | custom-call | flops 1048576 | bytes 65536 | tf_op jit(solution)/shard_map/attend/pallas_call | solution.py:113
  359.6 25.6 %attend.6 = (f32[512,512]{1,0:T(8,128)S(1)}, f32[8,512]{1,0:T(8,128)S(1)}) custom-call(f32[16,512]{1,0:T(8,128)S(1)} %compare_select_fusion.bias_ref, bf16[512,2048]{1,0:T(8,128)(2,1)S(1)} %copy-done.4, bf16[4096,256]{1,0:T(8,128)(2,1)S(1)} %bitcast.171, bf16[256,4096]{1,0:T(8,128)(2,1)S(1)} %copy-done.9), custom_call_target="tpu_custom_call" | custom-call | flops 1048576 | bytes 65536 | tf_op jit(solution)/shard_map/attend/pallas_call | solution.py:113
  394.9 40.3 %collective-permute-done.22 = bf16[2,2,64,5632]{3,2,1,0:T(8,128)(2,1)} collective-permute-done((bf16[2,2,64,5632]{3,2,1,0:T(8,128)(2,1)}, bf16[2,2,64,5632]{3,2,1,0:T(8,128)(2,1)}, u32[]{:S(2)}, u32[]{:S(2)}) %collective-permute-start.22) | collective-permute-done | bytes 2883616 | tf_op jit(solution)/shard_map/ppermute | solution.py:362
  439.1 18.1 %placed.6 = bf16[32,176,2048]{2,1,0:T(8,128)(2,1)} custom-call(s32[32]{0:T(128)S(1)} %get-tuple-element.369.order_ref, bf16[16,176,2048]{2,1,0:T(8,128)(2,1)} %pad_maximum_fusion.refs_0_, bf16[16,176,2048]{2,1,0:T(8,128)(2,1)} %collective-permute-done.21.refs_1_), custom_call_target="tpu_custom_call" | custom-call | bytes 46137344 | tf_op jit(solution)/shard_map/placed/pallas_call | solution.py:550
  457.2 25.9 %attend.7 = (f32[512,512]{1,0:T(8,128)S(1)}, f32[8,512]{1,0:T(8,128)S(1)}) custom-call(f32[16,512]{1,0:T(8,128)S(1)} %compare_select_fusion.bias_ref, bf16[512,2048]{1,0:T(8,128)(2,1)S(1)} %copy-done.5, bf16[4096,256]{1,0:T(8,128)(2,1)S(1)} %bitcast.172, bf16[256,4096]{1,0:T(8,128)(2,1)S(1)} %copy-done.10), custom_call_target="tpu_custom_call" | custom-call | flops 1048576 | bytes 65536 | tf_op jit(solution)/shard_map/attend/pallas_call | solution.py:113
  496.0 19.7 %fusion.127 = f32[512,5632]{1,0:T(8,128)} fusion(bf16[512,2048]{1,0:T(8,128)(2,1)} %bitcast.213, bf16[5632,2048]{1,0:T(8,128)(2,1)} %bitcast.203), kind=kOutput, calls=%fused_computation.301 | convolution fusion | flops 11811160064 | bytes 36700160 | tf_op jit(solution)/shard_map/dot_general | solution.py:26
  515.7 56.9 %collective-permute-done.28 = bf16[2,2,64,2048]{3,2,1,0:T(8,128)(2,1)} collective-permute-done((bf16[2,2,64,2048]{3,2,1,0:T(8,128)(2,1)}, bf16[2,2,64,2048]{3,2,1,0:T(8,128)(2,1)}, u32[]{:S(2)}, u32[]{:S(2)}) %collective-permute-start.28) | collective-permute-done | bytes 1048608 | tf_op jit(solution)/shard_map/ppermute | solution.py:373
  624.4 17.5 %placed.8 = bf16[32,64,5632]{2,1,0:T(8,128)(2,1)} custom-call(s32[32]{0:T(128)S(1)} %get-tuple-element.367.order_ref, bf16[4,64,5632]{2,1,0:T(8,128)(2,1)} %bitcast.75.refs_0_, bf16[4,64,5632]{2,1,0:T(8,128)(2,1)} %bitcast.76.refs_1_, bf16[4,64,5632]{2,1,0:T(8,128)(2,1)} %bitcast.77.refs_2_, bf16[4,64,5632]{2,1,0:T(8,128)(2,1)} %bitcast.78.refs_3_, ...), custom_call_target="tpu_custom_call" | custom-call | bytes 46137344 | tf_op jit(solution)/shard_map/placed/pallas_call | solution.py:550
  641.9 19.4 %fusion.128 = f32[512,5632]{1,0:T(8,128)} fusion(bf16[512,2048]{1,0:T(8,128)(2,1)S(1)} %multiply_convert_fusion.3.x_ref, bf16[2048,5632]{1,0:T(8,128)(2,1)} %bitcast.205), kind=kOutput, calls=%fused_computation.302 | convolution fusion | flops 11811160064 | bytes 36700160 | tf_op jit(solution)/shard_map/dot_general | solution.py:26
  661.3 17.4 %placed.9 = bf16[32,64,5632]{2,1,0:T(8,128)(2,1)} custom-call(s32[32]{0:T(128)S(1)} %get-tuple-element.369.order_ref, bf16[16,64,5632]{2,1,0:T(8,128)(2,1)} %pad_maximum_fusion.1.refs_0_, bf16[16,64,5632]{2,1,0:T(8,128)(2,1)} %collective-permute-done.35.refs_1_), custom_call_target="tpu_custom_call" | custom-call | bytes 46137344 | tf_op jit(solution)/shard_map/placed/pallas_call | solution.py:550
  678.7 19.1 %fusion.129 = f32[512,5632]{1,0:T(8,128)} fusion(bf16[512,2048]{1,0:T(8,128)(2,1)S(1)} %multiply_convert_fusion.3.x_ref, bf16[2048,5632]{1,0:T(8,128)(2,1)} %bitcast.207), kind=kOutput, calls=%fused_computation.303 | convolution fusion | flops 11811160064 | bytes 36700160 | tf_op jit(solution)/shard_map/dot_general | solution.py:26
  741.4 19.8 %fusion.130 = f32[512,2048]{1,0:T(8,128)} fusion(bf16[512,5632]{1,0:T(8,128)(2,1)} %copy-done.65, bf16[2048,5632]{1,0:T(8,128)(2,1)} %bitcast.208), kind=kOutput, calls=%fused_computation.304 | convolution fusion | flops 11811160064 | bytes 33030144 | tf_op jit(solution)/shard_map/dot_general | solution.py:26
  761.3 19.8 %multiply_reduce_fusion.1 = (f32[512]{0:T(512)S(1)}, bf16[2048]{0:T(1024)(128)(2,1)S(1)}, f32[512,2048]{1,0:T(8,128)}) fusion(f32[512,2048]{1,0:T(8,128)} %copy-done.69, f32[2048]{0:T(1024)S(1)} %bitcast.242, f32[512]{0:T(512)S(1)} %copy-done.121, f32[512,2048]{1,0:T(8,128)} %fusion.130, bf16[512,5632]{1,0:T(8,128)(2,1)} %copy-done.64, ...), kind=kOutput, calls=%fused_computation.56 | convolution fusion | flops 11818498048 | bytes 41435136 | tf_op jit(solution)/shard_map/dot_general | solution.py:26
  844.0 51.0 %attend_back.4 = (f32[512,512]{1,0:T(8,128)S(1)}, bf16[4096,128]{1,0:T(8,128)(2,1)S(1)}) custom-call(s32[8]{0:T(128)S(1)} %copy-done.62, f32[16,512]{1,0:T(8,128)S(1)} %compare_select_fusion.bias_ref, f32[8,512]{1,0:T(8,128)S(1)} %get-tuple-element.199.lse_ref, f32[512,512]{1,0:T(8,128)S(1)} %copy-done.36, bf16[512,2048]{1,0:T(8,128)(2,1)S(1)} %copy-done.6, ...), custom_call_target="tpu_custom_call" | custom-call | flops 1048576 | bytes 65536 | tf_op jit(solution)/shard_map/attend_back/pallas_call | solution.py:233
  921.3 51.1 %attend_back.5 = (f32[512,512]{1,0:T(8,128)S(1)}, bf16[4096,128]{1,0:T(8,128)(2,1)S(1)}) custom-call(s32[8]{0:T(128)S(1)} %copy-done.62, f32[16,512]{1,0:T(8,128)S(1)} %compare_select_fusion.bias_ref, f32[8,512]{1,0:T(8,128)S(1)} %get-tuple-element.256.lse_ref, f32[512,512]{1,0:T(8,128)S(1)} %copy-done.33, bf16[512,2048]{1,0:T(8,128)(2,1)S(1)} %copy-done.6, ...), custom_call_target="tpu_custom_call" | custom-call | flops 1048576 | bytes 65536 | tf_op jit(solution)/shard_map/attend_back/pallas_call | solution.py:233
  1005.7 50.8 %attend_back.6 = (f32[512,512]{1,0:T(8,128)S(1)}, bf16[4096,128]{1,0:T(8,128)(2,1)S(1)}) custom-call(s32[8]{0:T(128)S(1)} %copy-done.62, f32[16,512]{1,0:T(8,128)S(1)} %compare_select_fusion.bias_ref, f32[8,512]{1,0:T(8,128)S(1)} %get-tuple-element.262.lse_ref, f32[512,512]{1,0:T(8,128)S(1)} %copy-done.30, bf16[512,2048]{1,0:T(8,128)(2,1)S(1)} %copy-done.6, ...), custom_call_target="tpu_custom_call" | custom-call | flops 1048576 | bytes 65536 | tf_op jit(solution)/shard_map/attend_back/pallas_call | solution.py:233
  1097.6 50.7 %attend_back.7 = (f32[512,512]{1,0:T(8,128)S(1)}, bf16[4096,128]{1,0:T(8,128)(2,1)S(1)}) custom-call(s32[8]{0:T(128)S(1)} %copy-done.62, f32[16,512]{1,0:T(8,128)S(1)} %compare_select_fusion.bias_ref, f32[8,512]{1,0:T(8,128)S(1)} %get-tuple-element.271.lse_ref, f32[512,512]{1,0:T(8,128)S(1)} %get-tuple-element.235.o_ref, bf16[512,2048]{1,0:T(8,128)(2,1)S(1)} %copy-done.6, ...), custom_call_target="tpu_custom_call" | custom-call | flops 1048576 | bytes 65536 | tf_op jit(solution)/shard_map/attend_back/pallas_call | solution.py:233
  1240.9 25.7 %collective-permute-done.66 = bf16[176,2048]{1,0:T(8,128)(2,1)} collective-permute-done((bf16[176,2048]{1,0:T(8,128)(2,1)}, bf16[176,2048]{1,0:T(8,128)(2,1)}, u32[]{:S(2)}, u32[]{:S(2)}) %collective-permute-start.66) | collective-permute-done | bytes 720928 | tf_op jit(solution)/shard_map/ppermute | solution.py:373
  1299.8 19.1 %fusion.18 = bf16[1,512,2048]{2,1,0:T(8,128)(2,1)} fusion(f32[512,2048]{1,0:T(8,128)S(1)} %copy-done.71, bf16[512,5632]{1,0:T(8,128)(2,1)} %copy-done.11, bf16[5632,2048]{1,0:T(8,128)(2,1)} %bitcast.204), kind=kOutput, calls=%fused_computation.76 | convolution fusion | flops 11813257216 | bytes 35127296 | tf_op jit(solution)/shard_map/dot_general | solution.py:26
  (659 shorter events, 627.7 us)
Async XLA Ops:
  7.2 92.8 %all-gather.7.cloned.1.call-start = ((), (), s32[]{:S(2)}) async-start(), calls=%async_computation.8 | async-start | bytes 3604480 | tf_op jit(solution)/shard_map/all_gather | solution.py:579
  7.9 298.8 %all-gather.9.cloned.1.call-start = ((), (), s32[]{:S(2)}) async-start(), calls=%async_computation.9 | async-start | bytes 3604480 | tf_op jit(solution)/shard_map/all_gather | solution.py:579
  136.0 258.9 %all-gather.11.cloned.1.call-start = ((), (), s32[]{:S(2)}) async-start(), calls=%async_computation.10 | async-start | bytes 1310720 | tf_op jit(solution)/shard_map/all_gather | solution.py:579
  148.4 158.3 %collective-permute-start.18 = (bf16[2,2,64,5632]{3,2,1,0:T(8,128)(2,1)}, bf16[2,2,64,5632]{3,2,1,0:T(8,128)(2,1)}, u32[]{:S(2)}, u32[]{:S(2)}) collective-permute-start(bf16[2,2,64,5632]{3,2,1,0:T(8,128)(2,1)} %get-tuple-element.386), channel_id=1, source_target_pairs={{0,8},{8,24},{24,16},{16,0},{1,9},{9,25},{25,17},{17,1},{2,10},{10... | collective-permute-start | bytes 8650760 | tf_op jit(solution)/shard_map/ppermute | solution.py:362
  181.2 154.3 %collective-permute-start.19 = (bf16[2,2,176,2048]{3,2,1,0:T(8,128)(2,1)}, bf16[2,2,176,2048]{3,2,1,0:T(8,128)(2,1)}, u32[]{:S(2)}, u32[]{:S(2)}) collective-permute-start(bf16[2,2,176,2048]{3,2,1,0:T(8,128)(2,1)} %pad_maximum_fusion.7), channel_id=1, source_target_pairs={{0,2},{1,3},{2,0},{3,1},{4,6},{5,7},{6,4},{7,5},{8,10},{9,11},{10,... | collective-permute-start | bytes 8650760 | tf_op jit(solution)/shard_map/ppermute | solution.py:373
  186.2 149.3 %collective-permute-start.20 = (bf16[2,2,176,2048]{3,2,1,0:T(8,128)(2,1)}, bf16[2,2,176,2048]{3,2,1,0:T(8,128)(2,1)}, u32[]{:S(2)}, u32[]{:S(2)}) collective-permute-start(bf16[2,2,176,2048]{3,2,1,0:T(8,128)(2,1)} %pad_maximum_fusion.8), channel_id=1, source_target_pairs={{0,4},{1,5},{2,6},{3,7},{4,0},{5,1},{6,2},{7,3},{8,12},{9,13},{10,... | collective-permute-start | bytes 8650760 | tf_op jit(solution)/shard_map/ppermute | solution.py:373
  347.1 88.1 %collective-permute-start.21 = (bf16[16,176,2048]{2,1,0:T(8,128)(2,1)}, bf16[16,176,2048]{2,1,0:T(8,128)(2,1)}, u32[]{:S(2)}, u32[]{:S(2)}) collective-permute-start(bf16[16,176,2048]{2,1,0:T(8,128)(2,1)} %pad_maximum_fusion.refs_0_), channel_id=1, source_target_pairs={{0,1},{1,0},{2,3},{3,2},{4,5},{5,4},{6,7},{7,6},{8,9},{9,8},{10,11... | collective-permute-start | bytes 34603016 | tf_op jit(solution)/shard_map/ppermute | solution.py:373
  352.0 83.2 %collective-permute-start.23 = (bf16[2,2,2,64,5632]{4,3,2,1,0:T(8,128)(2,1)}, bf16[2,2,2,64,5632]{4,3,2,1,0:T(8,128)(2,1)}, u32[]{:S(2)}, u32[]{:S(2)}) collective-permute-start(bf16[2,2,2,64,5632]{4,3,2,1,0:T(8,128)(2,1)} %pad_maximum_fusion.2), channel_id=1, source_target_pairs={{0,1},{1,0},{2,3},{3,2},{4,5},{5,4},{6,7},{7,6},{8,9},{9,8},{10,11... | collective-permute-start | bytes 17301512 | tf_op jit(solution)/shard_map/ppermute | solution.py:373
  352.4 797.9 %reduce-scatter.5.cloned.1.call-start = ((), (), s32[]{:S(2)}) async-start(), calls=%async_computation.4 | async-start | bytes 3604480 | tf_op jit(solution)/shard_map/reduce_scatter | solution.py:501
  352.5 82.7 %collective-permute-start.22 = (bf16[2,2,64,5632]{3,2,1,0:T(8,128)(2,1)}, bf16[2,2,64,5632]{3,2,1,0:T(8,128)(2,1)}, u32[]{:S(2)}, u32[]{:S(2)}) collective-permute-start(bf16[2,2,64,5632]{3,2,1,0:T(8,128)(2,1)} %collective-permute-done.18), channel_id=1, source_target_pairs={{0,8},{8,24},{24,16},{16,0},{1,9},{9,25},{25,17},{17,1},{2,10},{10... | collective-permute-start | bytes 8650760 | tf_op jit(solution)/shard_map/ppermute | solution.py:362
  439.1 137.4 %collective-permute-start.30 = (bf16[2,2,64,5632]{3,2,1,0:T(8,128)(2,1)}, bf16[2,2,64,5632]{3,2,1,0:T(8,128)(2,1)}, u32[]{:S(2)}, u32[]{:S(2)}) collective-permute-start(bf16[2,2,64,5632]{3,2,1,0:T(8,128)(2,1)} %collective-permute-done.22), channel_id=1, source_target_pairs={{0,8},{8,24},{24,16},{16,0},{1,9},{9,25},{25,17},{17,1},{2,10},{10... | collective-permute-start | bytes 8650760 | tf_op jit(solution)/shard_map/ppermute | solution.py:362
  486.6 90.0 %collective-permute-start.31 = (bf16[2,2,64,5632]{3,2,1,0:T(8,128)(2,1)}, bf16[2,2,64,5632]{3,2,1,0:T(8,128)(2,1)}, u32[]{:S(2)}, u32[]{:S(2)}) collective-permute-start(bf16[2,2,64,5632]{3,2,1,0:T(8,128)(2,1)} %pad_maximum_fusion.9), channel_id=1, source_target_pairs={{0,2},{1,3},{2,0},{3,1},{4,6},{5,7},{6,4},{7,5},{8,10},{9,11},{10,... | collective-permute-start | bytes 8650760 | tf_op jit(solution)/shard_map/ppermute | solution.py:373
  490.9 85.7 %collective-permute-start.32 = (bf16[2,2,64,5632]{3,2,1,0:T(8,128)(2,1)}, bf16[2,2,64,5632]{3,2,1,0:T(8,128)(2,1)}, u32[]{:S(2)}, u32[]{:S(2)}) collective-permute-start(bf16[2,2,64,5632]{3,2,1,0:T(8,128)(2,1)} %pad_maximum_fusion.10), channel_id=1, source_target_pairs={{0,4},{1,5},{2,6},{3,7},{4,0},{5,1},{6,2},{7,3},{8,12},{9,13},{10,... | collective-permute-start | bytes 8650760 | tf_op jit(solution)/shard_map/ppermute | solution.py:373
  492.6 79.9 %collective-permute-start.28 = (bf16[2,2,64,2048]{3,2,1,0:T(8,128)(2,1)}, bf16[2,2,64,2048]{3,2,1,0:T(8,128)(2,1)}, u32[]{:S(2)}, u32[]{:S(2)}) collective-permute-start(bf16[2,2,64,2048]{3,2,1,0:T(8,128)(2,1)} %pad_maximum_fusion.22), channel_id=1, source_target_pairs={{0,2},{1,3},{2,0},{3,1},{4,6},{5,7},{6,4},{7,5},{8,10},{9,11},{10,... | collective-permute-start | bytes 3145736 | tf_op jit(solution)/shard_map/ppermute | solution.py:373
  494.6 81.9 %collective-permute-start.29 = (bf16[2,2,64,2048]{3,2,1,0:T(8,128)(2,1)}, bf16[2,2,64,2048]{3,2,1,0:T(8,128)(2,1)}, u32[]{:S(2)}, u32[]{:S(2)}) collective-permute-start(bf16[2,2,64,2048]{3,2,1,0:T(8,128)(2,1)} %pad_maximum_fusion.23), channel_id=1, source_target_pairs={{0,4},{1,5},{2,6},{3,7},{4,0},{5,1},{6,2},{7,3},{8,12},{9,13},{10,... | collective-permute-start | bytes 3145736 | tf_op jit(solution)/shard_map/ppermute | solution.py:373
  807.6 87.4 %collective-permute-start.39 = (bf16[256,5632]{1,0:T(8,128)(2,1)}, bf16[256,5632]{1,0:T(8,128)(2,1)}, u32[]{:S(2)}, u32[]{:S(2)}) collective-permute-start(bf16[256,5632]{1,0:T(8,128)(2,1)} %add_convert_fusion.18), channel_id=1, source_target_pairs={{0,2},{1,3},{2,0},{3,1},{4,6},{5,7},{6,4},{7,5},{8,10},{9,11},{10,... | collective-permute-start | bytes 8650760 | tf_op jit(solution)/shard_map/ppermute | solution.py:373
  808.6 86.4 %collective-permute-start.40 = (bf16[256,5632]{1,0:T(8,128)(2,1)}, bf16[256,5632]{1,0:T(8,128)(2,1)}, u32[]{:S(2)}, u32[]{:S(2)}) collective-permute-start(bf16[256,5632]{1,0:T(8,128)(2,1)} %add_convert_fusion.17), channel_id=1, source_target_pairs={{0,4},{1,5},{2,6},{3,7},{4,0},{5,1},{6,2},{7,3},{8,12},{9,13},{10,... | collective-permute-start | bytes 8650760 | tf_op jit(solution)/shard_map/ppermute | solution.py:373
  814.5 80.5 %collective-permute-start.41 = (bf16[704,2048]{1,0:T(8,128)(2,1)}, bf16[704,2048]{1,0:T(8,128)(2,1)}, u32[]{:S(2)}, u32[]{:S(2)}) collective-permute-start(bf16[704,2048]{1,0:T(8,128)(2,1)} %add_convert_fusion.16), channel_id=1, source_target_pairs={{0,8},{8,24},{24,16},{16,0},{1,9},{9,25},{25,17},{17,1},{2,10},{10... | collective-permute-start | bytes 8650760 | tf_op jit(solution)/shard_map/ppermute | solution.py:362
  836.3 136.2 %collective-permute-start.42 = (bf16[256,5632]{1,0:T(8,128)(2,1)}, bf16[256,5632]{1,0:T(8,128)(2,1)}, u32[]{:S(2)}, u32[]{:S(2)}) collective-permute-start(bf16[256,5632]{1,0:T(8,128)(2,1)} %add_convert_fusion.15), channel_id=1, source_target_pairs={{0,2},{1,3},{2,0},{3,1},{4,6},{5,7},{6,4},{7,5},{8,10},{9,11},{10,... | collective-permute-start | bytes 8650760 | tf_op jit(solution)/shard_map/ppermute | solution.py:373
  842.5 130.0 %collective-permute-start.43 = (bf16[256,5632]{1,0:T(8,128)(2,1)}, bf16[256,5632]{1,0:T(8,128)(2,1)}, u32[]{:S(2)}, u32[]{:S(2)}) collective-permute-start(bf16[256,5632]{1,0:T(8,128)(2,1)} %add_convert_fusion.14), channel_id=1, source_target_pairs={{0,4},{1,5},{2,6},{3,7},{4,0},{5,1},{6,2},{7,3},{8,12},{9,13},{10,... | collective-permute-start | bytes 8650760 | tf_op jit(solution)/shard_map/ppermute | solution.py:373
  1064.0 176.8 %reduce-scatter.7.cloned.1.call-start = ((), (), s32[]{:S(2)}) async-start(), calls=%async_computation.5 | async-start | bytes 3604480 | tf_op jit(solution)/shard_map/reduce_scatter | solution.py:501
  1071.9 78.4 %collective-permute-start.51 = (bf16[2048,384]{1,0:T(8,128)(2,1)}, bf16[2048,384]{1,0:T(8,128)(2,1)}, u32[]{:S(2)}, u32[]{:S(2)}) collective-permute-start(bf16[2048,384]{1,0:T(8,128)(2,1)} %slice.498), channel_id=1, source_target_pairs={{0,1},{1,0},{2,3},{3,2},{4,5},{5,4},{6,7},{7,6},{8,9},{9,8},{10,11... | collective-permute-start | bytes 4718600 | tf_op jit(solution)/shard_map/ppermute | solution.py:373
  1093.1 230.9 %reduce-scatter.9.cloned.1.call-start = ((), (), s32[]{:S(2)}) async-start(), calls=%async_computation.6 | async-start | bytes 1310720 | tf_op jit(solution)/shard_map/reduce_scatter | solution.py:501
  1200.6 154.1 %reduce-scatter.11.cloned.1.call-start = ((), (), s32[]{:S(2)}) async-start(), calls=%async_computation.7 | async-start | bytes 1310720 | tf_op jit(solution)/shard_map/reduce_scatter | solution.py:501
  (208 other events, 4120.9 us)
Sparse Core Ops, SparseCore 0:
  9.6 76.3 all-gather.6
  136.1 94.6 all-gather.8
  352.6 42.3 all-gather.10
  1064.1 55.1 reduce-scatter.4
  1121.5 56.0 reduce-scatter.6
  1200.8 24.8 reduce-scatter.8
  1322.5 30.9 reduce-scatter.10

commit v10 on v9

--- a/solution.py
+++ b/solution.py
@@ -768,7 +768,7 @@
     gain_two = first_weights[:, width + 2 * kv_width + 1].astype(F32)
 
     first_in = (normed_one * gain_one).astype(BF16)
-    first_in = meet(first_in, down_chain)
+    first_in = meet(first_in, hold=(down_chain,))
     raw = mm(first_in, attn_all, NN)
     queries, own_kv = rotated(raw, cosine, sine, kv_width)
     kv_chain = Chain(gather_keys(grid, own_kv))
@@ -777,29 +777,31 @@
     bias = jnp.where(later, MASKED, 0.0).astype(F32)
     bias = meet(bias, kv_chain)
     bias = meet(bias, kv_chain)
-    bias = meet(bias, kv_chain)
+    bias = meet(bias, kv_chain, down_chain, hold=(gate_chain,))
     all_keys, all_values = finish(kv_chain)
     kt, vt = all_keys.T, all_values.T
 
     grad_rows = out_grad.reshape(rows, model)
     plan = (
-        ((gate_chain, up_chain), ()),
-        ((down_chain,), ()),
+        ((gate_chain,), ()),
+        ((down_chain, up_chain), ()),
         ((down_chain, merge_chain, up_chain), (gate_chain,)),
-        ((merge_chain, gate_chain), ()),
+        ((merge_chain, gate_chain, up_chain), ()),
     )
     outs, log_sums = [], []
     for group in range(kv_heads):
         out, log_sum = attend(group, places, bias, queries, all_keys, vt)
         on, hold = plan[group % 4]
         queries, out, grad_rows = meet((queries, out, grad_rows), *on, hold=hold)
+        if group == 2:
+            down_all = finish(down_chain)
+            queries, down_all = meet((queries, down_all), merge_chain, gate_chain)
+            grad_hidden = mm(grad_rows, down_all, NT)
+            queries, grad_hidden = lax.optimization_barrier((queries, grad_hidden))
         outs.append(out)
         log_sums.append(log_sum)
-    down_all = finish(down_chain)
-    grad_hidden = mm(grad_rows, down_all, NT)
-    outs, grad_hidden = meet((outs, grad_hidden), merge_chain, up_chain, hold=(gate_chain,))
     mixed = jnp.concatenate([out.astype(BF16) for out in outs], 1)
-    mixed = meet(mixed, merge_chain, gate_chain)
+    mixed = meet(mixed, merge_chain)
     merge_all = finish(merge_chain)
     middle = rows_in + mm(mixed, merge_all, NN)
     normed_two, factor_two = normalize(middle)
@@ -853,7 +855,7 @@
     query_grads = unrotated(unrotate_queries_kernel, dqs, cosine, sine)
     query_sum = Chain(reduce_term(grid, first_turned, query_grads))
     grad_first = mm(query_grads, attn_all[:, :width], NT)
-    grad_first = meet(grad_first, last_keys, keys_sum)
+    grad_first = meet(grad_first, last_keys, keys_sum, down_sum, hold=(query_sum,))
     grad_first = meet(grad_first, last_keys, keys_sum, merge_sum)
     grad_first = meet(grad_first, last_keys, query_sum, down_sum)
     wide = finish(keys_sum)

time: 1370 us -> 1300 us (0.949)
  waiting for transfers between devices: 348 us -> 289 us
    ppermute x64, waiting for transfers between devices: 239 us -> 174 us  [next(): return lax.ppermute(values, 'ctx', pairs)]
    unnamed x307 -> x315, local copies, waits for them, and re-layouts: 49.3 us -> 40.7 us
  transfers between devices with their start and end apart: 83 -> 83, of which waited for: 28 -> 31; matrix products, arithmetic and copies ran while one was open for 29% -> 31% of each run, Pallas kernels for 27% -> 29%
where the time goes in v10:
time: 1300 us; the launch traced here: 1290 us
  Pallas kernels  394 us (30%)
  waiting for transfers between devices  289 us (22%)
  matrix products  285 us (22%)
  other arithmetic  149 us (11%)
  local copies, waits for them, and re-layouts  78.4 us (6%)
  starting transfers between devices  71.7 us (6%)
  between operations  17.4 us (1%)
    dot_general x41, matrix products, mm(): return lax.dot_general(left, right, dims, preferred_element_type=F32)  285 us
    pallas_call x4, Pallas kernels, attend_back(): pl.pallas_call(functools.partial(attend_back_kernel, which=group % 2, unr...  204 us
    ppermute x64, waiting for transfers between devices, next(): return lax.ppermute(values, 'ctx', pairs)  174 us
    ppermute x12, waiting for transfers between devices, next(): return lax.ppermute(values, 'dp', list(zip(self.ring, around)))  103 us
    pallas_call x4, Pallas kernels, attend(): pl.pallas_call(functools.partial(attend_kernel, which=group % 2, places=p...  103 us
    pallas_call x5, Pallas kernels, placed(): pl.pallas_call(functools.partial(place_kernel, sources=sources, slots=slo...  71.7 us
    ppermute x64, starting transfers between devices, next(): return lax.ppermute(values, 'ctx', pairs)  49.8 us
    unnamed x315, local copies, waits for them, and re-layouts  40.7 us
  transfers between devices with their start and end apart: 83, of which 31 were waited for; matrix products, arithmetic and copies ran while one was open for 31% of the time, Pallas kernels for 29%

profile of v10, /device:TPU:0, one launch (start us, length us, event | category | flops | bytes accessed | tf_op | source)
XLA Modules:
  0.0 1291.8 jit_solution(2471560716358726948)
XLA Ops:
  37.0 18.6 %collective-permute-done.2 = bf16[64,2688]{1,0:T(8,128)(2,1)S(1)} collective-permute-done((bf16[64,2688]{1,0:T(8,128)(2,1)S(1)}, bf16[64,2688]{1,0:T(8,128)(2,1)S(1)}, u32[]{:S(2)}, u32[]{:S(2)}) %collective-permute-start.2) | collective-permute-done | bytes 344096 | tf_op jit(solution)/shard_map/ppermute | solution.py:362
  63.9 18.4 %collective-permute-done.3 = bf16[64,2688]{1,0:T(8,128)(2,1)S(1)} collective-permute-done((bf16[64,2688]{1,0:T(8,128)(2,1)S(1)}, bf16[64,2688]{1,0:T(8,128)(2,1)S(1)}, u32[]{:S(2)}, u32[]{:S(2)}) %collective-permute-start.3) | collective-permute-done | bytes 344096 | tf_op jit(solution)/shard_map/ppermute | solution.py:362
  84.6 15.1 %collective-permute-done.6 = bf16[2,64,2688]{2,1,0:T(8,128)(2,1)S(1)} collective-permute-done((bf16[2,64,2688]{2,1,0:T(8,128)(2,1)S(1)}, bf16[2,64,2688]{2,1,0:T(8,128)(2,1)S(1)}, u32[]{:S(2)}, u32[]{:S(2)}) %collective-permute-start.6) | collective-permute-done | bytes 688160 | tf_op jit(solution)/shard_map/ppermute | solution.py:373
  101.6 28.3 %collective-permute-done.8 = bf16[2,2,64,2688]{3,2,1,0:T(8,128)(2,1)S(1)} collective-permute-done((bf16[2,2,64,2688]{3,2,1,0:T(8,128)(2,1)S(1)}, bf16[2,2,64,2688]{3,2,1,0:T(8,128)(2,1)S(1)}, u32[]{:S(2)}, u32[]{:S(2)}) %collective-permute-start.8) | collective-permute-done | bytes 1376288 | tf_op jit(solution)/shard_map/ppermute | solution.py:373
  233.5 25.6 %attend.4 = (f32[512,512]{1,0:T(8,128)S(1)}, f32[8,512]{1,0:T(8,128)S(1)}) custom-call(f32[16,512]{1,0:T(8,128)S(1)} %compare_select_fusion.bias_ref, bf16[512,2048]{1,0:T(8,128)(2,1)S(1)} %copy-done.2, bf16[4096,256]{1,0:T(8,128)(2,1)S(1)} %bitcast.169, bf16[256,4096]{1,0:T(8,128)(2,1)S(1)} %copy-done.6), custom_call_target="tpu_custom_call" | custom-call | flops 1048576 | bytes 65536 | tf_op jit(solution)/shard_map/attend/pallas_call | solution.py:113
  260.1 25.7 %attend.5 = (f32[512,512]{1,0:T(8,128)S(1)}, f32[8,512]{1,0:T(8,128)S(1)}) custom-call(f32[16,512]{1,0:T(8,128)S(1)} %compare_select_fusion.bias_ref, bf16[512,2048]{1,0:T(8,128)(2,1)S(1)} %copy-done.2, bf16[4096,256]{1,0:T(8,128)(2,1)S(1)} %bitcast.170, bf16[256,4096]{1,0:T(8,128)(2,1)S(1)} %copy-done.6), custom_call_target="tpu_custom_call" | custom-call | flops 1048576 | bytes 65536 | tf_op jit(solution)/shard_map/attend/pallas_call | solution.py:113
  313.3 25.8 %attend.6 = (f32[512,512]{1,0:T(8,128)S(1)}, f32[8,512]{1,0:T(8,128)S(1)}) custom-call(f32[16,512]{1,0:T(8,128)S(1)} %compare_select_fusion.bias_ref, bf16[512,2048]{1,0:T(8,128)(2,1)S(1)} %copy-done.3, bf16[4096,256]{1,0:T(8,128)(2,1)S(1)} %bitcast.171, bf16[256,4096]{1,0:T(8,128)(2,1)S(1)} %copy-done.7), custom_call_target="tpu_custom_call" | custom-call | flops 1048576 | bytes 65536 | tf_op jit(solution)/shard_map/attend/pallas_call | solution.py:113
  349.8 39.2 %collective-permute-done.22 = bf16[2,2,64,5632]{3,2,1,0:T(8,128)(2,1)} collective-permute-done((bf16[2,2,64,5632]{3,2,1,0:T(8,128)(2,1)}, bf16[2,2,64,5632]{3,2,1,0:T(8,128)(2,1)}, u32[]{:S(2)}, u32[]{:S(2)}) %collective-permute-start.22) | collective-permute-done | bytes 2883616 | tf_op jit(solution)/shard_map/ppermute | solution.py:362
  391.8 17.4 %placed.6 = bf16[32,176,2048]{2,1,0:T(8,128)(2,1)} custom-call(s32[32]{0:T(128)S(1)} %get-tuple-element.371.order_ref, bf16[16,176,2048]{2,1,0:T(8,128)(2,1)} %pad_maximum_fusion.refs_0_, bf16[16,176,2048]{2,1,0:T(8,128)(2,1)} %collective-permute-done.21.refs_1_), custom_call_target="tpu_custom_call" | custom-call | bytes 46137344 | tf_op jit(solution)/shard_map/placed/pallas_call | solution.py:550
  422.0 20.1 %fusion.127 = f32[512,5632]{1,0:T(8,128)} fusion(bf16[512,2048]{1,0:T(8,128)(2,1)} %bitcast.213, bf16[5632,2048]{1,0:T(8,128)(2,1)} %bitcast.203), kind=kOutput, calls=%fused_computation.301 | convolution fusion | flops 11811160064 | bytes 36700160 | tf_op jit(solution)/shard_map/dot_general | solution.py:26
  445.3 25.6 %attend.7 = (f32[512,512]{1,0:T(8,128)S(1)}, f32[8,512]{1,0:T(8,128)S(1)}) custom-call(f32[16,512]{1,0:T(8,128)S(1)} %compare_select_fusion.bias_ref, bf16[512,2048]{1,0:T(8,128)(2,1)S(1)} %copy-done.4, bf16[4096,256]{1,0:T(8,128)(2,1)S(1)} %bitcast.172, bf16[256,4096]{1,0:T(8,128)(2,1)S(1)} %copy-done.8), custom_call_target="tpu_custom_call" | custom-call | flops 1048576 | bytes 65536 | tf_op jit(solution)/shard_map/attend/pallas_call | solution.py:113
  470.9 27.4 %collective-permute-done.28 = bf16[2,2,64,2048]{3,2,1,0:T(8,128)(2,1)} collective-permute-done((bf16[2,2,64,2048]{3,2,1,0:T(8,128)(2,1)}, bf16[2,2,64,2048]{3,2,1,0:T(8,128)(2,1)}, u32[]{:S(2)}, u32[]{:S(2)}) %collective-permute-start.28) | collective-permute-done | bytes 1048608 | tf_op jit(solution)/shard_map/ppermute | solution.py:373
  555.8 17.4 %placed.8 = bf16[32,64,5632]{2,1,0:T(8,128)(2,1)} custom-call(s32[32]{0:T(128)S(1)} %get-tuple-element.369.order_ref, bf16[4,64,5632]{2,1,0:T(8,128)(2,1)} %bitcast.75.refs_0_, bf16[4,64,5632]{2,1,0:T(8,128)(2,1)} %bitcast.76.refs_1_, bf16[4,64,5632]{2,1,0:T(8,128)(2,1)} %bitcast.77.refs_2_, bf16[4,64,5632]{2,1,0:T(8,128)(2,1)} %bitcast.78.refs_3_, ...), custom_call_target="tpu_custom_call" | custom-call | bytes 46137344 | tf_op jit(solution)/shard_map/placed/pallas_call | solution.py:550
  573.2 19.1 %fusion.128 = f32[512,5632]{1,0:T(8,128)} fusion(bf16[512,2048]{1,0:T(8,128)(2,1)S(1)} %multiply_convert_fusion.3.x_ref, bf16[2048,5632]{1,0:T(8,128)(2,1)} %bitcast.205), kind=kOutput, calls=%fused_computation.302 | convolution fusion | flops 11811160064 | bytes 36700160 | tf_op jit(solution)/shard_map/dot_general | solution.py:26
  592.4 17.4 %placed.9 = bf16[32,64,5632]{2,1,0:T(8,128)(2,1)} custom-call(s32[32]{0:T(128)S(1)} %get-tuple-element.371.order_ref, bf16[16,64,5632]{2,1,0:T(8,128)(2,1)} %pad_maximum_fusion.1.refs_0_, bf16[16,64,5632]{2,1,0:T(8,128)(2,1)} %collective-permute-done.35.refs_1_), custom_call_target="tpu_custom_call" | custom-call | bytes 46137344 | tf_op jit(solution)/shard_map/placed/pallas_call | solution.py:550
  609.8 19.3 %fusion.129 = f32[512,5632]{1,0:T(8,128)} fusion(bf16[512,2048]{1,0:T(8,128)(2,1)S(1)} %multiply_convert_fusion.3.x_ref, bf16[2048,5632]{1,0:T(8,128)(2,1)} %bitcast.207), kind=kOutput, calls=%fused_computation.303 | convolution fusion | flops 11811160064 | bytes 36700160 | tf_op jit(solution)/shard_map/dot_general | solution.py:26
  673.4 19.5 %fusion.130 = f32[512,2048]{1,0:T(8,128)} fusion(bf16[512,5632]{1,0:T(8,128)(2,1)} %copy-done.61, bf16[2048,5632]{1,0:T(8,128)(2,1)} %bitcast.208), kind=kOutput, calls=%fused_computation.304 | convolution fusion | flops 11811160064 | bytes 33030144 | tf_op jit(solution)/shard_map/dot_general | solution.py:26
  692.9 20.0 %multiply_reduce_fusion.1 = (f32[512]{0:T(512)S(1)}, bf16[2048]{0:T(1024)(128)(2,1)S(1)}, f32[512,2048]{1,0:T(8,128)}) fusion(f32[512,2048]{1,0:T(8,128)} %copy-done.65, f32[2048]{0:T(1024)S(1)} %bitcast.242, f32[512]{0:T(512)S(1)} %copy-done.123, f32[512,2048]{1,0:T(8,128)} %fusion.130, bf16[512,5632]{1,0:T(8,128)(2,1)} %copy-done.60, ...), kind=kOutput, calls=%fused_computation.56 | convolution fusion | flops 11818498048 | bytes 41435136 | tf_op jit(solution)/shard_map/dot_general | solution.py:26
  776.1 51.3 %attend_back.4 = (f32[512,512]{1,0:T(8,128)S(1)}, bf16[4096,128]{1,0:T(8,128)(2,1)S(1)}) custom-call(s32[8]{0:T(128)S(1)} %copy-done.58, f32[16,512]{1,0:T(8,128)S(1)} %compare_select_fusion.bias_ref, f32[8,512]{1,0:T(8,128)S(1)} %get-tuple-element.202.lse_ref, f32[512,512]{1,0:T(8,128)S(1)} %copy-done.29, bf16[512,2048]{1,0:T(8,128)(2,1)S(1)} %copy-done.5, ...), custom_call_target="tpu_custom_call" | custom-call | flops 1048576 | bytes 65536 | tf_op jit(solution)/shard_map/attend_back/pallas_call | solution.py:233
  856.5 51.1 %attend_back.5 = (f32[512,512]{1,0:T(8,128)S(1)}, bf16[4096,128]{1,0:T(8,128)(2,1)S(1)}) custom-call(s32[8]{0:T(128)S(1)} %copy-done.58, f32[16,512]{1,0:T(8,128)S(1)} %compare_select_fusion.bias_ref, f32[8,512]{1,0:T(8,128)S(1)} %get-tuple-element.257.lse_ref, f32[512,512]{1,0:T(8,128)S(1)} %copy-done.24, bf16[512,2048]{1,0:T(8,128)(2,1)S(1)} %copy-done.5, ...), custom_call_target="tpu_custom_call" | custom-call | flops 1048576 | bytes 65536 | tf_op jit(solution)/shard_map/attend_back/pallas_call | solution.py:233
  935.0 50.8 %attend_back.6 = (f32[512,512]{1,0:T(8,128)S(1)}, bf16[4096,128]{1,0:T(8,128)(2,1)S(1)}) custom-call(s32[8]{0:T(128)S(1)} %copy-done.58, f32[16,512]{1,0:T(8,128)S(1)} %compare_select_fusion.bias_ref, f32[8,512]{1,0:T(8,128)S(1)} %get-tuple-element.263.lse_ref, f32[512,512]{1,0:T(8,128)S(1)} %get-tuple-element.237.o_ref, bf16[512,2048]{1,0:T(8,128)(2,1)S(1)} %copy-done.5, ...), custom_call_target="tpu_custom_call" | custom-call | flops 1048576 | bytes 65536 | tf_op jit(solution)/shard_map/attend_back/pallas_call | solution.py:233
  1017.3 51.0 %attend_back.7 = (f32[512,512]{1,0:T(8,128)S(1)}, bf16[4096,128]{1,0:T(8,128)(2,1)S(1)}) custom-call(s32[8]{0:T(128)S(1)} %copy-done.58, f32[16,512]{1,0:T(8,128)S(1)} %compare_select_fusion.bias_ref, f32[8,512]{1,0:T(8,128)S(1)} %get-tuple-element.272.lse_ref, f32[512,512]{1,0:T(8,128)S(1)} %copy-done.27, bf16[512,2048]{1,0:T(8,128)(2,1)S(1)} %copy-done.5, ...), custom_call_target="tpu_custom_call" | custom-call | flops 1048576 | bytes 65536 | tf_op jit(solution)/shard_map/attend_back/pallas_call | solution.py:233
  1133.4 13.5 %collective-permute-done.62 = bf16[512,128]{1,0:T(8,128)(2,1)S(1)} collective-permute-done((bf16[512,128]{1,0:T(8,128)(2,1)}, bf16[512,128]{1,0:T(8,128)(2,1)S(1)}, u32[]{:S(2)}, u32[]{:S(2)}) %collective-permute-start.62) | collective-permute-done | bytes 131104 | tf_op jit(solution)/shard_map/ppermute | solution.py:373
  1227.8 19.1 %fusion.18 = bf16[1,512,2048]{2,1,0:T(8,128)(2,1)} fusion(f32[512,2048]{1,0:T(8,128)S(1)} %copy-done.67, bf16[512,5632]{1,0:T(8,128)(2,1)} %copy-done.9, bf16[5632,2048]{1,0:T(8,128)(2,1)} %bitcast.204), kind=kOutput, calls=%fused_computation.76 | convolution fusion | flops 11813257216 | bytes 35127296 | tf_op jit(solution)/shard_map/dot_general | solution.py:26
  (666 shorter events, 637.6 us)
Async XLA Ops:
  7.2 92.5 %all-gather.7.cloned.1.call-start = ((), (), s32[]{:S(2)}) async-start(), calls=%async_computation.8 | async-start | bytes 3604480 | tf_op jit(solution)/shard_map/all_gather | solution.py:579
  7.9 209.5 %all-gather.9.cloned.1.call-start = ((), (), s32[]{:S(2)}) async-start(), calls=%async_computation.9 | async-start | bytes 3604480 | tf_op jit(solution)/shard_map/all_gather | solution.py:579
  134.3 215.6 %all-gather.11.cloned.1.call-start = ((), (), s32[]{:S(2)}) async-start(), calls=%async_computation.10 | async-start | bytes 1310720 | tf_op jit(solution)/shard_map/all_gather | solution.py:579
  301.0 88.0 %collective-permute-start.21 = (bf16[16,176,2048]{2,1,0:T(8,128)(2,1)}, bf16[16,176,2048]{2,1,0:T(8,128)(2,1)}, u32[]{:S(2)}, u32[]{:S(2)}) collective-permute-start(bf16[16,176,2048]{2,1,0:T(8,128)(2,1)} %pad_maximum_fusion.refs_0_), channel_id=1, source_target_pairs={{0,1},{1,0},{2,3},{3,2},{4,5},{5,4},{6,7},{7,6},{8,9},{9,8},{10,11... | collective-permute-start | bytes 34603016 | tf_op jit(solution)/shard_map/ppermute | solution.py:373
  305.9 83.2 %collective-permute-start.23 = (bf16[2,2,2,64,5632]{4,3,2,1,0:T(8,128)(2,1)}, bf16[2,2,2,64,5632]{4,3,2,1,0:T(8,128)(2,1)}, u32[]{:S(2)}, u32[]{:S(2)}) collective-permute-start(bf16[2,2,2,64,5632]{4,3,2,1,0:T(8,128)(2,1)} %pad_maximum_fusion.2), channel_id=1, source_target_pairs={{0,1},{1,0},{2,3},{3,2},{4,5},{5,4},{6,7},{7,6},{8,9},{9,8},{10,11... | collective-permute-start | bytes 17301512 | tf_op jit(solution)/shard_map/ppermute | solution.py:373
  306.4 768.2 %reduce-scatter.5.cloned.1.call-start = ((), (), s32[]{:S(2)}) async-start(), calls=%async_computation.4 | async-start | bytes 3604480 | tf_op jit(solution)/shard_map/reduce_scatter | solution.py:501
  306.5 82.6 %collective-permute-start.22 = (bf16[2,2,64,5632]{3,2,1,0:T(8,128)(2,1)}, bf16[2,2,64,5632]{3,2,1,0:T(8,128)(2,1)}, u32[]{:S(2)}, u32[]{:S(2)}) collective-permute-start(bf16[2,2,64,5632]{3,2,1,0:T(8,128)(2,1)} %collective-permute-done.20), channel_id=1, source_target_pairs={{0,8},{8,24},{24,16},{16,0},{1,9},{9,25},{25,17},{17,1},{2,10},{10... | collective-permute-start | bytes 8650760 | tf_op jit(solution)/shard_map/ppermute | solution.py:362
  391.6 111.3 %collective-permute-start.32 = (bf16[2,2,64,5632]{3,2,1,0:T(8,128)(2,1)}, bf16[2,2,64,5632]{3,2,1,0:T(8,128)(2,1)}, u32[]{:S(2)}, u32[]{:S(2)}) collective-permute-start(bf16[2,2,64,5632]{3,2,1,0:T(8,128)(2,1)} %collective-permute-done.22), channel_id=1, source_target_pairs={{0,8},{8,24},{24,16},{16,0},{1,9},{9,25},{25,17},{17,1},{2,10},{10... | collective-permute-start | bytes 8650760 | tf_op jit(solution)/shard_map/ppermute | solution.py:362
  412.6 90.3 %collective-permute-start.30 = (bf16[2,2,64,5632]{3,2,1,0:T(8,128)(2,1)}, bf16[2,2,64,5632]{3,2,1,0:T(8,128)(2,1)}, u32[]{:S(2)}, u32[]{:S(2)}) collective-permute-start(bf16[2,2,64,5632]{3,2,1,0:T(8,128)(2,1)} %pad_maximum_fusion.9), channel_id=1, source_target_pairs={{0,2},{1,3},{2,0},{3,1},{4,6},{5,7},{6,4},{7,5},{8,10},{9,11},{10,... | collective-permute-start | bytes 8650760 | tf_op jit(solution)/shard_map/ppermute | solution.py:373
  417.4 85.5 %collective-permute-start.31 = (bf16[2,2,64,5632]{3,2,1,0:T(8,128)(2,1)}, bf16[2,2,64,5632]{3,2,1,0:T(8,128)(2,1)}, u32[]{:S(2)}, u32[]{:S(2)}) collective-permute-start(bf16[2,2,64,5632]{3,2,1,0:T(8,128)(2,1)} %pad_maximum_fusion.10), channel_id=1, source_target_pairs={{0,4},{1,5},{2,6},{3,7},{4,0},{5,1},{6,2},{7,3},{8,12},{9,13},{10,... | collective-permute-start | bytes 8650760 | tf_op jit(solution)/shard_map/ppermute | solution.py:373
  419.8 78.5 %collective-permute-start.28 = (bf16[2,2,64,2048]{3,2,1,0:T(8,128)(2,1)}, bf16[2,2,64,2048]{3,2,1,0:T(8,128)(2,1)}, u32[]{:S(2)}, u32[]{:S(2)}) collective-permute-start(bf16[2,2,64,2048]{3,2,1,0:T(8,128)(2,1)} %pad_maximum_fusion.22), channel_id=1, source_target_pairs={{0,2},{1,3},{2,0},{3,1},{4,6},{5,7},{6,4},{7,5},{8,10},{9,11},{10,... | collective-permute-start | bytes 3145736 | tf_op jit(solution)/shard_map/ppermute | solution.py:373
  421.3 81.6 %collective-permute-start.29 = (bf16[2,2,64,2048]{3,2,1,0:T(8,128)(2,1)}, bf16[2,2,64,2048]{3,2,1,0:T(8,128)(2,1)}, u32[]{:S(2)}, u32[]{:S(2)}) collective-permute-start(bf16[2,2,64,2048]{3,2,1,0:T(8,128)(2,1)} %pad_maximum_fusion.23), channel_id=1, source_target_pairs={{0,4},{1,5},{2,6},{3,7},{4,0},{5,1},{6,2},{7,3},{8,12},{9,13},{10,... | collective-permute-start | bytes 3145736 | tf_op jit(solution)/shard_map/ppermute | solution.py:373
  513.1 79.2 %collective-permute-start.35 = (bf16[16,64,5632]{2,1,0:T(8,128)(2,1)}, bf16[16,64,5632]{2,1,0:T(8,128)(2,1)}, u32[]{:S(2)}, u32[]{:S(2)}) collective-permute-start(bf16[16,64,5632]{2,1,0:T(8,128)(2,1)} %pad_maximum_fusion.1.refs_0_), channel_id=1, source_target_pairs={{0,1},{1,0},{2,3},{3,2},{4,5},{5,4},{6,7},{7,6},{8,9},{9,8},{10,11... | collective-permute-start | bytes 34603016 | tf_op jit(solution)/shard_map/ppermute | solution.py:373
  663.9 74.8 %collective-permute-start.37 = (bf16[2816,2048]{1,0:T(8,128)(2,1)}, bf16[2816,2048]{1,0:T(8,128)(2,1)}, u32[]{:S(2)}, u32[]{:S(2)}) collective-permute-start(bf16[2816,2048]{1,0:T(8,128)(2,1)} %convolution_convert_fusion.1), channel_id=1, source_target_pairs={{0,1},{1,0},{2,3},{3,2},{4,5},{5,4},{6,7},{7,6},{8,9},{9,8},{10,11... | collective-permute-start | bytes 34603016 | tf_op jit(solution)/shard_map/ppermute | solution.py:373
  738.7 88.7 %collective-permute-start.39 = (bf16[256,5632]{1,0:T(8,128)(2,1)}, bf16[256,5632]{1,0:T(8,128)(2,1)}, u32[]{:S(2)}, u32[]{:S(2)}) collective-permute-start(bf16[256,5632]{1,0:T(8,128)(2,1)} %add_convert_fusion.18), channel_id=1, source_target_pairs={{0,2},{1,3},{2,0},{3,1},{4,6},{5,7},{6,4},{7,5},{8,10},{9,11},{10,... | collective-permute-start | bytes 8650760 | tf_op jit(solution)/shard_map/ppermute | solution.py:373
  739.0 88.4 %collective-permute-start.40 = (bf16[256,5632]{1,0:T(8,128)(2,1)}, bf16[256,5632]{1,0:T(8,128)(2,1)}, u32[]{:S(2)}, u32[]{:S(2)}) collective-permute-start(bf16[256,5632]{1,0:T(8,128)(2,1)} %add_convert_fusion.17), channel_id=1, source_target_pairs={{0,4},{1,5},{2,6},{3,7},{4,0},{5,1},{6,2},{7,3},{8,12},{9,13},{10,... | collective-permute-start | bytes 8650760 | tf_op jit(solution)/shard_map/ppermute | solution.py:373
  745.7 81.7 %collective-permute-start.41 = (bf16[704,2048]{1,0:T(8,128)(2,1)}, bf16[704,2048]{1,0:T(8,128)(2,1)}, u32[]{:S(2)}, u32[]{:S(2)}) collective-permute-start(bf16[704,2048]{1,0:T(8,128)(2,1)} %add_convert_fusion.16), channel_id=1, source_target_pairs={{0,8},{8,24},{24,16},{16,0},{1,9},{9,25},{25,17},{17,1},{2,10},{10... | collective-permute-start | bytes 8650760 | tf_op jit(solution)/shard_map/ppermute | solution.py:362
  768.6 139.0 %collective-permute-start.42 = (bf16[256,5632]{1,0:T(8,128)(2,1)}, bf16[256,5632]{1,0:T(8,128)(2,1)}, u32[]{:S(2)}, u32[]{:S(2)}) collective-permute-start(bf16[256,5632]{1,0:T(8,128)(2,1)} %add_convert_fusion.15), channel_id=1, source_target_pairs={{0,2},{1,3},{2,0},{3,1},{4,6},{5,7},{6,4},{7,5},{8,10},{9,11},{10,... | collective-permute-start | bytes 8650760 | tf_op jit(solution)/shard_map/ppermute | solution.py:373
  775.4 132.2 %collective-permute-start.43 = (bf16[256,5632]{1,0:T(8,128)(2,1)}, bf16[256,5632]{1,0:T(8,128)(2,1)}, u32[]{:S(2)}, u32[]{:S(2)}) collective-permute-start(bf16[256,5632]{1,0:T(8,128)(2,1)} %add_convert_fusion.14), channel_id=1, source_target_pairs={{0,4},{1,5},{2,6},{3,7},{4,0},{5,1},{6,2},{7,3},{8,12},{9,13},{10,... | collective-permute-start | bytes 8650760 | tf_op jit(solution)/shard_map/ppermute | solution.py:373
  912.0 77.1 %collective-permute-start.49 = (bf16[1024,2048]{1,0:T(8,128)(2,1)}, bf16[1024,2048]{1,0:T(8,128)(2,1)}, u32[]{:S(2)}, u32[]{:S(2)}) collective-permute-start(bf16[1024,2048]{1,0:T(8,128)(2,1)} %convolution_convert_fusion.4), channel_id=1, source_target_pairs={{0,1},{1,0},{2,3},{3,2},{4,5},{5,4},{6,7},{7,6},{8,9},{9,8},{10,11... | collective-permute-start | bytes 12582920 | tf_op jit(solution)/shard_map/ppermute | solution.py:373
  994.3 186.9 %reduce-scatter.7.cloned.1.call-start = ((), (), s32[]{:S(2)}) async-start(), calls=%async_computation.5 | async-start | bytes 3604480 | tf_op jit(solution)/shard_map/reduce_scatter | solution.py:501
  1000.4 74.2 %collective-permute-start.51 = (bf16[2048,384]{1,0:T(8,128)(2,1)S(1)}, bf16[2048,384]{1,0:T(8,128)(2,1)}, u32[]{:S(2)}, u32[]{:S(2)}) collective-permute-start(bf16[2048,384]{1,0:T(8,128)(2,1)S(1)} %slice.498), channel_id=1, source_target_pairs={{0,1},{1,0},{2,3},{3,2},{4,5},{5,4},{6,7},{7,6},{8,9},{9,8},{10,11... | collective-permute-start | bytes 4718600 | tf_op jit(solution)/shard_map/ppermute | solution.py:373
  1086.8 164.4 %reduce-scatter.9.cloned.1.call-start = ((), (), s32[]{:S(2)}) async-start(), calls=%async_computation.6 | async-start | bytes 1310720 | tf_op jit(solution)/shard_map/reduce_scatter | solution.py:501
  1132.2 150.8 %reduce-scatter.11.cloned.1.call-start = ((), (), s32[]{:S(2)}) async-start(), calls=%async_computation.7 | async-start | bytes 1310720 | tf_op jit(solution)/shard_map/reduce_scatter | solution.py:501
  (211 other events, 4064.8 us)
Sparse Core Ops, SparseCore 0:
  9.6 76.3 all-gather.6
  134.4 56.0 all-gather.8
  306.5 43.2 all-gather.10
  994.4 54.7 reduce-scatter.4
  1087.0 53.3 reduce-scatter.6
  1142.5 26.9 reduce-scatter.8
  1250.6 29.9 reduce-scatter.10

commit v11 on v8

--- a/solution.py
+++ b/solution.py
@@ -857,7 +857,7 @@
     grad_first = mm(query_grads, attn_all[:, :width], NT)
     grad_first = meet(grad_first, last_keys, keys_sum, query_sum, merge_sum)
     grad_first = meet(grad_first, last_keys, keys_sum, down_sum)
-    grad_first = meet(grad_first, last_keys)
+    grad_first = meet(grad_first, last_keys, query_sum, hold=(merge_sum,))
     wide = finish(keys_sum)
     dkv_parts = [wide[:, at : at + WIDE] for at in range(0, wide.shape[1], WIDE)]
     dkv_parts.append(finish(last_keys))
@@ -872,10 +872,10 @@
     input_grad = (grad_middle + grad_norm_one).astype(BF16).reshape(layer_in.shape)
     last.flight, input_grad = lax.optimization_barrier((last.flight, input_grad))
     input_grad = meet(input_grad, last, query_sum, up_sum, down_sum)
-    input_grad, hidden = meet((input_grad, hidden), last, query_sum)
+    input_grad, hidden = meet((input_grad, hidden), last)
     result = middle + mm(hidden, down_all, NN)
     layer_out = result.astype(BF16).reshape(layer_in.shape)
-    input_grad = meet(input_grad, last)
+    input_grad = meet(input_grad, last, query_sum)
     input_grad, layer_out = meet((input_grad, layer_out), last, merge_sum)
     while not last.done:
         input_grad = meet(input_grad, last)

time: 1250 us -> 1240 us (level)
    unnamed x329 -> x337, local copies, waits for them, and re-layouts: 40.3 us -> 45.4 us
  transfers between devices with their start and end apart: 83 -> 83, of which waited for: 26 -> 29; matrix products, arithmetic and copies ran while one was open for 32% -> 31% of each run, Pallas kernels for 30% -> 30%
where the time goes in v11:
time: 1240 us; the launch traced here: 1230 us
  Pallas kernels  391 us (32%)
  matrix products  291 us (23%)
  waiting for transfers between devices  241 us (19%)
  other arithmetic  130 us (10%)
  local copies, waits for them, and re-layouts  80 us (6%)
  starting transfers between devices  75.7 us (6%)
  between operations  17.3 us (1%)
    dot_general x41, matrix products, mm(): return lax.dot_general(left, right, dims, preferred_element_type=F32)  291 us
    pallas_call x4, Pallas kernels, attend_back(): pl.pallas_call(functools.partial(attend_back_kernel, which=group % 2, unr...  204 us
    ppermute x64, waiting for transfers between devices, next(): return lax.ppermute(values, 'ctx', pairs)  127 us
    pallas_call x4, Pallas kernels, attend(): pl.pallas_call(functools.partial(attend_kernel, which=group % 2, places=p...  103 us
    ppermute x12, waiting for transfers between devices, next(): return lax.ppermute(values, 'dp', list(zip(self.ring, around)))  99.3 us
    pallas_call x5, Pallas kernels, placed(): pl.pallas_call(functools.partial(place_kernel, sources=sources, slots=slo...  69.3 us
    ppermute x64, starting transfers between devices, next(): return lax.ppermute(values, 'ctx', pairs)  55.7 us
    unnamed x337, local copies, waits for them, and re-layouts  45.4 us
  transfers between devices with their start and end apart: 83, of which 29 were waited for; matrix products, arithmetic and copies ran while one was open for 31% of the time, Pallas kernels for 30%

profile of v11, /device:TPU:0, one launch (start us, length us, event | category | flops | bytes accessed | tf_op | source)
XLA Modules:
  0.0 1234.3 jit_solution(8435340761601870049)
XLA Ops:
  39.7 19.4 %collective-permute-done.2 = bf16[64,2688]{1,0:T(8,128)(2,1)S(1)} collective-permute-done((bf16[64,2688]{1,0:T(8,128)(2,1)}, bf16[64,2688]{1,0:T(8,128)(2,1)S(1)}, u32[]{:S(2)}, u32[]{:S(2)}) %collective-permute-start.2) | collective-permute-done | bytes 344096 | tf_op jit(solution)/shard_map/ppermute | solution.py:362
  65.5 19.5 %collective-permute-done.3 = bf16[64,2688]{1,0:T(8,128)(2,1)S(1)} collective-permute-done((bf16[64,2688]{1,0:T(8,128)(2,1)S(1)}, bf16[64,2688]{1,0:T(8,128)(2,1)S(1)}, u32[]{:S(2)}, u32[]{:S(2)}) %collective-permute-start.3) | collective-permute-done | bytes 344096 | tf_op jit(solution)/shard_map/ppermute | solution.py:362
  103.5 21.0 %collective-permute-done.8 = bf16[2,2,64,2688]{3,2,1,0:T(8,128)(2,1)S(1)} collective-permute-done((bf16[2,2,64,2688]{3,2,1,0:T(8,128)(2,1)S(1)}, bf16[2,2,64,2688]{3,2,1,0:T(8,128)(2,1)S(1)}, u32[]{:S(2)}, u32[]{:S(2)}) %collective-permute-start.8) | collective-permute-done | bytes 1376288 | tf_op jit(solution)/shard_map/ppermute | solution.py:373
  232.9 19.4 %collective-permute-done.18 = bf16[2,2,64,5632]{3,2,1,0:T(8,128)(2,1)} collective-permute-done((bf16[2,2,64,5632]{3,2,1,0:T(8,128)(2,1)S(1)}, bf16[2,2,64,5632]{3,2,1,0:T(8,128)(2,1)}, u32[]{:S(2)}, u32[]{:S(2)}) %collective-permute-start.18) | collective-permute-done | bytes 2883616 | tf_op jit(solution)/shard_map/ppermute | solution.py:362
  266.1 25.6 %attend.4 = (f32[512,512]{1,0:T(8,128)S(1)}, f32[8,512]{1,0:T(8,128)S(1)}) custom-call(f32[16,512]{1,0:T(8,128)S(1)} %compare_select_fusion.bias_ref, bf16[512,2048]{1,0:T(8,128)(2,1)S(1)} %copy-done.2, bf16[4096,256]{1,0:T(8,128)(2,1)S(1)} %bitcast.169, bf16[256,4096]{1,0:T(8,128)(2,1)S(1)} %copy-done.6), custom_call_target="tpu_custom_call" | custom-call | flops 1048576 | bytes 65536 | tf_op jit(solution)/shard_map/attend/pallas_call | solution.py:113
  292.7 25.8 %attend.5 = (f32[512,512]{1,0:T(8,128)S(1)}, f32[8,512]{1,0:T(8,128)S(1)}) custom-call(f32[16,512]{1,0:T(8,128)S(1)} %compare_select_fusion.bias_ref, bf16[512,2048]{1,0:T(8,128)(2,1)S(1)} %copy-done.2, bf16[4096,256]{1,0:T(8,128)(2,1)S(1)} %bitcast.170, bf16[256,4096]{1,0:T(8,128)(2,1)S(1)} %copy-done.6), custom_call_target="tpu_custom_call" | custom-call | flops 1048576 | bytes 65536 | tf_op jit(solution)/shard_map/attend/pallas_call | solution.py:113
  319.5 15.6 %collective-permute-done.21 = bf16[2,2,64,5632]{3,2,1,0:T(8,128)(2,1)} collective-permute-done((bf16[2,2,64,5632]{3,2,1,0:T(8,128)(2,1)}, bf16[2,2,64,5632]{3,2,1,0:T(8,128)(2,1)}, u32[]{:S(2)}, u32[]{:S(2)}) %collective-permute-start.21) | collective-permute-done | bytes 2883616 | tf_op jit(solution)/shard_map/ppermute | solution.py:362
  349.1 26.1 %attend.6 = (f32[512,512]{1,0:T(8,128)S(1)}, f32[8,512]{1,0:T(8,128)S(1)}) custom-call(f32[16,512]{1,0:T(8,128)S(1)} %compare_select_fusion.bias_ref, bf16[512,2048]{1,0:T(8,128)(2,1)S(1)} %copy-done.3, bf16[4096,256]{1,0:T(8,128)(2,1)S(1)} %bitcast.171, bf16[256,4096]{1,0:T(8,128)(2,1)S(1)} %copy-done.7), custom_call_target="tpu_custom_call" | custom-call | flops 1048576 | bytes 65536 | tf_op jit(solution)/shard_map/attend/pallas_call | solution.py:113
  386.0 15.0 %placed.6 = bf16[32,176,2048]{2,1,0:T(8,128)(2,1)} custom-call(s32[32]{0:T(128)S(1)} %get-tuple-element.367.order_ref, bf16[16,176,2048]{2,1,0:T(8,128)(2,1)S(1)} %pad_maximum_fusion.refs_0_, bf16[16,176,2048]{2,1,0:T(8,128)(2,1)} %collective-permute-done.24.refs_1_), custom_call_target="tpu_custom_call" | custom-call | bytes 46137344 | tf_op jit(solution)/shard_map/placed/pallas_call | solution.py:550
  414.5 19.9 %fusion.127 = f32[512,5632]{1,0:T(8,128)} fusion(bf16[512,2048]{1,0:T(8,128)(2,1)} %bitcast.216, bf16[5632,2048]{1,0:T(8,128)(2,1)} %bitcast.200), kind=kOutput, calls=%fused_computation.301 | convolution fusion | flops 11811160064 | bytes 36700160 | tf_op jit(solution)/shard_map/dot_general | solution.py:26
  437.6 25.5 %attend.7 = (f32[512,512]{1,0:T(8,128)S(1)}, f32[8,512]{1,0:T(8,128)S(1)}) custom-call(f32[16,512]{1,0:T(8,128)S(1)} %compare_select_fusion.bias_ref, bf16[512,2048]{1,0:T(8,128)(2,1)S(1)} %copy-done.4, bf16[4096,256]{1,0:T(8,128)(2,1)S(1)} %bitcast.172, bf16[256,4096]{1,0:T(8,128)(2,1)S(1)} %copy-done.8), custom_call_target="tpu_custom_call" | custom-call | flops 1048576 | bytes 65536 | tf_op jit(solution)/shard_map/attend/pallas_call | solution.py:113
  523.5 17.4 %placed.8 = bf16[32,64,5632]{2,1,0:T(8,128)(2,1)} custom-call(s32[32]{0:T(128)S(1)} %get-tuple-element.365.order_ref, bf16[4,64,5632]{2,1,0:T(8,128)(2,1)S(1)} %bitcast.184, bf16[4,64,5632]{2,1,0:T(8,128)(2,1)} %bitcast.78.refs_1_, bf16[4,64,5632]{2,1,0:T(8,128)(2,1)} %bitcast.79.refs_2_, bf16[4,64,5632]{2,1,0:T(8,128)(2,1)} %bitcast.80.refs_3_, ...), custom_call_target="tpu_custom_call" | custom-call | bytes 46137344 | tf_op jit(solution)/shard_map/placed/pallas_call | solution.py:550
  540.9 19.0 %fusion.128 = f32[512,5632]{1,0:T(8,128)} fusion(bf16[512,2048]{1,0:T(8,128)(2,1)S(1)} %multiply_convert_fusion.3.x_ref, bf16[2048,5632]{1,0:T(8,128)(2,1)} %bitcast.202), kind=kOutput, calls=%fused_computation.302 | convolution fusion | flops 11811160064 | bytes 36700160 | tf_op jit(solution)/shard_map/dot_general | solution.py:26
  560.0 17.4 %placed.9 = bf16[32,64,5632]{2,1,0:T(8,128)(2,1)} custom-call(s32[32]{0:T(128)S(1)} %get-tuple-element.367.order_ref, bf16[16,64,5632]{2,1,0:T(8,128)(2,1)} %pad_maximum_fusion.1.refs_0_, bf16[16,64,5632]{2,1,0:T(8,128)(2,1)} %collective-permute-done.35.refs_1_), custom_call_target="tpu_custom_call" | custom-call | bytes 46137344 | tf_op jit(solution)/shard_map/placed/pallas_call | solution.py:550
  577.4 29.2 %multiply_convert_fusion = (bf16[512,5632]{1,0:T(8,128)(2,1)}, bf16[512,5632]{1,0:T(8,128)(2,1)}, bf16[512,5632]{1,0:T(8,128)(2,1)}) fusion(f32[512,5632]{1,0:T(8,128)} %fusion.127, f32[512,5632]{1,0:T(8,128)} %fusion.128, bf16[512,2048]{1,0:T(8,128)(2,1)} %copy-done.16, bf16[2048,5632]{1,0:T(8,128)(2,1)} %bitcast.204), kind=kOutput, calls=%fused_computation.3 | convolution fusion | flops 11854413824 | bytes 65536000 | tf_op jit(solution)/shard_map/dot_general | solution.py:26
  638.8 19.6 %fusion.129 = f32[512,2048]{1,0:T(8,128)} fusion(bf16[512,5632]{1,0:T(8,128)(2,1)} %get-tuple-element.245, bf16[2048,5632]{1,0:T(8,128)(2,1)} %bitcast.205), kind=kOutput, calls=%fused_computation.303 | convolution fusion | flops 11811160064 | bytes 33030144 | tf_op jit(solution)/shard_map/dot_general | solution.py:26
  658.4 19.8 %multiply_reduce_fusion.1 = (f32[512]{0:T(512)S(1)}, bf16[2048]{0:T(1024)(128)(2,1)S(1)}, f32[512,2048]{1,0:T(8,128)}) fusion(f32[512,2048]{1,0:T(8,128)} %copy-done.66, f32[2048]{0:T(1024)S(1)} %bitcast.242, f32[512]{0:T(512)S(1)} %copy-done.131, f32[512,2048]{1,0:T(8,128)} %fusion.129, bf16[512,5632]{1,0:T(8,128)(2,1)} %get-tuple-element.248, ...), kind=kOutput, calls=%fused_computation.56 | convolution fusion | flops 11818498048 | bytes 41435136 | tf_op jit(solution)/shard_map/dot_general | solution.py:26
  739.6 50.8 %attend_back.4 = (f32[512,512]{1,0:T(8,128)S(1)}, bf16[4096,128]{1,0:T(8,128)(2,1)S(1)}) custom-call(s32[8]{0:T(128)S(1)} %copy-done.61, f32[16,512]{1,0:T(8,128)S(1)} %compare_select_fusion.bias_ref, f32[8,512]{1,0:T(8,128)S(1)} %get-tuple-element.199.lse_ref, f32[512,512]{1,0:T(8,128)S(1)} %copy-done.30, bf16[512,2048]{1,0:T(8,128)(2,1)S(1)} %copy-done.5, ...), custom_call_target="tpu_custom_call" | custom-call | flops 1048576 | bytes 65536 | tf_op jit(solution)/shard_map/attend_back/pallas_call | solution.py:233
  816.5 51.3 %attend_back.5 = (f32[512,512]{1,0:T(8,128)S(1)}, bf16[4096,128]{1,0:T(8,128)(2,1)S(1)}) custom-call(s32[8]{0:T(128)S(1)} %copy-done.61, f32[16,512]{1,0:T(8,128)S(1)} %compare_select_fusion.bias_ref, f32[8,512]{1,0:T(8,128)S(1)} %get-tuple-element.252.lse_ref, f32[512,512]{1,0:T(8,128)S(1)} %copy-done.28, bf16[512,2048]{1,0:T(8,128)(2,1)S(1)} %copy-done.5, ...), custom_call_target="tpu_custom_call" | custom-call | flops 1048576 | bytes 65536 | tf_op jit(solution)/shard_map/attend_back/pallas_call | solution.py:233
  895.7 50.8 %attend_back.6 = (f32[512,512]{1,0:T(8,128)S(1)}, bf16[4096,128]{1,0:T(8,128)(2,1)S(1)}) custom-call(s32[8]{0:T(128)S(1)} %copy-done.61, f32[16,512]{1,0:T(8,128)S(1)} %compare_select_fusion.bias_ref, f32[8,512]{1,0:T(8,128)S(1)} %get-tuple-element.258.lse_ref, f32[512,512]{1,0:T(8,128)S(1)} %copy-done.26, bf16[512,2048]{1,0:T(8,128)(2,1)S(1)} %copy-done.5, ...), custom_call_target="tpu_custom_call" | custom-call | flops 1048576 | bytes 65536 | tf_op jit(solution)/shard_map/attend_back/pallas_call | solution.py:233
  976.0 50.8 %attend_back.7 = (f32[512,512]{1,0:T(8,128)S(1)}, bf16[4096,128]{1,0:T(8,128)(2,1)S(1)}) custom-call(s32[8]{0:T(128)S(1)} %copy-done.61, f32[16,512]{1,0:T(8,128)S(1)} %copy-done.37, f32[8,512]{1,0:T(8,128)S(1)} %get-tuple-element.267.lse_ref, f32[512,512]{1,0:T(8,128)S(1)} %get-tuple-element.231.o_ref, bf16[512,2048]{1,0:T(8,128)(2,1)S(1)} %copy-done.5, ...), custom_call_target="tpu_custom_call" | custom-call | flops 1048576 | bytes 65536 | tf_op jit(solution)/shard_map/attend_back/pallas_call | solution.py:233
  1069.4 13.7 %collective-permute-done.59 = bf16[128,2048]{1,0:T(8,128)(2,1)S(1)} collective-permute-done((bf16[128,2048]{1,0:T(8,128)(2,1)S(1)}, bf16[128,2048]{1,0:T(8,128)(2,1)S(1)}, u32[]{:S(2)}, u32[]{:S(2)}) %collective-permute-start.59) | collective-permute-done | bytes 524320 | tf_op jit(solution)/shard_map/ppermute | solution.py:373
  1111.2 19.4 %collective-permute-done.62 = bf16[512,128]{1,0:T(8,128)(2,1)S(1)} collective-permute-done((bf16[512,128]{1,0:T(8,128)(2,1)S(1)}, bf16[512,128]{1,0:T(8,128)(2,1)S(1)}, u32[]{:S(2)}, u32[]{:S(2)}) %collective-permute-start.62) | collective-permute-done | bytes 131104 | tf_op jit(solution)/shard_map/ppermute | solution.py:373
  1185.5 19.8 %fusion.18 = bf16[1,512,2048]{2,1,0:T(8,128)(2,1)} fusion(f32[512,2048]{1,0:T(8,128)} %copy-done.66, bf16[512,5632]{1,0:T(8,128)(2,1)} %get-tuple-element.321.x_ref, bf16[5632,2048]{1,0:T(8,128)(2,1)} %bitcast.201), kind=kOutput, calls=%fused_computation.76 | convolution fusion | flops 11813257216 | bytes 35127296 | tf_op jit(solution)/shard_map/dot_general | solution.py:26
  (688 shorter events, 605.1 us)
Async XLA Ops:
  7.2 94.2 %all-gather.7.cloned.1.call-start = ((), (), s32[]{:S(2)}) async-start(), calls=%async_computation.8 | async-start | bytes 3604480 | tf_op jit(solution)/shard_map/all_gather | solution.py:579
  7.9 224.9 %all-gather.9.cloned.1.call-start = ((), (), s32[]{:S(2)}) async-start(), calls=%async_computation.9 | async-start | bytes 3604480 | tf_op jit(solution)/shard_map/all_gather | solution.py:579
  131.3 188.1 %all-gather.11.cloned.1.call-start = ((), (), s32[]{:S(2)}) async-start(), calls=%async_computation.10 | async-start | bytes 1310720 | tf_op jit(solution)/shard_map/all_gather | solution.py:579
  140.1 112.1 %collective-permute-start.18 = (bf16[2,2,64,5632]{3,2,1,0:T(8,128)(2,1)S(1)}, bf16[2,2,64,5632]{3,2,1,0:T(8,128)(2,1)}, u32[]{:S(2)}, u32[]{:S(2)}) collective-permute-start(bf16[2,2,64,5632]{3,2,1,0:T(8,128)(2,1)S(1)} %get-tuple-element.380), channel_id=1, source_target_pairs={{0,8},{8,24},{24,16},{16,0},{1,9},{9,25},{25,17},{17,1},{2,10},{10... | collective-permute-start | bytes 8650760 | tf_op jit(solution)/shard_map/ppermute | solution.py:362
  213.8 816.2 %reduce-scatter.5.cloned.1.call-start = ((), (), s32[]{:S(2)}) async-start(), calls=%async_computation.4 | async-start | bytes 3604480 | tf_op jit(solution)/shard_map/reduce_scatter | solution.py:501
  217.7 101.8 %collective-permute-start.19 = (bf16[2,2,176,2048]{3,2,1,0:T(8,128)(2,1)}, bf16[2,2,176,2048]{3,2,1,0:T(8,128)(2,1)}, u32[]{:S(2)}, u32[]{:S(2)}) collective-permute-start(bf16[2,2,176,2048]{3,2,1,0:T(8,128)(2,1)} %pad_maximum_fusion.7), channel_id=1, source_target_pairs={{0,2},{1,3},{2,0},{3,1},{4,6},{5,7},{6,4},{7,5},{8,10},{9,11},{10,... | collective-permute-start | bytes 8650760 | tf_op jit(solution)/shard_map/ppermute | solution.py:373
  221.3 98.2 %collective-permute-start.20 = (bf16[2,2,176,2048]{3,2,1,0:T(8,128)(2,1)}, bf16[2,2,176,2048]{3,2,1,0:T(8,128)(2,1)}, u32[]{:S(2)}, u32[]{:S(2)}) collective-permute-start(bf16[2,2,176,2048]{3,2,1,0:T(8,128)(2,1)} %pad_maximum_fusion.8), channel_id=1, source_target_pairs={{0,4},{1,5},{2,6},{3,7},{4,0},{5,1},{6,2},{7,3},{8,12},{9,13},{10,... | collective-permute-start | bytes 8650760 | tf_op jit(solution)/shard_map/ppermute | solution.py:373
  252.2 82.9 %collective-permute-start.21 = (bf16[2,2,64,5632]{3,2,1,0:T(8,128)(2,1)}, bf16[2,2,64,5632]{3,2,1,0:T(8,128)(2,1)}, u32[]{:S(2)}, u32[]{:S(2)}) collective-permute-start(bf16[2,2,64,5632]{3,2,1,0:T(8,128)(2,1)} %collective-permute-done.18), channel_id=1, source_target_pairs={{0,8},{8,24},{24,16},{16,0},{1,9},{9,25},{25,17},{17,1},{2,10},{10... | collective-permute-start | bytes 8650760 | tf_op jit(solution)/shard_map/ppermute | solution.py:362
  347.0 116.1 %collective-permute-start.32 = (bf16[2,2,2,64,5632]{4,3,2,1,0:T(8,128)(2,1)}, bf16[2,2,2,64,5632]{4,3,2,1,0:T(8,128)(2,1)}, u32[]{:S(2)}, u32[]{:S(2)}) collective-permute-start(bf16[2,2,2,64,5632]{4,3,2,1,0:T(8,128)(2,1)} %pad_maximum_fusion.2), channel_id=1, source_target_pairs={{0,1},{1,0},{2,3},{3,2},{4,5},{5,4},{6,7},{7,6},{8,9},{9,8},{10,11... | collective-permute-start | bytes 17301512 | tf_op jit(solution)/shard_map/ppermute | solution.py:373
  378.8 91.7 %collective-permute-start.29 = (bf16[2,2,64,5632]{3,2,1,0:T(8,128)(2,1)}, bf16[2,2,64,5632]{3,2,1,0:T(8,128)(2,1)}, u32[]{:S(2)}, u32[]{:S(2)}) collective-permute-start(bf16[2,2,64,5632]{3,2,1,0:T(8,128)(2,1)} %pad_maximum_fusion.9), channel_id=1, source_target_pairs={{0,2},{1,3},{2,0},{3,1},{4,6},{5,7},{6,4},{7,5},{8,10},{9,11},{10,... | collective-permute-start | bytes 8650760 | tf_op jit(solution)/shard_map/ppermute | solution.py:373
  384.0 86.4 %collective-permute-start.30 = (bf16[2,2,64,5632]{3,2,1,0:T(8,128)(2,1)}, bf16[2,2,64,5632]{3,2,1,0:T(8,128)(2,1)}, u32[]{:S(2)}, u32[]{:S(2)}) collective-permute-start(bf16[2,2,64,5632]{3,2,1,0:T(8,128)(2,1)} %pad_maximum_fusion.10), channel_id=1, source_target_pairs={{0,4},{1,5},{2,6},{3,7},{4,0},{5,1},{6,2},{7,3},{8,12},{9,13},{10,... | collective-permute-start | bytes 8650760 | tf_op jit(solution)/shard_map/ppermute | solution.py:373
  385.8 80.2 %collective-permute-start.27 = (bf16[2,2,64,2048]{3,2,1,0:T(8,128)(2,1)}, bf16[2,2,64,2048]{3,2,1,0:T(8,128)(2,1)}, u32[]{:S(2)}, u32[]{:S(2)}) collective-permute-start(bf16[2,2,64,2048]{3,2,1,0:T(8,128)(2,1)} %pad_maximum_fusion.22), channel_id=1, source_target_pairs={{0,2},{1,3},{2,0},{3,1},{4,6},{5,7},{6,4},{7,5},{8,10},{9,11},{10,... | collective-permute-start | bytes 3145736 | tf_op jit(solution)/shard_map/ppermute | solution.py:373
  480.7 79.3 %collective-permute-start.35 = (bf16[16,64,5632]{2,1,0:T(8,128)(2,1)}, bf16[16,64,5632]{2,1,0:T(8,128)(2,1)}, u32[]{:S(2)}, u32[]{:S(2)}) collective-permute-start(bf16[16,64,5632]{2,1,0:T(8,128)(2,1)} %pad_maximum_fusion.1.refs_0_), channel_id=1, source_target_pairs={{0,1},{1,0},{2,3},{3,2},{4,5},{5,4},{6,7},{7,6},{8,9},{9,8},{10,11... | collective-permute-start | bytes 34603016 | tf_op jit(solution)/shard_map/ppermute | solution.py:373
  629.2 75.0 %collective-permute-start.37 = (bf16[2816,2048]{1,0:T(8,128)(2,1)}, bf16[2816,2048]{1,0:T(8,128)(2,1)}, u32[]{:S(2)}, u32[]{:S(2)}) collective-permute-start(bf16[2816,2048]{1,0:T(8,128)(2,1)} %convolution_convert_fusion.1), channel_id=1, source_target_pairs={{0,1},{1,0},{2,3},{3,2},{4,5},{5,4},{6,7},{7,6},{8,9},{9,8},{10,11... | collective-permute-start | bytes 34603016 | tf_op jit(solution)/shard_map/ppermute | solution.py:373
  704.2 86.2 %collective-permute-start.39 = (bf16[256,5632]{1,0:T(8,128)(2,1)}, bf16[256,5632]{1,0:T(8,128)(2,1)}, u32[]{:S(2)}, u32[]{:S(2)}) collective-permute-start(bf16[256,5632]{1,0:T(8,128)(2,1)} %add_convert_fusion.18), channel_id=1, source_target_pairs={{0,2},{1,3},{2,0},{3,1},{4,6},{5,7},{6,4},{7,5},{8,10},{9,11},{10,... | collective-permute-start | bytes 8650760 | tf_op jit(solution)/shard_map/ppermute | solution.py:373
  704.6 85.8 %collective-permute-start.40 = (bf16[256,5632]{1,0:T(8,128)(2,1)}, bf16[256,5632]{1,0:T(8,128)(2,1)}, u32[]{:S(2)}, u32[]{:S(2)}) collective-permute-start(bf16[256,5632]{1,0:T(8,128)(2,1)} %add_convert_fusion.17), channel_id=1, source_target_pairs={{0,4},{1,5},{2,6},{3,7},{4,0},{5,1},{6,2},{7,3},{8,12},{9,13},{10,... | collective-permute-start | bytes 8650760 | tf_op jit(solution)/shard_map/ppermute | solution.py:373
  711.4 79.1 %collective-permute-start.41 = (bf16[704,2048]{1,0:T(8,128)(2,1)}, bf16[704,2048]{1,0:T(8,128)(2,1)}, u32[]{:S(2)}, u32[]{:S(2)}) collective-permute-start(bf16[704,2048]{1,0:T(8,128)(2,1)} %add_convert_fusion.16), channel_id=1, source_target_pairs={{0,8},{8,24},{24,16},{16,0},{1,9},{9,25},{25,17},{17,1},{2,10},{10... | collective-permute-start | bytes 8650760 | tf_op jit(solution)/shard_map/ppermute | solution.py:362
  732.3 135.4 %collective-permute-start.42 = (bf16[256,5632]{1,0:T(8,128)(2,1)}, bf16[256,5632]{1,0:T(8,128)(2,1)}, u32[]{:S(2)}, u32[]{:S(2)}) collective-permute-start(bf16[256,5632]{1,0:T(8,128)(2,1)} %add_convert_fusion.15), channel_id=1, source_target_pairs={{0,2},{1,3},{2,0},{3,1},{4,6},{5,7},{6,4},{7,5},{8,10},{9,11},{10,... | collective-permute-start | bytes 8650760 | tf_op jit(solution)/shard_map/ppermute | solution.py:373
  738.0 129.8 %collective-permute-start.43 = (bf16[256,5632]{1,0:T(8,128)(2,1)}, bf16[256,5632]{1,0:T(8,128)(2,1)}, u32[]{:S(2)}, u32[]{:S(2)}) collective-permute-start(bf16[256,5632]{1,0:T(8,128)(2,1)} %add_convert_fusion.14), channel_id=1, source_target_pairs={{0,4},{1,5},{2,6},{3,7},{4,0},{5,1},{6,2},{7,3},{8,12},{9,13},{10,... | collective-permute-start | bytes 8650760 | tf_op jit(solution)/shard_map/ppermute | solution.py:373
  872.3 77.2 %collective-permute-start.49 = (bf16[1024,2048]{1,0:T(8,128)(2,1)}, bf16[1024,2048]{1,0:T(8,128)(2,1)}, u32[]{:S(2)}, u32[]{:S(2)}) collective-permute-start(bf16[1024,2048]{1,0:T(8,128)(2,1)} %convolution_convert_fusion.4), channel_id=1, source_target_pairs={{0,1},{1,0},{2,3},{3,2},{4,5},{5,4},{6,7},{7,6},{8,9},{9,8},{10,11... | collective-permute-start | bytes 12582920 | tf_op jit(solution)/shard_map/ppermute | solution.py:373
  953.6 177.1 %reduce-scatter.7.cloned.1.call-start = ((), (), s32[]{:S(2)}) async-start(), calls=%async_computation.5 | async-start | bytes 1310720 | tf_op jit(solution)/shard_map/reduce_scatter | solution.py:501
  959.0 71.1 %collective-permute-start.51 = (bf16[2048,384]{1,0:T(8,128)(2,1)S(1)}, bf16[2048,384]{1,0:T(8,128)(2,1)}, u32[]{:S(2)}, u32[]{:S(2)}) collective-permute-start(bf16[2048,384]{1,0:T(8,128)(2,1)S(1)} %slice.498), channel_id=1, source_target_pairs={{0,1},{1,0},{2,3},{3,2},{4,5},{5,4},{6,7},{7,6},{8,9},{9,8},{10,11... | collective-permute-start | bytes 4718600 | tf_op jit(solution)/shard_map/ppermute | solution.py:373
  1085.0 83.3 %reduce-scatter.9.cloned.1.call-start = ((), (), s32[]{:S(2)}) async-start(), calls=%async_computation.6 | async-start | bytes 3604480 | tf_op jit(solution)/shard_map/reduce_scatter | solution.py:501
  1089.2 116.2 %reduce-scatter.11.cloned.1.call-start = ((), (), s32[]{:S(2)}) async-start(), calls=%async_computation.7 | async-start | bytes 1310720 | tf_op jit(solution)/shard_map/reduce_scatter | solution.py:501
  (222 other events, 4713.8 us)
Sparse Core Ops, SparseCore 0:
  9.6 76.3 all-gather.6
  131.5 101.3 all-gather.8
  234.4 61.2 all-gather.10
  953.7 54.9 reduce-scatter.4
  1085.2 25.9 reduce-scatter.6
  1113.5 54.8 reduce-scatter.8
  1177.4 25.1 reduce-scatter.10
